TPU v7x, 32 devices: a whole 2x2x4 slice. The times are simulated.
32 devices in a mesh: row: 4 (over y, x), col: 8 (over z, core).
Axes of the slice: x: 2, y: 2, z: 4, core: 2. Of those that a mesh axis runs over, the one named last changes fastest.
Arguments:
- object_field: float32 [2, 2048, 4096], P(None, 'row', 'col'), may hold values from -6 to 6
- probe_field: float32 [2, 128, 128], replicated, may hold values from -1 to 1
- amplitudes: float32 [96, 128, 1024], P('row', None, 'col'), may hold values from 0 to 2
- positions: int32 [4, 8, 2, 24], P('row', 'col'), may hold values from -32 to 416
- counts: int32 [4, 8], P('row', 'col'), may hold values from 8 to 24, as said below
Outputs:
- estimate: float32 [2, 2048, 4096], P(None, 'row', 'col')
- correction: float32 [2, 2048, 4096], P(None, 'row', 'col')
Inputs may be any that keep to these rules, and one draw needn't show every extreme that they name: `counts`: between 8 and 24 live slots per tile; some tile has exactly 24 and some exactly 8; slots at or beyond a tile's count carry data that is not used.
All inputs are finite; a program needn't handle non-finite values.
Results may differ from a plain program's by a relative error of at most 0.0001.
Values sent between devices are 32-bit elements; how exact they have to be, the bound alone decides.
No kernel may reach another device: no remote copies, remote signals or barrier semaphores. Data moves between devices by JAX's collectives and lax.ppermute only.
A program may use at most 128 MiB of HBM per device.

v0:
```python
import jax
import jax.numpy as jnp
from jax import lax
from jax.sharding import PartitionSpec as P

BORDER = 32
ITERS = 2


smoothing = 0.5
step_gain = 0.5
highest = lax.Precision.HIGHEST


def extended_2(cells, sides, width):
    for axis, dim in sides:
        count = lax.axis_size(axis)
        ends = count - 1
        head = lax.slice_in_dim(cells, 0, width, axis=dim)
        tail = lax.slice_in_dim(cells, cells.shape[dim] - width, cells.shape[dim], axis=dim)
        cells = jnp.concatenate(
            [
                lax.ppermute(tail, axis, [(i, (i + 1) % count) for i in range(ends)]),
                cells,
                lax.ppermute(head, axis, [((i + 1) % count, i) for i in range(ends)]),
            ],
            axis=dim,
        )
    return cells


def dft_tables(length):
    counter = jnp.arange(length, dtype=jnp.int32)
    product = counter[:, None] * counter[None, :] % length
    angles = 2.0 * jnp.pi / length * product.astype(jnp.float32)
    factor = 1.0 / jnp.sqrt(jnp.float32(length))
    return (jnp.cos(angles) * factor, -jnp.sin(angles) * factor)


def transform(real_part, imag_part, table_real, table_imag):
    left_real = jnp.einsum("kp,spq->skq", table_real, real_part, precision=highest) - jnp.einsum(
        "kp,spq->skq", table_imag, imag_part, precision=highest
    )
    left_imag = jnp.einsum("kp,spq->skq", table_real, imag_part, precision=highest) + jnp.einsum(
        "kp,spq->skq", table_imag, real_part, precision=highest
    )
    right_real = jnp.einsum("spq,qk->spk", left_real, table_real, precision=highest) - jnp.einsum(
        "spq,qk->spk", left_imag, table_imag, precision=highest
    )
    right_imag = jnp.einsum("spq,qk->spk", left_real, table_imag, precision=highest) + jnp.einsum(
        "spq,qk->spk", left_imag, table_real, precision=highest
    )
    return (right_real, right_imag)


def probe_gradient(patch_real, patch_imag, probe_field, amplitude, table_real, table_imag):
    probe_real = probe_field[0]
    probe_imag = probe_field[1]
    exit_real = probe_real * patch_real - probe_imag * patch_imag
    exit_imag = probe_real * patch_imag + probe_imag * patch_real
    wave_real, wave_imag = transform(exit_real, exit_imag, table_real, table_imag)
    modulus = jnp.sqrt(wave_real * wave_real + wave_imag * wave_imag + smoothing)
    shrink = amplitude / modulus - 1.0
    back_real, back_imag = transform(
        wave_real * shrink, wave_imag * shrink, table_real, -table_imag
    )
    grad_real = probe_real * back_real + probe_imag * back_imag
    grad_imag = probe_real * back_imag - probe_imag * back_real
    return (grad_real, grad_imag)


def on_device(object_field, probe_field, amplitudes, positions, counts):
    tile_size = object_field.shape[1]
    probe_size = probe_field.shape[1]
    slot_total = amplitudes.shape[0]
    extent = tile_size + 2 * BORDER
    table_real, table_imag = dft_tables(probe_size)
    step_rate = step_gain / (
        jnp.max(probe_field[0] * probe_field[0] + probe_field[1] * probe_field[1]) + 1e-06
    )
    row_start = positions[0, 0, 0] + BORDER
    col_start = positions[0, 0, 1] + BORDER
    live_count = counts[0, 0]
    zero_index = jnp.zeros((), jnp.int32)
    band_width = 2 * BORDER
    row_cells = lax.axis_index("row") * tile_size + jnp.arange(extent, dtype=jnp.int32) - BORDER
    col_cells = lax.axis_index("col") * tile_size + jnp.arange(extent, dtype=jnp.int32) - BORDER
    inside_rows = (row_cells >= 0) & (row_cells < tile_size * lax.axis_size("row"))
    inside_cols = (col_cells >= 0) & (col_cells < tile_size * lax.axis_size("col"))
    grid_mask = (inside_rows[:, None] & inside_cols[None, :]).astype(jnp.float32)
    wide_object = extended_2(object_field, (("row", 1), ("col", 2)), BORDER)
    wide_correction = jnp.zeros((2, extent, extent), jnp.float32)
    for iteration in range(ITERS):
        empty_sum = jnp.zeros((2, extent, extent), jnp.float32)
        extended = wide_object + wide_correction

        def cut_patch(start_row, start_col):
            return lax.dynamic_slice(
                extended, (zero_index, start_row, start_col), (2, probe_size, probe_size)
            )

        patches = jax.vmap(cut_patch)(row_start, col_start)
        grad_real, grad_imag = probe_gradient(
            patches[:, 0], patches[:, 1], probe_field, amplitudes, table_real, table_imag
        )
        live_mask = (jnp.arange(slot_total, dtype=jnp.int32) < live_count).astype(jnp.float32)[
            :, None, None
        ]
        gradient = jnp.stack([grad_real * live_mask, grad_imag * live_mask], axis=1)

        def accumulate(slot_index, partial_value):
            corner = (zero_index, row_start[slot_index], col_start[slot_index])
            current = lax.dynamic_slice(partial_value, corner, (2, probe_size, probe_size))
            return lax.dynamic_update_slice(partial_value, current + gradient[slot_index], corner)

        gradient_sum = lax.fori_loop(0, slot_total, accumulate, empty_sum)
        framed = extended_2(gradient_sum, (("row", 1), ("col", 2)), band_width)
        rows_done = framed[:, band_width : band_width + extent, :]
        rows_done = rows_done.at[:, 0:band_width, :].add(framed[:, 0:band_width, :])
        rows_done = rows_done.at[:, extent - band_width :, :].add(
            framed[:, extent + band_width :, :]
        )
        full_sum = rows_done[:, :, band_width : band_width + extent]
        full_sum = full_sum.at[:, :, 0:band_width].add(rows_done[:, :, 0:band_width])
        full_sum = full_sum.at[:, :, extent - band_width :].add(
            rows_done[:, :, extent + band_width :]
        )
        wide_correction = wide_correction + step_rate * (full_sum * grid_mask)
    correction = wide_correction[:, BORDER : BORDER + tile_size, BORDER : BORDER + tile_size]
    return (object_field + correction, correction)


def solution(mesh):
    placed = (
        P(None, "row", "col"),
        P(),
        P("row", None, "col"),
        P("row", "col", None, None),
        P("row", "col"),
    )
    return jax.shard_map(
        on_device,
        mesh=mesh,
        in_specs=placed,
        out_specs=(P(None, "row", "col"), P(None, "row", "col")),
        check_vma=False,
    )
```

profile of v0, /device:TPU:1, one launch (start us, length us, event | category | flops | bytes accessed | tf_op | source)
XLA Modules:
  0.0 867.3 jit_solution(15857554206058394676)
XLA Ops:
  2.8 4.1 collective-permute-start
  8.9 8.5 collective-permute-done
  17.5 13.2 %collective-permute-done.1 = f32[2,32,512]{1,2,0:T(8,128)S(1)} collective-permute-done((f32[2,32,512]{1,2,0:T(8,128)S(1)}, f32[2,32,512]{1,2,0:T(8,128)S(1)}, u32[]{:S(2)}, u32[]{:S(2)}) %collective-permute-start.1) | collective-permute-done | bytes 131104 | tf_op jit(solution)/shard_map/ppermute | solution.py:25
  31.6 4.6 collective-permute-start.2
  38.7 4.4 collective-permute-done.3
  46.9 74.3 %while.38 = (s32[]{:T(128)}, f32[2,576,576]{1,2,0:T(8,128)}, s32[24,3]{0,1:T(4,128)S(1)}, f32[24,2,128,128]{3,2,0,1:T(8,128)S(1)}, s32[]{:T(128)}) while((s32[]{:T(128)}, f32[2,576,576]{1,2,0:T(8,128)}, s32[24,3]{0,1:T(4,128)S(1)}, f32[24,2,128,128]{3,2,0,1:T(8,128)S(1)}, s32[]{:T(128)}) %tuple.141), condition=%wide.while_cond.8, body=%wide.while_body.8.sunk | while | flops 2 | bytes 786549 | solution.py:98
  173.1 236.6 %while.36 = (s32[]{:T(128)}, f32[2,576,576]{2,1,0:T(8,128)}, s32[24]{0:T(128)S(1)}, s32[24]{0:T(128)S(1)}, f32[24,2,128,128]{3,2,0,1:T(8,128)}, /*index=5*/s32[]{:T(128)}, s32[]{:T(128)}, s32[]{:T(128)}) while((s32[]{:T(128)}, f32[2,576,576]{2,1,0:T(8,128)}, s32[24]{0:T(128)S(1)}, s32[24]{0:T(128)S(1)}, f32[24,2,128,128]{3,2,0,1:T(8,128)}, ...), condition=%wide.region_2.3_spmd, body=%wide.region_1.2_spmd.sunk | while | flops 32776 | bytes 655553 | solution.py:116
  179.3 3.7 dynamic_update_slice.16
  248.5 3.7 dynamic_update_slice.16
  278.2 3.7 dynamic_update_slice.16
  376.3 3.7 dynamic_update_slice.16
  396.1 3.7 dynamic_update_slice.16
  420.1 6.0 collective-permute-done.5
  427.8 4.2 collective-permute-start.6
  436.7 4.4 collective-permute-done.7
  446.2 5.8 scatter-add.26
  459.0 4.5 fusion.308
  465.5 88.1 %while.39 = (s32[]{:T(128)}, f32[2,576,576]{1,2,0:T(8,128)}, s32[24,3]{0,1:T(4,128)S(1)}, f32[24,2,128,128]{3,2,0,1:T(8,128)}, s32[]{:T(128)}) while((s32[]{:T(128)}, f32[2,576,576]{1,2,0:T(8,128)}, s32[24,3]{0,1:T(4,128)S(1)}, f32[24,2,128,128]{3,2,0,1:T(8,128)}, s32[]{:T(128)}) %tuple.153), condition=%wide.while_cond.9, body=%wide.while_body.9.sunk | while | flops 2 | bytes 787057 | solution.py:98
  553.7 4.8 fusion.81
  605.6 205.1 %while.37 = (s32[]{:T(128)}, f32[2,576,576]{2,1,0:T(8,128)S(1)}, s32[24]{0:T(128)S(1)}, s32[24]{0:T(128)S(1)}, f32[24,2,128,128]{3,2,0,1:T(8,128)}, /*index=5*/s32[]{:T(128)}, s32[]{:T(128)}, s32[]{:T(128)}) while((s32[]{:T(128)}, f32[2,576,576]{2,1,0:T(8,128)S(1)}, s32[24]{0:T(128)S(1)}, s32[24]{0:T(128)S(1)}, f32[24,2,128,128]{3,2,0,1:T(8,128)}, ...), condition=%wide.region_4.5_spmd, body=%wide.region_3.4_spmd.sunk | while | flops 32776 | bytes 655553 | solution.py:116
  818.5 5.0 collective-permute-done.9
  826.8 5.9 collective-permute-start.10
  837.4 4.4 collective-permute-done.11
  847.0 5.9 scatter-add.34
  (566 shorter events, 574.5 us)
Async XLA Ops:
  2.6 40.6 %copy-start.2 = (f32[2,512,512]{1,2,0:T(8,128)}, f32[2,512,512]{1,2,0:T(8,128)S(1)}, u32[]{:S(2)}) copy-start(f32[2,512,512]{1,2,0:T(8,128)S(1)} %copy.146) | copy-start | bytes 6291460
  2.6 5.6 copy-start.23
  2.6 5.6 copy-start.21
  2.8 14.7 %collective-permute-start = (f32[2,32,512]{1,2,0:T(8,128)S(1)}, f32[2,32,512]{1,2,0:T(8,128)S(1)}, u32[]{:S(2)}, u32[]{:S(2)}) collective-permute-start(f32[2,32,512]{1,2,0:T(8,128)S(1)} %get-tuple-element.412), channel_id=1, source_target_pairs={{0,8},{8,16},{16,24},{1,9},{9,17},{17,25},{2,10},{10,18},{18,26},{... | collective-permute-start | bytes 393224 | tf_op jit(solution)/shard_map/ppermute | solution.py:23
  6.9 23.7 %collective-permute-start.1 = (f32[2,32,512]{1,2,0:T(8,128)S(1)}, f32[2,32,512]{1,2,0:T(8,128)S(1)}, u32[]{:S(2)}, u32[]{:S(2)}) collective-permute-start(f32[2,32,512]{1,2,0:T(8,128)S(1)} %get-tuple-element.413), channel_id=1, source_target_pairs={{8,0},{16,8},{24,16},{9,1},{17,9},{25,17},{10,2},{18,10},{26,18},{... | collective-permute-start | bytes 393224 | tf_op jit(solution)/shard_map/ppermute | solution.py:25
  17.5 25.7 %copy-start.11 = (f32[2,32,512]{1,2,0:T(8,128)}, f32[2,32,512]{1,2,0:T(8,128)S(1)}, u32[]{:S(2)}) copy-start(f32[2,32,512]{1,2,0:T(8,128)S(1)} %collective-permute-done) | copy-start | bytes 393220
  30.6 12.5 %copy-start.13 = (f32[2,32,512]{1,2,0:T(8,128)}, f32[2,32,512]{1,2,0:T(8,128)S(1)}, u32[]{:S(2)}) copy-start(f32[2,32,512]{1,2,0:T(8,128)S(1)} %collective-permute-done.1) | copy-start | bytes 393220
  31.6 7.2 collective-permute-start.2
  36.2 7.0 collective-permute-start.3
  38.7 7.8 copy-start.19
  173.1 241.9 %copy-start.22 = (f32[2,128,128]{2,1,0:T(8,128)S(1)}, f32[2,128,128]{2,1,0:T(8,128)}, u32[]{:S(2)}) copy-start(f32[2,128,128]{2,1,0:T(8,128)} %param.26) | copy-start | bytes 393220
  410.9 9.0 %collective-permute-start.4 = (f32[2,64,576]{2,1,0:T(8,128)S(1)}, f32[2,64,576]{2,1,0:T(8,128)S(1)}, u32[]{:S(2)}, u32[]{:S(2)}) collective-permute-start(f32[2,64,576]{2,1,0:T(8,128)S(1)} %get-tuple-element.410), channel_id=1, source_target_pairs={{0,8},{8,16},{16,24},{1,9},{9,17},{17,25},{2,10},{10,18},{18,26},{... | collective-permute-start | bytes 884744 | tf_op jit(solution)/shard_map/ppermute | solution.py:23
  413.7 12.3 %collective-permute-start.5 = (f32[2,64,576]{2,1,0:T(8,128)S(1)}, f32[2,64,576]{2,1,0:T(8,128)S(1)}, u32[]{:S(2)}, u32[]{:S(2)}) collective-permute-start(f32[2,64,576]{2,1,0:T(8,128)S(1)} %get-tuple-element.411), channel_id=1, source_target_pairs={{8,0},{16,8},{24,16},{9,1},{17,9},{25,17},{10,2},{18,10},{26,18},{... | collective-permute-start | bytes 884744 | tf_op jit(solution)/shard_map/ppermute | solution.py:25
  426.3 14.8 %copy-start.1 = (f32[2,576,576]{1,2,0:T(8,128)S(1)}, f32[2,576,576]{1,2,0:T(8,128)}, u32[]{:S(2)}) copy-start(f32[2,576,576]{1,2,0:T(8,128)} %copy.121) | copy-start | bytes 7962628
  427.8 8.9 %collective-permute-start.6 = (f32[2,704,64]{1,2,0:T(8,128)S(1)}, f32[2,704,64]{1,2,0:T(8,128)S(1)}, u32[]{:S(2)}, u32[]{:S(2)}) collective-permute-start(f32[2,704,64]{1,2,0:T(8,128)S(1)} %get-tuple-element.400), channel_id=1, source_target_pairs={{0,1},{1,2},{2,3},{3,4},{4,5},{5,6},{6,7},{8,9},{9,10},{10,11},{11... | collective-permute-start | bytes 1081352 | tf_op jit(solution)/shard_map/ppermute | solution.py:23
  432.0 9.1 %collective-permute-start.7 = (f32[2,704,64]{1,2,0:T(8,128)S(1)}, f32[2,704,64]{1,2,0:T(8,128)S(1)}, u32[]{:S(2)}, u32[]{:S(2)}) collective-permute-start(f32[2,704,64]{1,2,0:T(8,128)S(1)} %get-tuple-element.401), channel_id=1, source_target_pairs={{1,0},{2,1},{3,2},{4,3},{5,4},{6,5},{7,6},{9,8},{10,9},{11,10},{12... | collective-permute-start | bytes 1081352 | tf_op jit(solution)/shard_map/ppermute | solution.py:25
  553.7 4.9 copy-start.5
  811.7 5.7 collective-permute-start.8
  813.7 9.8 %collective-permute-start.9 = (f32[2,64,576]{2,1,0:T(8,128)}, f32[2,64,576]{2,1,0:T(8,128)}, u32[]{:S(2)}, u32[]{:S(2)}) collective-permute-start(f32[2,64,576]{2,1,0:T(8,128)} %get-tuple-element.409), channel_id=1, source_target_pairs={{8,0},{16,8},{24,16},{9,1},{17,9},{25,17},{10,2},{18,10},{26,18},{... | collective-permute-start | bytes 884744 | tf_op jit(solution)/shard_map/ppermute | solution.py:25
  825.5 9.2 %copy-start.9 = (f32[576,576]{0,1:T(8,128)S(1)}, f32[576,576]{0,1:T(8,128)}, u32[]{:S(2)}) copy-start(f32[576,576]{0,1:T(8,128)} %and_convert_fusion) | copy-start | bytes 3981316
  826.8 15.1 %copy-start.7 = (f32[2,64,576]{1,2,0:T(8,128)S(1)}, f32[2,64,576]{1,2,0:T(8,128)}, u32[]{:S(2)}) copy-start(f32[2,64,576]{1,2,0:T(8,128)} %copy.145) | copy-start | bytes 884740
  826.8 10.7 %collective-permute-start.10 = (f32[2,704,64]{1,2,0:T(8,128)S(1)}, f32[2,704,64]{1,2,0:T(8,128)S(1)}, u32[]{:S(2)}, u32[]{:S(2)}) collective-permute-start(f32[2,704,64]{1,2,0:T(8,128)S(1)} %get-tuple-element.398), channel_id=1, source_target_pairs={{0,1},{1,2},{2,3},{3,4},{4,5},{5,6},{6,7},{8,9},{9,10},{10,11},{11... | collective-permute-start | bytes 1081352 | tf_op jit(solution)/shard_map/ppermute | solution.py:23
  832.7 9.1 %collective-permute-start.11 = (f32[2,704,64]{1,2,0:T(8,128)S(1)}, f32[2,704,64]{1,2,0:T(8,128)S(1)}, u32[]{:S(2)}, u32[]{:S(2)}) collective-permute-start(f32[2,704,64]{1,2,0:T(8,128)S(1)} %get-tuple-element.399), channel_id=1, source_target_pairs={{1,0},{2,1},{3,2},{4,3},{5,4},{6,5},{7,6},{9,8},{10,9},{11,10},{12... | collective-permute-start | bytes 1081352 | tf_op jit(solution)/shard_map/ppermute | solution.py:25
  837.4 8.2 copy-start.17
  (12 other events, 43.1 us)
where the time goes:
time: 879 us; the launch traced here: 867 us
  local copies, waits for them, and re-layouts  412 us (47%)
  loops' own time  186 us (21%)
  matrix products  97.7 us (11%)
  other arithmetic  86.1 us (10%)
  waiting for transfers between devices  49.4 us (6%)
  starting transfers between devices  33.3 us (4%)
    another operation x2, loops' own time, on_device(): gradient_sum = lax.fori_loop(0, slot_total, accumulate, empty_sum)  184 us
    gather x240, local copies, waits for them, and re-layouts  161 us
    dynamic_update_slice x48, local copies, waits for them, and re-layouts, accumulate(): lax.dynamic_update_slice(partial_value, current + gradient[slot_index], c...  146 us
    dynamic_slice x96, local copies, waits for them, and re-layouts, accumulate(): corner = (zero_index, row_start[slot_index], col_start[slot_index])  59.4 us
    add x48, other arithmetic, accumulate(): current + gradient[slot_index]  52.1 us
    ppermute x6, waiting for transfers between devices, extended_2(): lax.ppermute(head, axis, [((i + 1) % count, i) for i in range(ends)])  37.3 us
    ppermute x6, starting transfers between devices, extended_2(): lax.ppermute(tail, axis, [(i, (i + 1) % count) for i in range(ends)])  23.7 us
  transfers between devices with their start and end apart: 12, of which 10 were waited for; matrix products, arithmetic and copies ran while one was open for 1% of the time, Pallas kernels for 0%

commit v1 on v0

v1 whole, which is shorter than its diff:
```python
import functools

import jax
import jax.numpy as jnp
import numpy as np
from jax import lax
from jax.experimental import pallas as pl
from jax.experimental.pallas import tpu as pltpu
from jax.sharding import PartitionSpec as P

BORDER = 32
BAND = 2 * BORDER
ITERS = 2
LANES = 128
SUBLANES = 8
GROUP = 4

smoothing = 0.5
step_gain = 0.5


def split_host(table):
    high = table.astype(jnp.bfloat16)
    low = (table - high.astype(np.float64)).astype(jnp.bfloat16)
    return high, low


def dft_blocks(length):
    counter = np.arange(length)
    angles = 2.0 * np.pi * (np.outer(counter, counter) % length) / length
    real, imag = np.cos(angles) / np.sqrt(length), -np.sin(angles) / np.sqrt(length)
    blocks = []
    for sign in (1.0, -1.0):
        right = np.block([[real, sign * imag], [-sign * imag, real]])
        high, low = split_host(right)
        blocks.append(np.concatenate([high, high, low], axis=0))
        left = np.block([[real, -sign * imag], [sign * imag, real]])
        high, low = split_host(left)
        blocks.append(np.concatenate([high, high, low], axis=1))
    return blocks


def split(value):
    high = value.astype(jnp.bfloat16)
    low = (value - high.astype(jnp.float32)).astype(jnp.bfloat16)
    return high, low


def dot(left, right):
    return jnp.dot(left, right, preferred_element_type=jnp.float32)


def times_right(rows, block):
    high, low = split(rows)
    return dot(jnp.concatenate([high, low, high], axis=1), block)


def times_left(block, columns):
    high, low = split(columns)
    return dot(block, jnp.concatenate([high, low, high], axis=0))


def lane_iota(rows):
    return lax.broadcasted_iota(jnp.int32, (rows, LANES), 1)


def edge_lanes(rows):
    lane = lane_iota(rows)
    return (lane < BORDER) | (lane >= LANES - BORDER)


def pack_planes(real, imag):
    return jnp.where(edge_lanes(real.shape[0]), real, pltpu.roll(imag, LANES // 2, 1))


def unpack_planes(packed):
    return packed, pltpu.roll(packed, LANES // 2, 1)


def gradient_slots(cur, acc, doubled, amplitudes, positions, live, tables):
    right_f, left_f, right_b, left_b = tables
    probe = doubled.shape[1] // 2
    frame = probe + SUBLANES
    lane = lane_iota(frame)
    sub = lax.broadcasted_iota(jnp.int32, (SUBLANES, LANES), 0)
    slot_total = amplitudes.shape[0]

    def group_body(group, carry):
        places, probes, exits = [], [], []
        for member in range(GROUP):
            slot = group * GROUP + member
            at = jnp.minimum(slot, slot_total - 1)
            row = positions[0, at] + BORDER
            col = positions[1, at] + LANES
            row_at = pl.multiple_of(row // SUBLANES * SUBLANES, SUBLANES)
            col_at = pl.multiple_of(col // LANES * LANES, LANES)
            row_off, col_off = row - row_at, col - col_at
            from_left = lane >= col_off
            from_top = sub >= row_off
            planes, rolled = [], []
            for plane in range(2):
                wide = jnp.where(
                    from_left,
                    cur[plane, pl.ds(row_at, frame), pl.ds(col_at, LANES)],
                    cur[plane, pl.ds(row_at, frame), pl.ds(col_at + LANES, LANES)],
                )
                first = jnp.where(from_top, wide[:SUBLANES], wide[probe:])
                planes.append(jnp.concatenate([first, wide[SUBLANES:probe]], axis=0))
                shifted = doubled[plane, pl.ds(probe - row_off, probe), :]
                rolled.append(pltpu.roll(shifted, col_off, 1))
            places.append((at, slot, row_at, col_at, from_left, from_top))
            probes.append(rolled)
            exits.append(
                jnp.concatenate(
                    [
                        rolled[0] * planes[0] - rolled[1] * planes[1],
                        rolled[0] * planes[1] + rolled[1] * planes[0],
                    ],
                    axis=1,
                )
            )
        half = times_right(jnp.concatenate(exits, axis=0), right_f[...])
        shrunk = []
        for pair in range(0, GROUP, 2):
            first = half[pair * probe : (pair + 1) * probe]
            second = half[(pair + 1) * probe : (pair + 2) * probe]
            stacked = jnp.concatenate(
                [
                    jnp.concatenate([first[:, :probe], second[:, :probe]], axis=1),
                    jnp.concatenate([first[:, probe:], second[:, probe:]], axis=1),
                ],
                axis=0,
            )
            wave = times_left(left_f[...], stacked)
            for member in range(2):
                at = places[pair + member][0]
                real = wave[:probe, member * probe : (member + 1) * probe]
                imag = wave[probe:, member * probe : (member + 1) * probe]
                shrink = amplitudes[at] * lax.rsqrt(real * real + imag * imag + smoothing) - 1.0
                shrunk.append(jnp.concatenate([real * shrink, imag * shrink], axis=1))
        half = times_right(jnp.concatenate(shrunk, axis=0), right_b[...])
        for pair in range(0, GROUP, 2):
            first = half[pair * probe : (pair + 1) * probe]
            second = half[(pair + 1) * probe : (pair + 2) * probe]
            stacked = jnp.concatenate(
                [
                    jnp.concatenate([first[:, :probe], second[:, :probe]], axis=1),
                    jnp.concatenate([first[:, probe:], second[:, probe:]], axis=1),
                ],
                axis=0,
            )
            back = times_left(left_b[...], stacked)
            for member in range(2):
                at, slot, row_at, col_at, from_left, from_top = places[pair + member]
                real = back[:probe, member * probe : (member + 1) * probe]
                imag = back[probe:, member * probe : (member + 1) * probe]
                rolled = probes[pair + member]
                grads = (
                    rolled[0] * real + rolled[1] * imag,
                    rolled[0] * imag - rolled[1] * real,
                )
                is_live = slot < live
                keep_left = from_left & is_live
                keep_right = jnp.logical_not(from_left) & is_live
                for plane in range(2):
                    grad = grads[plane]
                    frame_grad = jnp.concatenate(
                        [
                            jnp.where(from_top, grad[:SUBLANES], 0.0),
                            grad[SUBLANES:],
                            jnp.where(from_top, 0.0, grad[:SUBLANES]),
                        ],
                        axis=0,
                    )
                    rows = pl.ds(row_at, frame)
                    acc[plane, rows, pl.ds(col_at, LANES)] += jnp.where(keep_left, frame_grad, 0.0)
                    acc[plane, rows, pl.ds(col_at + LANES, LANES)] += jnp.where(
                        keep_right, frame_grad, 0.0
                    )
        return carry

    lax.fori_loop(0, (live + GROUP - 1) // GROUP, group_body, 0)


def double_probe(probe, doubled):
    size = probe.shape[1]
    for plane in range(2):
        doubled[plane, :size, :] = probe[plane]
        doubled[plane, size:, :] = probe[plane]


def step_of(probe):
    return step_gain / (jnp.max(probe[0] * probe[0] + probe[1] * probe[1]) + 1e-06)


def pack_row_band(acc, row, count, out):
    rows = slice(row, row + count)
    width = acc.shape[2] - 2 * LANES
    halo = []
    for plane in range(2):
        out[:, plane * width : (plane + 1) * width] = acc[plane, rows, LANES : LANES + width]
        halo.append(
            jnp.where(
                lane_iota(count) < BORDER,
                acc[plane, rows, LANES + width :],
                acc[plane, rows, :LANES],
            )
        )
    out[:, 2 * width :] = pack_planes(*halo)


def pack_side_bands(acc, height, to_left, to_right):
    width = acc.shape[2] - 2 * LANES
    is_low = lane_iota(height) < BORDER
    for out, high_block in ((to_left, 0), (to_right, width)):
        out[...] = pack_planes(
            *[
                jnp.where(
                    is_low,
                    acc[plane, :height, high_block + LANES : high_block + 2 * LANES],
                    acc[plane, :height, high_block : high_block + LANES],
                )
                for plane in range(2)
            ]
        )


def add_row_band(acc, row, band):
    count = band.shape[0]
    rows = slice(row, row + count)
    width = acc.shape[2] - 2 * LANES
    lane = lane_iota(count)
    halo = unpack_planes(band[:, 2 * width :])
    for plane in range(2):
        acc[plane, rows, LANES : LANES + width] += band[:, plane * width : (plane + 1) * width]
        acc[plane, rows, :LANES] += jnp.where(lane >= LANES - BORDER, halo[plane], 0.0)
        acc[plane, rows, LANES + width :] += jnp.where(lane < BORDER, halo[plane], 0.0)


def add_side_band(acc, block, band):
    height = band.shape[0]
    lane = lane_iota(height)
    both = unpack_planes(band[...])
    for plane in range(2):
        acc[plane, :height, block : block + LANES] += jnp.where(
            lane >= LANES - BORDER, both[plane], 0.0
        )
        acc[plane, :height, block + LANES : block + 2 * LANES] += jnp.where(
            lane < BORDER, both[plane], 0.0
        )


def object_pack_kernel(left, right, up_left, up_right, down_left, down_right, out):
    tile = left.shape[1]
    for row, low, high in (
        (0, up_left, up_right),
        (BORDER, left, right),
        (BORDER + tile, down_left, down_right),
    ):
        count = low.shape[1]
        is_low = lane_iota(count) < BORDER
        out[row : row + count, :] = pack_planes(
            *[jnp.where(is_low, low[plane], high[plane]) for plane in range(2)]
        )


def load_object(cur, objects, up, down, left, right):
    tile, width = objects.shape[1], objects.shape[2]
    extent = tile + BAND
    lane = lane_iota(extent)
    lefts, rights = unpack_planes(left[...]), unpack_planes(right[...])
    for plane in range(2):
        cur[plane, :extent, :LANES] = jnp.where(lane >= LANES - BORDER, lefts[plane], 0.0)
        cur[plane, :extent, LANES + width :] = jnp.where(lane < BORDER, rights[plane], 0.0)
        inner = slice(LANES, LANES + width)
        cur[plane, :BORDER, inner] = up[plane]
        cur[plane, BORDER : BORDER + tile, inner] = objects[plane]
        cur[plane, BORDER + tile : extent, inner] = down[plane]
        cur[plane, extent:, :] = jnp.zeros_like(cur[plane, extent:, :])


def first_kernel(
    positions, counts, objects, up, down, left, right, probe, amplitudes,
    right_f, left_f, right_b, left_b,
    acc, to_up, to_down, to_left, to_right, cur, doubled,
):
    tile = objects.shape[1]
    double_probe(probe, doubled)
    load_object(cur, objects, up, down, left, right)
    acc[...] = jnp.zeros_like(acc)
    gradient_slots(
        cur, acc, doubled, amplitudes, positions, counts[0, 0], (right_f, left_f, right_b, left_b)
    )
    pack_row_band(acc, 0, BAND, to_up)
    pack_row_band(acc, tile, BAND, to_down)
    pack_side_bands(acc, tile + BAND, to_left, to_right)


def corner_kernel(inset, up, down, left, right, to_left, to_right):
    count = up.shape[0]
    width = (up.shape[1] - LANES) // 2
    is_low = lane_iota(count) < BORDER
    for source, out, low_block, high_block in (
        (left, to_left, 0, None),
        (right, to_right, None, width - LANES),
    ):
        out[...] = source[...]
        for band, row in ((up, inset), (down, source.shape[0] - inset - count)):
            halo = unpack_planes(band[:, 2 * width :])
            parts = []
            for plane in range(2):
                if low_block is not None:
                    low = band[:, plane * width + low_block : plane * width + low_block + LANES]
                    parts.append(jnp.where(is_low, low, halo[plane]))
                else:
                    high = band[:, plane * width + high_block : plane * width + high_block + LANES]
                    parts.append(jnp.where(is_low, halo[plane], high))
            out[row : row + count, :] += pack_planes(*parts)


def second_kernel(
    row_count, col_count, positions, counts, objects, up, down, left, right, probe, amplitudes,
    right_f, left_f, right_b, left_b, first, band_up, band_down, band_left, band_right,
    base, to_up, to_down, to_left, to_right, cur, acc, doubled,
):
    tile, width = objects.shape[1], objects.shape[2]
    extent = tile + BAND
    rate = step_of(probe)
    double_probe(probe, doubled)
    load_object(cur, objects, up, down, left, right)
    acc[...] = first[...]
    add_row_band(acc, 0, band_up)
    add_row_band(acc, tile, band_down)
    add_side_band(acc, 0, band_left)
    add_side_band(acc, width, band_right)
    row_at, row_last = lax.axis_index("row"), row_count - 1
    col_at, col_last = lax.axis_index("col"), col_count - 1

    def rate_if(inside):
        return jnp.where(inside, rate, 0.0)

    inner = slice(LANES, LANES + width)
    middle = slice(BORDER, BORDER + tile)
    for plane in range(2):
        base[plane] = rate * acc[plane, middle, inner]
        cur[plane, middle, inner] += base[plane]
        for rows, row_in in (
            (slice(0, BORDER), row_at > 0),
            (middle, True),
            (slice(BORDER + tile, extent), row_at < row_last),
        ):
            for lanes, col_in in (
                (slice(0, LANES), col_at > 0),
                (inner, True),
                (slice(LANES + width, None), col_at < col_last),
            ):
                if row_in is True and col_in is True:
                    continue
                inside = col_in if row_in is True else row_in if col_in is True else row_in & col_in
                cur[plane, rows, lanes] += rate_if(inside) * acc[plane, rows, lanes]
    acc[...] = jnp.zeros_like(acc)
    gradient_slots(
        cur, acc, doubled, amplitudes, positions, counts[0, 0], (right_f, left_f, right_b, left_b)
    )
    for plane in range(2):
        base[plane] += rate * acc[plane, middle, inner]
    pack_row_band(acc, 0, BORDER, to_up)
    pack_row_band(acc, BORDER + tile, BORDER, to_down)
    pack_side_bands(acc, extent, to_left, to_right)


def last_kernel(objects, base, probe, up, down, left, right, estimate, correction):
    tile, width = objects.shape[1], objects.shape[2]
    rate = step_of(probe)
    lane = lane_iota(tile)
    lefts = unpack_planes(left[BORDER : BORDER + tile, :])
    rights = unpack_planes(right[BORDER : BORDER + tile, :])
    for plane in range(2):
        correction[plane] = base[plane]
        correction[plane, :BORDER, :] += rate * up[:, plane * width : (plane + 1) * width]
        correction[plane, tile - BORDER :, :] += rate * down[:, plane * width : (plane + 1) * width]
        correction[plane, :, :LANES] += rate * jnp.where(lane < BORDER, lefts[plane], 0.0)
        correction[plane, :, width - LANES :] += rate * jnp.where(
            lane >= LANES - BORDER, rights[plane], 0.0
        )
        estimate[plane] = objects[plane] + correction[plane]


VMEM = pl.BlockSpec(memory_space=pltpu.VMEM)
SMEM = pl.BlockSpec(memory_space=pltpu.SMEM)


def f32(*shape):
    return jax.ShapeDtypeStruct(shape, jnp.float32)


def swap_along(axis, to_before, to_after):
    count = lax.axis_size(axis)
    forth = [(i, i + 1) for i in range(count - 1)]
    back = [(i + 1, i) for i in range(count - 1)]
    return lax.ppermute(to_after, axis, forth), lax.ppermute(to_before, axis, back)


def on_device(object_field, probe_field, amplitudes, positions, counts):
    tile, width = object_field.shape[1:]
    probe = probe_field.shape[1]
    extent = tile + BAND
    padded = (2, extent + SUBLANES, width + 2 * LANES)
    row_band = 2 * width + LANES
    tables = dft_blocks(probe)
    places = positions[0, 0]
    last_block = width // LANES - 1

    up, down = swap_along(
        "row", object_field[:, :BORDER, :], object_field[:, tile - BORDER :, :]
    )

    def block_of(rows, index):
        return pl.BlockSpec((2, rows, LANES), lambda i: (0, 0, index))

    sides = pl.pallas_call(
        object_pack_kernel,
        grid=(1,),
        out_shape=f32(extent, LANES),
        in_specs=[
            block_of(rows, index) for rows in (tile, BORDER, BORDER) for index in (0, last_block)
        ],
        out_specs=pl.BlockSpec((extent, LANES), lambda i: (0, 0)),
        name="object_pack",
    )(object_field, object_field, up, up, down, down)
    left, right = swap_along("col", sides, sides)

    common = (object_field, up, down, left, right, probe_field, amplitudes, *tables)
    acc, to_up, to_down, to_left, to_right = pl.pallas_call(
        first_kernel,
        out_shape=(
            f32(*padded), f32(BAND, row_band), f32(BAND, row_band),
            f32(extent, LANES), f32(extent, LANES),
        ),
        in_specs=[SMEM, SMEM] + [VMEM] * len(common),
        out_specs=(VMEM,) * 5,
        scratch_shapes=[
            pltpu.VMEM(padded, jnp.float32), pltpu.VMEM((2, 2 * probe, probe), jnp.float32),
        ],
        name="first_iteration",
    )(places, counts, *common)
    band_up, band_down = swap_along("row", to_up, to_down)
    to_left, to_right = pl.pallas_call(
        functools.partial(corner_kernel, 0),
        out_shape=(f32(extent, LANES), f32(extent, LANES)),
        in_specs=[VMEM] * 4,
        out_specs=(VMEM,) * 2,
        name="corners",
    )(band_up, band_down, to_left, to_right)
    band_left, band_right = swap_along("col", to_left, to_right)

    bands = (acc, band_up, band_down, band_left, band_right)
    base, to_up, to_down, to_left, to_right = pl.pallas_call(
        functools.partial(second_kernel, lax.axis_size("row"), lax.axis_size("col")),
        out_shape=(
            f32(2, tile, width), f32(BORDER, row_band), f32(BORDER, row_band),
            f32(extent, LANES), f32(extent, LANES),
        ),
        in_specs=[SMEM, SMEM] + [VMEM] * (len(common) + len(bands)),
        out_specs=(VMEM,) * 5,
        scratch_shapes=[
            pltpu.VMEM(padded, jnp.float32), pltpu.VMEM(padded, jnp.float32),
            pltpu.VMEM((2, 2 * probe, probe), jnp.float32),
        ],
        name="second_iteration",
    )(places, counts, *common, *bands)
    band_up, band_down = swap_along("row", to_up, to_down)
    to_left, to_right = pl.pallas_call(
        functools.partial(corner_kernel, BORDER),
        out_shape=(f32(extent, LANES), f32(extent, LANES)),
        in_specs=[VMEM] * 4,
        out_specs=(VMEM,) * 2,
        name="last_corners",
    )(band_up, band_down, to_left, to_right)
    band_left, band_right = swap_along("col", to_left, to_right)
    estimate, correction = pl.pallas_call(
        last_kernel,
        out_shape=(f32(2, tile, width), f32(2, tile, width)),
        in_specs=[VMEM] * 7,
        out_specs=(VMEM,) * 2,
        name="finish",
    )(object_field, base, probe_field, band_up, band_down, band_left, band_right)
    return estimate, correction


def solution(mesh):
    placed = (
        P(None, "row", "col"),
        P(),
        P("row", None, "col"),
        P("row", "col", None, None),
        P("row", "col"),
    )
    return jax.shard_map(
        on_device,
        mesh=mesh,
        in_specs=placed,
        out_specs=(P(None, "row", "col"), P(None, "row", "col")),
        check_vma=False,
    )
```

time: 879 us -> 119 us (0.14); the launches traced: 867 us -> 117 us
  local copies, waits for them, and re-layouts: 412 us -> 5.16 us
  loops' own time: 186 us -> 0 us
  matrix products: 97.7 us -> 0 us
  other arithmetic: 86.1 us -> 0 us
  Pallas kernels: 0 us -> 36.7 us
    another operation x4 -> x0, loops' own time: 186 us -> none  [the longest x2 184 us: on_device(): gradient_sum = lax.fori_loop(0, slot_total, accumulate, empty_sum)]
    gather x240 -> x0, local copies, waits for them, and re-layouts: 161 us -> none
    dynamic_update_slice x48 -> x0, local copies, waits for them, and re-layouts: 146 us -> none  [accumulate(): lax.dynamic_update_slice(partial_value, current + gradient[slot_index], c...]
    dot_general x32 -> x0, matrix products: 97.7 us -> none  [the longest x4 14.5 us: transform(): jnp.einsum('kp,spq->skq', table_real, real_part, precision=highest)]
    add x53 -> x0, other arithmetic: 61.7 us -> none  [the longest x48 52.1 us: accumulate(): current + gradient[slot_index]]
    dynamic_slice x96 -> x0, local copies, waits for them, and re-layouts: 59.4 us -> none  [accumulate(): corner = (zero_index, row_start[slot_index], col_start[slot_index])]
    pallas_call x0 -> x6, Pallas kernels: none -> 36.7 us  [the longest x1 13.3 us: on_device(): pl.pallas_call(functools.partial(second_kernel, lax.axis_size('row'), lax...]
    slice x8 -> x1, local copies, waits for them, and re-layouts: 13.5 us -> 0.99 us  [on_device(): object_field[:, :BORDER, :]]
  transfers between devices with their start and end apart: 12 -> 12, of which waited for: 10 -> 12; matrix products, arithmetic and copies ran while one was open for 1% -> 0% of each run, Pallas kernels for 0% -> 0%
where the time goes in v1:
time: 119 us; the launch traced here: 117 us
  waiting for transfers between devices  41.6 us (35%)
  Pallas kernels  36.7 us (31%)
  starting transfers between devices  32.4 us (27%)
  local copies, waits for them, and re-layouts  5.16 us (4%)
  between operations  1.4 us (1%)
    ppermute x6, waiting for transfers between devices, swap_along(): lax.ppermute(to_before, axis, back)  32.2 us
    ppermute x6, starting transfers between devices, swap_along(): lax.ppermute(to_after, axis, forth)  20.3 us
    pallas_call x1, Pallas kernels, on_device(): pl.pallas_call(functools.partial(second_kernel, lax.axis_size('row'), lax...  13.3 us
    ppermute x6, starting transfers between devices, swap_along(): lax.ppermute(to_before, axis, back)  12.1 us
    pallas_call x1, Pallas kernels, on_device(): pl.pallas_call(first_kernel, out_shape=(f32(*padded), f32(BAND, row_band)...  11.8 us
    ppermute x6, waiting for transfers between devices, swap_along(): lax.ppermute(to_after, axis, forth)  9.35 us
    pallas_call x1, Pallas kernels, on_device(): pl.pallas_call(last_kernel, out_shape=(f32(2, tile, width), f32(2, tile,...  5.14 us
    unnamed x24, local copies, waits for them, and re-layouts  4.17 us
  transfers between devices with their start and end apart: 12, of which 12 were waited for; matrix products, arithmetic and copies ran while one was open for 0% of the time, Pallas kernels for 0%

profile of v1, /device:TPU:1, one launch (start us, length us, event | category | flops | bytes accessed | tf_op | source)
XLA Modules:
  0.0 117.2 jit_solution(7772978953752400497)
XLA Ops:
  1.6 1.3 %collective-permute-start.1 = (f32[2,32,512]{2,1,0:T(8,128)S(1)}, f32[2,32,512]{2,1,0:T(8,128)S(1)}, u32[]{:S(2)}, u32[]{:S(2)}) collective-permute-start(f32[2,32,512]{2,1,0:T(8,128)S(1)} %get-tuple-element.30), channel_id=1, source_target_pairs={{8,0},{16,8},{24,16},{9,1},{17,9},{25,17},{10,2},{18,10},{26,18},{... | collective-permute-start | bytes 393224 | tf_op jit(solution)/shard_map/ppermute | solution.py:401
  2.9 4.6 %collective-permute-start = (f32[2,32,512]{2,1,0:T(8,128)S(1)}, f32[2,32,512]{2,1,0:T(8,128)S(1)}, u32[]{:S(2)}, u32[]{:S(2)}) collective-permute-start(f32[2,32,512]{2,1,0:T(8,128)S(1)} %get-tuple-element.31), channel_id=1, source_target_pairs={{0,8},{8,16},{16,24},{1,9},{9,17},{17,25},{2,10},{10,18},{18,26},{... | collective-permute-start | bytes 393224 | tf_op jit(solution)/shard_map/ppermute | solution.py:401
  10.3 2.1 %object_pack.1 = f32[576,128]{1,0:T(8,128)} custom-call(f32[2,512,512]{2,1,0:T(8,128)} %objects.5, f32[2,512,512]{2,1,0:T(8,128)} %objects.5, f32[2,32,512]{2,1,0:T(8,128)} %copy-done.1, f32[2,32,512]{2,1,0:T(8,128)} %copy-done.1, f32[2,32,512]{2,1,0:T(8,128)} %copy-done, f32[2,32,512]{2,1,0:T(8,128)} %copy-done), custom_call_target="tpu_custom_call" | custom-call | tf_op jit(solution)/shard_map/object_pack/pallas_call | solution.py:421
  12.4 3.4 %collective-permute-start.3 = (f32[576,128]{1,0:T(8,128)}, f32[576,128]{1,0:T(8,128)S(1)}, u32[]{:S(2)}, u32[]{:S(2)}) collective-permute-start(f32[576,128]{1,0:T(8,128)} %object_pack.1), channel_id=1, source_target_pairs={{1,0},{2,1},{3,2},{4,3},{5,4},{6,5},{7,6},{9,8},{10,9},{11,10},{12... | collective-permute-start | bytes 884744 | tf_op jit(solution)/shard_map/ppermute | solution.py:401
  15.8 3.4 %collective-permute-start.2 = (f32[576,128]{1,0:T(8,128)}, f32[576,128]{1,0:T(8,128)S(1)}, u32[]{:S(2)}, u32[]{:S(2)}) collective-permute-start(f32[576,128]{1,0:T(8,128)} %object_pack.1), channel_id=1, source_target_pairs={{0,1},{1,2},{2,3},{3,4},{4,5},{5,6},{6,7},{8,9},{9,10},{10,11},{11... | collective-permute-start | bytes 884744 | tf_op jit(solution)/shard_map/ppermute | solution.py:401
  19.9 2.0 %collective-permute-done.3.right = f32[576,128]{1,0:T(8,128)S(1)} collective-permute-done((f32[576,128]{1,0:T(8,128)}, f32[576,128]{1,0:T(8,128)S(1)}, u32[]{:S(2)}, u32[]{:S(2)}) %collective-permute-start.3) | collective-permute-done | bytes 294944 | tf_op jit(solution)/shard_map/ppermute | solution.py:401
  23.9 11.8 %first_iteration.1 = (f32[2,584,768]{2,1,0:T(8,128)}, f32[64,1152]{1,0:T(8,128)}, f32[64,1152]{1,0:T(8,128)}, f32[576,128]{1,0:T(8,128)}, f32[576,128]{1,0:T(8,128)}) custom-call(s32[2,24]{1,0:T(2,128)} %bitcast.1, s32[1,1]{1,0:T(1,128)S(6)} %copy.11.counts, f32[2,512,512]{2,1,0:T(8,128)} %objects.5, f32[2,32,512]{2,1,0:T(8,128)} %copy-done.1, ...), custom_call_target="tpu_custom_call" | custom-call | tf_op jit(solution)/shard_map/first_iteration/pallas_call | solution.py:434
  35.7 4.1 %collective-permute-start.4 = (f32[64,1152]{1,0:T(8,128)}, f32[64,1152]{1,0:T(8,128)S(1)}, u32[]{:S(2)}, u32[]{:S(2)}) collective-permute-start(f32[64,1152]{1,0:T(8,128)} %get-tuple-element.17), channel_id=1, source_target_pairs={{0,8},{8,16},{16,24},{1,9},{9,17},{17,25},{2,10},{10,18},{18,26},{... | collective-permute-start | bytes 884744 | tf_op jit(solution)/shard_map/ppermute | solution.py:401
  41.1 3.0 %collective-permute-done.4.up.band_up = f32[64,1152]{1,0:T(8,128)S(1)} collective-permute-done((f32[64,1152]{1,0:T(8,128)}, f32[64,1152]{1,0:T(8,128)S(1)}, u32[]{:S(2)}, u32[]{:S(2)}) %collective-permute-start.4) | collective-permute-done | bytes 294944 | tf_op jit(solution)/shard_map/ppermute | solution.py:401
  44.1 13.9 %collective-permute-done.5.down.band_down = f32[64,1152]{1,0:T(8,128)S(1)} collective-permute-done((f32[64,1152]{1,0:T(8,128)}, f32[64,1152]{1,0:T(8,128)S(1)}, u32[]{:S(2)}, u32[]{:S(2)}) %collective-permute-start.5) | collective-permute-done | bytes 294944 | tf_op jit(solution)/shard_map/ppermute | solution.py:401
  58.7 2.2 %corners.1 = (f32[576,128]{1,0:T(8,128)}, f32[576,128]{1,0:T(8,128)}) custom-call(f32[64,1152]{1,0:T(8,128)} %copy-done.2, f32[64,1152]{1,0:T(8,128)} %copy-done.3, f32[576,128]{1,0:T(8,128)} %get-tuple-element.19.left, f32[576,128]{1,0:T(8,128)} %get-tuple-element.20.right), custom_call_target="tpu_custom_call" | custom-call | tf_op jit(solution)/shard_map/corners/pallas_call | solution.py:448
  60.9 1.9 %collective-permute-start.6 = (f32[576,128]{1,0:T(8,128)}, f32[576,128]{1,0:T(8,128)S(1)}, u32[]{:S(2)}, u32[]{:S(2)}) collective-permute-start(f32[576,128]{1,0:T(8,128)} %get-tuple-element.21), channel_id=1, source_target_pairs={{0,1},{1,2},{2,3},{3,4},{4,5},{5,6},{6,7},{8,9},{9,10},{10,11},{11... | collective-permute-start | bytes 884744 | tf_op jit(solution)/shard_map/ppermute | solution.py:401
  62.9 2.4 %collective-permute-start.7 = (f32[576,128]{1,0:T(8,128)}, f32[576,128]{1,0:T(8,128)S(1)}, u32[]{:S(2)}, u32[]{:S(2)}) collective-permute-start(f32[576,128]{1,0:T(8,128)} %get-tuple-element.22), channel_id=1, source_target_pairs={{1,0},{2,1},{3,2},{4,3},{5,4},{6,5},{7,6},{9,8},{10,9},{11,10},{12... | collective-permute-start | bytes 884744 | tf_op jit(solution)/shard_map/ppermute | solution.py:401
  65.3 1.5 %collective-permute-done.6.band_left = f32[576,128]{1,0:T(8,128)S(1)} collective-permute-done((f32[576,128]{1,0:T(8,128)}, f32[576,128]{1,0:T(8,128)S(1)}, u32[]{:S(2)}, u32[]{:S(2)}) %collective-permute-start.6) | collective-permute-done | bytes 294944 | tf_op jit(solution)/shard_map/ppermute | solution.py:401
  66.8 4.3 %collective-permute-done.7.band_right = f32[576,128]{1,0:T(8,128)S(1)} collective-permute-done((f32[576,128]{1,0:T(8,128)}, f32[576,128]{1,0:T(8,128)S(1)}, u32[]{:S(2)}, u32[]{:S(2)}) %collective-permute-start.7) | collective-permute-done | bytes 294944 | tf_op jit(solution)/shard_map/ppermute | solution.py:401
  71.8 13.3 %second_iteration.1 = (f32[2,512,512]{2,1,0:T(8,128)}, f32[32,1152]{1,0:T(8,128)}, f32[32,1152]{1,0:T(8,128)}, f32[576,128]{1,0:T(8,128)}, f32[576,128]{1,0:T(8,128)}) custom-call(s32[2,24]{1,0:T(2,128)} %bitcast.2, s32[1,1]{1,0:T(1,128)S(6)} %copy.11.counts, f32[2,512,512]{2,1,0:T(8,128)} %objects.5, f32[2,32,512]{2,1,0:T(8,128)} %copy-done.1, ...), custom_call_target="tpu_custom_call" | custom-call | tf_op jit(solution)/shard_map/second_iteration/pallas_call | solution.py:458
  85.1 4.4 %collective-permute-start.8 = (f32[32,1152]{1,0:T(8,128)}, f32[32,1152]{1,0:T(8,128)S(1)}, u32[]{:S(2)}, u32[]{:S(2)}) collective-permute-start(f32[32,1152]{1,0:T(8,128)} %get-tuple-element.24), channel_id=1, source_target_pairs={{0,8},{8,16},{16,24},{1,9},{9,17},{17,25},{2,10},{10,18},{18,26},{... | collective-permute-start | bytes 442376 | tf_op jit(solution)/shard_map/ppermute | solution.py:401
  91.9 6.5 %collective-permute-done.9.down = f32[32,1152]{1,0:T(8,128)S(1)} collective-permute-done((f32[32,1152]{1,0:T(8,128)}, f32[32,1152]{1,0:T(8,128)S(1)}, u32[]{:S(2)}, u32[]{:S(2)}) %collective-permute-start.9) | collective-permute-done | bytes 147488 | tf_op jit(solution)/shard_map/ppermute | solution.py:401
  99.0 2.2 %last_corners.1 = (f32[576,128]{1,0:T(8,128)}, f32[576,128]{1,0:T(8,128)}) custom-call(f32[32,1152]{1,0:T(8,128)} %copy-done.6, f32[32,1152]{1,0:T(8,128)} %copy-done.7, f32[576,128]{1,0:T(8,128)} %get-tuple-element.26.left, f32[576,128]{1,0:T(8,128)} %get-tuple-element.27.right), custom_call_target="tpu_custom_call" | custom-call | tf_op jit(solution)/shard_map/last_corners/pallas_call | solution.py:473
  101.2 1.9 %collective-permute-start.10 = (f32[576,128]{1,0:T(8,128)}, f32[576,128]{1,0:T(8,128)S(1)}, u32[]{:S(2)}, u32[]{:S(2)}) collective-permute-start(f32[576,128]{1,0:T(8,128)} %get-tuple-element.28), channel_id=1, source_target_pairs={{0,1},{1,2},{2,3},{3,4},{4,5},{5,6},{6,7},{8,9},{9,10},{10,11},{11... | collective-permute-start | bytes 884744 | tf_op jit(solution)/shard_map/ppermute | solution.py:401
  103.1 2.4 %collective-permute-start.11 = (f32[576,128]{1,0:T(8,128)}, f32[576,128]{1,0:T(8,128)S(1)}, u32[]{:S(2)}, u32[]{:S(2)}) collective-permute-start(f32[576,128]{1,0:T(8,128)} %get-tuple-element.29), channel_id=1, source_target_pairs={{1,0},{2,1},{3,2},{4,3},{5,4},{6,5},{7,6},{9,8},{10,9},{11,10},{12... | collective-permute-start | bytes 884744 | tf_op jit(solution)/shard_map/ppermute | solution.py:401
  105.5 1.5 %collective-permute-done.10.left = f32[576,128]{1,0:T(8,128)S(1)} collective-permute-done((f32[576,128]{1,0:T(8,128)}, f32[576,128]{1,0:T(8,128)S(1)}, u32[]{:S(2)}, u32[]{:S(2)}) %collective-permute-start.10) | collective-permute-done | bytes 294944 | tf_op jit(solution)/shard_map/ppermute | solution.py:401
  107.1 4.3 %collective-permute-done.11.right = f32[576,128]{1,0:T(8,128)S(1)} collective-permute-done((f32[576,128]{1,0:T(8,128)}, f32[576,128]{1,0:T(8,128)S(1)}, u32[]{:S(2)}, u32[]{:S(2)}) %collective-permute-start.11) | collective-permute-done | bytes 294944 | tf_op jit(solution)/shard_map/ppermute | solution.py:401
  112.1 5.1 %finish.1 = (f32[2,512,512]{2,1,0:T(8,128)}, f32[2,512,512]{2,1,0:T(8,128)}) custom-call(f32[2,512,512]{2,1,0:T(8,128)} %objects.5, f32[2,512,512]{2,1,0:T(8,128)} %get-tuple-element.23.base, f32[2,128,128]{2,1,0:T(8,128)} %probe.5, f32[32,1152]{1,0:T(8,128)} %copy-done.6, f32[32,1152]{1,0:T(8,128)} %copy-done.7, f32[576,128]{1,0:T(8,128)} %copy-done.10, ...), custom_call_target="tpu_custom_call" | custom-call | tf_op jit(solution)/shard_map/finish/pallas_call | solution.py:481
  (31 shorter events, 12.3 us)
Async XLA Ops:
  1.6 7.1 %collective-permute-start.1 = (f32[2,32,512]{2,1,0:T(8,128)S(1)}, f32[2,32,512]{2,1,0:T(8,128)S(1)}, u32[]{:S(2)}, u32[]{:S(2)}) collective-permute-start(f32[2,32,512]{2,1,0:T(8,128)S(1)} %get-tuple-element.30), channel_id=1, source_target_pairs={{8,0},{16,8},{24,16},{9,1},{17,9},{25,17},{10,2},{18,10},{26,18},{... | collective-permute-start | bytes 393224 | tf_op jit(solution)/shard_map/ppermute | solution.py:401
  2.9 6.7 %collective-permute-start = (f32[2,32,512]{2,1,0:T(8,128)S(1)}, f32[2,32,512]{2,1,0:T(8,128)S(1)}, u32[]{:S(2)}, u32[]{:S(2)}) collective-permute-start(f32[2,32,512]{2,1,0:T(8,128)S(1)} %get-tuple-element.31), channel_id=1, source_target_pairs={{0,8},{8,16},{16,24},{1,9},{9,17},{17,25},{2,10},{10,18},{18,26},{... | collective-permute-start | bytes 393224 | tf_op jit(solution)/shard_map/ppermute | solution.py:401
  8.8 0.9 copy-start
  9.7 0.7 copy-start.1
  12.4 9.5 %collective-permute-start.3 = (f32[576,128]{1,0:T(8,128)}, f32[576,128]{1,0:T(8,128)S(1)}, u32[]{:S(2)}, u32[]{:S(2)}) collective-permute-start(f32[576,128]{1,0:T(8,128)} %object_pack.1), channel_id=1, source_target_pairs={{1,0},{2,1},{3,2},{4,3},{5,4},{6,5},{7,6},{9,8},{10,9},{11,10},{12... | collective-permute-start | bytes 884744 | tf_op jit(solution)/shard_map/ppermute | solution.py:401
  15.8 7.4 %collective-permute-start.2 = (f32[576,128]{1,0:T(8,128)}, f32[576,128]{1,0:T(8,128)S(1)}, u32[]{:S(2)}, u32[]{:S(2)}) collective-permute-start(f32[576,128]{1,0:T(8,128)} %object_pack.1), channel_id=1, source_target_pairs={{0,1},{1,2},{2,3},{3,4},{4,5},{5,6},{6,7},{8,9},{9,10},{10,11},{11... | collective-permute-start | bytes 884744 | tf_op jit(solution)/shard_map/ppermute | solution.py:401
  21.9 1.3 %copy-start.4 = (f32[576,128]{1,0:T(8,128)}, f32[576,128]{1,0:T(8,128)S(1)}, u32[]{:S(2)}) copy-start(f32[576,128]{1,0:T(8,128)S(1)} %collective-permute-done.3.right) | copy-start | bytes 884740
  23.2 0.7 copy-start.5
  35.7 8.4 %collective-permute-start.4 = (f32[64,1152]{1,0:T(8,128)}, f32[64,1152]{1,0:T(8,128)S(1)}, u32[]{:S(2)}, u32[]{:S(2)}) collective-permute-start(f32[64,1152]{1,0:T(8,128)} %get-tuple-element.17), channel_id=1, source_target_pairs={{0,8},{8,16},{16,24},{1,9},{9,17},{17,25},{2,10},{10,18},{18,26},{... | collective-permute-start | bytes 884744 | tf_op jit(solution)/shard_map/ppermute | solution.py:401
  39.8 18.2 %collective-permute-start.5 = (f32[64,1152]{1,0:T(8,128)}, f32[64,1152]{1,0:T(8,128)S(1)}, u32[]{:S(2)}, u32[]{:S(2)}) collective-permute-start(f32[64,1152]{1,0:T(8,128)} %get-tuple-element.18), channel_id=1, source_target_pairs={{8,0},{16,8},{24,16},{9,1},{17,9},{25,17},{10,2},{18,10},{26,18},{... | collective-permute-start | bytes 884744 | tf_op jit(solution)/shard_map/ppermute | solution.py:401
  44.1 13.9 %copy-start.2 = (f32[64,1152]{1,0:T(8,128)}, f32[64,1152]{1,0:T(8,128)S(1)}, u32[]{:S(2)}) copy-start(f32[64,1152]{1,0:T(8,128)S(1)} %collective-permute-done.4.up.band_up) | copy-start | bytes 884740
  58.0 0.7 copy-start.3
  60.9 5.9 %collective-permute-start.6 = (f32[576,128]{1,0:T(8,128)}, f32[576,128]{1,0:T(8,128)S(1)}, u32[]{:S(2)}, u32[]{:S(2)}) collective-permute-start(f32[576,128]{1,0:T(8,128)} %get-tuple-element.21), channel_id=1, source_target_pairs={{0,1},{1,2},{2,3},{3,4},{4,5},{5,6},{6,7},{8,9},{9,10},{10,11},{11... | collective-permute-start | bytes 884744 | tf_op jit(solution)/shard_map/ppermute | solution.py:401
  62.9 8.3 %collective-permute-start.7 = (f32[576,128]{1,0:T(8,128)}, f32[576,128]{1,0:T(8,128)S(1)}, u32[]{:S(2)}, u32[]{:S(2)}) collective-permute-start(f32[576,128]{1,0:T(8,128)} %get-tuple-element.22), channel_id=1, source_target_pairs={{1,0},{2,1},{3,2},{4,3},{5,4},{6,5},{7,6},{9,8},{10,9},{11,10},{12... | collective-permute-start | bytes 884744 | tf_op jit(solution)/shard_map/ppermute | solution.py:401
  66.8 4.3 %copy-start.8 = (f32[576,128]{1,0:T(8,128)}, f32[576,128]{1,0:T(8,128)S(1)}, u32[]{:S(2)}) copy-start(f32[576,128]{1,0:T(8,128)S(1)} %collective-permute-done.6.band_left) | copy-start | bytes 884740
  71.1 0.7 copy-start.9
  85.1 6.8 %collective-permute-start.8 = (f32[32,1152]{1,0:T(8,128)}, f32[32,1152]{1,0:T(8,128)S(1)}, u32[]{:S(2)}, u32[]{:S(2)}) collective-permute-start(f32[32,1152]{1,0:T(8,128)} %get-tuple-element.24), channel_id=1, source_target_pairs={{0,8},{8,16},{16,24},{1,9},{9,17},{17,25},{2,10},{10,18},{18,26},{... | collective-permute-start | bytes 442376 | tf_op jit(solution)/shard_map/ppermute | solution.py:401
  89.5 8.9 %collective-permute-start.9 = (f32[32,1152]{1,0:T(8,128)}, f32[32,1152]{1,0:T(8,128)S(1)}, u32[]{:S(2)}, u32[]{:S(2)}) collective-permute-start(f32[32,1152]{1,0:T(8,128)} %get-tuple-element.25), channel_id=1, source_target_pairs={{8,0},{16,8},{24,16},{9,1},{17,9},{25,17},{10,2},{18,10},{26,18},{... | collective-permute-start | bytes 442376 | tf_op jit(solution)/shard_map/ppermute | solution.py:401
  91.9 6.5 %copy-start.6 = (f32[32,1152]{1,0:T(8,128)}, f32[32,1152]{1,0:T(8,128)S(1)}, u32[]{:S(2)}) copy-start(f32[32,1152]{1,0:T(8,128)S(1)} %collective-permute-done.8.up) | copy-start | bytes 442372
  98.4 0.7 copy-start.7
  101.2 5.9 %collective-permute-start.10 = (f32[576,128]{1,0:T(8,128)}, f32[576,128]{1,0:T(8,128)S(1)}, u32[]{:S(2)}, u32[]{:S(2)}) collective-permute-start(f32[576,128]{1,0:T(8,128)} %get-tuple-element.28), channel_id=1, source_target_pairs={{0,1},{1,2},{2,3},{3,4},{4,5},{5,6},{6,7},{8,9},{9,10},{10,11},{11... | collective-permute-start | bytes 884744 | tf_op jit(solution)/shard_map/ppermute | solution.py:401
  103.1 8.3 %collective-permute-start.11 = (f32[576,128]{1,0:T(8,128)}, f32[576,128]{1,0:T(8,128)S(1)}, u32[]{:S(2)}, u32[]{:S(2)}) collective-permute-start(f32[576,128]{1,0:T(8,128)} %get-tuple-element.29), channel_id=1, source_target_pairs={{1,0},{2,1},{3,2},{4,3},{5,4},{6,5},{7,6},{9,8},{10,9},{11,10},{12... | collective-permute-start | bytes 884744 | tf_op jit(solution)/shard_map/ppermute | solution.py:401
  107.1 4.3 %copy-start.10 = (f32[576,128]{1,0:T(8,128)}, f32[576,128]{1,0:T(8,128)S(1)}, u32[]{:S(2)}) copy-start(f32[576,128]{1,0:T(8,128)S(1)} %collective-permute-done.10.left) | copy-start | bytes 884740
  111.4 0.7 copy-start.11

commit v2 on v1

v2 whole, which is shorter than its diff:
```python
import functools

import jax
import jax.numpy as jnp
import numpy as np
from jax import lax
from jax.experimental import pallas as pl
from jax.experimental.pallas import tpu as pltpu
from jax.sharding import PartitionSpec as P

BORDER = 32
BAND = 2 * BORDER
ITERS = 2
LANES = 128
SUBLANES = 8
GROUP = 8
RIGHT = 4

smoothing = 0.5
step_gain = 0.5


def split_host(table):
    high = table.astype(jnp.bfloat16)
    low = (table - high.astype(np.float64)).astype(jnp.bfloat16)
    return high, low


def dft_blocks(length):
    counter = np.arange(length)
    angles = 2.0 * np.pi * (np.outer(counter, counter) % length) / length
    real, imag = np.cos(angles) / np.sqrt(length), -np.sin(angles) / np.sqrt(length)
    blocks = []
    for sign in (1.0, -1.0):
        right = np.block([[real, sign * imag], [-sign * imag, real]])
        high, low = split_host(right)
        blocks.append(np.concatenate([high, high, low], axis=0))
        left = np.block([[real, -sign * imag], [sign * imag, real]])
        high, low = split_host(left)
        blocks.append(np.concatenate([high, high, low], axis=1))
    return blocks


def split(value):
    high = value.astype(jnp.bfloat16)
    low = (value - high.astype(jnp.float32)).astype(jnp.bfloat16)
    return high, low


def dot(left, right):
    return jnp.dot(left, right, preferred_element_type=jnp.float32)


def times_right(rows, block):
    high, low = split(rows)
    return dot(jnp.concatenate([high, low, high], axis=1), block)


def right_groups(members, block):
    rows = members[0].shape[0]
    results = []
    for start in range(0, len(members), RIGHT):
        product = times_right(jnp.concatenate(members[start : start + RIGHT], axis=0), block[...])
        results += [product[i * rows : (i + 1) * rows] for i in range(RIGHT)]
    return results


def times_left(block, columns):
    high, low = split(columns)
    return dot(block, jnp.concatenate([high, low, high], axis=0))


def lane_iota(rows):
    return lax.broadcasted_iota(jnp.int32, (rows, LANES), 1)


def edge_lanes(rows):
    lane = lane_iota(rows)
    return (lane < BORDER) | (lane >= LANES - BORDER)


def pack_planes(real, imag):
    return jnp.where(edge_lanes(real.shape[0]), real, pltpu.roll(imag, LANES // 2, 1))


def unpack_planes(packed):
    return packed, pltpu.roll(packed, LANES // 2, 1)


def list_slots(order, positions, live, low, high, inside):
    def visit(slot, found):
        row, col = positions[0, slot], positions[1, slot]
        within = (row >= low) & (row <= high) & (col >= low) & (col <= high)
        order[found] = slot
        return found + jnp.where(within == inside, 1, 0)

    return lax.fori_loop(0, live, visit, 0)


def gradient_slots(cur, acc, doubled, amplitudes, positions, order, begin, stop, tables):
    right_f, left_f, right_b, left_b = tables
    probe = doubled.shape[1] // 2
    frame = probe + SUBLANES
    lane = lane_iota(frame)
    sub = lax.broadcasted_iota(jnp.int32, (SUBLANES, LANES), 0)

    def group_body(group, carry):
        places, probes, exits = [], [], []
        for member in range(GROUP):
            slot = begin + group * GROUP + member
            at = order[jnp.minimum(slot, stop - 1)]
            row = positions[0, at] + BORDER
            col = positions[1, at] + LANES
            row_at = pl.multiple_of(row // SUBLANES * SUBLANES, SUBLANES)
            col_at = pl.multiple_of(col // LANES * LANES, LANES)
            row_off, col_off = row - row_at, col - col_at
            from_left = lane >= col_off
            from_top = sub >= row_off
            planes, rolled = [], []
            for plane in range(2):
                wide = jnp.where(
                    from_left,
                    cur[plane, pl.ds(row_at, frame), pl.ds(col_at, LANES)],
                    cur[plane, pl.ds(row_at, frame), pl.ds(col_at + LANES, LANES)],
                )
                first = jnp.where(from_top, wide[:SUBLANES], wide[probe:])
                planes.append(jnp.concatenate([first, wide[SUBLANES:probe]], axis=0))
                shifted = doubled[plane, pl.ds(probe - row_off, probe), :]
                rolled.append(pltpu.roll(shifted, col_off, 1))
            places.append((at, slot, row_at, col_at, from_left, from_top))
            probes.append(rolled)
            exits.append(
                jnp.concatenate(
                    [
                        rolled[0] * planes[0] - rolled[1] * planes[1],
                        rolled[0] * planes[1] + rolled[1] * planes[0],
                    ],
                    axis=1,
                )
            )
        half = right_groups(exits, right_f)
        shrunk = []
        for pair in range(0, GROUP, 2):
            first, second = half[pair], half[pair + 1]
            stacked = jnp.concatenate(
                [
                    jnp.concatenate([first[:, :probe], second[:, :probe]], axis=1),
                    jnp.concatenate([first[:, probe:], second[:, probe:]], axis=1),
                ],
                axis=0,
            )
            wave = times_left(left_f[...], stacked)
            for member in range(2):
                at = places[pair + member][0]
                real = wave[:probe, member * probe : (member + 1) * probe]
                imag = wave[probe:, member * probe : (member + 1) * probe]
                shrink = amplitudes[at] * lax.rsqrt(real * real + imag * imag + smoothing) - 1.0
                shrunk.append(jnp.concatenate([real * shrink, imag * shrink], axis=1))
        half = right_groups(shrunk, right_b)
        for pair in range(0, GROUP, 2):
            first, second = half[pair], half[pair + 1]
            stacked = jnp.concatenate(
                [
                    jnp.concatenate([first[:, :probe], second[:, :probe]], axis=1),
                    jnp.concatenate([first[:, probe:], second[:, probe:]], axis=1),
                ],
                axis=0,
            )
            back = times_left(left_b[...], stacked)
            for member in range(2):
                at, slot, row_at, col_at, from_left, from_top = places[pair + member]
                real = back[:probe, member * probe : (member + 1) * probe]
                imag = back[probe:, member * probe : (member + 1) * probe]
                rolled = probes[pair + member]
                grads = (
                    rolled[0] * real + rolled[1] * imag,
                    rolled[0] * imag - rolled[1] * real,
                )
                is_live = slot < stop
                keep_left = from_left & is_live
                keep_right = jnp.logical_not(from_left) & is_live
                for plane in range(2):
                    grad = grads[plane]
                    frame_grad = jnp.concatenate(
                        [
                            jnp.where(from_top, grad[:SUBLANES], 0.0),
                            grad[SUBLANES:],
                            jnp.where(from_top, 0.0, grad[:SUBLANES]),
                        ],
                        axis=0,
                    )
                    rows = pl.ds(row_at, frame)
                    acc[plane, rows, pl.ds(col_at, LANES)] += jnp.where(keep_left, frame_grad, 0.0)
                    acc[plane, rows, pl.ds(col_at + LANES, LANES)] += jnp.where(
                        keep_right, frame_grad, 0.0
                    )
        return carry

    lax.fori_loop(0, (stop - begin + GROUP - 1) // GROUP, group_body, 0)


def double_probe(probe, doubled):
    size = probe.shape[1]
    for plane in range(2):
        doubled[plane, :size, :] = probe[plane]
        doubled[plane, size:, :] = probe[plane]


def step_of(probe):
    return step_gain / (jnp.max(probe[0] * probe[0] + probe[1] * probe[1]) + 1e-06)


def pack_row_band(acc, row, count, out):
    rows = slice(row, row + count)
    width = acc.shape[2] - 2 * LANES
    halo = []
    for plane in range(2):
        out[:, plane * width : (plane + 1) * width] = acc[plane, rows, LANES : LANES + width]
        halo.append(
            jnp.where(
                lane_iota(count) < BORDER,
                acc[plane, rows, LANES + width :],
                acc[plane, rows, :LANES],
            )
        )
    out[:, 2 * width :] = pack_planes(*halo)


def pack_side_bands(acc, height, to_left, to_right):
    width = acc.shape[2] - 2 * LANES
    is_low = lane_iota(height) < BORDER
    for out, high_block in ((to_left, 0), (to_right, width)):
        out[...] = pack_planes(
            *[
                jnp.where(
                    is_low,
                    acc[plane, :height, high_block + LANES : high_block + 2 * LANES],
                    acc[plane, :height, high_block : high_block + LANES],
                )
                for plane in range(2)
            ]
        )


def add_row_band(acc, row, band):
    count = band.shape[0]
    rows = slice(row, row + count)
    width = acc.shape[2] - 2 * LANES
    lane = lane_iota(count)
    halo = unpack_planes(band[:, 2 * width :])
    for plane in range(2):
        acc[plane, rows, LANES : LANES + width] += band[:, plane * width : (plane + 1) * width]
        acc[plane, rows, :LANES] += jnp.where(lane >= LANES - BORDER, halo[plane], 0.0)
        acc[plane, rows, LANES + width :] += jnp.where(lane < BORDER, halo[plane], 0.0)


def add_side_band(acc, block, band):
    height = band.shape[0]
    lane = lane_iota(height)
    both = unpack_planes(band[...])
    for plane in range(2):
        acc[plane, :height, block : block + LANES] += jnp.where(
            lane >= LANES - BORDER, both[plane], 0.0
        )
        acc[plane, :height, block + LANES : block + 2 * LANES] += jnp.where(
            lane < BORDER, both[plane], 0.0
        )


def inner_start_kernel(
    positions, counts, objects, probe, amplitudes, right_f, left_f, right_b, left_b,
    cur, acc, doubled, held, order, sems,
):
    tile, width = objects.shape[1:]
    loads = [
        pltpu.make_async_copy(
            objects.at[plane],
            cur.at[plane, pl.ds(BORDER, tile), pl.ds(LANES, width)],
            sems.at[plane],
        )
        for plane in range(2)
    ]
    loads.append(pltpu.make_async_copy(amplitudes, held, sems.at[2]))
    for load in loads:
        load.start()
    double_probe(probe, doubled)
    acc[...] = jnp.zeros_like(acc)
    found = list_slots(order, positions, counts[0, 0], 0, tile - probe.shape[1], True)
    for load in loads:
        load.wait()
    gradient_slots(
        cur, acc, doubled, held, positions, order, 0, jnp.minimum(found, GROUP),
        (right_f, left_f, right_b, left_b),
    )


def inner_rest_kernel(
    positions, counts, cur, doubled, amplitudes, right_f, left_f, right_b, left_b, acc_in,
    acc, order,
):
    tile = cur.shape[1] - SUBLANES - BAND
    found = list_slots(order, positions, counts[0, 0], 0, tile - doubled.shape[2], True)
    gradient_slots(
        cur, acc, doubled, amplitudes, positions, order, jnp.minimum(found, GROUP), found,
        (right_f, left_f, right_b, left_b),
    )


def object_pack_kernel(cur, up, down, out):
    count = up.shape[0]
    width = up.shape[1] // 2
    tile = out.shape[0] - 2 * count
    is_low = lane_iota(count) < BORDER
    for row, band in ((0, up), (count + tile, down)):
        out[row : row + count, :] = pack_planes(
            *[
                jnp.where(
                    is_low,
                    band[:, plane * width : plane * width + LANES],
                    band[:, (plane + 1) * width - LANES : (plane + 1) * width],
                )
                for plane in range(2)
            ]
        )
    rows = slice(count, count + tile)
    is_low = lane_iota(tile) < BORDER
    out[rows, :] = pack_planes(
        *[
            jnp.where(is_low, cur[plane, rows, LANES : 2 * LANES], cur[plane, rows, width : width + LANES])
            for plane in range(2)
        ]
    )


def outer_kernel(
    positions, counts, up, down, left, right, doubled, amplitudes,
    right_f, left_f, right_b, left_b, cur_in, acc_in,
    cur, acc, to_up, to_down, to_left, to_right, order,
):
    extent = left.shape[0]
    tile, width = extent - BAND, up.shape[1] // 2
    lane = lane_iota(extent)
    lefts, rights = unpack_planes(left[...]), unpack_planes(right[...])
    for plane in range(2):
        cur[plane, :extent, :LANES] = jnp.where(lane >= LANES - BORDER, lefts[plane], 0.0)
        cur[plane, :extent, LANES + width :] = jnp.where(lane < BORDER, rights[plane], 0.0)
        inner = slice(LANES, LANES + width)
        cur[plane, :BORDER, inner] = up[:, plane * width : (plane + 1) * width]
        cur[plane, BORDER + tile : extent, inner] = down[:, plane * width : (plane + 1) * width]
        cur[plane, extent:, :] = jnp.zeros_like(cur[plane, extent:, :])
    found = list_slots(order, positions, counts[0, 0], 0, tile - doubled.shape[2], False)
    gradient_slots(
        cur, acc, doubled, amplitudes, positions, order, 0, found, (right_f, left_f, right_b, left_b)
    )
    pack_row_band(acc, 0, BAND, to_up)
    pack_row_band(acc, tile, BAND, to_down)
    pack_side_bands(acc, extent, to_left, to_right)


def corner_kernel(inset, up, down, left, right, to_left, to_right):
    count = up.shape[0]
    width = (up.shape[1] - LANES) // 2
    is_low = lane_iota(count) < BORDER
    for source, out in ((left, to_left), (right, to_right)):
        out[...] = source[...]
        for band, row in ((up, inset), (down, source.shape[0] - inset - count)):
            halo = unpack_planes(band[:, 2 * width :])
            parts = []
            for plane in range(2):
                if out is to_left:
                    low = band[:, plane * width : plane * width + LANES]
                    parts.append(jnp.where(is_low, low, halo[plane]))
                else:
                    high = band[:, (plane + 1) * width - LANES : (plane + 1) * width]
                    parts.append(jnp.where(is_low, halo[plane], high))
            out[row : row + count, :] += pack_planes(*parts)


def deep_kernel(
    positions, counts, probe, doubled, amplitudes, right_f, left_f, right_b, left_b, cur_in, acc_in,
    cur, acc, order,
):
    tile, width = cur.shape[1] - SUBLANES - BAND, cur.shape[2] - 2 * LANES
    rate = step_of(probe)
    middle, inner = slice(BORDER, BORDER + tile), slice(LANES, LANES + width)
    for plane in range(2):
        cur[plane, middle, inner] += rate * acc[plane, middle, inner]
    found = list_slots(
        order, positions, counts[0, 0], BORDER, tile - doubled.shape[2] - BORDER, True
    )
    gradient_slots(
        cur, acc, doubled, amplitudes, positions, order, 0, found, (right_f, left_f, right_b, left_b)
    )


def second_kernel(
    row_count, col_count,
    positions, counts, probe, doubled, amplitudes, right_f, left_f, right_b, left_b,
    up, down, left, right, cur_in, acc_in,
    cur, acc, to_up, to_down, to_left, to_right, order,
):
    tile, width = cur.shape[1] - SUBLANES - BAND, cur.shape[2] - 2 * LANES
    extent = tile + BAND
    rate = step_of(probe)
    row_at, row_last = lax.axis_index("row"), row_count - 1
    col_at, col_last = lax.axis_index("col"), col_count - 1
    top = jnp.where(row_at > 0, 1.0, 0.0)
    bottom = jnp.where(row_at < row_last, 1.0, 0.0)
    before = jnp.where(col_at > 0, 1.0, 0.0)
    after = jnp.where(col_at < col_last, 1.0, 0.0)
    found = list_slots(
        order, positions, counts[0, 0], BORDER, tile - doubled.shape[2] - BORDER, False
    )
    inner = slice(LANES, LANES + width)
    lane = lane_iota(extent)
    is_low, is_high = lane < BORDER, lane >= LANES - BORDER
    lefts, rights = unpack_planes(left[...]), unpack_planes(right[...])
    row_id = lax.broadcasted_iota(jnp.int32, (extent, LANES), 0)
    row_gain = rate * jnp.where(
        row_id < BORDER, top, jnp.where(row_id >= BORDER + tile, bottom, 1.0)
    )
    for plane in range(2):
        for row, band, on_grid in ((0, up, top), (tile, down, bottom)):
            halo_first = row == 0
            values = band[:, plane * width : (plane + 1) * width]
            own, out = (BORDER, 0) if halo_first else (0, BORDER)
            own_rows = slice(row + own, row + own + BORDER)
            out_rows = slice(row + out, row + out + BORDER)
            cur[plane, own_rows, inner] += rate * values[own : own + BORDER]
            acc[plane, own_rows, inner] += values[own : own + BORDER]
            cur[plane, out_rows, inner] += (rate * on_grid) * (
                acc[plane, out_rows, inner] + values[out : out + BORDER]
            )
            acc[plane, out_rows, inner] = jnp.zeros_like(acc[plane, out_rows, inner])
            halo = unpack_planes(band[:, 2 * width :])[plane]
            for lanes, keep in (
                (slice(0, LANES), is_high[:BAND]),
                (slice(LANES + width, None), is_low[:BAND]),
            ):
                acc[plane, row : row + BAND, lanes] += jnp.where(keep, halo, 0.0)
        for block, band, on_grid, own_first in (
            (0, lefts[plane], before, False),
            (width, rights[plane], after, True),
        ):
            low_block = slice(block, block + LANES)
            high_block = slice(block + LANES, block + 2 * LANES)
            own, out = (low_block, high_block) if own_first else (high_block, low_block)
            keep_own, keep_out = (is_high, is_low) if own_first else (is_low, is_high)
            own_band = jnp.where(keep_own, band, 0.0)
            cur[plane, :extent, own] += row_gain * own_band
            acc[plane, BORDER : BORDER + tile, own] += own_band[BORDER : BORDER + tile]
            cur[plane, :extent, out] += (row_gain * on_grid) * (
                acc[plane, :extent, out] + jnp.where(keep_out, band, 0.0)
            )
            acc[plane, :extent, out] = jnp.zeros_like(acc[plane, :extent, out])
    gradient_slots(
        cur, acc, doubled, amplitudes, positions, order, 0, found, (right_f, left_f, right_b, left_b)
    )
    pack_row_band(acc, 0, BORDER, to_up)
    pack_row_band(acc, BORDER + tile, BORDER, to_down)
    pack_side_bands(acc, extent, to_left, to_right)


CHUNKS = 4


def last_kernel(
    objects, probe, up, down, left, right, acc, estimate, correction,
    held, estimated, corrected, load_sems, store_sems,
):
    tile, width = objects.shape[1:]
    step = tile // CHUNKS

    def rows_of(ref, chunk):
        return ref.at[:, pl.ds(chunk * step, step), :]

    loads = [
        pltpu.make_async_copy(rows_of(objects, i), rows_of(held, i), load_sems.at[i])
        for i in range(CHUNKS)
    ]
    for load in loads:
        load.start()
    rate = step_of(probe)
    lane = lane_iota(tile)
    rows = slice(BORDER, BORDER + tile)
    lefts, rights = unpack_planes(left[rows, :]), unpack_planes(right[rows, :])
    for plane in range(2):
        lanes = slice(plane * width, (plane + 1) * width)
        corrected[plane] = acc[plane, rows, LANES : LANES + width]
        corrected[plane, :BORDER, :] += up[:, lanes]
        corrected[plane, tile - BORDER :, :] += down[:, lanes]
        corrected[plane, :, :LANES] += jnp.where(lane < BORDER, lefts[plane], 0.0)
        corrected[plane, :, width - LANES :] += jnp.where(
            lane >= LANES - BORDER, rights[plane], 0.0
        )
    stores = []
    for i in range(CHUNKS):
        loads[i].wait()
        part = slice(i * step, (i + 1) * step)
        corrected[:, part, :] = rate * corrected[:, part, :]
        estimated[:, part, :] = held[:, part, :] + corrected[:, part, :]
        for number, (source, target) in enumerate(
            ((corrected, correction), (estimated, estimate))
        ):
            store = pltpu.make_async_copy(
                rows_of(source, i), rows_of(target, i), store_sems.at[number, i]
            )
            store.start()
            stores.append(store)
    for store in stores:
        store.wait()


VMEM = pl.BlockSpec(memory_space=pltpu.VMEM)
SMEM = pl.BlockSpec(memory_space=pltpu.SMEM)
ANY = pl.BlockSpec(memory_space=pl.ANY)
PARAMS = pltpu.CompilerParams(vmem_limit_bytes=32 * 1024 * 1024)


def f32(*shape):
    return pltpu.VMEM(shape, jnp.float32)


def in_vmem(array):
    return pltpu.with_memory_space_constraint(array, pltpu.VMEM)


def swap_along(axis, to_before, to_after):
    count = lax.axis_size(axis)
    forth = [(i, i + 1) for i in range(count - 1)]
    back = [(i + 1, i) for i in range(count - 1)]
    return (
        in_vmem(lax.ppermute(to_after, axis, forth)),
        in_vmem(lax.ppermute(to_before, axis, back)),
    )


def on_device(object_field, probe_field, amplitudes, positions, counts):
    tile, width = object_field.shape[1:]
    probe = probe_field.shape[1]
    extent = tile + BAND
    padded = f32(2, extent + SUBLANES, width + 2 * LANES)
    doubled_shape = f32(2, 2 * probe, probe)
    tables = tuple(in_vmem(jnp.asarray(table)) for table in dft_blocks(probe))
    places = positions[0, 0]
    order = pltpu.SMEM((amplitudes.shape[0],), jnp.int32)
    sides = (f32(extent, LANES), f32(extent, LANES))

    def row_bands(count):
        band = f32(count, 2 * width + LANES)
        return (band, band)

    def call(kernel, name, scalars, arrays, outs, scratch=(), aliases=None):
        return pl.pallas_call(
            kernel,
            out_shape=outs,
            in_specs=[SMEM] * len(scalars) + [VMEM] * len(arrays),
            out_specs=jax.tree.map(lambda out: VMEM, outs),
            scratch_shapes=list(scratch),
            input_output_aliases=aliases or {},
            compiler_params=PARAMS,
            name=name,
        )(*scalars, *arrays)

    slots = (places, counts)
    strips = [
        jnp.concatenate([object_field[0, rows], object_field[1, rows]], axis=1)
        for rows in (slice(0, BORDER), slice(tile - BORDER, tile))
    ]
    up, down = swap_along("row", *strips)
    cur, acc, doubled, held = pl.pallas_call(
        inner_start_kernel,
        out_shape=(padded, padded, doubled_shape, f32(*amplitudes.shape)),
        in_specs=[SMEM, SMEM, ANY, VMEM, ANY] + [VMEM] * 4,
        out_specs=(VMEM,) * 4,
        scratch_shapes=[order, pltpu.SemaphoreType.DMA((3,))],
        compiler_params=PARAMS,
        name="inner_start",
    )(*slots, object_field, probe_field, amplitudes, *tables)
    packed = call(object_pack_kernel, "object_pack", (), (cur, up, down), sides[0])
    left, right = swap_along("col", packed, packed)
    acc = call(
        inner_rest_kernel, "inner_rest", slots, (cur, doubled, held, *tables, acc),
        padded, (order,), {9: 0},
    )
    cur, acc, to_up, to_down, to_left, to_right = call(
        outer_kernel, "outer", slots, (up, down, left, right, doubled, held, *tables, cur, acc),
        (padded, padded, *row_bands(BAND), *sides), (order,), {12: 0, 13: 1},
    )
    up, down = swap_along("row", to_up, to_down)
    cur, acc = call(
        deep_kernel, "deep", slots, (probe_field, doubled, held, *tables, cur, acc),
        (padded, padded), (order,), {9: 0, 10: 1},
    )
    to_left, to_right = call(
        functools.partial(corner_kernel, 0), "corners", (), (up, down, to_left, to_right), sides
    )
    left, right = swap_along("col", to_left, to_right)
    cur, acc, to_up, to_down, to_left, to_right = call(
        functools.partial(second_kernel, lax.axis_size("row"), lax.axis_size("col")),
        "second", slots,
        (probe_field, doubled, held, *tables, up, down, left, right, cur, acc),
        (padded, padded, *row_bands(BORDER), *sides), (order,), {13: 0, 14: 1},
    )
    up, down = swap_along("row", to_up, to_down)
    to_left, to_right = call(
        functools.partial(corner_kernel, BORDER), "last_corners", (),
        (up, down, to_left, to_right), sides,
    )
    left, right = swap_along("col", to_left, to_right)
    whole = pltpu.VMEM((2, tile, width), jnp.float32)
    result = jax.ShapeDtypeStruct((2, tile, width), jnp.float32)
    estimate, correction = pl.pallas_call(
        last_kernel,
        out_shape=(result, result),
        in_specs=[ANY] + [VMEM] * 6,
        out_specs=(ANY, ANY),
        scratch_shapes=[
            whole, whole, whole,
            pltpu.SemaphoreType.DMA((CHUNKS,)), pltpu.SemaphoreType.DMA((2, CHUNKS)),
        ],
        compiler_params=PARAMS,
        name="finish",
    )(object_field, probe_field, up, down, left, right, acc)
    return estimate, correction


def solution(mesh):
    placed = (
        P(None, "row", "col"),
        P(),
        P("row", None, "col"),
        P("row", "col", None, None),
        P("row", "col"),
    )
    return jax.shard_map(
        on_device,
        mesh=mesh,
        in_specs=placed,
        out_specs=(P(None, "row", "col"), P(None, "row", "col")),
        check_vma=False,
    )
```

time: 119 us -> 93.3 us (0.78)
  waiting for transfers between devices: 41.6 us -> 25.1 us
  Pallas kernels: 36.7 us -> 21.1 us
  local copies, waits for them, and re-layouts: 5.16 us -> 9.52 us
  starting transfers between devices: 32.4 us -> 35 us
    pallas_call x6 -> x9, Pallas kernels: 36.7 us -> 21.1 us  [the longest x7 14.7 us: call(): pl.pallas_call(kernel, out_shape=outs, in_specs=[SMEM] * len(scalars) + [...]
    ppermute x6, waiting for transfers between devices: 32.2 us -> 17.2 us  [swap_along(): lax.ppermute(to_before, axis, back)]
    unnamed x24 -> x20, local copies, waits for them, and re-layouts: 4.17 us -> 8.56 us
    ppermute x6, starting transfers between devices: 20.3 us -> 24.5 us  [swap_along(): lax.ppermute(to_after, axis, forth)]
    ppermute x6, starting transfers between devices: 12.1 us -> 10.5 us  [swap_along(): lax.ppermute(to_before, axis, back)]
    ppermute x6, waiting for transfers between devices: 9.35 us -> 7.85 us  [swap_along(): lax.ppermute(to_after, axis, forth)]
  transfers between devices with their start and end apart: 12 -> 12, of which waited for: 12 -> 8; matrix products, arithmetic and copies ran while one was open for 0% -> 0% of each run, Pallas kernels for 0% -> 11%
where the time goes in v2:
time: 93.3 us; the launch traced here: 92.4 us
  starting transfers between devices  35 us (38%)
  waiting for transfers between devices  25.1 us (27%)
  Pallas kernels  21.1 us (23%)
  local copies, waits for them, and re-layouts  9.52 us (10%)
  between operations  1.66 us (2%)
    ppermute x6, starting transfers between devices, swap_along(): lax.ppermute(to_after, axis, forth)  24.5 us
    ppermute x6, waiting for transfers between devices, swap_along(): lax.ppermute(to_before, axis, back)  17.2 us
    pallas_call x7, Pallas kernels, call(): pl.pallas_call(kernel, out_shape=outs, in_specs=[SMEM] * len(scalars) + [...  14.7 us
    ppermute x6, starting transfers between devices, swap_along(): lax.ppermute(to_before, axis, back)  10.5 us
    unnamed x20, local copies, waits for them, and re-layouts  8.56 us
    ppermute x6, waiting for transfers between devices, swap_along(): lax.ppermute(to_after, axis, forth)  7.85 us
    pallas_call x1, Pallas kernels, on_device(): pl.pallas_call(inner_start_kernel, out_shape=(padded, padded, doubled_sha...  3.72 us
    pallas_call x1, Pallas kernels, on_device(): pl.pallas_call(last_kernel, out_shape=(result, result), in_specs=[ANY] +...  2.6 us
  transfers between devices with their start and end apart: 12, of which 8 were waited for; matrix products, arithmetic and copies ran while one was open for 0% of the time, Pallas kernels for 11%

profile of v2, /device:TPU:1, one launch (start us, length us, event | category | flops | bytes accessed | tf_op | source)
XLA Modules:
  0.0 92.4 jit_solution(11694942881967696530)
XLA Ops:
  1.6 3.9 %collective-permute-start = (f32[32,1024]{1,0:T(8,128)S(1)}, f32[32,1024]{1,0:T(8,128)S(1)}, u32[]{:S(2)}, u32[]{:S(2)}) collective-permute-start(f32[32,1024]{1,0:T(8,128)S(1)} %pad_maximum_fusion), channel_id=1, source_target_pairs={{0,8},{8,16},{16,24},{1,9},{9,17},{17,25},{2,10},{10,18},{18,26},{... | collective-permute-start | bytes 393224 | tf_op jit(solution)/shard_map/ppermute | solution.py:533
  5.6 1.3 %collective-permute-start.1 = (f32[32,1024]{1,0:T(8,128)S(1)}, f32[32,1024]{1,0:T(8,128)S(1)}, u32[]{:S(2)}, u32[]{:S(2)}) collective-permute-start(f32[32,1024]{1,0:T(8,128)S(1)} %pad_maximum_fusion.1), channel_id=1, source_target_pairs={{8,0},{16,8},{24,16},{9,1},{17,9},{25,17},{10,2},{18,10},{26,18},{... | collective-permute-start | bytes 393224 | tf_op jit(solution)/shard_map/ppermute | solution.py:534
  11.5 1.6 %copy-done.5 = f32[2,512,512]{2,1,0:T(8,128)S(1)} copy-done((f32[2,512,512]{2,1,0:T(8,128)S(1)}, f32[2,512,512]{2,1,0:T(8,128)}, u32[]{:S(2)}) %copy-start.5) | copy-done | bytes 2097176
  14.0 1.4 %copy-done.8 = f32[24,128,128]{2,1,0:T(8,128)S(1)} copy-done((f32[24,128,128]{2,1,0:T(8,128)S(1)}, f32[24,128,128]{2,1,0:T(8,128)}, u32[]{:S(2)}) %copy-start.8) | copy-done | bytes 1572888
  16.1 3.7 %inner_start.1 = (f32[2,584,768]{2,1,0:T(8,128)S(1)}, f32[2,584,768]{2,1,0:T(8,128)S(1)}, f32[2,256,128]{2,1,0:T(8,128)S(1)}, f32[24,128,128]{2,1,0:T(8,128)S(1)}) custom-call(s32[2,24]{1,0:T(2,128)S(1)} %bitcast.9, s32[1,1]{1,0:T(1,128)S(6)} %copy.25.counts, f32[2,512,512]{2,1,0:T(8,128)S(1)} %copy-done.5, f32[2,128,128]{2,1,0:T(8,128)S(1)} %copy-done.7, ...), custom_call_target="tpu_custom_call" | custom-call | tf_op jit(solution)/shard_map/inner_start/pallas_call | solution.py:571
  20.0 2.8 %collective-permute-start.3 = (f32[576,128]{1,0:T(8,128)S(1)}, f32[576,128]{1,0:T(8,128)S(1)}, u32[]{:S(2)}, u32[]{:S(2)}) collective-permute-start(f32[576,128]{1,0:T(8,128)S(1)} %object_pack.1), channel_id=1, source_target_pairs={{1,0},{2,1},{3,2},{4,3},{5,4},{6,5},{7,6},{9,8},{10,9},{11,10},{12... | collective-permute-start | bytes 884744 | tf_op jit(solution)/shard_map/ppermute | solution.py:534
  22.8 3.1 %collective-permute-start.2 = (f32[576,128]{1,0:T(8,128)S(1)}, f32[576,128]{1,0:T(8,128)S(1)}, u32[]{:S(2)}, u32[]{:S(2)}) collective-permute-start(f32[576,128]{1,0:T(8,128)S(1)} %object_pack.1), channel_id=1, source_target_pairs={{0,1},{1,2},{2,3},{3,4},{4,5},{5,6},{6,7},{8,9},{9,10},{10,11},{11... | collective-permute-start | bytes 884744 | tf_op jit(solution)/shard_map/ppermute | solution.py:533
  26.0 3.1 %inner_rest.1.acc_in = f32[2,584,768]{2,1,0:T(8,128)S(1)} custom-call(s32[2,24]{1,0:T(2,128)S(1)} %bitcast.10, s32[1,1]{1,0:T(1,128)S(6)} %copy.25.counts, f32[2,584,768]{2,1,0:T(8,128)S(1)} %get-tuple-element.25.cur.cur_in, f32[2,256,128]{2,1,0:T(8,128)S(1)} %get-tuple-element.23.doubled, ...), custom_call_target="tpu_custom_call", output_to_operand_aliasing={{}: (9, {})} | custom-call | tf_op jit(solution)/shard_map/inner_rest/pallas_call | solution.py:554
  29.6 3.5 %outer.1 = (f32[2,584,768]{2,1,0:T(8,128)S(1)}, f32[2,584,768]{2,1,0:T(8,128)S(1)}, f32[64,1152]{1,0:T(8,128)S(1)}, f32[64,1152]{1,0:T(8,128)S(1)}, f32[576,128]{1,0:T(8,128)S(1)}, /*index=5*/f32[576,128]{1,0:T(8,128)S(1)}) custom-call(s32[2,24]{1,0:T(2,128)S(1)} %bitcast.11, ...), custom_call_target="tpu_custom_call", output_to_operand_aliasing={{0}: (12, {}), {1}: (13, {})} | custom-call | tf_op jit(solution)/shard_map/outer/pallas_call | solution.py:554
  33.1 4.3 %collective-permute-start.4 = (f32[64,1152]{1,0:T(8,128)S(1)}, f32[64,1152]{1,0:T(8,128)S(1)}, u32[]{:S(2)}, u32[]{:S(2)}) collective-permute-start(f32[64,1152]{1,0:T(8,128)S(1)} %get-tuple-element.27), channel_id=1, source_target_pairs={{0,8},{8,16},{16,24},{1,9},{9,17},{17,25},{2,10},{10,18},{18,26},{... | collective-permute-start | bytes 884744 | tf_op jit(solution)/shard_map/ppermute | solution.py:533
  38.8 4.8 %collective-permute-done.4.up = f32[64,1152]{1,0:T(8,128)S(1)} collective-permute-done((f32[64,1152]{1,0:T(8,128)S(1)}, f32[64,1152]{1,0:T(8,128)S(1)}, u32[]{:S(2)}, u32[]{:S(2)}) %collective-permute-start.4) | collective-permute-done | bytes 294944 | tf_op jit(solution)/shard_map/ppermute | solution.py:533
  43.6 6.5 %collective-permute-done.5.down = f32[64,1152]{1,0:T(8,128)S(1)} collective-permute-done((f32[64,1152]{1,0:T(8,128)S(1)}, f32[64,1152]{1,0:T(8,128)S(1)}, u32[]{:S(2)}, u32[]{:S(2)}) %collective-permute-start.5) | collective-permute-done | bytes 294944 | tf_op jit(solution)/shard_map/ppermute | solution.py:534
  50.3 6.8 %collective-permute-start.6 = (f32[576,128]{1,0:T(8,128)S(1)}, f32[576,128]{1,0:T(8,128)S(1)}, u32[]{:S(2)}, u32[]{:S(2)}) collective-permute-start(f32[576,128]{1,0:T(8,128)S(1)} %get-tuple-element.31), channel_id=1, source_target_pairs={{0,1},{1,2},{2,3},{3,4},{4,5},{5,6},{6,7},{8,9},{9,10},{10,11},{11... | collective-permute-start | bytes 884744 | tf_op jit(solution)/shard_map/ppermute | solution.py:533
  57.0 1.9 %collective-permute-start.7 = (f32[576,128]{1,0:T(8,128)S(1)}, f32[576,128]{1,0:T(8,128)S(1)}, u32[]{:S(2)}, u32[]{:S(2)}) collective-permute-start(f32[576,128]{1,0:T(8,128)S(1)} %get-tuple-element.32), channel_id=1, source_target_pairs={{1,0},{2,1},{3,2},{4,3},{5,4},{6,5},{7,6},{9,8},{10,9},{11,10},{12... | collective-permute-start | bytes 884744 | tf_op jit(solution)/shard_map/ppermute | solution.py:534
  58.9 3.6 %deep.1 = (f32[2,584,768]{2,1,0:T(8,128)S(1)}, f32[2,584,768]{2,1,0:T(8,128)S(1)}) custom-call(s32[2,24]{1,0:T(2,128)S(1)} %bitcast.12, s32[1,1]{1,0:T(1,128)S(6)} %copy.25.counts, f32[2,128,128]{2,1,0:T(8,128)S(1)} %copy-done.7, f32[2,256,128]{2,1,0:T(8,128)S(1)} %get-tuple-element.23.doubled, ...), custom_call_target="tpu_custom_call", output_to_operand_aliasing={{0}: (9, {}), {1}: (10, {})} | custom-call | tf_op jit(solution)/shard_map/deep/pallas_call | solution.py:554
  62.5 2.5 %collective-permute-done.7.right = f32[576,128]{1,0:T(8,128)S(1)} collective-permute-done((f32[576,128]{1,0:T(8,128)S(1)}, f32[576,128]{1,0:T(8,128)S(1)}, u32[]{:S(2)}, u32[]{:S(2)}) %collective-permute-start.7) | collective-permute-done | bytes 294944 | tf_op jit(solution)/shard_map/ppermute | solution.py:534
  65.1 4.2 %second.1 = (f32[2,584,768]{2,1,0:T(8,128)S(1)}, f32[2,584,768]{2,1,0:T(8,128)S(1)}, f32[32,1152]{1,0:T(8,128)S(1)}, f32[32,1152]{1,0:T(8,128)S(1)}, f32[576,128]{1,0:T(8,128)S(1)}, /*index=5*/f32[576,128]{1,0:T(8,128)S(1)}) custom-call(s32[2,24]{1,0:T(2,128)S(1)} %bitcast.13, ...), custom_call_target="tpu_custom_call", output_to_operand_aliasing={{0}: (13, {}), {1}: (14, {})} | custom-call | tf_op jit(solution)/shard_map/second/pallas_call | solution.py:554
  69.2 2.3 %collective-permute-start.8 = (f32[32,1152]{1,0:T(8,128)S(1)}, f32[32,1152]{1,0:T(8,128)S(1)}, u32[]{:S(2)}, u32[]{:S(2)}) collective-permute-start(f32[32,1152]{1,0:T(8,128)S(1)} %get-tuple-element.37), channel_id=1, source_target_pairs={{0,8},{8,16},{16,24},{1,9},{9,17},{17,25},{2,10},{10,18},{18,26},{... | collective-permute-start | bytes 442376 | tf_op jit(solution)/shard_map/ppermute | solution.py:533
  73.6 3.8 %collective-permute-done.9.down = f32[32,1152]{1,0:T(8,128)S(1)} collective-permute-done((f32[32,1152]{1,0:T(8,128)S(1)}, f32[32,1152]{1,0:T(8,128)S(1)}, u32[]{:S(2)}, u32[]{:S(2)}) %collective-permute-start.9) | collective-permute-done | bytes 147488 | tf_op jit(solution)/shard_map/ppermute | solution.py:534
  77.6 4.0 %collective-permute-start.10 = (f32[576,128]{1,0:T(8,128)S(1)}, f32[576,128]{1,0:T(8,128)S(1)}, u32[]{:S(2)}, u32[]{:S(2)}) collective-permute-start(f32[576,128]{1,0:T(8,128)S(1)} %get-tuple-element.41), channel_id=1, source_target_pairs={{0,1},{1,2},{2,3},{3,4},{4,5},{5,6},{6,7},{8,9},{9,10},{10,11},{11... | collective-permute-start | bytes 884744 | tf_op jit(solution)/shard_map/ppermute | solution.py:533
  81.6 1.9 %collective-permute-start.11 = (f32[576,128]{1,0:T(8,128)S(1)}, f32[576,128]{1,0:T(8,128)S(1)}, u32[]{:S(2)}, u32[]{:S(2)}) collective-permute-start(f32[576,128]{1,0:T(8,128)S(1)} %get-tuple-element.42), channel_id=1, source_target_pairs={{1,0},{2,1},{3,2},{4,3},{5,4},{6,5},{7,6},{9,8},{10,9},{11,10},{12... | collective-permute-start | bytes 884744 | tf_op jit(solution)/shard_map/ppermute | solution.py:534
  83.5 1.7 %collective-permute-done.10.left = f32[576,128]{1,0:T(8,128)S(1)} collective-permute-done((f32[576,128]{1,0:T(8,128)S(1)}, f32[576,128]{1,0:T(8,128)S(1)}, u32[]{:S(2)}, u32[]{:S(2)}) %collective-permute-start.10) | collective-permute-done | bytes 294944 | tf_op jit(solution)/shard_map/ppermute | solution.py:533
  85.2 4.4 %collective-permute-done.11.right = f32[576,128]{1,0:T(8,128)S(1)} collective-permute-done((f32[576,128]{1,0:T(8,128)S(1)}, f32[576,128]{1,0:T(8,128)S(1)}, u32[]{:S(2)}, u32[]{:S(2)}) %collective-permute-start.11) | collective-permute-done | bytes 294944 | tf_op jit(solution)/shard_map/ppermute | solution.py:534
  89.6 2.6 %finish.1 = (f32[2,512,512]{2,1,0:T(8,128)}, f32[2,512,512]{2,1,0:T(8,128)}) custom-call(f32[2,512,512]{2,1,0:T(8,128)S(1)} %copy-done.6, f32[2,128,128]{2,1,0:T(8,128)S(1)} %copy-done.7, f32[32,1152]{1,0:T(8,128)S(1)} %collective-permute-done.8.up, f32[32,1152]{1,0:T(8,128)S(1)} %collective-permute-done.9.down, ...), custom_call_target="tpu_custom_call" | custom-call | tf_op jit(solution)/shard_map/finish/pallas_call | solution.py:613
  (32 shorter events, 10.9 us)
Async XLA Ops:
  1.6 18.2 %collective-permute-start = (f32[32,1024]{1,0:T(8,128)S(1)}, f32[32,1024]{1,0:T(8,128)S(1)}, u32[]{:S(2)}, u32[]{:S(2)}) collective-permute-start(f32[32,1024]{1,0:T(8,128)S(1)} %pad_maximum_fusion), channel_id=1, source_target_pairs={{0,8},{8,16},{16,24},{1,9},{9,17},{17,25},{2,10},{10,18},{18,26},{... | collective-permute-start | bytes 393224 | tf_op jit(solution)/shard_map/ppermute | solution.py:533
  5.6 14.3 %collective-permute-start.1 = (f32[32,1024]{1,0:T(8,128)S(1)}, f32[32,1024]{1,0:T(8,128)S(1)}, u32[]{:S(2)}, u32[]{:S(2)}) collective-permute-start(f32[32,1024]{1,0:T(8,128)S(1)} %pad_maximum_fusion.1), channel_id=1, source_target_pairs={{8,0},{16,8},{24,16},{9,1},{17,9},{25,17},{10,2},{18,10},{26,18},{... | collective-permute-start | bytes 393224 | tf_op jit(solution)/shard_map/ppermute | solution.py:534
  7.5 1.0 %copy-start = (bf16[256,768]{1,0:T(8,128)(2,1)S(1)}, bf16[256,768]{1,0:T(8,128)(2,1)}, u32[]{:S(2)}) copy-start(bf16[256,768]{1,0:T(8,128)(2,1)} %constant.11.clone.left_b) | copy-start | bytes 1179652
  8.5 1.0 %copy-start.1 = (bf16[768,256]{1,0:T(8,128)(2,1)S(1)}, bf16[768,256]{1,0:T(8,128)(2,1)}, u32[]{:S(2)}) copy-start(bf16[768,256]{1,0:T(8,128)(2,1)} %constant.10.clone.right_b) | copy-start | bytes 1179652
  9.5 1.0 %copy-start.2 = (bf16[256,768]{1,0:T(8,128)(2,1)S(1)}, bf16[256,768]{1,0:T(8,128)(2,1)}, u32[]{:S(2)}) copy-start(bf16[256,768]{1,0:T(8,128)(2,1)} %constant.9.clone.left_f) | copy-start | bytes 1179652
  10.5 1.0 %copy-start.3 = (bf16[768,256]{1,0:T(8,128)(2,1)S(1)}, bf16[768,256]{1,0:T(8,128)(2,1)}, u32[]{:S(2)}) copy-start(bf16[768,256]{1,0:T(8,128)(2,1)} %constant.8.clone.right_f) | copy-start | bytes 1179652
  11.5 1.6 %copy-start.5 = (f32[2,512,512]{2,1,0:T(8,128)S(1)}, f32[2,512,512]{2,1,0:T(8,128)}, u32[]{:S(2)}) copy-start(f32[2,512,512]{2,1,0:T(8,128)} %objects.3) | copy-start | bytes 6291460
  13.1 0.9 copy-start.7
  14.0 1.4 %copy-start.8 = (f32[24,128,128]{2,1,0:T(8,128)S(1)}, f32[24,128,128]{2,1,0:T(8,128)}, u32[]{:S(2)}) copy-start(f32[24,128,128]{2,1,0:T(8,128)} %amplitudes.1) | copy-start | bytes 4718596
  15.4 0.7 copy-start.9
  16.1 9.9 %copy-start.4 = (bf16[768,256]{1,0:T(8,128)(2,1)S(1)}, bf16[768,256]{1,0:T(8,128)(2,1)}, u32[]{:S(2)}) copy-start(bf16[768,256]{1,0:T(8,128)(2,1)} %constant.8.clone.right_f) | copy-start | bytes 1179652
  20.0 9.1 %collective-permute-start.3 = (f32[576,128]{1,0:T(8,128)S(1)}, f32[576,128]{1,0:T(8,128)S(1)}, u32[]{:S(2)}, u32[]{:S(2)}) collective-permute-start(f32[576,128]{1,0:T(8,128)S(1)} %object_pack.1), channel_id=1, source_target_pairs={{1,0},{2,1},{3,2},{4,3},{5,4},{6,5},{7,6},{9,8},{10,9},{11,10},{12... | collective-permute-start | bytes 884744 | tf_op jit(solution)/shard_map/ppermute | solution.py:534
  22.8 6.8 %collective-permute-start.2 = (f32[576,128]{1,0:T(8,128)S(1)}, f32[576,128]{1,0:T(8,128)S(1)}, u32[]{:S(2)}, u32[]{:S(2)}) collective-permute-start(f32[576,128]{1,0:T(8,128)S(1)} %object_pack.1), channel_id=1, source_target_pairs={{0,1},{1,2},{2,3},{3,4},{4,5},{5,6},{6,7},{8,9},{9,10},{10,11},{11... | collective-permute-start | bytes 884744 | tf_op jit(solution)/shard_map/ppermute | solution.py:533
  33.1 10.4 %collective-permute-start.4 = (f32[64,1152]{1,0:T(8,128)S(1)}, f32[64,1152]{1,0:T(8,128)S(1)}, u32[]{:S(2)}, u32[]{:S(2)}) collective-permute-start(f32[64,1152]{1,0:T(8,128)S(1)} %get-tuple-element.27), channel_id=1, source_target_pairs={{0,8},{8,16},{16,24},{1,9},{9,17},{17,25},{2,10},{10,18},{18,26},{... | collective-permute-start | bytes 884744 | tf_op jit(solution)/shard_map/ppermute | solution.py:533
  37.5 12.6 %collective-permute-start.5 = (f32[64,1152]{1,0:T(8,128)S(1)}, f32[64,1152]{1,0:T(8,128)S(1)}, u32[]{:S(2)}, u32[]{:S(2)}) collective-permute-start(f32[64,1152]{1,0:T(8,128)S(1)} %get-tuple-element.28), channel_id=1, source_target_pairs={{8,0},{16,8},{24,16},{9,1},{17,9},{25,17},{10,2},{18,10},{26,18},{... | collective-permute-start | bytes 884744 | tf_op jit(solution)/shard_map/ppermute | solution.py:534
  50.3 12.3 %collective-permute-start.6 = (f32[576,128]{1,0:T(8,128)S(1)}, f32[576,128]{1,0:T(8,128)S(1)}, u32[]{:S(2)}, u32[]{:S(2)}) collective-permute-start(f32[576,128]{1,0:T(8,128)S(1)} %get-tuple-element.31), channel_id=1, source_target_pairs={{0,1},{1,2},{2,3},{3,4},{4,5},{5,6},{6,7},{8,9},{9,10},{10,11},{11... | collective-permute-start | bytes 884744 | tf_op jit(solution)/shard_map/ppermute | solution.py:533
  57.0 8.0 %collective-permute-start.7 = (f32[576,128]{1,0:T(8,128)S(1)}, f32[576,128]{1,0:T(8,128)S(1)}, u32[]{:S(2)}, u32[]{:S(2)}) collective-permute-start(f32[576,128]{1,0:T(8,128)S(1)} %get-tuple-element.32), channel_id=1, source_target_pairs={{1,0},{2,1},{3,2},{4,3},{5,4},{6,5},{7,6},{9,8},{10,9},{11,10},{12... | collective-permute-start | bytes 884744 | tf_op jit(solution)/shard_map/ppermute | solution.py:534
  65.1 24.6 %copy-start.6 = (f32[2,512,512]{2,1,0:T(8,128)S(1)}, f32[2,512,512]{2,1,0:T(8,128)}, u32[]{:S(2)}) copy-start(f32[2,512,512]{2,1,0:T(8,128)} %objects.3) | copy-start | bytes 6291460
  69.2 4.4 %collective-permute-start.8 = (f32[32,1152]{1,0:T(8,128)S(1)}, f32[32,1152]{1,0:T(8,128)S(1)}, u32[]{:S(2)}, u32[]{:S(2)}) collective-permute-start(f32[32,1152]{1,0:T(8,128)S(1)} %get-tuple-element.37), channel_id=1, source_target_pairs={{0,8},{8,16},{16,24},{1,9},{9,17},{17,25},{2,10},{10,18},{18,26},{... | collective-permute-start | bytes 442376 | tf_op jit(solution)/shard_map/ppermute | solution.py:533
  71.6 5.9 %collective-permute-start.9 = (f32[32,1152]{1,0:T(8,128)S(1)}, f32[32,1152]{1,0:T(8,128)S(1)}, u32[]{:S(2)}, u32[]{:S(2)}) collective-permute-start(f32[32,1152]{1,0:T(8,128)S(1)} %get-tuple-element.38), channel_id=1, source_target_pairs={{8,0},{16,8},{24,16},{9,1},{17,9},{25,17},{10,2},{18,10},{26,18},{... | collective-permute-start | bytes 442376 | tf_op jit(solution)/shard_map/ppermute | solution.py:534
  77.6 7.6 %collective-permute-start.10 = (f32[576,128]{1,0:T(8,128)S(1)}, f32[576,128]{1,0:T(8,128)S(1)}, u32[]{:S(2)}, u32[]{:S(2)}) collective-permute-start(f32[576,128]{1,0:T(8,128)S(1)} %get-tuple-element.41), channel_id=1, source_target_pairs={{0,1},{1,2},{2,3},{3,4},{4,5},{5,6},{6,7},{8,9},{9,10},{10,11},{11... | collective-permute-start | bytes 884744 | tf_op jit(solution)/shard_map/ppermute | solution.py:533
  81.6 8.0 %collective-permute-start.11 = (f32[576,128]{1,0:T(8,128)S(1)}, f32[576,128]{1,0:T(8,128)S(1)}, u32[]{:S(2)}, u32[]{:S(2)}) collective-permute-start(f32[576,128]{1,0:T(8,128)S(1)} %get-tuple-element.42), channel_id=1, source_target_pairs={{1,0},{2,1},{3,2},{4,3},{5,4},{6,5},{7,6},{9,8},{10,9},{11,10},{12... | collective-permute-start | bytes 884744 | tf_op jit(solution)/shard_map/ppermute | solution.py:534

commit v3 on v2

--- a/solution.py
+++ b/solution.py
@@ -10,7 +10,6 @@
 
 BORDER = 32
 BAND = 2 * BORDER
-ITERS = 2
 LANES = 128
 SUBLANES = 8
 GROUP = 8
@@ -199,13 +198,6 @@
     lax.fori_loop(0, (stop - begin + GROUP - 1) // GROUP, group_body, 0)
 
 
-def double_probe(probe, doubled):
-    size = probe.shape[1]
-    for plane in range(2):
-        doubled[plane, :size, :] = probe[plane]
-        doubled[plane, size:, :] = probe[plane]
-
-
 def step_of(probe):
     return step_gain / (jnp.max(probe[0] * probe[0] + probe[1] * probe[1]) + 1e-06)
 
@@ -242,55 +234,37 @@
         )
 
 
-def add_row_band(acc, row, band):
-    count = band.shape[0]
-    rows = slice(row, row + count)
-    width = acc.shape[2] - 2 * LANES
-    lane = lane_iota(count)
-    halo = unpack_planes(band[:, 2 * width :])
+def inner_start_kernel(
+    positions, counts, objects, probe_in, amplitudes, *refs
+):
+    table_count = (len(refs) - 6) // 2
+    tables_in, refs = refs[:table_count], refs[table_count:]
+    cur, acc, doubled, held = refs[:4]
+    tables, (order, sems) = refs[4:-2], refs[-2:]
+    tile, width = objects.shape[1:]
+    probe = probe_in.shape[1]
+    sources = [(amplitudes, held)] + list(zip(tables_in, tables))
     for plane in range(2):
-        acc[plane, rows, LANES : LANES + width] += band[:, plane * width : (plane + 1) * width]
-        acc[plane, rows, :LANES] += jnp.where(lane >= LANES - BORDER, halo[plane], 0.0)
-        acc[plane, rows, LANES + width :] += jnp.where(lane < BORDER, halo[plane], 0.0)
-
-
-def add_side_band(acc, block, band):
-    height = band.shape[0]
-    lane = lane_iota(height)
-    both = unpack_planes(band[...])
-    for plane in range(2):
-        acc[plane, :height, block : block + LANES] += jnp.where(
-            lane >= LANES - BORDER, both[plane], 0.0
+        sources.append(
+            (
+                objects.at[plane],
+                cur.at[plane, pl.ds(BORDER, tile), pl.ds(LANES, width)],
+            )
         )
-        acc[plane, :height, block + LANES : block + 2 * LANES] += jnp.where(
-            lane < BORDER, both[plane], 0.0
-        )
-
-
-def inner_start_kernel(
-    positions, counts, objects, probe, amplitudes, right_f, left_f, right_b, left_b,
-    cur, acc, doubled, held, order, sems,
-):
-    tile, width = objects.shape[1:]
+        for row in (0, probe):
+            sources.append((probe_in.at[plane], doubled.at[plane, pl.ds(row, probe), :]))
     loads = [
-        pltpu.make_async_copy(
-            objects.at[plane],
-            cur.at[plane, pl.ds(BORDER, tile), pl.ds(LANES, width)],
-            sems.at[plane],
-        )
-        for plane in range(2)
+        pltpu.make_async_copy(source, target, sems.at[i])
+        for i, (source, target) in enumerate(sources)
     ]
-    loads.append(pltpu.make_async_copy(amplitudes, held, sems.at[2]))
     for load in loads:
         load.start()
-    double_probe(probe, doubled)
     acc[...] = jnp.zeros_like(acc)
-    found = list_slots(order, positions, counts[0, 0], 0, tile - probe.shape[1], True)
+    found = list_slots(order, positions, counts[0, 0], 0, tile - probe, True)
     for load in loads:
         load.wait()
     gradient_slots(
-        cur, acc, doubled, held, positions, order, 0, jnp.minimum(found, GROUP),
-        (right_f, left_f, right_b, left_b),
+        cur, acc, doubled, held, positions, order, 0, jnp.minimum(found, GROUP), tables
     )
 
 
@@ -357,23 +331,48 @@
     pack_side_bands(acc, extent, to_left, to_right)
 
 
-def corner_kernel(inset, up, down, left, right, to_left, to_right):
+def corner_parts(band, width):
+    is_low = lane_iota(band.shape[0]) < BORDER
+    halo = unpack_planes(band[:, 2 * width :])
+    lefts, rights = [], []
+    for plane in range(2):
+        low = band[:, plane * width : plane * width + LANES]
+        high = band[:, (plane + 1) * width - LANES : (plane + 1) * width]
+        lefts.append(jnp.where(is_low, low, halo[plane]))
+        rights.append(jnp.where(is_low, halo[plane], high))
+    return pack_planes(*lefts), pack_planes(*rights)
+
+
+def corner_kernel(up, down, after, to_left, to_right):
     count = up.shape[0]
     width = (up.shape[1] - LANES) // 2
-    is_low = lane_iota(count) < BORDER
-    for source, out in ((left, to_left), (right, to_right)):
-        out[...] = source[...]
-        for band, row in ((up, inset), (down, source.shape[0] - inset - count)):
-            halo = unpack_planes(band[:, 2 * width :])
-            parts = []
-            for plane in range(2):
-                if out is to_left:
-                    low = band[:, plane * width : plane * width + LANES]
-                    parts.append(jnp.where(is_low, low, halo[plane]))
-                else:
-                    high = band[:, (plane + 1) * width - LANES : (plane + 1) * width]
-                    parts.append(jnp.where(is_low, halo[plane], high))
-            out[row : row + count, :] += pack_planes(*parts)
+    for row, band in ((0, up), (count, down)):
+        to_left[row : row + count, :], to_right[row : row + count, :] = corner_parts(band, width)
+
+
+def half_lanes(rows, first):
+    low = lane_iota(rows) % (LANES // 2) < BORDER
+    return low if first else jnp.logical_not(low)
+
+
+def last_corner_kernel(up, down, left, right, to_left, to_right, whole):
+    count = up.shape[0]
+    tile = left.shape[0] - BAND
+    width = (up.shape[1] - LANES) // 2
+    half = tile // 2
+    tops, bottoms = corner_parts(up, width), corner_parts(down, width)
+    for side, (source, out) in enumerate(((left, to_left), (right, to_right))):
+        whole[...] = source[BORDER : BORDER + tile, :]
+        whole[:count, :] += tops[side]
+        whole[tile - count :, :] += bottoms[side]
+        out[...] = jnp.where(
+            half_lanes(half, side == 1), whole[:half, :], pltpu.roll(whole[half:, :], BORDER, 1)
+        )
+
+
+def unfold_side(packed):
+    both = jnp.concatenate([packed, pltpu.roll(packed, LANES - BORDER, 1)], axis=0)
+    return unpack_planes(both)
 
 
 def deep_kernel(
@@ -396,7 +395,7 @@
 def second_kernel(
     row_count, col_count,
     positions, counts, probe, doubled, amplitudes, right_f, left_f, right_b, left_b,
-    up, down, left, right, cur_in, acc_in,
+    up, down, left, right, left_corners, right_corners, cur_in, acc_in,
     cur, acc, to_up, to_down, to_left, to_right, order,
 ):
     tile, width = cur.shape[1] - SUBLANES - BAND, cur.shape[2] - 2 * LANES
@@ -414,7 +413,19 @@
     inner = slice(LANES, LANES + width)
     lane = lane_iota(extent)
     is_low, is_high = lane < BORDER, lane >= LANES - BORDER
-    lefts, rights = unpack_planes(left[...]), unpack_planes(right[...])
+    lefts, rights = (
+        unpack_planes(
+            jnp.concatenate(
+                [
+                    side[:BAND, :] + corners[:BAND, :],
+                    side[BAND:tile, :],
+                    side[tile:, :] + corners[BAND:, :],
+                ],
+                axis=0,
+            )
+        )
+        for side, corners in ((left, left_corners), (right, right_corners))
+    )
     row_id = lax.broadcasted_iota(jnp.int32, (extent, LANES), 0)
     row_gain = rate * jnp.where(
         row_id < BORDER, top, jnp.where(row_id >= BORDER + tile, bottom, 1.0)
@@ -483,7 +494,7 @@
     rate = step_of(probe)
     lane = lane_iota(tile)
     rows = slice(BORDER, BORDER + tile)
-    lefts, rights = unpack_planes(left[rows, :]), unpack_planes(right[rows, :])
+    lefts, rights = unfold_side(left[...]), unfold_side(right[...])
     for plane in range(2):
         lanes = slice(plane * width, (plane + 1) * width)
         corrected[plane] = acc[plane, rows, LANES : LANES + width]
@@ -513,12 +524,16 @@
 
 VMEM = pl.BlockSpec(memory_space=pltpu.VMEM)
 SMEM = pl.BlockSpec(memory_space=pltpu.SMEM)
-ANY = pl.BlockSpec(memory_space=pl.ANY)
+HBM = pl.BlockSpec(memory_space=pltpu.HBM)
 PARAMS = pltpu.CompilerParams(vmem_limit_bytes=32 * 1024 * 1024)
 
 
 def f32(*shape):
     return pltpu.VMEM(shape, jnp.float32)
+
+
+def in_hbm(array):
+    return pltpu.with_memory_space_constraint(array, pltpu.HBM)
 
 
 def in_vmem(array):
@@ -541,7 +556,7 @@
     extent = tile + BAND
     padded = f32(2, extent + SUBLANES, width + 2 * LANES)
     doubled_shape = f32(2, 2 * probe, probe)
-    tables = tuple(in_vmem(jnp.asarray(table)) for table in dft_blocks(probe))
+    tables = tuple(jnp.asarray(table) for table in dft_blocks(probe))
     places = positions[0, 0]
     order = pltpu.SMEM((amplitudes.shape[0],), jnp.int32)
     sides = (f32(extent, LANES), f32(extent, LANES))
@@ -550,7 +565,7 @@
         band = f32(count, 2 * width + LANES)
         return (band, band)
 
-    def call(kernel, name, scalars, arrays, outs, scratch=(), aliases=None):
+    def call(kernel, scalars, arrays, outs, scratch=(), aliases=None):
         return pl.pallas_call(
             kernel,
             out_shape=outs,
@@ -559,7 +574,6 @@
             scratch_shapes=list(scratch),
             input_output_aliases=aliases or {},
             compiler_params=PARAMS,
-            name=name,
         )(*scalars, *arrays)
 
     slots = (places, counts)
@@ -567,45 +581,49 @@
         jnp.concatenate([object_field[0, rows], object_field[1, rows]], axis=1)
         for rows in (slice(0, BORDER), slice(tile - BORDER, tile))
     ]
+    table_shapes = tuple(pltpu.VMEM(table.shape, table.dtype) for table in tables)
     up, down = swap_along("row", *strips)
-    cur, acc, doubled, held = pl.pallas_call(
+    cur, acc, doubled, held, *tables = pl.pallas_call(
         inner_start_kernel,
-        out_shape=(padded, padded, doubled_shape, f32(*amplitudes.shape)),
-        in_specs=[SMEM, SMEM, ANY, VMEM, ANY] + [VMEM] * 4,
-        out_specs=(VMEM,) * 4,
-        scratch_shapes=[order, pltpu.SemaphoreType.DMA((3,))],
+        out_shape=(padded, padded, doubled_shape, f32(*amplitudes.shape), *table_shapes),
+        in_specs=[SMEM, SMEM] + [HBM] * (3 + len(tables)),
+        out_specs=(VMEM,) * (4 + len(tables)),
+        scratch_shapes=[order, pltpu.SemaphoreType.DMA((7 + len(tables),))],
         compiler_params=PARAMS,
         name="inner_start",
-    )(*slots, object_field, probe_field, amplitudes, *tables)
-    packed = call(object_pack_kernel, "object_pack", (), (cur, up, down), sides[0])
+    )(*slots, *map(in_hbm, (object_field, probe_field, amplitudes, *tables)))
+    packed = call(object_pack_kernel, (), (cur, up, down), sides[0])
     left, right = swap_along("col", packed, packed)
     acc = call(
-        inner_rest_kernel, "inner_rest", slots, (cur, doubled, held, *tables, acc),
+        inner_rest_kernel, slots, (cur, doubled, held, *tables, acc),
         padded, (order,), {9: 0},
     )
     cur, acc, to_up, to_down, to_left, to_right = call(
-        outer_kernel, "outer", slots, (up, down, left, right, doubled, held, *tables, cur, acc),
+        outer_kernel, slots, (up, down, left, right, doubled, held, *tables, cur, acc),
         (padded, padded, *row_bands(BAND), *sides), (order,), {12: 0, 13: 1},
     )
     up, down = swap_along("row", to_up, to_down)
+    left, right = swap_along("col", to_left, to_right)
     cur, acc = call(
-        deep_kernel, "deep", slots, (probe_field, doubled, held, *tables, cur, acc),
+        deep_kernel, slots, (probe_field, doubled, held, *tables, cur, acc),
         (padded, padded), (order,), {9: 0, 10: 1},
     )
-    to_left, to_right = call(
-        functools.partial(corner_kernel, 0), "corners", (), (up, down, to_left, to_right), sides
-    )
-    left, right = swap_along("col", to_left, to_right)
+    corners = (f32(2 * BAND, LANES),) * 2
+    left_corners, right_corners = swap_along("col", *call(corner_kernel, (), (up, down, acc), corners))
     cur, acc, to_up, to_down, to_left, to_right = call(
         functools.partial(second_kernel, lax.axis_size("row"), lax.axis_size("col")),
-        "second", slots,
-        (probe_field, doubled, held, *tables, up, down, left, right, cur, acc),
-        (padded, padded, *row_bands(BORDER), *sides), (order,), {13: 0, 14: 1},
+        slots,
+        (
+            probe_field, doubled, held, *tables,
+            up, down, left, right, left_corners, right_corners, cur, acc,
+        ),
+        (padded, padded, *row_bands(BORDER), *sides), (order,), {15: 0, 16: 1},
     )
     up, down = swap_along("row", to_up, to_down)
+    folded = f32(tile // 2, LANES)
     to_left, to_right = call(
-        functools.partial(corner_kernel, BORDER), "last_corners", (),
-        (up, down, to_left, to_right), sides,
+        last_corner_kernel, (), (up, down, to_left, to_right),
+        (folded, folded), (f32(tile, LANES),),
     )
     left, right = swap_along("col", to_left, to_right)
     whole = pltpu.VMEM((2, tile, width), jnp.float32)
@@ -613,15 +631,15 @@
     estimate, correction = pl.pallas_call(
         last_kernel,
         out_shape=(result, result),
-        in_specs=[ANY] + [VMEM] * 6,
-        out_specs=(ANY, ANY),
+        in_specs=[HBM] + [VMEM] * 6,
+        out_specs=(HBM, HBM),
         scratch_shapes=[
             whole, whole, whole,
             pltpu.SemaphoreType.DMA((CHUNKS,)), pltpu.SemaphoreType.DMA((2, CHUNKS)),
         ],
         compiler_params=PARAMS,
         name="finish",
-    )(object_field, probe_field, up, down, left, right, acc)
+    )(in_hbm(object_field), probe_field, up, down, left, right, acc)
     return estimate, correction
 
 

time: 93.3 us -> 85 us (0.911)
  local copies, waits for them, and re-layouts: 9.52 us -> 1.64 us
  waiting for transfers between devices: 25.1 us -> 18.2 us
  starting transfers between devices: 35 us -> 41.8 us
    unnamed x20 -> x6, local copies, waits for them, and re-layouts: 8.56 us -> 0.69 us
    ppermute x6 -> x7, waiting for transfers between devices: 7.85 us -> 1.97 us  [swap_along(): lax.ppermute(to_after, axis, forth)]
    ppermute x6 -> x7, starting transfers between devices: 24.5 us -> 29.3 us  [swap_along(): lax.ppermute(to_after, axis, forth)]
    pallas_call x7, Pallas kernels: 14.7 us -> 12.2 us  [call(): pl.pallas_call(kernel, out_shape=outs, in_specs=[SMEM] * len(scalars) + [...]
    ppermute x6 -> x7, starting transfers between devices: 10.5 us -> 12.5 us  [swap_along(): lax.ppermute(to_before, axis, back)]
    pallas_call x1, Pallas kernels: 3.72 us -> 5.57 us  [on_device(): pl.pallas_call(inner_start_kernel, out_shape=(padded, padded, doubled_sha...]
    ppermute x6 -> x7, waiting for transfers between devices: 17.2 us -> 16.2 us  [swap_along(): lax.ppermute(to_before, axis, back)]
  transfers between devices with their start and end apart: 12 -> 14, of which waited for: 8 -> 7; matrix products, arithmetic and copies ran while one was open for 0% -> 0% of each run, Pallas kernels for 11% -> 12%
where the time goes in v3:
time: 85 us; the launch traced here: 84.4 us
  starting transfers between devices  41.8 us (49%)
  Pallas kernels  21 us (25%)
  waiting for transfers between devices  18.2 us (21%)
  between operations  1.71 us (2%)
  local copies, waits for them, and re-layouts  1.64 us (2%)
    ppermute x7, starting transfers between devices, swap_along(): lax.ppermute(to_after, axis, forth)  29.3 us
    ppermute x7, waiting for transfers between devices, swap_along(): lax.ppermute(to_before, axis, back)  16.2 us
    ppermute x7, starting transfers between devices, swap_along(): lax.ppermute(to_before, axis, back)  12.5 us
    pallas_call x7, Pallas kernels, call(): pl.pallas_call(kernel, out_shape=outs, in_specs=[SMEM] * len(scalars) + [...  12.2 us
    pallas_call x1, Pallas kernels, on_device(): pl.pallas_call(inner_start_kernel, out_shape=(padded, padded, doubled_sha...  5.57 us
    pallas_call x1, Pallas kernels, on_device(): pl.pallas_call(last_kernel, out_shape=(result, result), in_specs=[HBM] +...  3.24 us
    ppermute x7, waiting for transfers between devices, swap_along(): lax.ppermute(to_after, axis, forth)  1.97 us
  transfers between devices with their start and end apart: 14, of which 7 were waited for; matrix products, arithmetic and copies ran while one was open for 0% of the time, Pallas kernels for 12%

profile of v3, /device:TPU:1, one launch (start us, length us, event | category | flops | bytes accessed | tf_op | source)
XLA Modules:
  0.0 84.4 jit_solution(7440428270470416960)
XLA Ops:
  1.6 3.9 %collective-permute-start = (f32[32,1024]{1,0:T(8,128)S(1)}, f32[32,1024]{1,0:T(8,128)S(1)}, u32[]{:S(2)}, u32[]{:S(2)}) collective-permute-start(f32[32,1024]{1,0:T(8,128)S(1)} %pad_maximum_fusion), channel_id=1, source_target_pairs={{0,8},{8,16},{16,24},{1,9},{9,17},{17,25},{2,10},{10,18},{18,26},{... | collective-permute-start | bytes 393224 | tf_op jit(solution)/shard_map/ppermute | solution.py:548
  5.6 1.3 %collective-permute-start.1 = (f32[32,1024]{1,0:T(8,128)S(1)}, f32[32,1024]{1,0:T(8,128)S(1)}, u32[]{:S(2)}, u32[]{:S(2)}) collective-permute-start(f32[32,1024]{1,0:T(8,128)S(1)} %pad_maximum_fusion.1), channel_id=1, source_target_pairs={{8,0},{16,8},{24,16},{9,1},{17,9},{25,17},{10,2},{18,10},{26,18},{... | collective-permute-start | bytes 393224 | tf_op jit(solution)/shard_map/ppermute | solution.py:549
  8.2 5.6 %inner_start.1 = (f32[2,584,768]{2,1,0:T(8,128)S(1)}, f32[2,584,768]{2,1,0:T(8,128)S(1)}, f32[2,256,128]{2,1,0:T(8,128)S(1)}, f32[24,128,128]{2,1,0:T(8,128)S(1)...) custom-call(s32[2,24]{1,0:T(2,128)S(1)} %bitcast.9, ...), custom_call_target="tpu_custom_call" | custom-call | tf_op jit(solution)/shard_map/inner_start/pallas_call | solution.py:586
  14.0 2.9 %collective-permute-start.3 = (f32[576,128]{1,0:T(8,128)S(1)}, f32[576,128]{1,0:T(8,128)S(1)}, u32[]{:S(2)}, u32[]{:S(2)}) collective-permute-start(f32[576,128]{1,0:T(8,128)S(1)} %shard_map.104), channel_id=1, source_target_pairs={{1,0},{2,1},{3,2},{4,3},{5,4},{6,5},{7,6},{9,8},{10,9},{11,10},{12... | collective-permute-start | bytes 884744 | tf_op jit(solution)/shard_map/ppermute | solution.py:549
  16.8 3.1 %collective-permute-start.2 = (f32[576,128]{1,0:T(8,128)S(1)}, f32[576,128]{1,0:T(8,128)S(1)}, u32[]{:S(2)}, u32[]{:S(2)}) collective-permute-start(f32[576,128]{1,0:T(8,128)S(1)} %shard_map.104), channel_id=1, source_target_pairs={{0,1},{1,2},{2,3},{3,4},{4,5},{5,6},{6,7},{8,9},{9,10},{10,11},{11... | collective-permute-start | bytes 884744 | tf_op jit(solution)/shard_map/ppermute | solution.py:548
  20.6 1.8 %collective-permute-done.3.right = f32[576,128]{1,0:T(8,128)S(1)} collective-permute-done((f32[576,128]{1,0:T(8,128)S(1)}, f32[576,128]{1,0:T(8,128)S(1)}, u32[]{:S(2)}, u32[]{:S(2)}) %collective-permute-start.3) | collective-permute-done | bytes 294944 | tf_op jit(solution)/shard_map/ppermute | solution.py:549
  23.6 3.5 %shard_map.106 = (f32[2,584,768]{2,1,0:T(8,128)S(1)}, f32[2,584,768]{2,1,0:T(8,128)S(1)}, f32[64,1152]{1,0:T(8,128)S(1)}, f32[64,1152]{1,0:T(8,128)S(1)}, f32[57...) custom-call(s32[2,24]{1,0:T(2,128)S(1)} %bitcast.11, ...), custom_call_target="tpu_custom_call", output_to_operand_aliasing={{0}: (12, {}), {1}: (13, {})} | custom-call | tf_op jit(solution)/shard_map/pallas_call | solution.py:569
  27.0 6.4 %collective-permute-start.4 = (f32[64,1152]{1,0:T(8,128)S(1)}, f32[64,1152]{1,0:T(8,128)S(1)}, u32[]{:S(2)}, u32[]{:S(2)}) collective-permute-start(f32[64,1152]{1,0:T(8,128)S(1)} %get-tuple-element.35), channel_id=1, source_target_pairs={{0,8},{8,16},{16,24},{1,9},{9,17},{17,25},{2,10},{10,18},{18,26},{... | collective-permute-start | bytes 884744 | tf_op jit(solution)/shard_map/ppermute | solution.py:548
  33.4 1.3 %collective-permute-start.5 = (f32[64,1152]{1,0:T(8,128)S(1)}, f32[64,1152]{1,0:T(8,128)S(1)}, u32[]{:S(2)}, u32[]{:S(2)}) collective-permute-start(f32[64,1152]{1,0:T(8,128)S(1)} %get-tuple-element.36), channel_id=1, source_target_pairs={{8,0},{16,8},{24,16},{9,1},{17,9},{25,17},{10,2},{18,10},{26,18},{... | collective-permute-start | bytes 884744 | tf_op jit(solution)/shard_map/ppermute | solution.py:549
  34.7 2.6 %collective-permute-start.6 = (f32[576,128]{1,0:T(8,128)S(1)}, f32[576,128]{1,0:T(8,128)S(1)}, u32[]{:S(2)}, u32[]{:S(2)}) collective-permute-start(f32[576,128]{1,0:T(8,128)S(1)} %get-tuple-element.37), channel_id=1, source_target_pairs={{0,1},{1,2},{2,3},{3,4},{4,5},{5,6},{6,7},{8,9},{9,10},{10,11},{11... | collective-permute-start | bytes 884744 | tf_op jit(solution)/shard_map/ppermute | solution.py:548
  37.3 1.9 %collective-permute-start.7 = (f32[576,128]{1,0:T(8,128)S(1)}, f32[576,128]{1,0:T(8,128)S(1)}, u32[]{:S(2)}, u32[]{:S(2)}) collective-permute-start(f32[576,128]{1,0:T(8,128)S(1)} %get-tuple-element.38), channel_id=1, source_target_pairs={{1,0},{2,1},{3,2},{4,3},{5,4},{6,5},{7,6},{9,8},{10,9},{11,10},{12... | collective-permute-start | bytes 884744 | tf_op jit(solution)/shard_map/ppermute | solution.py:549
  39.2 3.5 %shard_map.107 = (f32[2,584,768]{2,1,0:T(8,128)S(1)}, f32[2,584,768]{2,1,0:T(8,128)S(1)}) custom-call(s32[2,24]{1,0:T(2,128)S(1)} %bitcast.12, s32[1,1]{1,0:T(1,128)S(6)} %copy.25.counts, f32[2,128,128]{2,1,0:T(8,128)S(1)} %copy-done, f32[2,256,128]{2,1,0:T(8,128)S(1)} %get-tuple-element.27.doubled, ...), custom_call_target="tpu_custom_call", output_to_operand_aliasing={{0}: (9, {}), {1}: (10, {})} | custom-call | tf_op jit(solution)/shard_map/pallas_call | solution.py:569
  42.8 1.5 %collective-permute-done.5.down = f32[64,1152]{1,0:T(8,128)S(1)} collective-permute-done((f32[64,1152]{1,0:T(8,128)S(1)}, f32[64,1152]{1,0:T(8,128)S(1)}, u32[]{:S(2)}, u32[]{:S(2)}) %collective-permute-start.5) | collective-permute-done | bytes 294944 | tf_op jit(solution)/shard_map/ppermute | solution.py:549
  44.4 6.5 %collective-permute-start.8 = (f32[128,128]{1,0:T(8,128)S(1)}, f32[128,128]{1,0:T(8,128)S(1)}, u32[]{:S(2)}, u32[]{:S(2)}) collective-permute-start(f32[128,128]{1,0:T(8,128)S(1)} %get-tuple-element.42), channel_id=1, source_target_pairs={{0,1},{1,2},{2,3},{3,4},{4,5},{5,6},{6,7},{8,9},{9,10},{10,11},{11... | collective-permute-start | bytes 196616 | tf_op jit(solution)/shard_map/ppermute | solution.py:548
  51.0 1.9 %collective-permute-start.9 = (f32[128,128]{1,0:T(8,128)S(1)}, f32[128,128]{1,0:T(8,128)S(1)}, u32[]{:S(2)}, u32[]{:S(2)}) collective-permute-start(f32[128,128]{1,0:T(8,128)S(1)} %get-tuple-element.43), channel_id=1, source_target_pairs={{1,0},{2,1},{3,2},{4,3},{5,4},{6,5},{7,6},{9,8},{10,9},{11,10},{12... | collective-permute-start | bytes 196616 | tf_op jit(solution)/shard_map/ppermute | solution.py:549
  52.9 3.6 %collective-permute-done.9.right_corners = f32[128,128]{1,0:T(8,128)S(1)} collective-permute-done((f32[128,128]{1,0:T(8,128)S(1)}, f32[128,128]{1,0:T(8,128)S(1)}, u32[]{:S(2)}, u32[]{:S(2)}) %collective-permute-start.9) | collective-permute-done | bytes 65568 | tf_op jit(solution)/shard_map/ppermute | solution.py:549
  56.6 4.1 %shard_map.109 = (f32[2,584,768]{2,1,0:T(8,128)S(1)}, f32[2,584,768]{2,1,0:T(8,128)S(1)}, f32[32,1152]{1,0:T(8,128)S(1)}, f32[32,1152]{1,0:T(8,128)S(1)}, f32[57...) custom-call(s32[2,24]{1,0:T(2,128)S(1)} %bitcast.13, ...), custom_call_target="tpu_custom_call", output_to_operand_aliasing={{0}: (15, {}), {1}: (16, {})} | custom-call | tf_op jit(solution)/shard_map/pallas_call | solution.py:569
  60.6 2.4 %collective-permute-start.10 = (f32[32,1152]{1,0:T(8,128)S(1)}, f32[32,1152]{1,0:T(8,128)S(1)}, u32[]{:S(2)}, u32[]{:S(2)}) collective-permute-start(f32[32,1152]{1,0:T(8,128)S(1)} %get-tuple-element.45), channel_id=1, source_target_pairs={{0,8},{8,16},{16,24},{1,9},{9,17},{17,25},{2,10},{10,18},{18,26},{... | collective-permute-start | bytes 442376 | tf_op jit(solution)/shard_map/ppermute | solution.py:548
  63.0 1.3 %collective-permute-start.11 = (f32[32,1152]{1,0:T(8,128)S(1)}, f32[32,1152]{1,0:T(8,128)S(1)}, u32[]{:S(2)}, u32[]{:S(2)}) collective-permute-start(f32[32,1152]{1,0:T(8,128)S(1)} %get-tuple-element.46), channel_id=1, source_target_pairs={{8,0},{16,8},{24,16},{9,1},{17,9},{25,17},{10,2},{18,10},{26,18},{... | collective-permute-start | bytes 442376 | tf_op jit(solution)/shard_map/ppermute | solution.py:549
  65.1 4.9 %collective-permute-done.11.down = f32[32,1152]{1,0:T(8,128)S(1)} collective-permute-done((f32[32,1152]{1,0:T(8,128)S(1)}, f32[32,1152]{1,0:T(8,128)S(1)}, u32[]{:S(2)}, u32[]{:S(2)}) %collective-permute-start.11) | collective-permute-done | bytes 147488 | tf_op jit(solution)/shard_map/ppermute | solution.py:549
  70.3 4.4 %collective-permute-start.12 = (f32[256,128]{1,0:T(8,128)S(1)}, f32[256,128]{1,0:T(8,128)S(1)}, u32[]{:S(2)}, u32[]{:S(2)}) collective-permute-start(f32[256,128]{1,0:T(8,128)S(1)} %get-tuple-element.49), channel_id=1, source_target_pairs={{0,1},{1,2},{2,3},{3,4},{4,5},{5,6},{6,7},{8,9},{9,10},{10,11},{11... | collective-permute-start | bytes 393224 | tf_op jit(solution)/shard_map/ppermute | solution.py:548
  74.7 1.9 %collective-permute-start.13 = (f32[256,128]{1,0:T(8,128)S(1)}, f32[256,128]{1,0:T(8,128)S(1)}, u32[]{:S(2)}, u32[]{:S(2)}) collective-permute-start(f32[256,128]{1,0:T(8,128)S(1)} %get-tuple-element.50), channel_id=1, source_target_pairs={{1,0},{2,1},{3,2},{4,3},{5,4},{6,5},{7,6},{9,8},{10,9},{11,10},{12... | collective-permute-start | bytes 393224 | tf_op jit(solution)/shard_map/ppermute | solution.py:549
  76.7 4.3 %collective-permute-done.13.right = f32[256,128]{1,0:T(8,128)S(1)} collective-permute-done((f32[256,128]{1,0:T(8,128)S(1)}, f32[256,128]{1,0:T(8,128)S(1)}, u32[]{:S(2)}, u32[]{:S(2)}) %collective-permute-start.13) | collective-permute-done | bytes 131104 | tf_op jit(solution)/shard_map/ppermute | solution.py:549
  81.0 3.2 %finish.1 = (f32[2,512,512]{2,1,0:T(8,128)}, f32[2,512,512]{2,1,0:T(8,128)}) custom-call(f32[2,512,512]{2,1,0:T(8,128)} %objects.3, f32[2,128,128]{2,1,0:T(8,128)S(1)} %copy-done, f32[32,1152]{1,0:T(8,128)S(1)} %collective-permute-done.10.up, f32[32,1152]{1,0:T(8,128)S(1)} %collective-permute-done.11.down, f32[256,128]{1,0:T(8,128)S(1)} %collective-permute-done.12.left, ...), custom_call_target="tpu_custom_call" | custom-call | tf_op jit(solution)/shard_map/finish/pallas_call | solution.py:631
  (22 shorter events, 4.8 us)
Async XLA Ops:
  1.6 12.2 %collective-permute-start = (f32[32,1024]{1,0:T(8,128)S(1)}, f32[32,1024]{1,0:T(8,128)S(1)}, u32[]{:S(2)}, u32[]{:S(2)}) collective-permute-start(f32[32,1024]{1,0:T(8,128)S(1)} %pad_maximum_fusion), channel_id=1, source_target_pairs={{0,8},{8,16},{16,24},{1,9},{9,17},{17,25},{2,10},{10,18},{18,26},{... | collective-permute-start | bytes 393224 | tf_op jit(solution)/shard_map/ppermute | solution.py:548
  5.6 8.2 %collective-permute-start.1 = (f32[32,1024]{1,0:T(8,128)S(1)}, f32[32,1024]{1,0:T(8,128)S(1)}, u32[]{:S(2)}, u32[]{:S(2)}) collective-permute-start(f32[32,1024]{1,0:T(8,128)S(1)} %pad_maximum_fusion.1), channel_id=1, source_target_pairs={{8,0},{16,8},{24,16},{9,1},{17,9},{25,17},{10,2},{18,10},{26,18},{... | collective-permute-start | bytes 393224 | tf_op jit(solution)/shard_map/ppermute | solution.py:549
  7.5 0.7 copy-start.1
  14.0 8.4 %collective-permute-start.3 = (f32[576,128]{1,0:T(8,128)S(1)}, f32[576,128]{1,0:T(8,128)S(1)}, u32[]{:S(2)}, u32[]{:S(2)}) collective-permute-start(f32[576,128]{1,0:T(8,128)S(1)} %shard_map.104), channel_id=1, source_target_pairs={{1,0},{2,1},{3,2},{4,3},{5,4},{6,5},{7,6},{9,8},{10,9},{11,10},{12... | collective-permute-start | bytes 884744 | tf_op jit(solution)/shard_map/ppermute | solution.py:549
  16.8 6.7 %collective-permute-start.2 = (f32[576,128]{1,0:T(8,128)S(1)}, f32[576,128]{1,0:T(8,128)S(1)}, u32[]{:S(2)}, u32[]{:S(2)}) collective-permute-start(f32[576,128]{1,0:T(8,128)S(1)} %shard_map.104), channel_id=1, source_target_pairs={{0,1},{1,2},{2,3},{3,4},{4,5},{5,6},{6,7},{8,9},{9,10},{10,11},{11... | collective-permute-start | bytes 884744 | tf_op jit(solution)/shard_map/ppermute | solution.py:548
  20.6 18.6 %copy-start = (f32[2,128,128]{2,1,0:T(8,128)S(1)}, f32[2,128,128]{2,1,0:T(8,128)}, u32[]{:S(2)}) copy-start(f32[2,128,128]{2,1,0:T(8,128)} %probe.5) | copy-start | bytes 393220
  27.0 15.7 %collective-permute-start.4 = (f32[64,1152]{1,0:T(8,128)S(1)}, f32[64,1152]{1,0:T(8,128)S(1)}, u32[]{:S(2)}, u32[]{:S(2)}) collective-permute-start(f32[64,1152]{1,0:T(8,128)S(1)} %get-tuple-element.35), channel_id=1, source_target_pairs={{0,8},{8,16},{16,24},{1,9},{9,17},{17,25},{2,10},{10,18},{18,26},{... | collective-permute-start | bytes 884744 | tf_op jit(solution)/shard_map/ppermute | solution.py:548
  33.4 10.9 %collective-permute-start.5 = (f32[64,1152]{1,0:T(8,128)S(1)}, f32[64,1152]{1,0:T(8,128)S(1)}, u32[]{:S(2)}, u32[]{:S(2)}) collective-permute-start(f32[64,1152]{1,0:T(8,128)S(1)} %get-tuple-element.36), channel_id=1, source_target_pairs={{8,0},{16,8},{24,16},{9,1},{17,9},{25,17},{10,2},{18,10},{26,18},{... | collective-permute-start | bytes 884744 | tf_op jit(solution)/shard_map/ppermute | solution.py:549
  34.7 18.2 %collective-permute-start.6 = (f32[576,128]{1,0:T(8,128)S(1)}, f32[576,128]{1,0:T(8,128)S(1)}, u32[]{:S(2)}, u32[]{:S(2)}) collective-permute-start(f32[576,128]{1,0:T(8,128)S(1)} %get-tuple-element.37), channel_id=1, source_target_pairs={{0,1},{1,2},{2,3},{3,4},{4,5},{5,6},{6,7},{8,9},{9,10},{10,11},{11... | collective-permute-start | bytes 884744 | tf_op jit(solution)/shard_map/ppermute | solution.py:548
  37.3 15.6 %collective-permute-start.7 = (f32[576,128]{1,0:T(8,128)S(1)}, f32[576,128]{1,0:T(8,128)S(1)}, u32[]{:S(2)}, u32[]{:S(2)}) collective-permute-start(f32[576,128]{1,0:T(8,128)S(1)} %get-tuple-element.38), channel_id=1, source_target_pairs={{1,0},{2,1},{3,2},{4,3},{5,4},{6,5},{7,6},{9,8},{10,9},{11,10},{12... | collective-permute-start | bytes 884744 | tf_op jit(solution)/shard_map/ppermute | solution.py:549
  42.7 13.8 %copy-start.2 = (s32[1,1,2,24]{3,2,1,0:T(2,128)S(1)}, s32[1,1,2,24]{3,2,1,0:T(2,128)}, u32[]{:S(2)}) copy-start(s32[1,1,2,24]{3,2,1,0:T(2,128)} %param.12) | copy-start | bytes 580
  44.4 8.5 %collective-permute-start.8 = (f32[128,128]{1,0:T(8,128)S(1)}, f32[128,128]{1,0:T(8,128)S(1)}, u32[]{:S(2)}, u32[]{:S(2)}) collective-permute-start(f32[128,128]{1,0:T(8,128)S(1)} %get-tuple-element.42), channel_id=1, source_target_pairs={{0,1},{1,2},{2,3},{3,4},{4,5},{5,6},{6,7},{8,9},{9,10},{10,11},{11... | collective-permute-start | bytes 196616 | tf_op jit(solution)/shard_map/ppermute | solution.py:548
  51.0 5.6 %collective-permute-start.9 = (f32[128,128]{1,0:T(8,128)S(1)}, f32[128,128]{1,0:T(8,128)S(1)}, u32[]{:S(2)}, u32[]{:S(2)}) collective-permute-start(f32[128,128]{1,0:T(8,128)S(1)} %get-tuple-element.43), channel_id=1, source_target_pairs={{1,0},{2,1},{3,2},{4,3},{5,4},{6,5},{7,6},{9,8},{10,9},{11,10},{12... | collective-permute-start | bytes 196616 | tf_op jit(solution)/shard_map/ppermute | solution.py:549
  60.6 4.5 %collective-permute-start.10 = (f32[32,1152]{1,0:T(8,128)S(1)}, f32[32,1152]{1,0:T(8,128)S(1)}, u32[]{:S(2)}, u32[]{:S(2)}) collective-permute-start(f32[32,1152]{1,0:T(8,128)S(1)} %get-tuple-element.45), channel_id=1, source_target_pairs={{0,8},{8,16},{16,24},{1,9},{9,17},{17,25},{2,10},{10,18},{18,26},{... | collective-permute-start | bytes 442376 | tf_op jit(solution)/shard_map/ppermute | solution.py:548
  63.0 7.0 %collective-permute-start.11 = (f32[32,1152]{1,0:T(8,128)S(1)}, f32[32,1152]{1,0:T(8,128)S(1)}, u32[]{:S(2)}, u32[]{:S(2)}) collective-permute-start(f32[32,1152]{1,0:T(8,128)S(1)} %get-tuple-element.46), channel_id=1, source_target_pairs={{8,0},{16,8},{24,16},{9,1},{17,9},{25,17},{10,2},{18,10},{26,18},{... | collective-permute-start | bytes 442376 | tf_op jit(solution)/shard_map/ppermute | solution.py:549
  70.3 6.4 %collective-permute-start.12 = (f32[256,128]{1,0:T(8,128)S(1)}, f32[256,128]{1,0:T(8,128)S(1)}, u32[]{:S(2)}, u32[]{:S(2)}) collective-permute-start(f32[256,128]{1,0:T(8,128)S(1)} %get-tuple-element.49), channel_id=1, source_target_pairs={{0,1},{1,2},{2,3},{3,4},{4,5},{5,6},{6,7},{8,9},{9,10},{10,11},{11... | collective-permute-start | bytes 393224 | tf_op jit(solution)/shard_map/ppermute | solution.py:548
  74.7 6.3 %collective-permute-start.13 = (f32[256,128]{1,0:T(8,128)S(1)}, f32[256,128]{1,0:T(8,128)S(1)}, u32[]{:S(2)}, u32[]{:S(2)}) collective-permute-start(f32[256,128]{1,0:T(8,128)S(1)} %get-tuple-element.50), channel_id=1, source_target_pairs={{1,0},{2,1},{3,2},{4,3},{5,4},{6,5},{7,6},{9,8},{10,9},{11,10},{12... | collective-permute-start | bytes 393224 | tf_op jit(solution)/shard_map/ppermute | solution.py:549

commit v4 on v3

--- a/solution.py
+++ b/solution.py
@@ -202,36 +202,34 @@
     return step_gain / (jnp.max(probe[0] * probe[0] + probe[1] * probe[1]) + 1e-06)
 
 
-def pack_row_band(acc, row, count, out):
+def pack_row_band(acc, row, count):
     rows = slice(row, row + count)
     width = acc.shape[2] - 2 * LANES
-    halo = []
-    for plane in range(2):
-        out[:, plane * width : (plane + 1) * width] = acc[plane, rows, LANES : LANES + width]
-        halo.append(
-            jnp.where(
-                lane_iota(count) < BORDER,
-                acc[plane, rows, LANES + width :],
-                acc[plane, rows, :LANES],
-            )
-        )
-    out[:, 2 * width :] = pack_planes(*halo)
-
-
-def pack_side_bands(acc, height, to_left, to_right):
+    is_low = lane_iota(count) < BORDER
+    halo = [
+        jnp.where(is_low, acc[plane, rows, LANES + width :], acc[plane, rows, :LANES])
+        for plane in range(2)
+    ]
+    own = [acc[plane, rows, LANES : LANES + width] for plane in range(2)]
+    return jnp.concatenate([*own, pack_planes(*halo)], axis=1)
+
+
+def pack_side_bands(acc, height):
     width = acc.shape[2] - 2 * LANES
     is_low = lane_iota(height) < BORDER
-    for out, high_block in ((to_left, 0), (to_right, width)):
-        out[...] = pack_planes(
+    return [
+        pack_planes(
             *[
                 jnp.where(
                     is_low,
-                    acc[plane, :height, high_block + LANES : high_block + 2 * LANES],
-                    acc[plane, :height, high_block : high_block + LANES],
+                    acc[plane, :height, block + LANES : block + 2 * LANES],
+                    acc[plane, :height, block : block + LANES],
                 )
                 for plane in range(2)
             ]
         )
+        for block in (0, width)
+    ]
 
 
 def inner_start_kernel(
@@ -280,11 +278,17 @@
     )
 
 
+def by_side(axis, first, second):
+    even = lax.axis_index(axis) % 2 == 0
+    return jnp.where(even, second, first), jnp.where(even, first, second)
+
+
 def object_pack_kernel(cur, up, down, out):
     count = up.shape[0]
     width = up.shape[1] // 2
     tile = out.shape[0] - 2 * count
     is_low = lane_iota(count) < BORDER
+    up, down = by_side("row", up[...], down[...])
     for row, band in ((0, up), (count + tile, down)):
         out[row : row + count, :] = pack_planes(
             *[
@@ -314,7 +318,8 @@
     extent = left.shape[0]
     tile, width = extent - BAND, up.shape[1] // 2
     lane = lane_iota(extent)
-    lefts, rights = unpack_planes(left[...]), unpack_planes(right[...])
+    up, down = by_side("row", up[...], down[...])
+    lefts, rights = map(unpack_planes, by_side("col", left[...], right[...]))
     for plane in range(2):
         cur[plane, :extent, :LANES] = jnp.where(lane >= LANES - BORDER, lefts[plane], 0.0)
         cur[plane, :extent, LANES + width :] = jnp.where(lane < BORDER, rights[plane], 0.0)
@@ -326,9 +331,7 @@
     gradient_slots(
         cur, acc, doubled, amplitudes, positions, order, 0, found, (right_f, left_f, right_b, left_b)
     )
-    pack_row_band(acc, 0, BAND, to_up)
-    pack_row_band(acc, tile, BAND, to_down)
-    pack_side_bands(acc, extent, to_left, to_right)
+    store_bands(acc, 0, tile, BAND, to_up, to_down, to_left, to_right)
 
 
 def corner_parts(band, width):
@@ -344,10 +347,12 @@
 
 
 def corner_kernel(up, down, after, to_left, to_right):
-    count = up.shape[0]
     width = (up.shape[1] - LANES) // 2
-    for row, band in ((0, up), (count, down)):
-        to_left[row : row + count, :], to_right[row : row + count, :] = corner_parts(band, width)
+    up, down = by_side("row", up[...], down[...])
+    tops, bottoms = corner_parts(up, width), corner_parts(down, width)
+    to_left[...], to_right[...] = by_side(
+        "col", *(jnp.concatenate([tops[i], bottoms[i]], axis=0) for i in range(2))
+    )
 
 
 def half_lanes(rows, first):
@@ -355,19 +360,26 @@
     return low if first else jnp.logical_not(low)
 
 
-def last_corner_kernel(up, down, left, right, to_left, to_right, whole):
+def last_corner_kernel(up, down, left, right, after, to_left, to_right, whole):
     count = up.shape[0]
     tile = left.shape[0] - BAND
     width = (up.shape[1] - LANES) // 2
     half = tile // 2
+    up, down = by_side("row", up[...], down[...])
     tops, bottoms = corner_parts(up, width), corner_parts(down, width)
-    for side, (source, out) in enumerate(((left, to_left), (right, to_right))):
+    parts = []
+    for side, source in enumerate((left, right)):
         whole[...] = source[BORDER : BORDER + tile, :]
         whole[:count, :] += tops[side]
         whole[tile - count :, :] += bottoms[side]
-        out[...] = jnp.where(
-            half_lanes(half, side == 1), whole[:half, :], pltpu.roll(whole[half:, :], BORDER, 1)
+        parts.append(
+            jnp.where(
+                half_lanes(half, side == 1),
+                whole[:half, :],
+                pltpu.roll(whole[half:, :], BORDER, 1),
+            )
         )
+    to_left[...], to_right[...] = by_side("col", *parts)
 
 
 def unfold_side(packed):
@@ -407,9 +419,7 @@
     bottom = jnp.where(row_at < row_last, 1.0, 0.0)
     before = jnp.where(col_at > 0, 1.0, 0.0)
     after = jnp.where(col_at < col_last, 1.0, 0.0)
-    found = list_slots(
-        order, positions, counts[0, 0], BORDER, tile - doubled.shape[2] - BORDER, False
-    )
+    early, _ = list_late_slots(order, positions, counts[0, 0], tile - doubled.shape[2])
     inner = slice(LANES, LANES + width)
     lane = lane_iota(extent)
     is_low, is_high = lane < BORDER, lane >= LANES - BORDER
@@ -424,8 +434,12 @@
                 axis=0,
             )
         )
-        for side, corners in ((left, left_corners), (right, right_corners))
-    )
+        for side, corners in zip(
+            by_side("col", left[...], right[...]),
+            by_side("col", left_corners[...], right_corners[...]),
+        )
+    )
+    up, down = by_side("row", up[...], down[...])
     row_id = lax.broadcasted_iota(jnp.int32, (extent, LANES), 0)
     row_gain = rate * jnp.where(
         row_id < BORDER, top, jnp.where(row_id >= BORDER + tile, bottom, 1.0)
@@ -465,59 +479,124 @@
             )
             acc[plane, :extent, out] = jnp.zeros_like(acc[plane, :extent, out])
     gradient_slots(
-        cur, acc, doubled, amplitudes, positions, order, 0, found, (right_f, left_f, right_b, left_b)
-    )
-    pack_row_band(acc, 0, BORDER, to_up)
-    pack_row_band(acc, BORDER + tile, BORDER, to_down)
-    pack_side_bands(acc, extent, to_left, to_right)
-
-
-CHUNKS = 4
+        cur, acc, doubled, amplitudes, positions, order, 0, early, (right_f, left_f, right_b, left_b)
+    )
+    store_bands(acc, 0, BORDER + tile, BORDER, to_up, to_down, to_left, to_right)
+
+
+def list_late_slots(order, positions, live, last):
+    reaching = list_slots(order, positions, live, 0, last, False)
+
+    def visit(slot, found):
+        row, col = positions[0, slot], positions[1, slot]
+        inner = (row >= 0) & (row <= last) & (col >= 0) & (col <= last)
+        deep = (row >= BORDER) & (row <= last - BORDER) & (col >= BORDER) & (col <= last - BORDER)
+        order[found] = slot
+        return found + jnp.where(inner & jnp.logical_not(deep), 1, 0)
+
+    found = lax.fori_loop(0, live, visit, reaching)
+    return jnp.minimum(found, (reaching + GROUP - 1) // GROUP * GROUP), found
+
+
+def second_rest_kernel(
+    positions, counts, cur, doubled, amplitudes, right_f, left_f, right_b, left_b, acc_in,
+    acc, order,
+):
+    tile = cur.shape[1] - SUBLANES - BAND
+    early, found = list_late_slots(order, positions, counts[0, 0], tile - doubled.shape[2])
+    gradient_slots(
+        cur, acc, doubled, amplitudes, positions, order, early, found,
+        (right_f, left_f, right_b, left_b),
+    )
+
+
+def store_bands(acc, top, bottom, count, to_up, to_down, to_left, to_right):
+    ups = pack_row_band(acc, top, count), pack_row_band(acc, bottom, count)
+    to_up[...], to_down[...] = by_side("row", *ups)
+    sides = pack_side_bands(acc, to_left.shape[0])
+    if count == BAND:
+        sides = by_side("col", *sides)
+    to_left[...], to_right[...] = sides
+
+
+def middle_kernel(objects, probe, acc, held, estimate, correction, estimated, corrected, sems):
+    tile, width = objects.shape[1:]
+    load = pltpu.make_async_copy(objects, held, sems.at[0])
+    load.start()
+    rate = step_of(probe)
+    rows, lanes = slice(BORDER, tile - BORDER), slice(LANES, width - LANES)
+    load.wait()
+    for plane in range(2):
+        corrected[plane] = rate * acc[plane, 2 * BORDER : tile, 2 * LANES : width]
+        estimated[plane] = held[plane, rows, lanes] + corrected[plane]
+    stores = [
+        pltpu.make_async_copy(
+            source,
+            target.at[:, pl.ds(BORDER, tile - BAND), pl.ds(LANES, width - 2 * LANES)],
+            sems.at[1 + i],
+        )
+        for i, (source, target) in enumerate(((corrected, correction), (estimated, estimate)))
+    ]
+    for store in stores:
+        store.start()
+    for store in stores:
+        store.wait()
 
 
 def last_kernel(
-    objects, probe, up, down, left, right, acc, estimate, correction,
-    held, estimated, corrected, load_sems, store_sems,
+    probe, up, down, left, right, acc, held, estimate_in, correction_in,
+    estimate, correction, side_parts, row_parts, sems,
 ):
-    tile, width = objects.shape[1:]
-    step = tile // CHUNKS
-
-    def rows_of(ref, chunk):
-        return ref.at[:, pl.ds(chunk * step, step), :]
-
-    loads = [
-        pltpu.make_async_copy(rows_of(objects, i), rows_of(held, i), load_sems.at[i])
-        for i in range(CHUNKS)
-    ]
-    for load in loads:
-        load.start()
+    tile, width = held.shape[1:]
     rate = step_of(probe)
     lane = lane_iota(tile)
     rows = slice(BORDER, BORDER + tile)
-    lefts, rights = unfold_side(left[...]), unfold_side(right[...])
-    for plane in range(2):
-        lanes = slice(plane * width, (plane + 1) * width)
-        corrected[plane] = acc[plane, rows, LANES : LANES + width]
-        corrected[plane, :BORDER, :] += up[:, lanes]
-        corrected[plane, tile - BORDER :, :] += down[:, lanes]
-        corrected[plane, :, :LANES] += jnp.where(lane < BORDER, lefts[plane], 0.0)
-        corrected[plane, :, width - LANES :] += jnp.where(
-            lane >= LANES - BORDER, rights[plane], 0.0
-        )
+    lefts, rights = map(unfold_side, by_side("col", left[...], right[...]))
+    up, down = by_side("row", up[...], down[...])
     stores = []
-    for i in range(CHUNKS):
-        loads[i].wait()
-        part = slice(i * step, (i + 1) * step)
-        corrected[:, part, :] = rate * corrected[:, part, :]
-        estimated[:, part, :] = held[:, part, :] + corrected[:, part, :]
-        for number, (source, target) in enumerate(
-            ((corrected, correction), (estimated, estimate))
-        ):
-            store = pltpu.make_async_copy(
-                rows_of(source, i), rows_of(target, i), store_sems.at[number, i]
-            )
-            store.start()
-            stores.append(store)
+
+    def send(index, source, target):
+        store = pltpu.make_async_copy(source, target, sems.at[index])
+        store.start()
+        stores.append(store)
+
+    for side, (block, bands) in enumerate(((0, lefts), (width - LANES, rights))):
+        keep = (lane < BORDER) if side == 0 else (lane >= LANES - BORDER)
+        for plane in range(2):
+            at = plane * width + block
+            total = acc[plane, rows, LANES + block : 2 * LANES + block]
+            total += jnp.where(keep, bands[plane], 0.0)
+            total = jnp.concatenate(
+                [
+                    total[:BORDER] + up[:, at : at + LANES],
+                    total[BORDER : tile - BORDER],
+                    total[tile - BORDER :] + down[:, at : at + LANES],
+                ],
+                axis=0,
+            )
+            side_parts[0, side, plane] = rate * total
+            side_parts[1, side, plane] = (
+                held[plane, :, block : block + LANES] + side_parts[0, side, plane]
+            )
+        for number, target in enumerate((correction, estimate)):
+            send(
+                2 * side + number, side_parts.at[number, side],
+                target.at[:, :, pl.ds(block, LANES)],
+            )
+    lanes = slice(LANES, width - LANES)
+    for end, (row, band) in enumerate(((0, up), (tile - BORDER, down))):
+        for plane in range(2):
+            total = acc[plane, BORDER + row : 2 * BORDER + row, 2 * LANES : width]
+            total += band[:, plane * width + LANES : (plane + 1) * width - LANES]
+            row_parts[0, end, plane] = rate * total
+            row_parts[1, end, plane] = (
+                held[plane, row : row + BORDER, lanes] + row_parts[0, end, plane]
+            )
+        for number, target in enumerate((correction, estimate)):
+            send(
+                4 + 2 * end + number, row_parts.at[number, end],
+                target.at[:, pl.ds(row, BORDER), pl.ds(LANES, width - 2 * LANES)],
+            )
     for store in stores:
         store.wait()
 
@@ -540,14 +619,14 @@
     return pltpu.with_memory_space_constraint(array, pltpu.VMEM)
 
 
-def swap_along(axis, to_before, to_after):
+def swap_pairs(axis, first, second):
     count = lax.axis_size(axis)
-    forth = [(i, i + 1) for i in range(count - 1)]
-    back = [(i + 1, i) for i in range(count - 1)]
-    return (
-        in_vmem(lax.ppermute(to_after, axis, forth)),
-        in_vmem(lax.ppermute(to_before, axis, back)),
-    )
+
+    def swap(array, begin):
+        ends = [(i, i + 1) for i in range(begin, count - 1, 2)]
+        return in_vmem(lax.ppermute(array, axis, ends + [(j, i) for i, j in ends]))
+
+    return swap(first, 0), swap(second, 1)
 
 
 def on_device(object_field, probe_field, amplitudes, positions, counts):
@@ -558,7 +637,7 @@
     doubled_shape = f32(2, 2 * probe, probe)
     tables = tuple(jnp.asarray(table) for table in dft_blocks(probe))
     places = positions[0, 0]
-    order = pltpu.SMEM((amplitudes.shape[0],), jnp.int32)
+    order = pltpu.SMEM((amplitudes.shape[0] + 1,), jnp.int32)
     sides = (f32(extent, LANES), f32(extent, LANES))
 
     def row_bands(count):
@@ -576,13 +655,13 @@
             compiler_params=PARAMS,
         )(*scalars, *arrays)
 
-    slots = (places, counts)
+    slots = (in_hbm(places), counts)
     strips = [
         jnp.concatenate([object_field[0, rows], object_field[1, rows]], axis=1)
         for rows in (slice(0, BORDER), slice(tile - BORDER, tile))
     ]
     table_shapes = tuple(pltpu.VMEM(table.shape, table.dtype) for table in tables)
-    up, down = swap_along("row", *strips)
+    up, down = swap_pairs("row", *by_side("row", *strips))
     cur, acc, doubled, held, *tables = pl.pallas_call(
         inner_start_kernel,
         out_shape=(padded, padded, doubled_shape, f32(*amplitudes.shape), *table_shapes),
@@ -593,7 +672,7 @@
         name="inner_start",
     )(*slots, *map(in_hbm, (object_field, probe_field, amplitudes, *tables)))
     packed = call(object_pack_kernel, (), (cur, up, down), sides[0])
-    left, right = swap_along("col", packed, packed)
+    left, right = swap_pairs("col", packed, packed)
     acc = call(
         inner_rest_kernel, slots, (cur, doubled, held, *tables, acc),
         padded, (order,), {9: 0},
@@ -602,14 +681,14 @@
         outer_kernel, slots, (up, down, left, right, doubled, held, *tables, cur, acc),
         (padded, padded, *row_bands(BAND), *sides), (order,), {12: 0, 13: 1},
     )
-    up, down = swap_along("row", to_up, to_down)
-    left, right = swap_along("col", to_left, to_right)
+    up, down = swap_pairs("row", to_up, to_down)
+    left, right = swap_pairs("col", to_left, to_right)
     cur, acc = call(
         deep_kernel, slots, (probe_field, doubled, held, *tables, cur, acc),
         (padded, padded), (order,), {9: 0, 10: 1},
     )
     corners = (f32(2 * BAND, LANES),) * 2
-    left_corners, right_corners = swap_along("col", *call(corner_kernel, (), (up, down, acc), corners))
+    left_corners, right_corners = swap_pairs("col", *call(corner_kernel, (), (up, down, acc), corners))
     cur, acc, to_up, to_down, to_left, to_right = call(
         functools.partial(second_kernel, lax.axis_size("row"), lax.axis_size("col")),
         slots,
@@ -619,27 +698,41 @@
         ),
         (padded, padded, *row_bands(BORDER), *sides), (order,), {15: 0, 16: 1},
     )
-    up, down = swap_along("row", to_up, to_down)
+    up, down = swap_pairs("row", to_up, to_down)
+    acc = call(
+        second_rest_kernel, slots, (cur, doubled, held, *tables, acc),
+        padded, (order,), {9: 0},
+    )
     folded = f32(tile // 2, LANES)
     to_left, to_right = call(
-        last_corner_kernel, (), (up, down, to_left, to_right),
+        last_corner_kernel, (), (up, down, to_left, to_right, acc),
         (folded, folded), (f32(tile, LANES),),
     )
-    left, right = swap_along("col", to_left, to_right)
-    whole = pltpu.VMEM((2, tile, width), jnp.float32)
+    left, right = swap_pairs("col", to_left, to_right)
     result = jax.ShapeDtypeStruct((2, tile, width), jnp.float32)
+    middle = f32(2, tile - BAND, width - 2 * LANES)
+    tile_held, estimate, correction = pl.pallas_call(
+        middle_kernel,
+        out_shape=(f32(2, tile, width), result, result),
+        in_specs=[HBM, VMEM, VMEM],
+        out_specs=(VMEM, HBM, HBM),
+        scratch_shapes=[middle, middle, pltpu.SemaphoreType.DMA((3,))],
+        compiler_params=PARAMS,
+        name="middle",
+    )(in_hbm(object_field), probe_field, acc)
     estimate, correction = pl.pallas_call(
         last_kernel,
         out_shape=(result, result),
-        in_specs=[HBM] + [VMEM] * 6,
+        in_specs=[VMEM] * 7 + [HBM] * 2,
         out_specs=(HBM, HBM),
         scratch_shapes=[
-            whole, whole, whole,
-            pltpu.SemaphoreType.DMA((CHUNKS,)), pltpu.SemaphoreType.DMA((2, CHUNKS)),
+            f32(2, 2, 2, tile, LANES), f32(2, 2, 2, BORDER, width - 2 * LANES),
+            pltpu.SemaphoreType.DMA((8,)),
         ],
+        input_output_aliases={7: 0, 8: 1},
         compiler_params=PARAMS,
         name="finish",
-    )(in_hbm(object_field), probe_field, up, down, left, right, acc)
+    )(probe_field, up, down, left, right, acc, tile_held, estimate, correction)
     return estimate, correction
 
 

time: 85 us -> 69.3 us (0.82)
  the two profiles are of different devices: /device:TPU:1 before, /device:TPU:19 now
where the time goes in v4:
time: 69.3 us; the launch traced here: 68.8 us
  Pallas kernels  27 us (39%)
  starting transfers between devices  25.2 us (36%)
  waiting for transfers between devices  13.9 us (20%)
  between operations  1.69 us (2%)
  local copies, waits for them, and re-layouts  0.96 us (1%)
    ppermute x14, starting transfers between devices, swap(): return in_vmem(lax.ppermute(array, axis, ends + [(j, i) for i, j in ends]))  25.2 us
    pallas_call x8, Pallas kernels, call(): pl.pallas_call(kernel, out_shape=outs, in_specs=[SMEM] * len(scalars) + [...  16.6 us
    ppermute x14, waiting for transfers between devices, swap(): return in_vmem(lax.ppermute(array, axis, ends + [(j, i) for i, j in ends]))  13.9 us
    pallas_call x1, Pallas kernels, on_device(): pl.pallas_call(inner_start_kernel, out_shape=(padded, padded, doubled_sha...  5.68 us
    pallas_call x1, Pallas kernels, on_device(): pl.pallas_call(middle_kernel, out_shape=(f32(2, tile, width), result, res...  3.01 us
    pallas_call x1, Pallas kernels, on_device(): pl.pallas_call(last_kernel, out_shape=(result, result), in_specs=[VMEM] *...  1.76 us
  transfers between devices with their start and end apart: 14, of which 6 were waited for; matrix products, arithmetic and copies ran while one was open for 0% of the time, Pallas kernels for 24%

profile of v4, /device:TPU:19, one launch (start us, length us, event | category | flops | bytes accessed | tf_op | source)
XLA Modules:
  0.0 68.8 jit_solution(15454344778532415392)
XLA Ops:
  1.6 3.1 %collective-permute-start.1 = (f32[32,1024]{1,0:T(8,128)S(1)}, f32[32,1024]{1,0:T(8,128)S(1)}, u32[]{:S(2)}, u32[]{:S(2)}) collective-permute-start(f32[32,1024]{1,0:T(8,128)S(1)} %get-tuple-element.64), channel_id=1, source_target_pairs={{8,16},{16,8},{9,17},{17,9},{10,18},{18,10},{11,19},{19,11},{12,20... | collective-permute-start | bytes 393224 | tf_op jit(solution)/shard_map/ppermute | solution.py:627
  5.5 5.7 %inner_start.1 = (f32[2,584,768]{2,1,0:T(8,128)S(1)}, f32[2,584,768]{2,1,0:T(8,128)S(1)}, f32[2,256,128]{2,1,0:T(8,128)S(1)}, f32[24,128,128]{2,1,0:T(8,128)S(1)...) custom-call(s32[2,24]{1,0:T(2,128)} %bitcast.9, ...), custom_call_target="tpu_custom_call" | custom-call | tf_op jit(solution)/shard_map/inner_start/pallas_call | solution.py:665
  11.3 4.1 %collective-permute-start.3 = (f32[576,128]{1,0:T(8,128)S(1)}, f32[576,128]{1,0:T(8,128)S(1)}, u32[]{:S(2)}, u32[]{:S(2)}) collective-permute-start(f32[576,128]{1,0:T(8,128)S(1)} %shard_map.104), channel_id=1, source_target_pairs={{1,2},{3,4},{5,6},{2,1},{4,3},{6,5},{9,10},{11,12},{13,14},{10,9},... | collective-permute-start | bytes 884744 | tf_op jit(solution)/shard_map/ppermute | solution.py:627
  15.5 3.2 %shard_map.105.acc_in = f32[2,584,768]{2,1,0:T(8,128)S(1)} custom-call(s32[2,24]{1,0:T(2,128)} %bitcast.10, s32[1,1]{1,0:T(1,128)S(6)} %copy.31.counts, f32[2,584,768]{2,1,0:T(8,128)S(1)} %get-tuple-element.37.cur.cur_in, f32[2,256,128]{2,1,0:T(8,128)S(1)} %get-tuple-element.31.doubled, ...), custom_call_target="tpu_custom_call", output_to_operand_aliasing={{}: (9, {})} | custom-call | tf_op jit(solution)/shard_map/pallas_call | solution.py:648
  18.7 1.3 %collective-permute-done.3.right = f32[576,128]{1,0:T(8,128)S(1)} collective-permute-done((f32[576,128]{1,0:T(8,128)S(1)}, f32[576,128]{1,0:T(8,128)S(1)}, u32[]{:S(2)}, u32[]{:S(2)}) %collective-permute-start.3) | collective-permute-done | bytes 294944 | tf_op jit(solution)/shard_map/ppermute | solution.py:627
  20.0 3.8 %shard_map.106 = (f32[2,584,768]{2,1,0:T(8,128)S(1)}, f32[2,584,768]{2,1,0:T(8,128)S(1)}, f32[64,1152]{1,0:T(8,128)S(1)}, f32[64,1152]{1,0:T(8,128)S(1)}, f32[57...) custom-call(s32[2,24]{1,0:T(2,128)} %bitcast.11, ...), custom_call_target="tpu_custom_call", output_to_operand_aliasing={{0}: (12, {}), {1}: (13, {})} | custom-call | tf_op jit(solution)/shard_map/pallas_call | solution.py:648
  23.7 1.7 %collective-permute-start.4 = (f32[64,1152]{1,0:T(8,128)S(1)}, f32[64,1152]{1,0:T(8,128)S(1)}, u32[]{:S(2)}, u32[]{:S(2)}) collective-permute-start(f32[64,1152]{1,0:T(8,128)S(1)} %get-tuple-element.39), channel_id=1, source_target_pairs={{0,8},{16,24},{8,0},{24,16},{1,9},{17,25},{9,1},{25,17},{2,10},{18... | collective-permute-start | bytes 884744 | tf_op jit(solution)/shard_map/ppermute | solution.py:627
  25.5 3.0 %collective-permute-start.5 = (f32[64,1152]{1,0:T(8,128)S(1)}, f32[64,1152]{1,0:T(8,128)S(1)}, u32[]{:S(2)}, u32[]{:S(2)}) collective-permute-start(f32[64,1152]{1,0:T(8,128)S(1)} %get-tuple-element.40), channel_id=1, source_target_pairs={{8,16},{16,8},{9,17},{17,9},{10,18},{18,10},{11,19},{19,11},{12,20... | collective-permute-start | bytes 884744 | tf_op jit(solution)/shard_map/ppermute | solution.py:627
  28.5 1.0 %collective-permute-start.6 = (f32[576,128]{1,0:T(8,128)S(1)}, f32[576,128]{1,0:T(8,128)S(1)}, u32[]{:S(2)}, u32[]{:S(2)}) collective-permute-start(f32[576,128]{1,0:T(8,128)S(1)} %get-tuple-element.41), channel_id=1, source_target_pairs={{0,1},{2,3},{4,5},{6,7},{1,0},{3,2},{5,4},{7,6},{8,9},{10,11},{12,... | collective-permute-start | bytes 884744 | tf_op jit(solution)/shard_map/ppermute | solution.py:627
  29.5 3.1 %collective-permute-start.7 = (f32[576,128]{1,0:T(8,128)S(1)}, f32[576,128]{1,0:T(8,128)S(1)}, u32[]{:S(2)}, u32[]{:S(2)}) collective-permute-start(f32[576,128]{1,0:T(8,128)S(1)} %get-tuple-element.42), channel_id=1, source_target_pairs={{1,2},{3,4},{5,6},{2,1},{4,3},{6,5},{9,10},{11,12},{13,14},{10,9},... | collective-permute-start | bytes 884744 | tf_op jit(solution)/shard_map/ppermute | solution.py:627
  32.6 3.6 %shard_map.107 = (f32[2,584,768]{2,1,0:T(8,128)S(1)}, f32[2,584,768]{2,1,0:T(8,128)S(1)}) custom-call(s32[2,24]{1,0:T(2,128)} %bitcast.12, s32[1,1]{1,0:T(1,128)S(6)} %copy.31.counts, f32[2,128,128]{2,1,0:T(8,128)S(1)} %copy-done, f32[2,256,128]{2,1,0:T(8,128)S(1)} %get-tuple-element.31.doubled, ...), custom_call_target="tpu_custom_call", output_to_operand_aliasing={{0}: (9, {}), {1}: (10, {})} | custom-call | tf_op jit(solution)/shard_map/pallas_call | solution.py:648
  36.3 3.4 %collective-permute-done.5.down = f32[64,1152]{1,0:T(8,128)S(1)} collective-permute-done((f32[64,1152]{1,0:T(8,128)S(1)}, f32[64,1152]{1,0:T(8,128)S(1)}, u32[]{:S(2)}, u32[]{:S(2)}) %collective-permute-start.5) | collective-permute-done | bytes 294944 | tf_op jit(solution)/shard_map/ppermute | solution.py:627
  39.8 1.3 %collective-permute-start.8 = (f32[128,128]{1,0:T(8,128)S(1)}, f32[128,128]{1,0:T(8,128)S(1)}, u32[]{:S(2)}, u32[]{:S(2)}) collective-permute-start(f32[128,128]{1,0:T(8,128)S(1)} %get-tuple-element.46), channel_id=1, source_target_pairs={{0,1},{2,3},{4,5},{6,7},{1,0},{3,2},{5,4},{7,6},{8,9},{10,11},{12,... | collective-permute-start | bytes 196616 | tf_op jit(solution)/shard_map/ppermute | solution.py:627
  41.1 1.9 %collective-permute-start.9 = (f32[128,128]{1,0:T(8,128)S(1)}, f32[128,128]{1,0:T(8,128)S(1)}, u32[]{:S(2)}, u32[]{:S(2)}) collective-permute-start(f32[128,128]{1,0:T(8,128)S(1)} %get-tuple-element.47), channel_id=1, source_target_pairs={{1,2},{3,4},{5,6},{2,1},{4,3},{6,5},{9,10},{11,12},{13,14},{10,9},... | collective-permute-start | bytes 196616 | tf_op jit(solution)/shard_map/ppermute | solution.py:627
  43.1 3.6 %collective-permute-done.9.right_corners = f32[128,128]{1,0:T(8,128)S(1)} collective-permute-done((f32[128,128]{1,0:T(8,128)S(1)}, f32[128,128]{1,0:T(8,128)S(1)}, u32[]{:S(2)}, u32[]{:S(2)}) %collective-permute-start.9) | collective-permute-done | bytes 65568 | tf_op jit(solution)/shard_map/ppermute | solution.py:627
  46.7 4.4 %shard_map.109 = (f32[2,584,768]{2,1,0:T(8,128)S(1)}, f32[2,584,768]{2,1,0:T(8,128)S(1)}, f32[32,1152]{1,0:T(8,128)S(1)}, f32[32,1152]{1,0:T(8,128)S(1)}, f32[57...) custom-call(s32[2,24]{1,0:T(2,128)} %bitcast.13, ...), custom_call_target="tpu_custom_call", output_to_operand_aliasing={{0}: (15, {}), {1}: (16, {})} | custom-call | tf_op jit(solution)/shard_map/pallas_call | solution.py:648
  51.2 3.1 %collective-permute-start.11 = (f32[32,1152]{1,0:T(8,128)S(1)}, f32[32,1152]{1,0:T(8,128)S(1)}, u32[]{:S(2)}, u32[]{:S(2)}) collective-permute-start(f32[32,1152]{1,0:T(8,128)S(1)} %get-tuple-element.50), channel_id=1, source_target_pairs={{8,16},{16,8},{9,17},{17,9},{10,18},{18,10},{11,19},{19,11},{12,20... | collective-permute-start | bytes 442376 | tf_op jit(solution)/shard_map/ppermute | solution.py:627
  54.3 1.0 %shard_map.110.after.acc = f32[2,584,768]{2,1,0:T(8,128)S(1)} custom-call(s32[2,24]{1,0:T(2,128)} %bitcast.14, s32[1,1]{1,0:T(1,128)S(6)} %copy.31.counts, f32[2,584,768]{2,1,0:T(8,128)S(1)} %get-tuple-element.53.cur, f32[2,256,128]{2,1,0:T(8,128)S(1)} %get-tuple-element.31.doubled, ...), custom_call_target="tpu_custom_call", output_to_operand_aliasing={{}: (9, {})} | custom-call | tf_op jit(solution)/shard_map/pallas_call | solution.py:648
  55.4 1.2 %collective-permute-done.10.up = f32[32,1152]{1,0:T(8,128)S(1)} collective-permute-done((f32[32,1152]{1,0:T(8,128)S(1)}, f32[32,1152]{1,0:T(8,128)S(1)}, u32[]{:S(2)}, u32[]{:S(2)}) %collective-permute-start.10) | collective-permute-done | bytes 147488 | tf_op jit(solution)/shard_map/ppermute | solution.py:627
  56.6 3.0 %collective-permute-done.11.down = f32[32,1152]{1,0:T(8,128)S(1)} collective-permute-done((f32[32,1152]{1,0:T(8,128)S(1)}, f32[32,1152]{1,0:T(8,128)S(1)}, u32[]{:S(2)}, u32[]{:S(2)}) %collective-permute-start.11) | collective-permute-done | bytes 147488 | tf_op jit(solution)/shard_map/ppermute | solution.py:627
  60.6 1.9 %collective-permute-start.13 = (f32[256,128]{1,0:T(8,128)S(1)}, f32[256,128]{1,0:T(8,128)S(1)}, u32[]{:S(2)}, u32[]{:S(2)}) collective-permute-start(f32[256,128]{1,0:T(8,128)S(1)} %get-tuple-element.56), channel_id=1, source_target_pairs={{1,2},{3,4},{5,6},{2,1},{4,3},{6,5},{9,10},{11,12},{13,14},{10,9},... | collective-permute-start | bytes 393224 | tf_op jit(solution)/shard_map/ppermute | solution.py:627
  62.6 3.0 %middle.1 = (f32[2,512,512]{2,1,0:T(8,128)S(1)}, f32[2,512,512]{2,1,0:T(8,128)}, f32[2,512,512]{2,1,0:T(8,128)}) custom-call(f32[2,512,512]{2,1,0:T(8,128)} %objects.3, f32[2,128,128]{2,1,0:T(8,128)S(1)} %copy-done, f32[2,584,768]{2,1,0:T(8,128)S(1)} %shard_map.110.after.acc), custom_call_target="tpu_custom_call" | custom-call | tf_op jit(solution)/shard_map/middle/pallas_call | solution.py:714
  65.6 1.3 %collective-permute-done.13.right = f32[256,128]{1,0:T(8,128)S(1)} collective-permute-done((f32[256,128]{1,0:T(8,128)S(1)}, f32[256,128]{1,0:T(8,128)S(1)}, u32[]{:S(2)}, u32[]{:S(2)}) %collective-permute-start.13) | collective-permute-done | bytes 131104 | tf_op jit(solution)/shard_map/ppermute | solution.py:627
  66.9 1.8 %finish.1 = (f32[2,512,512]{2,1,0:T(8,128)}, f32[2,512,512]{2,1,0:T(8,128)}) custom-call(f32[2,128,128]{2,1,0:T(8,128)S(1)} %copy-done, f32[32,1152]{1,0:T(8,128)S(1)} %collective-permute-done.10.up, f32[32,1152]{1,0:T(8,128)S(1)} %collective-permute-done.11.down, ...), custom_call_target="tpu_custom_call", output_to_operand_aliasing={{0}: (7, {}), {1}: (8, {})} | custom-call | tf_op jit(solution)/shard_map/finish/pallas_call | solution.py:723
  (19 shorter events, 2.6 us)
Async XLA Ops:
  1.6 9.5 %collective-permute-start.1 = (f32[32,1024]{1,0:T(8,128)S(1)}, f32[32,1024]{1,0:T(8,128)S(1)}, u32[]{:S(2)}, u32[]{:S(2)}) collective-permute-start(f32[32,1024]{1,0:T(8,128)S(1)} %get-tuple-element.64), channel_id=1, source_target_pairs={{8,16},{16,8},{9,17},{17,9},{10,18},{18,10},{11,19},{19,11},{12,20... | collective-permute-start | bytes 393224 | tf_op jit(solution)/shard_map/ppermute | solution.py:627
  4.8 6.4 %collective-permute-start = (f32[32,1024]{1,0:T(8,128)S(1)}, f32[32,1024]{1,0:T(8,128)S(1)}, u32[]{:S(2)}, u32[]{:S(2)}) collective-permute-start(f32[32,1024]{1,0:T(8,128)S(1)} %get-tuple-element.65), channel_id=1, source_target_pairs={{0,8},{16,24},{8,0},{24,16},{1,9},{17,25},{9,1},{25,17},{2,10},{18... | collective-permute-start | bytes 393224 | tf_op jit(solution)/shard_map/ppermute | solution.py:627
  11.3 8.6 %collective-permute-start.3 = (f32[576,128]{1,0:T(8,128)S(1)}, f32[576,128]{1,0:T(8,128)S(1)}, u32[]{:S(2)}, u32[]{:S(2)}) collective-permute-start(f32[576,128]{1,0:T(8,128)S(1)} %shard_map.104), channel_id=1, source_target_pairs={{1,2},{3,4},{5,6},{2,1},{4,3},{6,5},{9,10},{11,12},{13,14},{10,9},... | collective-permute-start | bytes 884744 | tf_op jit(solution)/shard_map/ppermute | solution.py:627
  15.4 4.6 %collective-permute-start.2 = (f32[576,128]{1,0:T(8,128)S(1)}, f32[576,128]{1,0:T(8,128)S(1)}, u32[]{:S(2)}, u32[]{:S(2)}) collective-permute-start(f32[576,128]{1,0:T(8,128)S(1)} %shard_map.104), channel_id=1, source_target_pairs={{0,1},{2,3},{4,5},{6,7},{1,0},{3,2},{5,4},{7,6},{8,9},{10,11},{12,... | collective-permute-start | bytes 884744 | tf_op jit(solution)/shard_map/ppermute | solution.py:627
  18.7 13.9 %copy-start = (f32[2,128,128]{2,1,0:T(8,128)S(1)}, f32[2,128,128]{2,1,0:T(8,128)}, u32[]{:S(2)}) copy-start(f32[2,128,128]{2,1,0:T(8,128)} %probe.7) | copy-start | bytes 393220
  23.7 12.5 %collective-permute-start.4 = (f32[64,1152]{1,0:T(8,128)S(1)}, f32[64,1152]{1,0:T(8,128)S(1)}, u32[]{:S(2)}, u32[]{:S(2)}) collective-permute-start(f32[64,1152]{1,0:T(8,128)S(1)} %get-tuple-element.39), channel_id=1, source_target_pairs={{0,8},{16,24},{8,0},{24,16},{1,9},{17,25},{9,1},{25,17},{2,10},{18... | collective-permute-start | bytes 884744 | tf_op jit(solution)/shard_map/ppermute | solution.py:627
  25.5 14.2 %collective-permute-start.5 = (f32[64,1152]{1,0:T(8,128)S(1)}, f32[64,1152]{1,0:T(8,128)S(1)}, u32[]{:S(2)}, u32[]{:S(2)}) collective-permute-start(f32[64,1152]{1,0:T(8,128)S(1)} %get-tuple-element.40), channel_id=1, source_target_pairs={{8,16},{16,8},{9,17},{17,9},{10,18},{18,10},{11,19},{19,11},{12,20... | collective-permute-start | bytes 884744 | tf_op jit(solution)/shard_map/ppermute | solution.py:627
  28.5 14.5 %collective-permute-start.6 = (f32[576,128]{1,0:T(8,128)S(1)}, f32[576,128]{1,0:T(8,128)S(1)}, u32[]{:S(2)}, u32[]{:S(2)}) collective-permute-start(f32[576,128]{1,0:T(8,128)S(1)} %get-tuple-element.41), channel_id=1, source_target_pairs={{0,1},{2,3},{4,5},{6,7},{1,0},{3,2},{5,4},{7,6},{8,9},{10,11},{12,... | collective-permute-start | bytes 884744 | tf_op jit(solution)/shard_map/ppermute | solution.py:627
  29.5 13.6 %collective-permute-start.7 = (f32[576,128]{1,0:T(8,128)S(1)}, f32[576,128]{1,0:T(8,128)S(1)}, u32[]{:S(2)}, u32[]{:S(2)}) collective-permute-start(f32[576,128]{1,0:T(8,128)S(1)} %get-tuple-element.42), channel_id=1, source_target_pairs={{1,2},{3,4},{5,6},{2,1},{4,3},{6,5},{9,10},{11,12},{13,14},{10,9},... | collective-permute-start | bytes 884744 | tf_op jit(solution)/shard_map/ppermute | solution.py:627
  39.8 3.2 %collective-permute-start.8 = (f32[128,128]{1,0:T(8,128)S(1)}, f32[128,128]{1,0:T(8,128)S(1)}, u32[]{:S(2)}, u32[]{:S(2)}) collective-permute-start(f32[128,128]{1,0:T(8,128)S(1)} %get-tuple-element.46), channel_id=1, source_target_pairs={{0,1},{2,3},{4,5},{6,7},{1,0},{3,2},{5,4},{7,6},{8,9},{10,11},{12,... | collective-permute-start | bytes 196616 | tf_op jit(solution)/shard_map/ppermute | solution.py:627
  41.1 5.6 %collective-permute-start.9 = (f32[128,128]{1,0:T(8,128)S(1)}, f32[128,128]{1,0:T(8,128)S(1)}, u32[]{:S(2)}, u32[]{:S(2)}) collective-permute-start(f32[128,128]{1,0:T(8,128)S(1)} %get-tuple-element.47), channel_id=1, source_target_pairs={{1,2},{3,4},{5,6},{2,1},{4,3},{6,5},{9,10},{11,12},{13,14},{10,9},... | collective-permute-start | bytes 196616 | tf_op jit(solution)/shard_map/ppermute | solution.py:627
  51.1 5.5 %collective-permute-start.10 = (f32[32,1152]{1,0:T(8,128)S(1)}, f32[32,1152]{1,0:T(8,128)S(1)}, u32[]{:S(2)}, u32[]{:S(2)}) collective-permute-start(f32[32,1152]{1,0:T(8,128)S(1)} %get-tuple-element.49), channel_id=1, source_target_pairs={{0,8},{16,24},{8,0},{24,16},{1,9},{17,25},{9,1},{25,17},{2,10},{18... | collective-permute-start | bytes 442376 | tf_op jit(solution)/shard_map/ppermute | solution.py:627
  51.2 8.4 %collective-permute-start.11 = (f32[32,1152]{1,0:T(8,128)S(1)}, f32[32,1152]{1,0:T(8,128)S(1)}, u32[]{:S(2)}, u32[]{:S(2)}) collective-permute-start(f32[32,1152]{1,0:T(8,128)S(1)} %get-tuple-element.50), channel_id=1, source_target_pairs={{8,16},{16,8},{9,17},{17,9},{10,18},{18,10},{11,19},{19,11},{12,20... | collective-permute-start | bytes 442376 | tf_op jit(solution)/shard_map/ppermute | solution.py:627
  59.9 5.7 %collective-permute-start.12 = (f32[256,128]{1,0:T(8,128)S(1)}, f32[256,128]{1,0:T(8,128)S(1)}, u32[]{:S(2)}, u32[]{:S(2)}) collective-permute-start(f32[256,128]{1,0:T(8,128)S(1)} %get-tuple-element.55), channel_id=1, source_target_pairs={{0,1},{2,3},{4,5},{6,7},{1,0},{3,2},{5,4},{7,6},{8,9},{10,11},{12,... | collective-permute-start | bytes 393224 | tf_op jit(solution)/shard_map/ppermute | solution.py:627
  60.6 6.3 %collective-permute-start.13 = (f32[256,128]{1,0:T(8,128)S(1)}, f32[256,128]{1,0:T(8,128)S(1)}, u32[]{:S(2)}, u32[]{:S(2)}) collective-permute-start(f32[256,128]{1,0:T(8,128)S(1)} %get-tuple-element.56), channel_id=1, source_target_pairs={{1,2},{3,4},{5,6},{2,1},{4,3},{6,5},{9,10},{11,12},{13,14},{10,9},... | collective-permute-start | bytes 393224 | tf_op jit(solution)/shard_map/ppermute | solution.py:627

commit v5 on v4

--- a/solution.py
+++ b/solution.py
@@ -36,7 +36,7 @@
         blocks.append(np.concatenate([high, high, low], axis=0))
         left = np.block([[real, -sign * imag], [sign * imag, real]])
         high, low = split_host(left)
-        blocks.append(np.concatenate([high, high, low], axis=1))
+        blocks.append(np.concatenate([high, low], axis=0))
     return blocks
 
 
@@ -66,7 +66,9 @@
 
 def times_left(block, columns):
     high, low = split(columns)
-    return dot(block, jnp.concatenate([high, low, high], axis=0))
+    count = block.shape[0] // 2
+    both = dot(block, high)
+    return both[:count] + (both[count:] + dot(block[:count], low))
 
 
 def lane_iota(rows):
@@ -278,36 +280,44 @@
     )
 
 
+def fold_side(whole, is_low):
+    half = whole.shape[0] // 2
+    low = lane_iota(half) % (LANES // 2) < BORDER
+    keep = low if is_low else jnp.logical_not(low)
+    return jnp.where(keep, whole[:half, :], pltpu.roll(whole[half:, :], BORDER, 1))
+
+
+def unfold_side(packed):
+    return unpack_planes(
+        jnp.concatenate([packed, pltpu.roll(packed, LANES - BORDER, 1)], axis=0)
+    )
+
+
 def by_side(axis, first, second):
     even = lax.axis_index(axis) % 2 == 0
     return jnp.where(even, second, first), jnp.where(even, first, second)
 
 
-def object_pack_kernel(cur, up, down, out):
+def object_pack_kernel(cur, up, down, to_left, to_right, whole):
     count = up.shape[0]
     width = up.shape[1] // 2
-    tile = out.shape[0] - 2 * count
-    is_low = lane_iota(count) < BORDER
+    extent = whole.shape[0]
+    rows = slice(count, extent - count)
     up, down = by_side("row", up[...], down[...])
-    for row, band in ((0, up), (count + tile, down)):
-        out[row : row + count, :] = pack_planes(
-            *[
-                jnp.where(
-                    is_low,
-                    band[:, plane * width : plane * width + LANES],
-                    band[:, (plane + 1) * width - LANES : (plane + 1) * width],
-                )
-                for plane in range(2)
-            ]
-        )
-    rows = slice(count, count + tile)
-    is_low = lane_iota(tile) < BORDER
-    out[rows, :] = pack_planes(
-        *[
-            jnp.where(is_low, cur[plane, rows, LANES : 2 * LANES], cur[plane, rows, width : width + LANES])
-            for plane in range(2)
-        ]
-    )
+    parts = []
+    for side in range(2):
+        block = side * (width - LANES)
+        for row, band in ((0, up), (extent - count, down)):
+            whole[row : row + count, :] = pack_planes(
+                *[
+                    band[:, plane * width + block : plane * width + block + LANES]
+                    for plane in range(2)
+                ]
+            )
+        lanes = slice(LANES + block, 2 * LANES + block)
+        whole[rows, :] = pack_planes(cur[0, rows, lanes], cur[1, rows, lanes])
+        parts.append(fold_side(whole, side == 0))
+    to_left[...], to_right[...] = by_side("col", *parts)
 
 
 def outer_kernel(
@@ -315,11 +325,11 @@
     right_f, left_f, right_b, left_b, cur_in, acc_in,
     cur, acc, to_up, to_down, to_left, to_right, order,
 ):
-    extent = left.shape[0]
+    extent = 2 * left.shape[0]
     tile, width = extent - BAND, up.shape[1] // 2
     lane = lane_iota(extent)
     up, down = by_side("row", up[...], down[...])
-    lefts, rights = map(unpack_planes, by_side("col", left[...], right[...]))
+    lefts, rights = map(unfold_side, by_side("col", left[...], right[...]))
     for plane in range(2):
         cur[plane, :extent, :LANES] = jnp.where(lane >= LANES - BORDER, lefts[plane], 0.0)
         cur[plane, :extent, LANES + width :] = jnp.where(lane < BORDER, rights[plane], 0.0)
@@ -355,16 +365,10 @@
     )
 
 
-def half_lanes(rows, first):
-    low = lane_iota(rows) % (LANES // 2) < BORDER
-    return low if first else jnp.logical_not(low)
-
-
 def last_corner_kernel(up, down, left, right, after, to_left, to_right, whole):
     count = up.shape[0]
     tile = left.shape[0] - BAND
     width = (up.shape[1] - LANES) // 2
-    half = tile // 2
     up, down = by_side("row", up[...], down[...])
     tops, bottoms = corner_parts(up, width), corner_parts(down, width)
     parts = []
@@ -372,19 +376,8 @@
         whole[...] = source[BORDER : BORDER + tile, :]
         whole[:count, :] += tops[side]
         whole[tile - count :, :] += bottoms[side]
-        parts.append(
-            jnp.where(
-                half_lanes(half, side == 1),
-                whole[:half, :],
-                pltpu.roll(whole[half:, :], BORDER, 1),
-            )
-        )
+        parts.append(fold_side(whole, side == 1))
     to_left[...], to_right[...] = by_side("col", *parts)
-
-
-def unfold_side(packed):
-    both = jnp.concatenate([packed, pltpu.roll(packed, LANES - BORDER, 1)], axis=0)
-    return unpack_planes(both)
 
 
 def deep_kernel(
@@ -626,7 +619,9 @@
         ends = [(i, i + 1) for i in range(begin, count - 1, 2)]
         return in_vmem(lax.ppermute(array, axis, ends + [(j, i) for i, j in ends]))
 
-    return swap(first, 0), swap(second, 1)
+    first = swap(first, 0)
+    second = swap(second, 1)
+    return first, second
 
 
 def on_device(object_field, probe_field, amplitudes, positions, counts):
@@ -671,8 +666,11 @@
         compiler_params=PARAMS,
         name="inner_start",
     )(*slots, *map(in_hbm, (object_field, probe_field, amplitudes, *tables)))
-    packed = call(object_pack_kernel, (), (cur, up, down), sides[0])
-    left, right = swap_pairs("col", packed, packed)
+    to_left, to_right = call(
+        object_pack_kernel, (), (cur, up, down),
+        (f32(extent // 2, LANES),) * 2, (f32(extent, LANES),),
+    )
+    left, right = swap_pairs("col", to_left, to_right)
     acc = call(
         inner_rest_kernel, slots, (cur, doubled, held, *tables, acc),
         padded, (order,), {9: 0},

time: 69.3 us -> 68.3 us (0.986)
  starting transfers between devices: 25.2 us -> 24.5 us
    ppermute x14, starting transfers between devices: 25.2 us -> 24.5 us  [swap(): return in_vmem(lax.ppermute(array, axis, ends + [(j, i) for i, j in ends]))]
where the time goes in v5:
time: 68.3 us; the launch traced here: 67.9 us
  Pallas kernels  27.1 us (40%)
  starting transfers between devices  24.5 us (36%)
  waiting for transfers between devices  13.6 us (20%)
  between operations  1.69 us (2%)
  local copies, waits for them, and re-layouts  0.96 us (1%)
    ppermute x14, starting transfers between devices, swap(): return in_vmem(lax.ppermute(array, axis, ends + [(j, i) for i, j in ends]))  24.5 us
    pallas_call x8, Pallas kernels, call(): pl.pallas_call(kernel, out_shape=outs, in_specs=[SMEM] * len(scalars) + [...  16.8 us
    ppermute x14, waiting for transfers between devices, swap(): return in_vmem(lax.ppermute(array, axis, ends + [(j, i) for i, j in ends]))  13.6 us
    pallas_call x1, Pallas kernels, on_device(): pl.pallas_call(inner_start_kernel, out_shape=(padded, padded, doubled_sha...  5.58 us
    pallas_call x1, Pallas kernels, on_device(): pl.pallas_call(middle_kernel, out_shape=(f32(2, tile, width), result, res...  3.01 us
    pallas_call x1, Pallas kernels, on_device(): pl.pallas_call(last_kernel, out_shape=(result, result), in_specs=[VMEM] *...  1.76 us
  transfers between devices with their start and end apart: 14, of which 6 were waited for; matrix products, arithmetic and copies ran while one was open for 0% of the time, Pallas kernels for 24%

profile of v5, /device:TPU:19, one launch (start us, length us, event | category | flops | bytes accessed | tf_op | source)
XLA Modules:
  0.0 67.9 jit_solution(11051473015382381753)
XLA Ops:
  0.6 1.0 %slice_bitcast_fusion.3 = (f32[32,512]{1,0:T(8,128)S(1)}, f32[32,512]{1,0:T(8,128)S(1)}, f32[32,512]{1,0:T(8,128)S(1)}, f32[32,512]{1,0:T(8,128)S(1)}) fusion(f32[2,512,512]{2,1,0:T(8,128)} %objects.3), kind=kLoop, calls=%fused_computation.7 | loop fusion | bytes 524288 | tf_op jit(solution)/shard_map/squeeze | solution.py:655
  1.6 3.1 %collective-permute-start.1 = (f32[32,1024]{1,0:T(8,128)S(1)}, f32[32,1024]{1,0:T(8,128)S(1)}, u32[]{:S(2)}, u32[]{:S(2)}) collective-permute-start(f32[32,1024]{1,0:T(8,128)S(1)} %get-tuple-element.68), channel_id=1, source_target_pairs={{8,16},{16,8},{9,17},{17,9},{10,18},{18,10},{11,19},{19,11},{12,20... | collective-permute-start | bytes 393224 | tf_op jit(solution)/shard_map/ppermute | solution.py:620
  5.5 5.6 %inner_start.1 = (f32[2,584,768]{2,1,0:T(8,128)S(1)}, f32[2,584,768]{2,1,0:T(8,128)S(1)}, f32[2,256,128]{2,1,0:T(8,128)S(1)}, f32[24,128,128]{2,1,0:T(8,128)S(1)...) custom-call(s32[2,24]{1,0:T(2,128)} %bitcast.9, ...), custom_call_target="tpu_custom_call" | custom-call | tf_op jit(solution)/shard_map/inner_start/pallas_call | solution.py:660
  11.5 1.0 %collective-permute-start.2 = (f32[288,128]{1,0:T(8,128)S(1)}, f32[288,128]{1,0:T(8,128)S(1)}, u32[]{:S(2)}, u32[]{:S(2)}) collective-permute-start(f32[288,128]{1,0:T(8,128)S(1)} %get-tuple-element.40), channel_id=1, source_target_pairs={{0,1},{2,3},{4,5},{6,7},{1,0},{3,2},{5,4},{7,6},{8,9},{10,11},{12,... | collective-permute-start | bytes 442376 | tf_op jit(solution)/shard_map/ppermute | solution.py:620
  12.5 3.1 %collective-permute-start.3 = (f32[288,128]{1,0:T(8,128)S(1)}, f32[288,128]{1,0:T(8,128)S(1)}, u32[]{:S(2)}, u32[]{:S(2)}) collective-permute-start(f32[288,128]{1,0:T(8,128)S(1)} %get-tuple-element.41), channel_id=1, source_target_pairs={{1,2},{3,4},{5,6},{2,1},{4,3},{6,5},{9,10},{11,12},{13,14},{10,9},... | collective-permute-start | bytes 442376 | tf_op jit(solution)/shard_map/ppermute | solution.py:620
  15.6 3.1 %shard_map.105.acc_in = f32[2,584,768]{2,1,0:T(8,128)S(1)} custom-call(s32[2,24]{1,0:T(2,128)} %bitcast.10, s32[1,1]{1,0:T(1,128)S(6)} %copy.31.counts, f32[2,584,768]{2,1,0:T(8,128)S(1)} %get-tuple-element.39.cur.cur_in, f32[2,256,128]{2,1,0:T(8,128)S(1)} %get-tuple-element.33.doubled, ...), custom_call_target="tpu_custom_call", output_to_operand_aliasing={{}: (9, {})} | custom-call | tf_op jit(solution)/shard_map/pallas_call | solution.py:643
  19.0 3.8 %shard_map.106 = (f32[2,584,768]{2,1,0:T(8,128)S(1)}, f32[2,584,768]{2,1,0:T(8,128)S(1)}, f32[64,1152]{1,0:T(8,128)S(1)}, f32[64,1152]{1,0:T(8,128)S(1)}, f32[57...) custom-call(s32[2,24]{1,0:T(2,128)} %bitcast.11, ...), custom_call_target="tpu_custom_call", output_to_operand_aliasing={{0}: (12, {}), {1}: (13, {})} | custom-call | tf_op jit(solution)/shard_map/pallas_call | solution.py:643
  22.8 1.7 %collective-permute-start.4 = (f32[64,1152]{1,0:T(8,128)S(1)}, f32[64,1152]{1,0:T(8,128)S(1)}, u32[]{:S(2)}, u32[]{:S(2)}) collective-permute-start(f32[64,1152]{1,0:T(8,128)S(1)} %get-tuple-element.43), channel_id=1, source_target_pairs={{0,8},{16,24},{8,0},{24,16},{1,9},{17,25},{9,1},{25,17},{2,10},{18... | collective-permute-start | bytes 884744 | tf_op jit(solution)/shard_map/ppermute | solution.py:620
  24.5 3.0 %collective-permute-start.5 = (f32[64,1152]{1,0:T(8,128)S(1)}, f32[64,1152]{1,0:T(8,128)S(1)}, u32[]{:S(2)}, u32[]{:S(2)}) collective-permute-start(f32[64,1152]{1,0:T(8,128)S(1)} %get-tuple-element.44), channel_id=1, source_target_pairs={{8,16},{16,8},{9,17},{17,9},{10,18},{18,10},{11,19},{19,11},{12,20... | collective-permute-start | bytes 884744 | tf_op jit(solution)/shard_map/ppermute | solution.py:620
  28.1 3.1 %collective-permute-start.7 = (f32[576,128]{1,0:T(8,128)S(1)}, f32[576,128]{1,0:T(8,128)S(1)}, u32[]{:S(2)}, u32[]{:S(2)}) collective-permute-start(f32[576,128]{1,0:T(8,128)S(1)} %get-tuple-element.46), channel_id=1, source_target_pairs={{1,2},{3,4},{5,6},{2,1},{4,3},{6,5},{9,10},{11,12},{13,14},{10,9},... | collective-permute-start | bytes 884744 | tf_op jit(solution)/shard_map/ppermute | solution.py:620
  31.3 3.6 %shard_map.107 = (f32[2,584,768]{2,1,0:T(8,128)S(1)}, f32[2,584,768]{2,1,0:T(8,128)S(1)}) custom-call(s32[2,24]{1,0:T(2,128)} %bitcast.12, s32[1,1]{1,0:T(1,128)S(6)} %copy.31.counts, f32[2,128,128]{2,1,0:T(8,128)S(1)} %copy-done, f32[2,256,128]{2,1,0:T(8,128)S(1)} %get-tuple-element.33.doubled, ...), custom_call_target="tpu_custom_call", output_to_operand_aliasing={{0}: (9, {}), {1}: (10, {})} | custom-call | tf_op jit(solution)/shard_map/pallas_call | solution.py:643
  34.9 4.2 %collective-permute-done.5.down = f32[64,1152]{1,0:T(8,128)S(1)} collective-permute-done((f32[64,1152]{1,0:T(8,128)S(1)}, f32[64,1152]{1,0:T(8,128)S(1)}, u32[]{:S(2)}, u32[]{:S(2)}) %collective-permute-start.5) | collective-permute-done | bytes 294944 | tf_op jit(solution)/shard_map/ppermute | solution.py:620
  39.3 0.9 %collective-permute-start.8 = (f32[128,128]{1,0:T(8,128)S(1)}, f32[128,128]{1,0:T(8,128)S(1)}, u32[]{:S(2)}, u32[]{:S(2)}) collective-permute-start(f32[128,128]{1,0:T(8,128)S(1)} %get-tuple-element.50), channel_id=1, source_target_pairs={{0,1},{2,3},{4,5},{6,7},{1,0},{3,2},{5,4},{7,6},{8,9},{10,11},{12,... | collective-permute-start | bytes 196616 | tf_op jit(solution)/shard_map/ppermute | solution.py:620
  40.2 1.9 %collective-permute-start.9 = (f32[128,128]{1,0:T(8,128)S(1)}, f32[128,128]{1,0:T(8,128)S(1)}, u32[]{:S(2)}, u32[]{:S(2)}) collective-permute-start(f32[128,128]{1,0:T(8,128)S(1)} %get-tuple-element.51), channel_id=1, source_target_pairs={{1,2},{3,4},{5,6},{2,1},{4,3},{6,5},{9,10},{11,12},{13,14},{10,9},... | collective-permute-start | bytes 196616 | tf_op jit(solution)/shard_map/ppermute | solution.py:620
  42.1 3.6 %collective-permute-done.9.right_corners = f32[128,128]{1,0:T(8,128)S(1)} collective-permute-done((f32[128,128]{1,0:T(8,128)S(1)}, f32[128,128]{1,0:T(8,128)S(1)}, u32[]{:S(2)}, u32[]{:S(2)}) %collective-permute-start.9) | collective-permute-done | bytes 65568 | tf_op jit(solution)/shard_map/ppermute | solution.py:620
  45.7 4.4 %shard_map.109 = (f32[2,584,768]{2,1,0:T(8,128)S(1)}, f32[2,584,768]{2,1,0:T(8,128)S(1)}, f32[32,1152]{1,0:T(8,128)S(1)}, f32[32,1152]{1,0:T(8,128)S(1)}, f32[57...) custom-call(s32[2,24]{1,0:T(2,128)} %bitcast.13, ...), custom_call_target="tpu_custom_call", output_to_operand_aliasing={{0}: (15, {}), {1}: (16, {})} | custom-call | tf_op jit(solution)/shard_map/pallas_call | solution.py:643
  50.2 3.1 %collective-permute-start.11 = (f32[32,1152]{1,0:T(8,128)S(1)}, f32[32,1152]{1,0:T(8,128)S(1)}, u32[]{:S(2)}, u32[]{:S(2)}) collective-permute-start(f32[32,1152]{1,0:T(8,128)S(1)} %get-tuple-element.54), channel_id=1, source_target_pairs={{8,16},{16,8},{9,17},{17,9},{10,18},{18,10},{11,19},{19,11},{12,20... | collective-permute-start | bytes 442376 | tf_op jit(solution)/shard_map/ppermute | solution.py:620
  53.4 1.0 %shard_map.110.after.acc = f32[2,584,768]{2,1,0:T(8,128)S(1)} custom-call(s32[2,24]{1,0:T(2,128)} %bitcast.14, s32[1,1]{1,0:T(1,128)S(6)} %copy.31.counts, f32[2,584,768]{2,1,0:T(8,128)S(1)} %get-tuple-element.57.cur, f32[2,256,128]{2,1,0:T(8,128)S(1)} %get-tuple-element.33.doubled, ...), custom_call_target="tpu_custom_call", output_to_operand_aliasing={{}: (9, {})} | custom-call | tf_op jit(solution)/shard_map/pallas_call | solution.py:643
  54.4 1.2 %collective-permute-done.10.up = f32[32,1152]{1,0:T(8,128)S(1)} collective-permute-done((f32[32,1152]{1,0:T(8,128)S(1)}, f32[32,1152]{1,0:T(8,128)S(1)}, u32[]{:S(2)}, u32[]{:S(2)}) %collective-permute-start.10) | collective-permute-done | bytes 147488 | tf_op jit(solution)/shard_map/ppermute | solution.py:620
  55.7 3.0 %collective-permute-done.11.down = f32[32,1152]{1,0:T(8,128)S(1)} collective-permute-done((f32[32,1152]{1,0:T(8,128)S(1)}, f32[32,1152]{1,0:T(8,128)S(1)}, u32[]{:S(2)}, u32[]{:S(2)}) %collective-permute-start.11) | collective-permute-done | bytes 147488 | tf_op jit(solution)/shard_map/ppermute | solution.py:620
  59.7 1.9 %collective-permute-start.13 = (f32[256,128]{1,0:T(8,128)S(1)}, f32[256,128]{1,0:T(8,128)S(1)}, u32[]{:S(2)}, u32[]{:S(2)}) collective-permute-start(f32[256,128]{1,0:T(8,128)S(1)} %get-tuple-element.60), channel_id=1, source_target_pairs={{1,2},{3,4},{5,6},{2,1},{4,3},{6,5},{9,10},{11,12},{13,14},{10,9},... | collective-permute-start | bytes 393224 | tf_op jit(solution)/shard_map/ppermute | solution.py:620
  61.6 3.0 %middle.1 = (f32[2,512,512]{2,1,0:T(8,128)S(1)}, f32[2,512,512]{2,1,0:T(8,128)}, f32[2,512,512]{2,1,0:T(8,128)}) custom-call(f32[2,512,512]{2,1,0:T(8,128)} %objects.3, f32[2,128,128]{2,1,0:T(8,128)S(1)} %copy-done, f32[2,584,768]{2,1,0:T(8,128)S(1)} %shard_map.110.after.acc), custom_call_target="tpu_custom_call" | custom-call | tf_op jit(solution)/shard_map/middle/pallas_call | solution.py:712
  64.6 1.3 %collective-permute-done.13.right = f32[256,128]{1,0:T(8,128)S(1)} collective-permute-done((f32[256,128]{1,0:T(8,128)S(1)}, f32[256,128]{1,0:T(8,128)S(1)}, u32[]{:S(2)}, u32[]{:S(2)}) %collective-permute-start.13) | collective-permute-done | bytes 131104 | tf_op jit(solution)/shard_map/ppermute | solution.py:620
  65.9 1.8 %finish.1 = (f32[2,512,512]{2,1,0:T(8,128)}, f32[2,512,512]{2,1,0:T(8,128)}) custom-call(f32[2,128,128]{2,1,0:T(8,128)S(1)} %copy-done, f32[32,1152]{1,0:T(8,128)S(1)} %collective-permute-done.10.up, f32[32,1152]{1,0:T(8,128)S(1)} %collective-permute-done.11.down, ...), custom_call_target="tpu_custom_call", output_to_operand_aliasing={{0}: (7, {}), {1}: (8, {})} | custom-call | tf_op jit(solution)/shard_map/finish/pallas_call | solution.py:721
  (19 shorter events, 2.5 us)
Async XLA Ops:
  1.6 9.4 %collective-permute-start.1 = (f32[32,1024]{1,0:T(8,128)S(1)}, f32[32,1024]{1,0:T(8,128)S(1)}, u32[]{:S(2)}, u32[]{:S(2)}) collective-permute-start(f32[32,1024]{1,0:T(8,128)S(1)} %get-tuple-element.68), channel_id=1, source_target_pairs={{8,16},{16,8},{9,17},{17,9},{10,18},{18,10},{11,19},{19,11},{12,20... | collective-permute-start | bytes 393224 | tf_op jit(solution)/shard_map/ppermute | solution.py:620
  4.8 6.3 %collective-permute-start = (f32[32,1024]{1,0:T(8,128)S(1)}, f32[32,1024]{1,0:T(8,128)S(1)}, u32[]{:S(2)}, u32[]{:S(2)}) collective-permute-start(f32[32,1024]{1,0:T(8,128)S(1)} %get-tuple-element.69), channel_id=1, source_target_pairs={{0,8},{16,24},{8,0},{24,16},{1,9},{17,25},{9,1},{25,17},{2,10},{18... | collective-permute-start | bytes 393224 | tf_op jit(solution)/shard_map/ppermute | solution.py:620
  11.5 7.3 %collective-permute-start.2 = (f32[288,128]{1,0:T(8,128)S(1)}, f32[288,128]{1,0:T(8,128)S(1)}, u32[]{:S(2)}, u32[]{:S(2)}) collective-permute-start(f32[288,128]{1,0:T(8,128)S(1)} %get-tuple-element.40), channel_id=1, source_target_pairs={{0,1},{2,3},{4,5},{6,7},{1,0},{3,2},{5,4},{7,6},{8,9},{10,11},{12,... | collective-permute-start | bytes 442376 | tf_op jit(solution)/shard_map/ppermute | solution.py:620
  12.5 6.5 %collective-permute-start.3 = (f32[288,128]{1,0:T(8,128)S(1)}, f32[288,128]{1,0:T(8,128)S(1)}, u32[]{:S(2)}, u32[]{:S(2)}) collective-permute-start(f32[288,128]{1,0:T(8,128)S(1)} %get-tuple-element.41), channel_id=1, source_target_pairs={{1,2},{3,4},{5,6},{2,1},{4,3},{6,5},{9,10},{11,12},{13,14},{10,9},... | collective-permute-start | bytes 442376 | tf_op jit(solution)/shard_map/ppermute | solution.py:620
  18.8 12.5 %copy-start = (f32[2,128,128]{2,1,0:T(8,128)S(1)}, f32[2,128,128]{2,1,0:T(8,128)}, u32[]{:S(2)}) copy-start(f32[2,128,128]{2,1,0:T(8,128)} %probe.7) | copy-start | bytes 393220
  22.8 12.1 %collective-permute-start.4 = (f32[64,1152]{1,0:T(8,128)S(1)}, f32[64,1152]{1,0:T(8,128)S(1)}, u32[]{:S(2)}, u32[]{:S(2)}) collective-permute-start(f32[64,1152]{1,0:T(8,128)S(1)} %get-tuple-element.43), channel_id=1, source_target_pairs={{0,8},{16,24},{8,0},{24,16},{1,9},{17,25},{9,1},{25,17},{2,10},{18... | collective-permute-start | bytes 884744 | tf_op jit(solution)/shard_map/ppermute | solution.py:620
  24.5 14.5 %collective-permute-start.5 = (f32[64,1152]{1,0:T(8,128)S(1)}, f32[64,1152]{1,0:T(8,128)S(1)}, u32[]{:S(2)}, u32[]{:S(2)}) collective-permute-start(f32[64,1152]{1,0:T(8,128)S(1)} %get-tuple-element.44), channel_id=1, source_target_pairs={{8,16},{16,8},{9,17},{17,9},{10,18},{18,10},{11,19},{19,11},{12,20... | collective-permute-start | bytes 884744 | tf_op jit(solution)/shard_map/ppermute | solution.py:620
  27.5 14.5 %collective-permute-start.6 = (f32[576,128]{1,0:T(8,128)S(1)}, f32[576,128]{1,0:T(8,128)S(1)}, u32[]{:S(2)}, u32[]{:S(2)}) collective-permute-start(f32[576,128]{1,0:T(8,128)S(1)} %get-tuple-element.45), channel_id=1, source_target_pairs={{0,1},{2,3},{4,5},{6,7},{1,0},{3,2},{5,4},{7,6},{8,9},{10,11},{12,... | collective-permute-start | bytes 884744 | tf_op jit(solution)/shard_map/ppermute | solution.py:620
  28.1 13.9 %collective-permute-start.7 = (f32[576,128]{1,0:T(8,128)S(1)}, f32[576,128]{1,0:T(8,128)S(1)}, u32[]{:S(2)}, u32[]{:S(2)}) collective-permute-start(f32[576,128]{1,0:T(8,128)S(1)} %get-tuple-element.46), channel_id=1, source_target_pairs={{1,2},{3,4},{5,6},{2,1},{4,3},{6,5},{9,10},{11,12},{13,14},{10,9},... | collective-permute-start | bytes 884744 | tf_op jit(solution)/shard_map/ppermute | solution.py:620
  39.3 2.8 %collective-permute-start.8 = (f32[128,128]{1,0:T(8,128)S(1)}, f32[128,128]{1,0:T(8,128)S(1)}, u32[]{:S(2)}, u32[]{:S(2)}) collective-permute-start(f32[128,128]{1,0:T(8,128)S(1)} %get-tuple-element.50), channel_id=1, source_target_pairs={{0,1},{2,3},{4,5},{6,7},{1,0},{3,2},{5,4},{7,6},{8,9},{10,11},{12,... | collective-permute-start | bytes 196616 | tf_op jit(solution)/shard_map/ppermute | solution.py:620
  40.2 5.6 %collective-permute-start.9 = (f32[128,128]{1,0:T(8,128)S(1)}, f32[128,128]{1,0:T(8,128)S(1)}, u32[]{:S(2)}, u32[]{:S(2)}) collective-permute-start(f32[128,128]{1,0:T(8,128)S(1)} %get-tuple-element.51), channel_id=1, source_target_pairs={{1,2},{3,4},{5,6},{2,1},{4,3},{6,5},{9,10},{11,12},{13,14},{10,9},... | collective-permute-start | bytes 196616 | tf_op jit(solution)/shard_map/ppermute | solution.py:620
  50.2 5.5 %collective-permute-start.10 = (f32[32,1152]{1,0:T(8,128)S(1)}, f32[32,1152]{1,0:T(8,128)S(1)}, u32[]{:S(2)}, u32[]{:S(2)}) collective-permute-start(f32[32,1152]{1,0:T(8,128)S(1)} %get-tuple-element.53), channel_id=1, source_target_pairs={{0,8},{16,24},{8,0},{24,16},{1,9},{17,25},{9,1},{25,17},{2,10},{18... | collective-permute-start | bytes 442376 | tf_op jit(solution)/shard_map/ppermute | solution.py:620
  50.2 8.4 %collective-permute-start.11 = (f32[32,1152]{1,0:T(8,128)S(1)}, f32[32,1152]{1,0:T(8,128)S(1)}, u32[]{:S(2)}, u32[]{:S(2)}) collective-permute-start(f32[32,1152]{1,0:T(8,128)S(1)} %get-tuple-element.54), channel_id=1, source_target_pairs={{8,16},{16,8},{9,17},{17,9},{10,18},{18,10},{11,19},{19,11},{12,20... | collective-permute-start | bytes 442376 | tf_op jit(solution)/shard_map/ppermute | solution.py:620
  58.9 5.7 %collective-permute-start.12 = (f32[256,128]{1,0:T(8,128)S(1)}, f32[256,128]{1,0:T(8,128)S(1)}, u32[]{:S(2)}, u32[]{:S(2)}) collective-permute-start(f32[256,128]{1,0:T(8,128)S(1)} %get-tuple-element.59), channel_id=1, source_target_pairs={{0,1},{2,3},{4,5},{6,7},{1,0},{3,2},{5,4},{7,6},{8,9},{10,11},{12,... | collective-permute-start | bytes 393224 | tf_op jit(solution)/shard_map/ppermute | solution.py:620
  59.7 6.3 %collective-permute-start.13 = (f32[256,128]{1,0:T(8,128)S(1)}, f32[256,128]{1,0:T(8,128)S(1)}, u32[]{:S(2)}, u32[]{:S(2)}) collective-permute-start(f32[256,128]{1,0:T(8,128)S(1)} %get-tuple-element.60), channel_id=1, source_target_pairs={{1,2},{3,4},{5,6},{2,1},{4,3},{6,5},{9,10},{11,12},{13,14},{10,9},... | collective-permute-start | bytes 393224 | tf_op jit(solution)/shard_map/ppermute | solution.py:620

commit v6 on v5

--- a/solution.py
+++ b/solution.py
@@ -10,9 +10,10 @@
 
 BORDER = 32
 BAND = 2 * BORDER
+ITERS = 2
 LANES = 128
 SUBLANES = 8
-GROUP = 8
+LARGE, MIDDLE, SMALL = 8, 4, 2
 RIGHT = 4
 
 smoothing = 0.5
@@ -58,9 +59,10 @@
 def right_groups(members, block):
     rows = members[0].shape[0]
     results = []
-    for start in range(0, len(members), RIGHT):
-        product = times_right(jnp.concatenate(members[start : start + RIGHT], axis=0), block[...])
-        results += [product[i * rows : (i + 1) * rows] for i in range(RIGHT)]
+    count = min(RIGHT, len(members))
+    for start in range(0, len(members), count):
+        product = times_right(jnp.concatenate(members[start : start + count], axis=0), block[...])
+        results += [product[i * rows : (i + 1) * rows] for i in range(count)]
     return results
 
 
@@ -88,17 +90,87 @@
     return packed, pltpu.roll(packed, LANES // 2, 1)
 
 
-def list_slots(order, positions, live, low, high, inside):
-    def visit(slot, found):
-        row, col = positions[0, slot], positions[1, slot]
-        within = (row >= low) & (row <= high) & (col >= low) & (col <= high)
-        order[found] = slot
-        return found + jnp.where(within == inside, 1, 0)
-
-    return lax.fori_loop(0, live, visit, 0)
-
-
-def gradient_slots(cur, acc, doubled, amplitudes, positions, order, begin, stop, tables):
+def slot_kinds(row, col, last):
+    row_out, col_out = (row < 0) | (row > last), (col < 0) | (col > last)
+    row_edge = (row < BORDER) | (row > last - BORDER)
+    col_edge = (col < BORDER) | (col > last - BORDER)
+    return row_out, col_out, row_edge, col_edge
+
+
+def is_deep(row_out, col_out, row_edge, col_edge):
+    return jnp.logical_not(row_edge | col_edge)
+
+
+def is_beside(row_out, col_out, row_edge, col_edge):
+    return col_out
+
+
+def is_early(row_out, col_out, row_edge, col_edge):
+    return (row_edge | col_edge) & jnp.logical_not(col_out)
+
+
+def is_reaching(row_out, col_out, row_edge, col_edge):
+    return (row_out | col_out) & jnp.logical_not(row_edge & col_edge)
+
+
+def is_rim(row_out, col_out, row_edge, col_edge):
+    return (row_edge ^ col_edge) & jnp.logical_not(row_out | col_out)
+
+
+def is_reaching_corner(row_out, col_out, row_edge, col_edge):
+    return (row_out | col_out) & row_edge & col_edge
+
+
+def is_rim_corner(row_out, col_out, row_edge, col_edge):
+    return row_edge & col_edge & jnp.logical_not(row_out | col_out)
+
+
+class Slots:
+    def __init__(self, positions, live, order, last):
+        self.positions, self.live, self.order, self.last = positions, live, order, last
+
+    def append(self, kind, begin, skip=0):
+        def visit(slot, carry):
+            found, seen = carry
+            kinds = slot_kinds(self.positions[0, slot], self.positions[1, slot], self.last)
+            of_kind = jnp.where(kind(*kinds), 1, 0)
+            self.order[found] = slot
+            return found + jnp.where(seen >= skip, of_kind, 0), seen + of_kind
+
+        return lax.fori_loop(0, self.live, visit, (begin, 0))[0]
+
+    def lead(self):
+        return jnp.minimum(self.append(is_deep, 0), MIDDLE)
+
+    def side(self):
+        lead = self.lead()
+        early = self.append(is_early, 0)
+        end = self.append(is_deep, early, lead)
+        stop = jnp.minimum(end, round_up(early))
+        return stop, lead + jnp.maximum(stop - early, 0), end
+
+    def band(self):
+        done = self.side()[1]
+        deep = self.append(is_deep, 0)
+        room = 2 * LARGE - (deep - done + LARGE - 1) // LARGE * LARGE
+        return done, deep, jnp.minimum(deep, jnp.maximum(room, 0))
+
+    def corner(self):
+        reaching = self.append(is_reaching, 0)
+        end = self.append(is_rim, reaching)
+        return jnp.minimum(end, round_up(reaching)), end
+
+    def rest(self):
+        deep_done = self.band()[2]
+        begin, end = self.corner()
+        return begin, self.append(is_deep, self.append(is_rim_corner, end), deep_done)
+
+
+def round_up(count):
+    return jnp.maximum((count + LARGE - 1) // LARGE, 1) * LARGE
+
+
+def gradient_slots(cur, acc, doubled, amplitudes, positions, order, begin, stop, tables, size=LARGE):
     right_f, left_f, right_b, left_b = tables
     probe = doubled.shape[1] // 2
     frame = probe + SUBLANES
@@ -107,8 +179,8 @@
 
     def group_body(group, carry):
         places, probes, exits = [], [], []
-        for member in range(GROUP):
-            slot = begin + group * GROUP + member
+        for member in range(size):
+            slot = begin + group * size + member
             at = order[jnp.minimum(slot, stop - 1)]
             row = positions[0, at] + BORDER
             col = positions[1, at] + LANES
@@ -141,7 +213,7 @@
             )
         half = right_groups(exits, right_f)
         shrunk = []
-        for pair in range(0, GROUP, 2):
+        for pair in range(0, size, 2):
             first, second = half[pair], half[pair + 1]
             stacked = jnp.concatenate(
                 [
@@ -158,7 +230,7 @@
                 shrink = amplitudes[at] * lax.rsqrt(real * real + imag * imag + smoothing) - 1.0
                 shrunk.append(jnp.concatenate([real * shrink, imag * shrink], axis=1))
         half = right_groups(shrunk, right_b)
-        for pair in range(0, GROUP, 2):
+        for pair in range(0, size, 2):
             first, second = half[pair], half[pair + 1]
             stacked = jnp.concatenate(
                 [
@@ -197,7 +269,7 @@
                     )
         return carry
 
-    lax.fori_loop(0, (stop - begin + GROUP - 1) // GROUP, group_body, 0)
+    lax.fori_loop(0, (stop - begin + size - 1) // size, group_body, 0)
 
 
 def step_of(probe):
@@ -260,22 +332,27 @@
     for load in loads:
         load.start()
     acc[...] = jnp.zeros_like(acc)
-    found = list_slots(order, positions, counts[0, 0], 0, tile - probe, True)
+    lead = Slots(positions, counts[0, 0], order, tile - probe).lead()
     for load in loads:
         load.wait()
+    gradient_slots(cur, acc, doubled, held, positions, order, 0, lead, tables, MIDDLE)
+
+
+def side_kernel(
+    positions, counts, up, down, doubled, amplitudes, right_f, left_f, right_b, left_b, cur_in, acc_in,
+    cur, acc, order,
+):
+    tile, width = cur.shape[1] - SUBLANES - BAND, cur.shape[2] - 2 * LANES
+    up, down = by_side("row", up[...], down[...])
+    inner = slice(LANES, LANES + width)
+    for plane in range(2):
+        lanes = slice(plane * width, (plane + 1) * width)
+        cur[plane, :BORDER, inner] = up[:, lanes]
+        cur[plane, BORDER + tile : BAND + tile, inner] = down[:, lanes]
+        cur[plane, BAND + tile :, :] = jnp.zeros_like(cur[plane, BAND + tile :, :])
+    slots = Slots(positions, counts[0, 0], order, tile - doubled.shape[2])
     gradient_slots(
-        cur, acc, doubled, held, positions, order, 0, jnp.minimum(found, GROUP), tables
-    )
-
-
-def inner_rest_kernel(
-    positions, counts, cur, doubled, amplitudes, right_f, left_f, right_b, left_b, acc_in,
-    acc, order,
-):
-    tile = cur.shape[1] - SUBLANES - BAND
-    found = list_slots(order, positions, counts[0, 0], 0, tile - doubled.shape[2], True)
-    gradient_slots(
-        cur, acc, doubled, amplitudes, positions, order, jnp.minimum(found, GROUP), found,
+        cur, acc, doubled, amplitudes, positions, order, 0, slots.side()[0],
         (right_f, left_f, right_b, left_b),
     )
 
@@ -321,25 +398,21 @@
 
 
 def outer_kernel(
-    positions, counts, up, down, left, right, doubled, amplitudes,
+    positions, counts, left, right, doubled, amplitudes,
     right_f, left_f, right_b, left_b, cur_in, acc_in,
     cur, acc, to_up, to_down, to_left, to_right, order,
 ):
     extent = 2 * left.shape[0]
-    tile, width = extent - BAND, up.shape[1] // 2
+    tile, width = extent - BAND, cur.shape[2] - 2 * LANES
     lane = lane_iota(extent)
-    up, down = by_side("row", up[...], down[...])
     lefts, rights = map(unfold_side, by_side("col", left[...], right[...]))
     for plane in range(2):
         cur[plane, :extent, :LANES] = jnp.where(lane >= LANES - BORDER, lefts[plane], 0.0)
         cur[plane, :extent, LANES + width :] = jnp.where(lane < BORDER, rights[plane], 0.0)
-        inner = slice(LANES, LANES + width)
-        cur[plane, :BORDER, inner] = up[:, plane * width : (plane + 1) * width]
-        cur[plane, BORDER + tile : extent, inner] = down[:, plane * width : (plane + 1) * width]
-        cur[plane, extent:, :] = jnp.zeros_like(cur[plane, extent:, :])
-    found = list_slots(order, positions, counts[0, 0], 0, tile - doubled.shape[2], False)
+    found = Slots(positions, counts[0, 0], order, tile - doubled.shape[2]).append(is_beside, 0)
     gradient_slots(
-        cur, acc, doubled, amplitudes, positions, order, 0, found, (right_f, left_f, right_b, left_b)
+        cur, acc, doubled, amplitudes, positions, order, 0, found,
+        (right_f, left_f, right_b, left_b), MIDDLE,
     )
     store_bands(acc, 0, tile, BAND, to_up, to_down, to_left, to_right)
 
@@ -387,56 +460,54 @@
     tile, width = cur.shape[1] - SUBLANES - BAND, cur.shape[2] - 2 * LANES
     rate = step_of(probe)
     middle, inner = slice(BORDER, BORDER + tile), slice(LANES, LANES + width)
-    for plane in range(2):
-        cur[plane, middle, inner] += rate * acc[plane, middle, inner]
-    found = list_slots(
-        order, positions, counts[0, 0], BORDER, tile - doubled.shape[2] - BORDER, True
-    )
-    gradient_slots(
-        cur, acc, doubled, amplitudes, positions, order, 0, found, (right_f, left_f, right_b, left_b)
-    )
+    slots = Slots(positions, counts[0, 0], order, tile - doubled.shape[2])
+    done, deep, room = slots.band()
+
+    def turn(iteration, carry):
+        @pl.when(iteration == 1)
+        def update():
+            for plane in range(2):
+                cur[plane, middle, inner] += rate * acc[plane, middle, inner]
+
+        gradient_slots(
+            cur, acc, doubled, amplitudes, positions, order,
+            jnp.where(iteration == 0, done, 0), jnp.where(iteration == 0, deep, room),
+            (right_f, left_f, right_b, left_b),
+        )
+        return carry
+
+    lax.fori_loop(0, ITERS, turn, 0)
+
+
+def grid_gains(row_count, col_count, tile, rate):
+    row_at, col_at = lax.axis_index("row"), lax.axis_index("col")
+    top = jnp.where(row_at > 0, 1.0, 0.0)
+    bottom = jnp.where(row_at < row_count - 1, 1.0, 0.0)
+    before = jnp.where(col_at > 0, 1.0, 0.0)
+    after = jnp.where(col_at < col_count - 1, 1.0, 0.0)
+    row_id = lax.broadcasted_iota(jnp.int32, (tile + BAND, LANES), 0)
+    row_gain = rate * jnp.where(
+        row_id < BORDER, top, jnp.where(row_id >= BORDER + tile, bottom, 1.0)
+    )
+    return row_gain, top, bottom, before, after
 
 
 def second_kernel(
     row_count, col_count,
     positions, counts, probe, doubled, amplitudes, right_f, left_f, right_b, left_b,
-    up, down, left, right, left_corners, right_corners, cur_in, acc_in,
-    cur, acc, to_up, to_down, to_left, to_right, order,
+    up, down, left, right, cur_in, acc_in,
+    cur, acc, order,
 ):
     tile, width = cur.shape[1] - SUBLANES - BAND, cur.shape[2] - 2 * LANES
     extent = tile + BAND
     rate = step_of(probe)
-    row_at, row_last = lax.axis_index("row"), row_count - 1
-    col_at, col_last = lax.axis_index("col"), col_count - 1
-    top = jnp.where(row_at > 0, 1.0, 0.0)
-    bottom = jnp.where(row_at < row_last, 1.0, 0.0)
-    before = jnp.where(col_at > 0, 1.0, 0.0)
-    after = jnp.where(col_at < col_last, 1.0, 0.0)
-    early, _ = list_late_slots(order, positions, counts[0, 0], tile - doubled.shape[2])
+    row_gain, top, bottom, before, after = grid_gains(row_count, col_count, tile, rate)
+    slots = Slots(positions, counts[0, 0], order, tile - doubled.shape[2])
     inner = slice(LANES, LANES + width)
     lane = lane_iota(extent)
     is_low, is_high = lane < BORDER, lane >= LANES - BORDER
-    lefts, rights = (
-        unpack_planes(
-            jnp.concatenate(
-                [
-                    side[:BAND, :] + corners[:BAND, :],
-                    side[BAND:tile, :],
-                    side[tile:, :] + corners[BAND:, :],
-                ],
-                axis=0,
-            )
-        )
-        for side, corners in zip(
-            by_side("col", left[...], right[...]),
-            by_side("col", left_corners[...], right_corners[...]),
-        )
-    )
+    lefts, rights = map(unpack_planes, by_side("col", left[...], right[...]))
     up, down = by_side("row", up[...], down[...])
-    row_id = lax.broadcasted_iota(jnp.int32, (extent, LANES), 0)
-    row_gain = rate * jnp.where(
-        row_id < BORDER, top, jnp.where(row_id >= BORDER + tile, bottom, 1.0)
-    )
     for plane in range(2):
         for row, band, on_grid in ((0, up, top), (tile, down, bottom)):
             halo_first = row == 0
@@ -472,23 +543,49 @@
             )
             acc[plane, :extent, out] = jnp.zeros_like(acc[plane, :extent, out])
     gradient_slots(
-        cur, acc, doubled, amplitudes, positions, order, 0, early, (right_f, left_f, right_b, left_b)
+        cur, acc, doubled, amplitudes, positions, order, 0, slots.corner()[0],
+        (right_f, left_f, right_b, left_b),
+    )
+
+
+def corner_slots_kernel(
+    row_count, col_count,
+    positions, counts, probe, doubled, amplitudes, right_f, left_f, right_b, left_b,
+    left, right, cur_in, acc_in,
+    cur, acc, to_up, to_down, to_left, to_right, order,
+):
+    tile, width = cur.shape[1] - SUBLANES - BAND, cur.shape[2] - 2 * LANES
+    row_gain, _, _, before, after = grid_gains(row_count, col_count, tile, step_of(probe))
+    lane = lane_iota(BAND)
+    is_low, is_high = lane < BORDER, lane >= LANES - BORDER
+    left, right = by_side("col", left[...], right[...])
+    for block, corners, on_grid, own_first in (
+        (0, left, before, False), (width, right, after, True),
+    ):
+        low_block = slice(block, block + LANES)
+        high_block = slice(block + LANES, block + 2 * LANES)
+        own, out = (low_block, high_block) if own_first else (high_block, low_block)
+        keep_own, keep_out = (is_high, is_low) if own_first else (is_low, is_high)
+        both = unpack_planes(corners)
+        for plane in range(2):
+            for row, own_at in ((0, BORDER), (tile, 0)):
+                rows = slice(row, row + BAND)
+                part = both[plane][:BAND] if row == 0 else both[plane][BAND:]
+                own_part = jnp.where(keep_own, part, 0.0)
+                gain = row_gain[rows]
+                cur[plane, rows, own] += gain * own_part
+                cur[plane, rows, out] += (gain * on_grid) * jnp.where(keep_out, part, 0.0)
+                acc[plane, row + own_at : row + own_at + BORDER, own] += own_part[
+                    own_at : own_at + BORDER
+                ]
+    found = Slots(positions, counts[0, 0], order, tile - doubled.shape[2]).append(
+        is_reaching_corner, 0
+    )
+    gradient_slots(
+        cur, acc, doubled, amplitudes, positions, order, 0, found,
+        (right_f, left_f, right_b, left_b), SMALL,
     )
     store_bands(acc, 0, BORDER + tile, BORDER, to_up, to_down, to_left, to_right)
-
-
-def list_late_slots(order, positions, live, last):
-    reaching = list_slots(order, positions, live, 0, last, False)
-
-    def visit(slot, found):
-        row, col = positions[0, slot], positions[1, slot]
-        inner = (row >= 0) & (row <= last) & (col >= 0) & (col <= last)
-        deep = (row >= BORDER) & (row <= last - BORDER) & (col >= BORDER) & (col <= last - BORDER)
-        order[found] = slot
-        return found + jnp.where(inner & jnp.logical_not(deep), 1, 0)
-
-    found = lax.fori_loop(0, live, visit, reaching)
-    return jnp.minimum(found, (reaching + GROUP - 1) // GROUP * GROUP), found
 
 
 def second_rest_kernel(
@@ -496,9 +593,10 @@
     acc, order,
 ):
     tile = cur.shape[1] - SUBLANES - BAND
-    early, found = list_late_slots(order, positions, counts[0, 0], tile - doubled.shape[2])
+    slots = Slots(positions, counts[0, 0], order, tile - doubled.shape[2])
+    begin, end = slots.rest()
     gradient_slots(
-        cur, acc, doubled, amplitudes, positions, order, early, found,
+        cur, acc, doubled, amplitudes, positions, order, begin, end,
         (right_f, left_f, right_b, left_b),
     )
 
@@ -671,13 +769,13 @@
         (f32(extent // 2, LANES),) * 2, (f32(extent, LANES),),
     )
     left, right = swap_pairs("col", to_left, to_right)
-    acc = call(
-        inner_rest_kernel, slots, (cur, doubled, held, *tables, acc),
-        padded, (order,), {9: 0},
+    cur, acc = call(
+        side_kernel, slots, (up, down, doubled, held, *tables, cur, acc),
+        (padded, padded), (order,), {10: 0, 11: 1},
     )
     cur, acc, to_up, to_down, to_left, to_right = call(
-        outer_kernel, slots, (up, down, left, right, doubled, held, *tables, cur, acc),
-        (padded, padded, *row_bands(BAND), *sides), (order,), {12: 0, 13: 1},
+        outer_kernel, slots, (left, right, doubled, held, *tables, cur, acc),
+        (padded, padded, *row_bands(BAND), *sides), (order,), {10: 0, 11: 1},
     )
     up, down = swap_pairs("row", to_up, to_down)
     left, right = swap_pairs("col", to_left, to_right)
@@ -687,14 +785,16 @@
     )
     corners = (f32(2 * BAND, LANES),) * 2
     left_corners, right_corners = swap_pairs("col", *call(corner_kernel, (), (up, down, acc), corners))
+    grid = (lax.axis_size("row"), lax.axis_size("col"))
+    cur, acc = call(
+        functools.partial(second_kernel, *grid), slots,
+        (probe_field, doubled, held, *tables, up, down, left, right, cur, acc),
+        (padded, padded), (order,), {13: 0, 14: 1},
+    )
     cur, acc, to_up, to_down, to_left, to_right = call(
-        functools.partial(second_kernel, lax.axis_size("row"), lax.axis_size("col")),
-        slots,
-        (
-            probe_field, doubled, held, *tables,
-            up, down, left, right, left_corners, right_corners, cur, acc,
-        ),
-        (padded, padded, *row_bands(BORDER), *sides), (order,), {15: 0, 16: 1},
+        functools.partial(corner_slots_kernel, *grid), slots,
+        (probe_field, doubled, held, *tables, left_corners, right_corners, cur, acc),
+        (padded, padded, *row_bands(BORDER), *sides), (order,), {11: 0, 12: 1},
     )
     up, down = swap_pairs("row", to_up, to_down)
     acc = call(

time: 68.3 us -> 69.1 us (1.012)
  the two profiles are of different devices: /device:TPU:19 before, /device:TPU:3 now
where the time goes in v6:
time: 69.1 us; the launch traced here: 68.6 us
  Pallas kernels  38.2 us (55%)
  starting transfers between devices  26.3 us (38%)
  between operations  1.75 us (3%)
  waiting for transfers between devices  1.36 us (2%)
  local copies, waits for them, and re-layouts  0.96 us (1%)
    pallas_call x9, Pallas kernels, call(): pl.pallas_call(kernel, out_shape=outs, in_specs=[SMEM] * len(scalars) + [...  28 us
    ppermute x14, starting transfers between devices, swap(): return in_vmem(lax.ppermute(array, axis, ends + [(j, i) for i, j in ends]))  26.3 us
    pallas_call x1, Pallas kernels, on_device(): pl.pallas_call(inner_start_kernel, out_shape=(padded, padded, doubled_sha...  5.4 us
    pallas_call x1, Pallas kernels, on_device(): pl.pallas_call(middle_kernel, out_shape=(f32(2, tile, width), result, res...  3.01 us
    pallas_call x1, Pallas kernels, on_device(): pl.pallas_call(last_kernel, out_shape=(result, result), in_specs=[VMEM] *...  1.76 us
  transfers between devices with their start and end apart: 14, of which 1 were waited for; matrix products, arithmetic and copies ran while one was open for 0% of the time, Pallas kernels for 46%

profile of v6, /device:TPU:3, one launch (start us, length us, event | category | flops | bytes accessed | tf_op | source)
XLA Modules:
  0.0 68.6 jit_solution(10494871297814281916)
XLA Ops:
  0.6 1.0 %slice_bitcast_fusion.3 = (f32[32,512]{1,0:T(8,128)S(1)}, f32[32,512]{1,0:T(8,128)S(1)}, f32[32,512]{1,0:T(8,128)S(1)}, f32[32,512]{1,0:T(8,128)S(1)}) fusion(f32[2,512,512]{2,1,0:T(8,128)} %objects.3), kind=kLoop, calls=%fused_computation.7 | loop fusion | bytes 524288 | tf_op jit(solution)/shard_map/squeeze | solution.py:753
  1.6 3.1 %collective-permute-start.1 = (f32[32,1024]{1,0:T(8,128)S(1)}, f32[32,1024]{1,0:T(8,128)S(1)}, u32[]{:S(2)}, u32[]{:S(2)}) collective-permute-start(f32[32,1024]{1,0:T(8,128)S(1)} %get-tuple-element.76), channel_id=1, source_target_pairs={{8,16},{16,8},{9,17},{17,9},{10,18},{18,10},{11,19},{19,11},{12,20... | collective-permute-start | bytes 393224 | tf_op jit(solution)/shard_map/ppermute | solution.py:718
  4.8 0.1 collective-permute-start
  5.5 5.4 %inner_start.1 = (f32[2,584,768]{2,1,0:T(8,128)S(1)}, f32[2,584,768]{2,1,0:T(8,128)S(1)}, f32[2,256,128]{2,1,0:T(8,128)S(1)}, f32[24,128,128]{2,1,0:T(8,128)S(1)...) custom-call(s32[2,24]{1,0:T(2,128)} %bitcast.9, ...), custom_call_target="tpu_custom_call" | custom-call | tf_op jit(solution)/shard_map/inner_start/pallas_call | solution.py:758
  10.9 0.4 shard_map.104
  11.3 1.0 %collective-permute-start.2 = (f32[288,128]{1,0:T(8,128)S(1)}, f32[288,128]{1,0:T(8,128)S(1)}, u32[]{:S(2)}, u32[]{:S(2)}) collective-permute-start(f32[288,128]{1,0:T(8,128)S(1)} %get-tuple-element.44), channel_id=1, source_target_pairs={{0,1},{2,3},{4,5},{6,7},{1,0},{3,2},{5,4},{7,6},{8,9},{10,11},{12,... | collective-permute-start | bytes 442376 | tf_op jit(solution)/shard_map/ppermute | solution.py:718
  12.3 3.1 %collective-permute-start.3 = (f32[288,128]{1,0:T(8,128)S(1)}, f32[288,128]{1,0:T(8,128)S(1)}, u32[]{:S(2)}, u32[]{:S(2)}) collective-permute-start(f32[288,128]{1,0:T(8,128)S(1)} %get-tuple-element.45), channel_id=1, source_target_pairs={{1,2},{3,4},{5,6},{2,1},{4,3},{6,5},{9,10},{11,12},{13,14},{10,9},... | collective-permute-start | bytes 442376 | tf_op jit(solution)/shard_map/ppermute | solution.py:718
  15.4 3.8 %shard_map.105 = (f32[2,584,768]{2,1,0:T(8,128)S(1)}, f32[2,584,768]{2,1,0:T(8,128)S(1)}) custom-call(s32[2,24]{1,0:T(2,128)} %bitcast.10, s32[1,1]{1,0:T(1,128)S(6)} %copy.37.counts, f32[32,1024]{1,0:T(8,128)S(1)} %collective-permute-done.up, f32[32,1024]{1,0:T(8,128)S(1)} %collective-permute-done.1.down, ...), custom_call_target="tpu_custom_call", output_to_operand_aliasing={{0}: (10, {}), {1}: (11, {})} | custom-call | tf_op jit(solution)/shard_map/pallas_call | solution.py:741
  19.3 1.6 %shard_map.106 = (f32[2,584,768]{2,1,0:T(8,128)S(1)}, f32[2,584,768]{2,1,0:T(8,128)S(1)}, f32[64,1152]{1,0:T(8,128)S(1)}, f32[64,1152]{1,0:T(8,128)S(1)}, f32[57...) custom-call(s32[2,24]{1,0:T(2,128)} %bitcast.11, ...), custom_call_target="tpu_custom_call", output_to_operand_aliasing={{0}: (10, {}), {1}: (11, {})} | custom-call | tf_op jit(solution)/shard_map/pallas_call | solution.py:741
  20.9 3.2 %collective-permute-start.4 = (f32[64,1152]{1,0:T(8,128)S(1)}, f32[64,1152]{1,0:T(8,128)S(1)}, u32[]{:S(2)}, u32[]{:S(2)}) collective-permute-start(f32[64,1152]{1,0:T(8,128)S(1)} %get-tuple-element.49), channel_id=1, source_target_pairs={{0,8},{16,24},{8,0},{24,16},{1,9},{17,25},{9,1},{25,17},{2,10},{18... | collective-permute-start | bytes 884744 | tf_op jit(solution)/shard_map/ppermute | solution.py:718
  24.1 1.9 %collective-permute-start.5 = (f32[64,1152]{1,0:T(8,128)S(1)}, f32[64,1152]{1,0:T(8,128)S(1)}, u32[]{:S(2)}, u32[]{:S(2)}) collective-permute-start(f32[64,1152]{1,0:T(8,128)S(1)} %get-tuple-element.50), channel_id=1, source_target_pairs={{8,16},{16,8},{9,17},{17,9},{10,18},{18,10},{11,19},{19,11},{12,20... | collective-permute-start | bytes 884744 | tf_op jit(solution)/shard_map/ppermute | solution.py:718
  26.2 4.8 %collective-permute-start.9 = (f32[576,128]{1,0:T(8,128)S(1)}, f32[576,128]{1,0:T(8,128)S(1)}, u32[]{:S(2)}, u32[]{:S(2)}) collective-permute-start(f32[576,128]{1,0:T(8,128)S(1)} %get-tuple-element.57), channel_id=1, source_target_pairs={{1,2},{3,4},{5,6},{2,1},{4,3},{6,5},{9,10},{11,12},{13,14},{10,9},... | collective-permute-start | bytes 884744 | tf_op jit(solution)/shard_map/ppermute | solution.py:718
  31.0 6.8 %shard_map.107 = (f32[2,584,768]{2,1,0:T(8,128)S(1)}, f32[2,584,768]{2,1,0:T(8,128)S(1)}) custom-call(s32[2,24]{1,0:T(2,128)} %bitcast.12, s32[1,1]{1,0:T(1,128)S(6)} %copy.37.counts, f32[2,128,128]{2,1,0:T(8,128)S(1)} %copy-done, f32[2,256,128]{2,1,0:T(8,128)S(1)} %get-tuple-element.37.doubled, ...), custom_call_target="tpu_custom_call", output_to_operand_aliasing={{0}: (9, {}), {1}: (10, {})} | custom-call | tf_op jit(solution)/shard_map/pallas_call | solution.py:741
  37.8 0.2 shard_map.108
  38.0 5.0 %collective-permute-start.7 = (f32[128,128]{1,0:T(8,128)S(1)}, f32[128,128]{1,0:T(8,128)S(1)}, u32[]{:S(2)}, u32[]{:S(2)}) collective-permute-start(f32[128,128]{1,0:T(8,128)S(1)} %get-tuple-element.55), channel_id=1, source_target_pairs={{1,2},{3,4},{5,6},{2,1},{4,3},{6,5},{9,10},{11,12},{13,14},{10,9},... | collective-permute-start | bytes 196616 | tf_op jit(solution)/shard_map/ppermute | solution.py:718
  43.0 4.6 %shard_map.109 = (f32[2,584,768]{2,1,0:T(8,128)S(1)}, f32[2,584,768]{2,1,0:T(8,128)S(1)}) custom-call(s32[2,24]{1,0:T(2,128)} %bitcast.13, s32[1,1]{1,0:T(1,128)S(6)} %copy.37.counts, f32[2,128,128]{2,1,0:T(8,128)S(1)} %copy-done, f32[2,256,128]{2,1,0:T(8,128)S(1)} %get-tuple-element.37.doubled, ...), custom_call_target="tpu_custom_call", output_to_operand_aliasing={{0}: (13, {}), {1}: (14, {})} | custom-call | tf_op jit(solution)/shard_map/pallas_call | solution.py:741
  47.6 2.9 %shard_map.110 = (f32[2,584,768]{2,1,0:T(8,128)S(1)}, f32[2,584,768]{2,1,0:T(8,128)S(1)}, f32[32,1152]{1,0:T(8,128)S(1)}, f32[32,1152]{1,0:T(8,128)S(1)}, f32[57...) custom-call(s32[2,24]{1,0:T(2,128)} %bitcast.14, ...), custom_call_target="tpu_custom_call", output_to_operand_aliasing={{0}: (11, {}), {1}: (12, {})} | custom-call | tf_op jit(solution)/shard_map/pallas_call | solution.py:741
  50.6 1.9 %collective-permute-start.11 = (f32[32,1152]{1,0:T(8,128)S(1)}, f32[32,1152]{1,0:T(8,128)S(1)}, u32[]{:S(2)}, u32[]{:S(2)}) collective-permute-start(f32[32,1152]{1,0:T(8,128)S(1)} %get-tuple-element.62), channel_id=1, source_target_pairs={{8,16},{16,8},{9,17},{17,9},{10,18},{18,10},{11,19},{19,11},{12,20... | collective-permute-start | bytes 442376 | tf_op jit(solution)/shard_map/ppermute | solution.py:718
  52.6 7.5 %shard_map.111.after.acc = f32[2,584,768]{2,1,0:T(8,128)S(1)} custom-call(s32[2,24]{1,0:T(2,128)} %bitcast.15, s32[1,1]{1,0:T(1,128)S(6)} %copy.37.counts, f32[2,584,768]{2,1,0:T(8,128)S(1)} %get-tuple-element.65.cur, f32[2,256,128]{2,1,0:T(8,128)S(1)} %get-tuple-element.37.doubled, ...), custom_call_target="tpu_custom_call", output_to_operand_aliasing={{}: (9, {})} | custom-call | tf_op jit(solution)/shard_map/pallas_call | solution.py:741
  60.1 0.2 shard_map.112
  60.4 1.9 %collective-permute-start.13 = (f32[256,128]{1,0:T(8,128)S(1)}, f32[256,128]{1,0:T(8,128)S(1)}, u32[]{:S(2)}, u32[]{:S(2)}) collective-permute-start(f32[256,128]{1,0:T(8,128)S(1)} %get-tuple-element.68), channel_id=1, source_target_pairs={{1,2},{3,4},{5,6},{2,1},{4,3},{6,5},{9,10},{11,12},{13,14},{10,9},... | collective-permute-start | bytes 393224 | tf_op jit(solution)/shard_map/ppermute | solution.py:718
  62.4 3.0 %middle.1 = (f32[2,512,512]{2,1,0:T(8,128)S(1)}, f32[2,512,512]{2,1,0:T(8,128)}, f32[2,512,512]{2,1,0:T(8,128)}) custom-call(f32[2,512,512]{2,1,0:T(8,128)} %objects.3, f32[2,128,128]{2,1,0:T(8,128)S(1)} %copy-done, f32[2,584,768]{2,1,0:T(8,128)S(1)} %shard_map.111.after.acc), custom_call_target="tpu_custom_call" | custom-call | tf_op jit(solution)/shard_map/middle/pallas_call | solution.py:812
  65.4 1.3 %collective-permute-done.13.right = f32[256,128]{1,0:T(8,128)S(1)} collective-permute-done((f32[256,128]{1,0:T(8,128)S(1)}, f32[256,128]{1,0:T(8,128)S(1)}, u32[]{:S(2)}, u32[]{:S(2)}) %collective-permute-start.13) | collective-permute-done | bytes 131104 | tf_op jit(solution)/shard_map/ppermute | solution.py:718
  66.7 1.8 %finish.1 = (f32[2,512,512]{2,1,0:T(8,128)}, f32[2,512,512]{2,1,0:T(8,128)}) custom-call(f32[2,128,128]{2,1,0:T(8,128)S(1)} %copy-done, f32[32,1152]{1,0:T(8,128)S(1)} %collective-permute-done.10.up, f32[32,1152]{1,0:T(8,128)S(1)} %collective-permute-done.11.down, ...), custom_call_target="tpu_custom_call", output_to_operand_aliasing={{0}: (7, {}), {1}: (8, {})} | custom-call | tf_op jit(solution)/shard_map/finish/pallas_call | solution.py:821
  (20 shorter events, 0.3 us)
Async XLA Ops:
  1.6 9.3 %collective-permute-start.1 = (f32[32,1024]{1,0:T(8,128)S(1)}, f32[32,1024]{1,0:T(8,128)S(1)}, u32[]{:S(2)}, u32[]{:S(2)}) collective-permute-start(f32[32,1024]{1,0:T(8,128)S(1)} %get-tuple-element.76), channel_id=1, source_target_pairs={{8,16},{16,8},{9,17},{17,9},{10,18},{18,10},{11,19},{19,11},{12,20... | collective-permute-start | bytes 393224 | tf_op jit(solution)/shard_map/ppermute | solution.py:718
  4.8 6.1 %collective-permute-start = (f32[32,1024]{1,0:T(8,128)S(1)}, f32[32,1024]{1,0:T(8,128)S(1)}, u32[]{:S(2)}, u32[]{:S(2)}) collective-permute-start(f32[32,1024]{1,0:T(8,128)S(1)} %get-tuple-element.77), channel_id=1, source_target_pairs={{0,8},{16,24},{8,0},{24,16},{1,9},{17,25},{9,1},{25,17},{2,10},{18... | collective-permute-start | bytes 393224 | tf_op jit(solution)/shard_map/ppermute | solution.py:718
  11.3 8.0 %collective-permute-start.2 = (f32[288,128]{1,0:T(8,128)S(1)}, f32[288,128]{1,0:T(8,128)S(1)}, u32[]{:S(2)}, u32[]{:S(2)}) collective-permute-start(f32[288,128]{1,0:T(8,128)S(1)} %get-tuple-element.44), channel_id=1, source_target_pairs={{0,1},{2,3},{4,5},{6,7},{1,0},{3,2},{5,4},{7,6},{8,9},{10,11},{12,... | collective-permute-start | bytes 442376 | tf_op jit(solution)/shard_map/ppermute | solution.py:718
  12.3 7.0 %collective-permute-start.3 = (f32[288,128]{1,0:T(8,128)S(1)}, f32[288,128]{1,0:T(8,128)S(1)}, u32[]{:S(2)}, u32[]{:S(2)}) collective-permute-start(f32[288,128]{1,0:T(8,128)S(1)} %get-tuple-element.45), channel_id=1, source_target_pairs={{1,2},{3,4},{5,6},{2,1},{4,3},{6,5},{9,10},{11,12},{13,14},{10,9},... | collective-permute-start | bytes 442376 | tf_op jit(solution)/shard_map/ppermute | solution.py:718
  19.3 11.7 %copy-start = (f32[2,128,128]{2,1,0:T(8,128)S(1)}, f32[2,128,128]{2,1,0:T(8,128)}, u32[]{:S(2)}) copy-start(f32[2,128,128]{2,1,0:T(8,128)} %probe.9) | copy-start | bytes 393220
  20.9 16.8 %collective-permute-start.4 = (f32[64,1152]{1,0:T(8,128)S(1)}, f32[64,1152]{1,0:T(8,128)S(1)}, u32[]{:S(2)}, u32[]{:S(2)}) collective-permute-start(f32[64,1152]{1,0:T(8,128)S(1)} %get-tuple-element.49), channel_id=1, source_target_pairs={{0,8},{16,24},{8,0},{24,16},{1,9},{17,25},{9,1},{25,17},{2,10},{18... | collective-permute-start | bytes 884744 | tf_op jit(solution)/shard_map/ppermute | solution.py:718
  24.1 13.6 %collective-permute-start.5 = (f32[64,1152]{1,0:T(8,128)S(1)}, f32[64,1152]{1,0:T(8,128)S(1)}, u32[]{:S(2)}, u32[]{:S(2)}) collective-permute-start(f32[64,1152]{1,0:T(8,128)S(1)} %get-tuple-element.50), channel_id=1, source_target_pairs={{8,16},{16,8},{9,17},{17,9},{10,18},{18,10},{11,19},{19,11},{12,20... | collective-permute-start | bytes 884744 | tf_op jit(solution)/shard_map/ppermute | solution.py:718
  26.1 17.0 %collective-permute-start.8 = (f32[576,128]{1,0:T(8,128)S(1)}, f32[576,128]{1,0:T(8,128)S(1)}, u32[]{:S(2)}, u32[]{:S(2)}) collective-permute-start(f32[576,128]{1,0:T(8,128)S(1)} %get-tuple-element.56), channel_id=1, source_target_pairs={{0,1},{2,3},{4,5},{6,7},{1,0},{3,2},{5,4},{7,6},{8,9},{10,11},{12,... | collective-permute-start | bytes 884744 | tf_op jit(solution)/shard_map/ppermute | solution.py:718
  26.2 16.9 %collective-permute-start.9 = (f32[576,128]{1,0:T(8,128)S(1)}, f32[576,128]{1,0:T(8,128)S(1)}, u32[]{:S(2)}, u32[]{:S(2)}) collective-permute-start(f32[576,128]{1,0:T(8,128)S(1)} %get-tuple-element.57), channel_id=1, source_target_pairs={{1,2},{3,4},{5,6},{2,1},{4,3},{6,5},{9,10},{11,12},{13,14},{10,9},... | collective-permute-start | bytes 884744 | tf_op jit(solution)/shard_map/ppermute | solution.py:718
  38.0 9.7 %collective-permute-start.6 = (f32[128,128]{1,0:T(8,128)S(1)}, f32[128,128]{1,0:T(8,128)S(1)}, u32[]{:S(2)}, u32[]{:S(2)}) collective-permute-start(f32[128,128]{1,0:T(8,128)S(1)} %get-tuple-element.54), channel_id=1, source_target_pairs={{0,1},{2,3},{4,5},{6,7},{1,0},{3,2},{5,4},{7,6},{8,9},{10,11},{12,... | collective-permute-start | bytes 196616 | tf_op jit(solution)/shard_map/ppermute | solution.py:718
  38.0 9.6 %collective-permute-start.7 = (f32[128,128]{1,0:T(8,128)S(1)}, f32[128,128]{1,0:T(8,128)S(1)}, u32[]{:S(2)}, u32[]{:S(2)}) collective-permute-start(f32[128,128]{1,0:T(8,128)S(1)} %get-tuple-element.55), channel_id=1, source_target_pairs={{1,2},{3,4},{5,6},{2,1},{4,3},{6,5},{9,10},{11,12},{13,14},{10,9},... | collective-permute-start | bytes 196616 | tf_op jit(solution)/shard_map/ppermute | solution.py:718
  50.6 9.5 %collective-permute-start.10 = (f32[32,1152]{1,0:T(8,128)S(1)}, f32[32,1152]{1,0:T(8,128)S(1)}, u32[]{:S(2)}, u32[]{:S(2)}) collective-permute-start(f32[32,1152]{1,0:T(8,128)S(1)} %get-tuple-element.61), channel_id=1, source_target_pairs={{0,8},{16,24},{8,0},{24,16},{1,9},{17,25},{9,1},{25,17},{2,10},{18... | collective-permute-start | bytes 442376 | tf_op jit(solution)/shard_map/ppermute | solution.py:718
  50.6 9.5 %collective-permute-start.11 = (f32[32,1152]{1,0:T(8,128)S(1)}, f32[32,1152]{1,0:T(8,128)S(1)}, u32[]{:S(2)}, u32[]{:S(2)}) collective-permute-start(f32[32,1152]{1,0:T(8,128)S(1)} %get-tuple-element.62), channel_id=1, source_target_pairs={{8,16},{16,8},{9,17},{17,9},{10,18},{18,10},{11,19},{19,11},{12,20... | collective-permute-start | bytes 442376 | tf_op jit(solution)/shard_map/ppermute | solution.py:718
  60.4 5.0 %collective-permute-start.12 = (f32[256,128]{1,0:T(8,128)S(1)}, f32[256,128]{1,0:T(8,128)S(1)}, u32[]{:S(2)}, u32[]{:S(2)}) collective-permute-start(f32[256,128]{1,0:T(8,128)S(1)} %get-tuple-element.67), channel_id=1, source_target_pairs={{0,1},{2,3},{4,5},{6,7},{1,0},{3,2},{5,4},{7,6},{8,9},{10,11},{12,... | collective-permute-start | bytes 393224 | tf_op jit(solution)/shard_map/ppermute | solution.py:718
  60.4 6.3 %collective-permute-start.13 = (f32[256,128]{1,0:T(8,128)S(1)}, f32[256,128]{1,0:T(8,128)S(1)}, u32[]{:S(2)}, u32[]{:S(2)}) collective-permute-start(f32[256,128]{1,0:T(8,128)S(1)} %get-tuple-element.68), channel_id=1, source_target_pairs={{1,2},{3,4},{5,6},{2,1},{4,3},{6,5},{9,10},{11,12},{13,14},{10,9},... | collective-permute-start | bytes 393224 | tf_op jit(solution)/shard_map/ppermute | solution.py:718

commit v7 on v6

--- a/solution.py
+++ b/solution.py
@@ -32,12 +32,8 @@
     real, imag = np.cos(angles) / np.sqrt(length), -np.sin(angles) / np.sqrt(length)
     blocks = []
     for sign in (1.0, -1.0):
-        right = np.block([[real, sign * imag], [-sign * imag, real]])
-        high, low = split_host(right)
-        blocks.append(np.concatenate([high, high, low], axis=0))
-        left = np.block([[real, -sign * imag], [sign * imag, real]])
-        high, low = split_host(left)
-        blocks.append(np.concatenate([high, low], axis=0))
+        block = np.block([[real, sign * imag], [-sign * imag, real]])
+        blocks.append(np.concatenate(split_host(block), axis=0))
     return blocks
 
 
@@ -53,7 +49,9 @@
 
 def times_right(rows, block):
     high, low = split(rows)
-    return dot(jnp.concatenate([high, low, high], axis=1), block)
+    count = block.shape[0] // 2
+    stacked = jnp.concatenate([block[:count], block], axis=0)
+    return dot(jnp.concatenate([high, low, high], axis=1), stacked)
 
 
 def right_groups(members, block):
@@ -125,53 +123,61 @@
     return row_edge & col_edge & jnp.logical_not(row_out | col_out)
 
 
-class Slots:
-    def __init__(self, positions, live, order, last):
-        self.positions, self.live, self.order, self.last = positions, live, order, last
-
-    def append(self, kind, begin, skip=0):
-        def visit(slot, carry):
-            found, seen = carry
-            kinds = slot_kinds(self.positions[0, slot], self.positions[1, slot], self.last)
-            of_kind = jnp.where(kind(*kinds), 1, 0)
-            self.order[found] = slot
-            return found + jnp.where(seen >= skip, of_kind, 0), seen + of_kind
-
-        return lax.fori_loop(0, self.live, visit, (begin, 0))[0]
-
-    def lead(self):
-        return jnp.minimum(self.append(is_deep, 0), MIDDLE)
-
-    def side(self):
-        lead = self.lead()
-        early = self.append(is_early, 0)
-        end = self.append(is_deep, early, lead)
-        stop = jnp.minimum(end, round_up(early))
-        return stop, lead + jnp.maximum(stop - early, 0), end
-
-    def band(self):
-        done = self.side()[1]
-        deep = self.append(is_deep, 0)
+class Plan:
+    DEEP, SIDE, BESIDE, SECOND, CORNER, ROW, COL, NUMBER = range(8)
+    LEAD, SIDE_STOP, BAND_BEGIN, BAND_END, SECOND_DEEP, BESIDE_END, SECOND_STOP, REST_END, CORNER_END = range(9)
+
+    @staticmethod
+    def shape(slot_total):
+        return 8, max(slot_total + 1, 9)
+
+    @staticmethod
+    def fill(plan, positions, live, last):
+        def append(row, kind, begin, skip=0):
+            def visit(slot, carry):
+                found, seen = carry
+                kinds = slot_kinds(positions[0, slot], positions[1, slot], last)
+                of_kind = jnp.where(kind(*kinds), 1, 0)
+                plan[row, found] = slot
+                return found + jnp.where(seen >= skip, of_kind, 0), seen + of_kind
+
+            return lax.fori_loop(0, live, visit, (begin, 0))[0]
+
+        def place(slot, carry):
+            plan[Plan.ROW, slot] = positions[0, slot]
+            plan[Plan.COL, slot] = positions[1, slot]
+            return carry
+
+        lax.fori_loop(0, live, place, 0)
+        deep = append(Plan.DEEP, is_deep, 0)
+        lead = jnp.minimum(deep, MIDDLE)
+        early = append(Plan.SIDE, is_early, 0)
+        side_end = append(Plan.SIDE, is_deep, early, lead)
+        side_stop = jnp.minimum(side_end, round_up(early))
+        done = lead + side_stop - early
         room = 2 * LARGE - (deep - done + LARGE - 1) // LARGE * LARGE
-        return done, deep, jnp.minimum(deep, jnp.maximum(room, 0))
-
-    def corner(self):
-        reaching = self.append(is_reaching, 0)
-        end = self.append(is_rim, reaching)
-        return jnp.minimum(end, round_up(reaching)), end
-
-    def rest(self):
-        deep_done = self.band()[2]
-        begin, end = self.corner()
-        return begin, self.append(is_deep, self.append(is_rim_corner, end), deep_done)
+        second_deep = jnp.minimum(deep, jnp.maximum(room, 0))
+        reaching = append(Plan.SECOND, is_reaching, 0)
+        rim = append(Plan.SECOND, is_rim, reaching)
+        rim_corner = append(Plan.SECOND, is_rim_corner, rim)
+        numbers = (
+            lead, side_stop, done, deep, second_deep,
+            append(Plan.BESIDE, is_beside, 0),
+            jnp.minimum(rim, round_up(reaching)),
+            append(Plan.SECOND, is_deep, rim_corner, second_deep),
+            append(Plan.CORNER, is_reaching_corner, 0),
+        )
+        for index, number in enumerate(numbers):
+            plan[Plan.NUMBER, index] = number
 
 
 def round_up(count):
     return jnp.maximum((count + LARGE - 1) // LARGE, 1) * LARGE
 
 
-def gradient_slots(cur, acc, doubled, amplitudes, positions, order, begin, stop, tables, size=LARGE):
-    right_f, left_f, right_b, left_b = tables
+def gradient_slots(cur, acc, doubled, amplitudes, plan, listed, begin, stop, tables, size=LARGE, before_use=None):
+    right_f, right_b = tables
+    left_f, left_b = right_b, right_f
     probe = doubled.shape[1] // 2
     frame = probe + SUBLANES
     lane = lane_iota(frame)
@@ -181,9 +187,9 @@
         places, probes, exits = [], [], []
         for member in range(size):
             slot = begin + group * size + member
-            at = order[jnp.minimum(slot, stop - 1)]
-            row = positions[0, at] + BORDER
-            col = positions[1, at] + LANES
+            at = plan[listed, jnp.minimum(slot, stop - 1)]
+            row = plan[Plan.ROW, at] + BORDER
+            col = plan[Plan.COL, at] + LANES
             row_at = pl.multiple_of(row // SUBLANES * SUBLANES, SUBLANES)
             col_at = pl.multiple_of(col // LANES * LANES, LANES)
             row_off, col_off = row - row_at, col - col_at
@@ -223,6 +229,8 @@
                 axis=0,
             )
             wave = times_left(left_f[...], stacked)
+            if before_use is not None and pair == 0:
+                before_use()
             for member in range(2):
                 at = places[pair + member][0]
                 real = wave[:probe, member * probe : (member + 1) * probe]
@@ -311,11 +319,11 @@
 ):
     table_count = (len(refs) - 6) // 2
     tables_in, refs = refs[:table_count], refs[table_count:]
-    cur, acc, doubled, held = refs[:4]
-    tables, (order, sems) = refs[4:-2], refs[-2:]
+    cur, acc, doubled, held, plan = refs[:5]
+    tables, sems = refs[5:-1], refs[-1]
     tile, width = objects.shape[1:]
     probe = probe_in.shape[1]
-    sources = [(amplitudes, held)] + list(zip(tables_in, tables))
+    sources = list(zip(tables_in, tables))
     for plane in range(2):
         sources.append(
             (
@@ -325,6 +333,7 @@
         )
         for row in (0, probe):
             sources.append((probe_in.at[plane], doubled.at[plane, pl.ds(row, probe), :]))
+    sources.append((amplitudes, held))
     loads = [
         pltpu.make_async_copy(source, target, sems.at[i])
         for i, (source, target) in enumerate(sources)
@@ -332,15 +341,22 @@
     for load in loads:
         load.start()
     acc[...] = jnp.zeros_like(acc)
-    lead = Slots(positions, counts[0, 0], order, tile - probe).lead()
-    for load in loads:
+    Plan.fill(plan, positions, counts[0, 0], tile - probe)
+    lead = plan[Plan.NUMBER, Plan.LEAD]
+    for load in loads[:-1]:
         load.wait()
-    gradient_slots(cur, acc, doubled, held, positions, order, 0, lead, tables, MIDDLE)
+    gradient_slots(
+        cur, acc, doubled, held, plan, Plan.DEEP, 0, lead, tables, MIDDLE, loads[-1].wait
+    )
+
+    @pl.when(lead == 0)
+    def unused():
+        loads[-1].wait()
 
 
 def side_kernel(
-    positions, counts, up, down, doubled, amplitudes, right_f, left_f, right_b, left_b, cur_in, acc_in,
-    cur, acc, order,
+    plan, up, down, doubled, amplitudes, forth, back, cur_in, acc_in,
+    cur, acc,
 ):
     tile, width = cur.shape[1] - SUBLANES - BAND, cur.shape[2] - 2 * LANES
     up, down = by_side("row", up[...], down[...])
@@ -350,10 +366,9 @@
         cur[plane, :BORDER, inner] = up[:, lanes]
         cur[plane, BORDER + tile : BAND + tile, inner] = down[:, lanes]
         cur[plane, BAND + tile :, :] = jnp.zeros_like(cur[plane, BAND + tile :, :])
-    slots = Slots(positions, counts[0, 0], order, tile - doubled.shape[2])
     gradient_slots(
-        cur, acc, doubled, amplitudes, positions, order, 0, slots.side()[0],
-        (right_f, left_f, right_b, left_b),
+        cur, acc, doubled, amplitudes, plan, Plan.SIDE, 0, plan[Plan.NUMBER, Plan.SIDE_STOP],
+        (forth, back),
     )
 
 
@@ -398,9 +413,9 @@
 
 
 def outer_kernel(
-    positions, counts, left, right, doubled, amplitudes,
-    right_f, left_f, right_b, left_b, cur_in, acc_in,
-    cur, acc, to_up, to_down, to_left, to_right, order,
+    plan, left, right, doubled, amplitudes,
+    forth, back, cur_in, acc_in,
+    cur, acc, to_up, to_down, to_left, to_right,
 ):
     extent = 2 * left.shape[0]
     tile, width = extent - BAND, cur.shape[2] - 2 * LANES
@@ -409,10 +424,9 @@
     for plane in range(2):
         cur[plane, :extent, :LANES] = jnp.where(lane >= LANES - BORDER, lefts[plane], 0.0)
         cur[plane, :extent, LANES + width :] = jnp.where(lane < BORDER, rights[plane], 0.0)
-    found = Slots(positions, counts[0, 0], order, tile - doubled.shape[2]).append(is_beside, 0)
     gradient_slots(
-        cur, acc, doubled, amplitudes, positions, order, 0, found,
-        (right_f, left_f, right_b, left_b), MIDDLE,
+        cur, acc, doubled, amplitudes, plan, Plan.BESIDE, 0, plan[Plan.NUMBER, Plan.BESIDE_END],
+        (forth, back), MIDDLE,
     )
     store_bands(acc, 0, tile, BAND, to_up, to_down, to_left, to_right)
 
@@ -430,6 +444,7 @@
 
 
 def corner_kernel(up, down, after, to_left, to_right):
+    count = up.shape[0]
     width = (up.shape[1] - LANES) // 2
     up, down = by_side("row", up[...], down[...])
     tops, bottoms = corner_parts(up, width), corner_parts(down, width)
@@ -454,14 +469,16 @@
 
 
 def deep_kernel(
-    positions, counts, probe, doubled, amplitudes, right_f, left_f, right_b, left_b, cur_in, acc_in,
-    cur, acc, order,
+    plan, objects, probe, doubled, amplitudes, forth, back, cur_in, acc_in,
+    cur, acc, tile_held, sem,
 ):
+    load = pltpu.make_async_copy(objects, tile_held, sem)
+    load.start()
     tile, width = cur.shape[1] - SUBLANES - BAND, cur.shape[2] - 2 * LANES
     rate = step_of(probe)
     middle, inner = slice(BORDER, BORDER + tile), slice(LANES, LANES + width)
-    slots = Slots(positions, counts[0, 0], order, tile - doubled.shape[2])
-    done, deep, room = slots.band()
+    begins = (plan[Plan.NUMBER, Plan.BAND_BEGIN], 0)
+    ends = (plan[Plan.NUMBER, Plan.BAND_END], plan[Plan.NUMBER, Plan.SECOND_DEEP])
 
     def turn(iteration, carry):
         @pl.when(iteration == 1)
@@ -470,13 +487,14 @@
                 cur[plane, middle, inner] += rate * acc[plane, middle, inner]
 
         gradient_slots(
-            cur, acc, doubled, amplitudes, positions, order,
-            jnp.where(iteration == 0, done, 0), jnp.where(iteration == 0, deep, room),
-            (right_f, left_f, right_b, left_b),
+            cur, acc, doubled, amplitudes, plan, Plan.DEEP,
+            jnp.where(iteration == 0, *begins), jnp.where(iteration == 0, *ends),
+            (forth, back),
         )
         return carry
 
     lax.fori_loop(0, ITERS, turn, 0)
+    load.wait()
 
 
 def grid_gains(row_count, col_count, tile, rate):
@@ -494,15 +512,14 @@
 
 def second_kernel(
     row_count, col_count,
-    positions, counts, probe, doubled, amplitudes, right_f, left_f, right_b, left_b,
+    plan, probe, doubled, amplitudes, forth, back,
     up, down, left, right, cur_in, acc_in,
-    cur, acc, order,
+    cur, acc,
 ):
     tile, width = cur.shape[1] - SUBLANES - BAND, cur.shape[2] - 2 * LANES
     extent = tile + BAND
     rate = step_of(probe)
     row_gain, top, bottom, before, after = grid_gains(row_count, col_count, tile, rate)
-    slots = Slots(positions, counts[0, 0], order, tile - doubled.shape[2])
     inner = slice(LANES, LANES + width)
     lane = lane_iota(extent)
     is_low, is_high = lane < BORDER, lane >= LANES - BORDER
@@ -543,16 +560,16 @@
             )
             acc[plane, :extent, out] = jnp.zeros_like(acc[plane, :extent, out])
     gradient_slots(
-        cur, acc, doubled, amplitudes, positions, order, 0, slots.corner()[0],
-        (right_f, left_f, right_b, left_b),
+        cur, acc, doubled, amplitudes, plan, Plan.SECOND, 0, plan[Plan.NUMBER, Plan.SECOND_STOP],
+        (forth, back),
     )
 
 
 def corner_slots_kernel(
     row_count, col_count,
-    positions, counts, probe, doubled, amplitudes, right_f, left_f, right_b, left_b,
+    plan, probe, doubled, amplitudes, forth, back,
     left, right, cur_in, acc_in,
-    cur, acc, to_up, to_down, to_left, to_right, order,
+    cur, acc, to_up, to_down, to_left, to_right,
 ):
     tile, width = cur.shape[1] - SUBLANES - BAND, cur.shape[2] - 2 * LANES
     row_gain, _, _, before, after = grid_gains(row_count, col_count, tile, step_of(probe))
@@ -578,26 +595,21 @@
                 acc[plane, row + own_at : row + own_at + BORDER, own] += own_part[
                     own_at : own_at + BORDER
                 ]
-    found = Slots(positions, counts[0, 0], order, tile - doubled.shape[2]).append(
-        is_reaching_corner, 0
-    )
     gradient_slots(
-        cur, acc, doubled, amplitudes, positions, order, 0, found,
-        (right_f, left_f, right_b, left_b), SMALL,
+        cur, acc, doubled, amplitudes, plan, Plan.CORNER, 0, plan[Plan.NUMBER, Plan.CORNER_END],
+        (forth, back), SMALL,
     )
     store_bands(acc, 0, BORDER + tile, BORDER, to_up, to_down, to_left, to_right)
 
 
 def second_rest_kernel(
-    positions, counts, cur, doubled, amplitudes, right_f, left_f, right_b, left_b, acc_in,
-    acc, order,
+    plan, cur, doubled, amplitudes, forth, back, acc_in,
+    acc,
 ):
-    tile = cur.shape[1] - SUBLANES - BAND
-    slots = Slots(positions, counts[0, 0], order, tile - doubled.shape[2])
-    begin, end = slots.rest()
     gradient_slots(
-        cur, acc, doubled, amplitudes, positions, order, begin, end,
-        (right_f, left_f, right_b, left_b),
+        cur, acc, doubled, amplitudes, plan, Plan.SECOND,
+        plan[Plan.NUMBER, Plan.SECOND_STOP], plan[Plan.NUMBER, Plan.REST_END],
+        (forth, back),
     )
 
 
@@ -610,13 +622,10 @@
     to_left[...], to_right[...] = sides
 
 
-def middle_kernel(objects, probe, acc, held, estimate, correction, estimated, corrected, sems):
-    tile, width = objects.shape[1:]
-    load = pltpu.make_async_copy(objects, held, sems.at[0])
-    load.start()
+def middle_kernel(probe, acc, held, estimate, correction, estimated, corrected, sems):
+    tile, width = held.shape[1:]
     rate = step_of(probe)
     rows, lanes = slice(BORDER, tile - BORDER), slice(LANES, width - LANES)
-    load.wait()
     for plane in range(2):
         corrected[plane] = rate * acc[plane, 2 * BORDER : tile, 2 * LANES : width]
         estimated[plane] = held[plane, rows, lanes] + corrected[plane]
@@ -624,7 +633,7 @@
         pltpu.make_async_copy(
             source,
             target.at[:, pl.ds(BORDER, tile - BAND), pl.ds(LANES, width - 2 * LANES)],
-            sems.at[1 + i],
+            sems.at[i],
         )
         for i, (source, target) in enumerate(((corrected, correction), (estimated, estimate)))
     ]
@@ -706,6 +715,10 @@
     return pltpu.with_memory_space_constraint(array, pltpu.HBM)
 
 
+def in_smem(array):
+    return pltpu.with_memory_space_constraint(array, pltpu.SMEM)
+
+
 def in_vmem(array):
     return pltpu.with_memory_space_constraint(array, pltpu.VMEM)
 
@@ -730,7 +743,7 @@
     doubled_shape = f32(2, 2 * probe, probe)
     tables = tuple(jnp.asarray(table) for table in dft_blocks(probe))
     places = positions[0, 0]
-    order = pltpu.SMEM((amplitudes.shape[0] + 1,), jnp.int32)
+    plan_shape = pltpu.SMEM(Plan.shape(amplitudes.shape[0]), jnp.int32)
     sides = (f32(extent, LANES), f32(extent, LANES))
 
     def row_bands(count):
@@ -755,15 +768,18 @@
     ]
     table_shapes = tuple(pltpu.VMEM(table.shape, table.dtype) for table in tables)
     up, down = swap_pairs("row", *by_side("row", *strips))
-    cur, acc, doubled, held, *tables = pl.pallas_call(
+    cur, acc, doubled, held, plan, *tables = pl.pallas_call(
         inner_start_kernel,
-        out_shape=(padded, padded, doubled_shape, f32(*amplitudes.shape), *table_shapes),
+        out_shape=(
+            padded, padded, doubled_shape, f32(*amplitudes.shape), plan_shape, *table_shapes,
+        ),
         in_specs=[SMEM, SMEM] + [HBM] * (3 + len(tables)),
-        out_specs=(VMEM,) * (4 + len(tables)),
-        scratch_shapes=[order, pltpu.SemaphoreType.DMA((7 + len(tables),))],
+        out_specs=(VMEM,) * 4 + (SMEM,) + (VMEM,) * len(tables),
+        scratch_shapes=[pltpu.SemaphoreType.DMA((7 + len(tables),))],
         compiler_params=PARAMS,
         name="inner_start",
     )(*slots, *map(in_hbm, (object_field, probe_field, amplitudes, *tables)))
+    slots = (in_smem(plan),)
     to_left, to_right = call(
         object_pack_kernel, (), (cur, up, down),
         (f32(extent // 2, LANES),) * 2, (f32(extent, LANES),),
@@ -771,35 +787,41 @@
     left, right = swap_pairs("col", to_left, to_right)
     cur, acc = call(
         side_kernel, slots, (up, down, doubled, held, *tables, cur, acc),
-        (padded, padded), (order,), {10: 0, 11: 1},
+        (padded, padded), (), {7: 0, 8: 1},
     )
     cur, acc, to_up, to_down, to_left, to_right = call(
         outer_kernel, slots, (left, right, doubled, held, *tables, cur, acc),
-        (padded, padded, *row_bands(BAND), *sides), (order,), {10: 0, 11: 1},
+        (padded, padded, *row_bands(BAND), *sides), (), {7: 0, 8: 1},
     )
     up, down = swap_pairs("row", to_up, to_down)
     left, right = swap_pairs("col", to_left, to_right)
-    cur, acc = call(
-        deep_kernel, slots, (probe_field, doubled, held, *tables, cur, acc),
-        (padded, padded), (order,), {9: 0, 10: 1},
-    )
+    cur, acc, tile_held = pl.pallas_call(
+        deep_kernel,
+        out_shape=(padded, padded, f32(2, tile, width)),
+        in_specs=[SMEM, HBM] + [VMEM] * 7,
+        out_specs=(VMEM,) * 3,
+        scratch_shapes=[pltpu.SemaphoreType.DMA(())],
+        input_output_aliases={7: 0, 8: 1},
+        compiler_params=PARAMS,
+        name="deep",
+    )(*slots, in_hbm(object_field), probe_field, doubled, held, *tables, cur, acc)
     corners = (f32(2 * BAND, LANES),) * 2
     left_corners, right_corners = swap_pairs("col", *call(corner_kernel, (), (up, down, acc), corners))
     grid = (lax.axis_size("row"), lax.axis_size("col"))
     cur, acc = call(
         functools.partial(second_kernel, *grid), slots,
         (probe_field, doubled, held, *tables, up, down, left, right, cur, acc),
-        (padded, padded), (order,), {13: 0, 14: 1},
+        (padded, padded), (), {10: 0, 11: 1},
     )
     cur, acc, to_up, to_down, to_left, to_right = call(
         functools.partial(corner_slots_kernel, *grid), slots,
         (probe_field, doubled, held, *tables, left_corners, right_corners, cur, acc),
-        (padded, padded, *row_bands(BORDER), *sides), (order,), {11: 0, 12: 1},
+        (padded, padded, *row_bands(BORDER), *sides), (), {8: 0, 9: 1},
     )
     up, down = swap_pairs("row", to_up, to_down)
     acc = call(
         second_rest_kernel, slots, (cur, doubled, held, *tables, acc),
-        padded, (order,), {9: 0},
+        padded, (), {6: 0},
     )
     folded = f32(tile // 2, LANES)
     to_left, to_right = call(
@@ -809,15 +831,15 @@
     left, right = swap_pairs("col", to_left, to_right)
     result = jax.ShapeDtypeStruct((2, tile, width), jnp.float32)
     middle = f32(2, tile - BAND, width - 2 * LANES)
-    tile_held, estimate, correction = pl.pallas_call(
+    estimate, correction = pl.pallas_call(
         middle_kernel,
-        out_shape=(f32(2, tile, width), result, result),
-        in_specs=[HBM, VMEM, VMEM],
-        out_specs=(VMEM, HBM, HBM),
-        scratch_shapes=[middle, middle, pltpu.SemaphoreType.DMA((3,))],
+        out_shape=(result, result),
+        in_specs=[VMEM] * 3,
+        out_specs=(HBM, HBM),
+        scratch_shapes=[middle, middle, pltpu.SemaphoreType.DMA((2,))],
         compiler_params=PARAMS,
         name="middle",
-    )(in_hbm(object_field), probe_field, acc)
+    )(probe_field, acc, tile_held)
     estimate, correction = pl.pallas_call(
         last_kernel,
         out_shape=(result, result),

time: 69.1 us -> 63.1 us (0.913)
  the two profiles are of different devices: /device:TPU:3 before, /device:TPU:11 now
where the time goes in v7:
time: 63.1 us; the launch traced here: 62.8 us
  starting transfers between devices  28.1 us (45%)
  Pallas kernels  22.9 us (36%)
  waiting for transfers between devices  9.12 us (14%)
  between operations  1.7 us (3%)
  local copies, waits for them, and re-layouts  0.96 us (2%)
    ppermute x14, starting transfers between devices, swap(): return in_vmem(lax.ppermute(array, axis, ends + [(j, i) for i, j in ends]))  28.1 us
    pallas_call x8, Pallas kernels, call(): pl.pallas_call(kernel, out_shape=outs, in_specs=[SMEM] * len(scalars) + [...  11.6 us
    ppermute x14, waiting for transfers between devices, swap(): return in_vmem(lax.ppermute(array, axis, ends + [(j, i) for i, j in ends]))  9.12 us
    pallas_call x1, Pallas kernels, on_device(): pl.pallas_call(inner_start_kernel, out_shape=(padded, padded, doubled_sha...  5.17 us
    pallas_call x1, Pallas kernels, on_device(): pl.pallas_call(deep_kernel, out_shape=(padded, padded, f32(2, tile, width...  2.72 us
    pallas_call x1, Pallas kernels, on_device(): pl.pallas_call(last_kernel, out_shape=(result, result), in_specs=[VMEM] *...  1.76 us
    pallas_call x1, Pallas kernels, on_device(): pl.pallas_call(middle_kernel, out_shape=(result, result), in_specs=[VMEM]...  1.59 us
  transfers between devices with their start and end apart: 14, of which 5 were waited for; matrix products, arithmetic and copies ran while one was open for 0% of the time, Pallas kernels for 28%

profile of v7, /device:TPU:11, one launch (start us, length us, event | category | flops | bytes accessed | tf_op | source)
XLA Modules:
  0.0 62.8 jit_solution(11175417831340862883)
XLA Ops:
  0.6 1.0 %slice_bitcast_fusion.3 = (f32[32,512]{1,0:T(8,128)S(1)}, f32[32,512]{1,0:T(8,128)S(1)}, f32[32,512]{1,0:T(8,128)S(1)}, f32[32,512]{1,0:T(8,128)S(1)}) fusion(f32[2,512,512]{2,1,0:T(8,128)} %objects.3), kind=kLoop, calls=%fused_computation.7 | loop fusion | bytes 524288 | tf_op jit(solution)/shard_map/squeeze | solution.py:766
  1.6 3.1 %collective-permute-start.1 = (f32[32,1024]{1,0:T(8,128)S(1)}, f32[32,1024]{1,0:T(8,128)S(1)}, u32[]{:S(2)}, u32[]{:S(2)}) collective-permute-start(f32[32,1024]{1,0:T(8,128)S(1)} %get-tuple-element.74), channel_id=1, source_target_pairs={{8,16},{16,8},{9,17},{17,9},{10,18},{18,10},{11,19},{19,11},{12,20... | collective-permute-start | bytes 393224 | tf_op jit(solution)/shard_map/ppermute | solution.py:731
  5.5 5.2 %inner_start.1 = (f32[2,584,768]{2,1,0:T(8,128)S(1)}, f32[2,584,768]{2,1,0:T(8,128)S(1)}, f32[2,256,128]{2,1,0:T(8,128)S(1)}, f32[24,128,128]{2,1,0:T(8,128)S(1)...) custom-call(s32[2,24]{1,0:T(2,128)} %bitcast.9, s32[1,1]{1,0:T(1,128)S(6)} %copy.35.counts, ...), custom_call_target="tpu_custom_call" | custom-call | tf_op jit(solution)/shard_map/inner_start/pallas_call | solution.py:771
  11.1 1.0 %collective-permute-start.2 = (f32[288,128]{1,0:T(8,128)S(1)}, f32[288,128]{1,0:T(8,128)S(1)}, u32[]{:S(2)}, u32[]{:S(2)}) collective-permute-start(f32[288,128]{1,0:T(8,128)S(1)} %get-tuple-element.42), channel_id=1, source_target_pairs={{0,1},{2,3},{4,5},{6,7},{1,0},{3,2},{5,4},{7,6},{8,9},{10,11},{12,... | collective-permute-start | bytes 442376 | tf_op jit(solution)/shard_map/ppermute | solution.py:731
  12.1 3.1 %collective-permute-start.3 = (f32[288,128]{1,0:T(8,128)S(1)}, f32[288,128]{1,0:T(8,128)S(1)}, u32[]{:S(2)}, u32[]{:S(2)}) collective-permute-start(f32[288,128]{1,0:T(8,128)S(1)} %get-tuple-element.43), channel_id=1, source_target_pairs={{1,2},{3,4},{5,6},{2,1},{4,3},{6,5},{9,10},{11,12},{13,14},{10,9},... | collective-permute-start | bytes 442376 | tf_op jit(solution)/shard_map/ppermute | solution.py:731
  15.2 2.3 %shard_map.87 = (f32[2,584,768]{2,1,0:T(8,128)S(1)}, f32[2,584,768]{2,1,0:T(8,128)S(1)}) custom-call(s32[8,25]{1,0:T(8,128)S(4)} %get-tuple-element.36.plan, f32[32,1024]{1,0:T(8,128)S(1)} %collective-permute-done.up, f32[32,1024]{1,0:T(8,128)S(1)} %collective-permute-done.1.down, ...), custom_call_target="tpu_custom_call", output_to_operand_aliasing={{0}: (7, {}), {1}: (8, {})} | custom-call | tf_op jit(solution)/shard_map/pallas_call | solution.py:754
  17.5 1.0 %collective-permute-done.3.right = f32[288,128]{1,0:T(8,128)S(1)} collective-permute-done((f32[288,128]{1,0:T(8,128)S(1)}, f32[288,128]{1,0:T(8,128)S(1)}, u32[]{:S(2)}, u32[]{:S(2)}) %collective-permute-start.3) | collective-permute-done | bytes 147488 | tf_op jit(solution)/shard_map/ppermute | solution.py:731
  18.5 2.7 %shard_map.88 = (f32[2,584,768]{2,1,0:T(8,128)S(1)}, f32[2,584,768]{2,1,0:T(8,128)S(1)}, f32[64,1152]{1,0:T(8,128)S(1)}, f32[64,1152]{1,0:T(8,128)S(1)}, f32[576,128]{1,0:T(8,128)S(1)}, /*index=5*/f32[576,128]{1,0:T(8,128)S(1)}) custom-call(s32[8,25]{1,0:T(8,128)S(4)} %get-tuple-element.36.plan, ...), custom_call_target="tpu_custom_call", output_to_operand_aliasing={{0}: (7, {}), {1}: (8, {})} | custom-call | tf_op jit(solution)/shard_map/pallas_call | solution.py:754
  21.3 4.9 %collective-permute-start.5 = (f32[64,1152]{1,0:T(8,128)S(1)}, f32[64,1152]{1,0:T(8,128)S(1)}, u32[]{:S(2)}, u32[]{:S(2)}) collective-permute-start(f32[64,1152]{1,0:T(8,128)S(1)} %get-tuple-element.48), channel_id=1, source_target_pairs={{8,16},{16,8},{9,17},{17,9},{10,18},{18,10},{11,19},{19,11},{12,20... | collective-permute-start | bytes 884744 | tf_op jit(solution)/shard_map/ppermute | solution.py:731
  26.2 0.6 %collective-permute-start.8 = (f32[576,128]{1,0:T(8,128)S(1)}, f32[576,128]{1,0:T(8,128)S(1)}, u32[]{:S(2)}, u32[]{:S(2)}) collective-permute-start(f32[576,128]{1,0:T(8,128)S(1)} %get-tuple-element.54), channel_id=1, source_target_pairs={{0,1},{2,3},{4,5},{6,7},{1,0},{3,2},{5,4},{7,6},{8,9},{10,11},{12,... | collective-permute-start | bytes 884744 | tf_op jit(solution)/shard_map/ppermute | solution.py:731
  26.8 3.1 %collective-permute-start.9 = (f32[576,128]{1,0:T(8,128)S(1)}, f32[576,128]{1,0:T(8,128)S(1)}, u32[]{:S(2)}, u32[]{:S(2)}) collective-permute-start(f32[576,128]{1,0:T(8,128)S(1)} %get-tuple-element.55), channel_id=1, source_target_pairs={{1,2},{3,4},{5,6},{2,1},{4,3},{6,5},{9,10},{11,12},{13,14},{10,9},... | collective-permute-start | bytes 884744 | tf_op jit(solution)/shard_map/ppermute | solution.py:731
  29.9 2.7 %deep.1 = (f32[2,584,768]{2,1,0:T(8,128)S(1)}, f32[2,584,768]{2,1,0:T(8,128)S(1)}, f32[2,512,512]{2,1,0:T(8,128)S(1)}) custom-call(s32[8,25]{1,0:T(8,128)S(4)} %get-tuple-element.36.plan, f32[2,512,512]{2,1,0:T(8,128)} %objects.3, f32[2,128,128]{2,1,0:T(8,128)S(1)} %copy-done, ...), custom_call_target="tpu_custom_call", output_to_operand_aliasing={{0}: (7, {}), {1}: (8, {})} | custom-call | tf_op jit(solution)/shard_map/deep/pallas_call | solution.py:798
  32.6 5.0 %collective-permute-done.5.down = f32[64,1152]{1,0:T(8,128)S(1)} collective-permute-done((f32[64,1152]{1,0:T(8,128)S(1)}, f32[64,1152]{1,0:T(8,128)S(1)}, u32[]{:S(2)}, u32[]{:S(2)}) %collective-permute-start.5) | collective-permute-done | bytes 294944 | tf_op jit(solution)/shard_map/ppermute | solution.py:731
  37.9 0.9 %collective-permute-start.6 = (f32[128,128]{1,0:T(8,128)S(1)}, f32[128,128]{1,0:T(8,128)S(1)}, u32[]{:S(2)}, u32[]{:S(2)}) collective-permute-start(f32[128,128]{1,0:T(8,128)S(1)} %get-tuple-element.52), channel_id=1, source_target_pairs={{0,1},{2,3},{4,5},{6,7},{1,0},{3,2},{5,4},{7,6},{8,9},{10,11},{12,... | collective-permute-start | bytes 196616 | tf_op jit(solution)/shard_map/ppermute | solution.py:731
  38.8 1.9 %collective-permute-start.7 = (f32[128,128]{1,0:T(8,128)S(1)}, f32[128,128]{1,0:T(8,128)S(1)}, u32[]{:S(2)}, u32[]{:S(2)}) collective-permute-start(f32[128,128]{1,0:T(8,128)S(1)} %get-tuple-element.53), channel_id=1, source_target_pairs={{1,2},{3,4},{5,6},{2,1},{4,3},{6,5},{9,10},{11,12},{13,14},{10,9},... | collective-permute-start | bytes 196616 | tf_op jit(solution)/shard_map/ppermute | solution.py:731
  40.7 3.2 %shard_map.90 = (f32[2,584,768]{2,1,0:T(8,128)S(1)}, f32[2,584,768]{2,1,0:T(8,128)S(1)}) custom-call(s32[8,25]{1,0:T(8,128)S(4)} %get-tuple-element.36.plan, f32[2,128,128]{2,1,0:T(8,128)S(1)} %copy-done, f32[2,256,128]{2,1,0:T(8,128)S(1)} %get-tuple-element.37.doubled, ...), custom_call_target="tpu_custom_call", output_to_operand_aliasing={{0}: (10, {}), {1}: (11, {})} | custom-call | tf_op jit(solution)/shard_map/pallas_call | solution.py:754
  44.9 3.9 %collective-permute-start.11 = (f32[32,1152]{1,0:T(8,128)S(1)}, f32[32,1152]{1,0:T(8,128)S(1)}, u32[]{:S(2)}, u32[]{:S(2)}) collective-permute-start(f32[32,1152]{1,0:T(8,128)S(1)} %get-tuple-element.60), channel_id=1, source_target_pairs={{8,16},{16,8},{9,17},{17,9},{10,18},{18,10},{11,19},{19,11},{12,20... | collective-permute-start | bytes 442376 | tf_op jit(solution)/shard_map/ppermute | solution.py:731
  48.8 2.3 %shard_map.92.after.acc = f32[2,584,768]{2,1,0:T(8,128)S(1)} custom-call(s32[8,25]{1,0:T(8,128)S(4)} %get-tuple-element.36.plan, f32[2,584,768]{2,1,0:T(8,128)S(1)} %get-tuple-element.63.cur, f32[2,256,128]{2,1,0:T(8,128)S(1)} %get-tuple-element.37.doubled, f32[24,128,128]{2,1,0:T(8,128)S(1)} %get-tuple-element.38.amplitudes, ...), custom_call_target="tpu_custom_call", output_to_operand_aliasing={{}: (6, {})} | custom-call | tf_op jit(solution)/shard_map/pallas_call | solution.py:754
  51.1 1.0 %collective-permute-done.11.down = f32[32,1152]{1,0:T(8,128)S(1)} collective-permute-done((f32[32,1152]{1,0:T(8,128)S(1)}, f32[32,1152]{1,0:T(8,128)S(1)}, u32[]{:S(2)}, u32[]{:S(2)}) %collective-permute-start.11) | collective-permute-done | bytes 147488 | tf_op jit(solution)/shard_map/ppermute | solution.py:731
  52.4 2.2 %collective-permute-start.12 = (f32[256,128]{1,0:T(8,128)S(1)}, f32[256,128]{1,0:T(8,128)S(1)}, u32[]{:S(2)}, u32[]{:S(2)}) collective-permute-start(f32[256,128]{1,0:T(8,128)S(1)} %get-tuple-element.65), channel_id=1, source_target_pairs={{0,1},{2,3},{4,5},{6,7},{1,0},{3,2},{5,4},{7,6},{8,9},{10,11},{12,... | collective-permute-start | bytes 393224 | tf_op jit(solution)/shard_map/ppermute | solution.py:731
  54.6 3.1 %collective-permute-start.13 = (f32[256,128]{1,0:T(8,128)S(1)}, f32[256,128]{1,0:T(8,128)S(1)}, u32[]{:S(2)}, u32[]{:S(2)}) collective-permute-start(f32[256,128]{1,0:T(8,128)S(1)} %get-tuple-element.66), channel_id=1, source_target_pairs={{1,2},{3,4},{5,6},{2,1},{4,3},{6,5},{9,10},{11,12},{13,14},{10,9},... | collective-permute-start | bytes 393224 | tf_op jit(solution)/shard_map/ppermute | solution.py:731
  57.6 1.6 %middle.1 = (f32[2,512,512]{2,1,0:T(8,128)}, f32[2,512,512]{2,1,0:T(8,128)}) custom-call(f32[2,128,128]{2,1,0:T(8,128)S(1)} %copy-done, f32[2,584,768]{2,1,0:T(8,128)S(1)} %shard_map.92.after.acc, f32[2,512,512]{2,1,0:T(8,128)S(1)} %get-tuple-element.67.held), custom_call_target="tpu_custom_call" | custom-call | tf_op jit(solution)/shard_map/middle/pallas_call | solution.py:834
  59.2 1.6 %collective-permute-done.13.right = f32[256,128]{1,0:T(8,128)S(1)} collective-permute-done((f32[256,128]{1,0:T(8,128)S(1)}, f32[256,128]{1,0:T(8,128)S(1)}, u32[]{:S(2)}, u32[]{:S(2)}) %collective-permute-start.13) | collective-permute-done | bytes 131104 | tf_op jit(solution)/shard_map/ppermute | solution.py:731
  60.8 1.8 %finish.1 = (f32[2,512,512]{2,1,0:T(8,128)}, f32[2,512,512]{2,1,0:T(8,128)}) custom-call(f32[2,128,128]{2,1,0:T(8,128)S(1)} %copy-done, f32[32,1152]{1,0:T(8,128)S(1)} %collective-permute-done.10.up, f32[32,1152]{1,0:T(8,128)S(1)} %collective-permute-done.11.down, ...), custom_call_target="tpu_custom_call", output_to_operand_aliasing={{0}: (7, {}), {1}: (8, {})} | custom-call | tf_op jit(solution)/shard_map/finish/pallas_call | solution.py:843
  (20 shorter events, 1.9 us)
Async XLA Ops:
  1.6 9.0 %collective-permute-start.1 = (f32[32,1024]{1,0:T(8,128)S(1)}, f32[32,1024]{1,0:T(8,128)S(1)}, u32[]{:S(2)}, u32[]{:S(2)}) collective-permute-start(f32[32,1024]{1,0:T(8,128)S(1)} %get-tuple-element.74), channel_id=1, source_target_pairs={{8,16},{16,8},{9,17},{17,9},{10,18},{18,10},{11,19},{19,11},{12,20... | collective-permute-start | bytes 393224 | tf_op jit(solution)/shard_map/ppermute | solution.py:731
  4.8 5.9 %collective-permute-start = (f32[32,1024]{1,0:T(8,128)S(1)}, f32[32,1024]{1,0:T(8,128)S(1)}, u32[]{:S(2)}, u32[]{:S(2)}) collective-permute-start(f32[32,1024]{1,0:T(8,128)S(1)} %get-tuple-element.75), channel_id=1, source_target_pairs={{0,8},{16,24},{8,0},{24,16},{1,9},{17,25},{9,1},{25,17},{2,10},{18... | collective-permute-start | bytes 393224 | tf_op jit(solution)/shard_map/ppermute | solution.py:731
  11.1 6.4 %collective-permute-start.2 = (f32[288,128]{1,0:T(8,128)S(1)}, f32[288,128]{1,0:T(8,128)S(1)}, u32[]{:S(2)}, u32[]{:S(2)}) collective-permute-start(f32[288,128]{1,0:T(8,128)S(1)} %get-tuple-element.42), channel_id=1, source_target_pairs={{0,1},{2,3},{4,5},{6,7},{1,0},{3,2},{5,4},{7,6},{8,9},{10,11},{12,... | collective-permute-start | bytes 442376 | tf_op jit(solution)/shard_map/ppermute | solution.py:731
  12.1 6.5 %collective-permute-start.3 = (f32[288,128]{1,0:T(8,128)S(1)}, f32[288,128]{1,0:T(8,128)S(1)}, u32[]{:S(2)}, u32[]{:S(2)}) collective-permute-start(f32[288,128]{1,0:T(8,128)S(1)} %get-tuple-element.43), channel_id=1, source_target_pairs={{1,2},{3,4},{5,6},{2,1},{4,3},{6,5},{9,10},{11,12},{13,14},{10,9},... | collective-permute-start | bytes 442376 | tf_op jit(solution)/shard_map/ppermute | solution.py:731
  18.5 11.4 %copy-start = (f32[2,128,128]{2,1,0:T(8,128)S(1)}, f32[2,128,128]{2,1,0:T(8,128)}, u32[]{:S(2)}) copy-start(f32[2,128,128]{2,1,0:T(8,128)} %probe.9) | copy-start | bytes 393220
  21.2 11.4 %collective-permute-start.4 = (f32[64,1152]{1,0:T(8,128)S(1)}, f32[64,1152]{1,0:T(8,128)S(1)}, u32[]{:S(2)}, u32[]{:S(2)}) collective-permute-start(f32[64,1152]{1,0:T(8,128)S(1)} %get-tuple-element.47), channel_id=1, source_target_pairs={{0,8},{16,24},{8,0},{24,16},{1,9},{17,25},{9,1},{25,17},{2,10},{18... | collective-permute-start | bytes 884744 | tf_op jit(solution)/shard_map/ppermute | solution.py:731
  21.3 16.4 %collective-permute-start.5 = (f32[64,1152]{1,0:T(8,128)S(1)}, f32[64,1152]{1,0:T(8,128)S(1)}, u32[]{:S(2)}, u32[]{:S(2)}) collective-permute-start(f32[64,1152]{1,0:T(8,128)S(1)} %get-tuple-element.48), channel_id=1, source_target_pairs={{8,16},{16,8},{9,17},{17,9},{10,18},{18,10},{11,19},{19,11},{12,20... | collective-permute-start | bytes 884744 | tf_op jit(solution)/shard_map/ppermute | solution.py:731
  26.2 14.5 %collective-permute-start.8 = (f32[576,128]{1,0:T(8,128)S(1)}, f32[576,128]{1,0:T(8,128)S(1)}, u32[]{:S(2)}, u32[]{:S(2)}) collective-permute-start(f32[576,128]{1,0:T(8,128)S(1)} %get-tuple-element.54), channel_id=1, source_target_pairs={{0,1},{2,3},{4,5},{6,7},{1,0},{3,2},{5,4},{7,6},{8,9},{10,11},{12,... | collective-permute-start | bytes 884744 | tf_op jit(solution)/shard_map/ppermute | solution.py:731
  26.8 13.9 %collective-permute-start.9 = (f32[576,128]{1,0:T(8,128)S(1)}, f32[576,128]{1,0:T(8,128)S(1)}, u32[]{:S(2)}, u32[]{:S(2)}) collective-permute-start(f32[576,128]{1,0:T(8,128)S(1)} %get-tuple-element.55), channel_id=1, source_target_pairs={{1,2},{3,4},{5,6},{2,1},{4,3},{6,5},{9,10},{11,12},{13,14},{10,9},... | collective-permute-start | bytes 884744 | tf_op jit(solution)/shard_map/ppermute | solution.py:731
  37.9 6.1 %collective-permute-start.6 = (f32[128,128]{1,0:T(8,128)S(1)}, f32[128,128]{1,0:T(8,128)S(1)}, u32[]{:S(2)}, u32[]{:S(2)}) collective-permute-start(f32[128,128]{1,0:T(8,128)S(1)} %get-tuple-element.52), channel_id=1, source_target_pairs={{0,1},{2,3},{4,5},{6,7},{1,0},{3,2},{5,4},{7,6},{8,9},{10,11},{12,... | collective-permute-start | bytes 196616 | tf_op jit(solution)/shard_map/ppermute | solution.py:731
  38.8 5.6 %collective-permute-start.7 = (f32[128,128]{1,0:T(8,128)S(1)}, f32[128,128]{1,0:T(8,128)S(1)}, u32[]{:S(2)}, u32[]{:S(2)}) collective-permute-start(f32[128,128]{1,0:T(8,128)S(1)} %get-tuple-element.53), channel_id=1, source_target_pairs={{1,2},{3,4},{5,6},{2,1},{4,3},{6,5},{9,10},{11,12},{13,14},{10,9},... | collective-permute-start | bytes 196616 | tf_op jit(solution)/shard_map/ppermute | solution.py:731
  44.8 6.3 %collective-permute-start.10 = (f32[32,1152]{1,0:T(8,128)S(1)}, f32[32,1152]{1,0:T(8,128)S(1)}, u32[]{:S(2)}, u32[]{:S(2)}) collective-permute-start(f32[32,1152]{1,0:T(8,128)S(1)} %get-tuple-element.59), channel_id=1, source_target_pairs={{0,8},{16,24},{8,0},{24,16},{1,9},{17,25},{9,1},{25,17},{2,10},{18... | collective-permute-start | bytes 442376 | tf_op jit(solution)/shard_map/ppermute | solution.py:731
  44.9 7.2 %collective-permute-start.11 = (f32[32,1152]{1,0:T(8,128)S(1)}, f32[32,1152]{1,0:T(8,128)S(1)}, u32[]{:S(2)}, u32[]{:S(2)}) collective-permute-start(f32[32,1152]{1,0:T(8,128)S(1)} %get-tuple-element.60), channel_id=1, source_target_pairs={{8,16},{16,8},{9,17},{17,9},{10,18},{18,10},{11,19},{19,11},{12,20... | collective-permute-start | bytes 442376 | tf_op jit(solution)/shard_map/ppermute | solution.py:731
  52.4 6.9 %collective-permute-start.12 = (f32[256,128]{1,0:T(8,128)S(1)}, f32[256,128]{1,0:T(8,128)S(1)}, u32[]{:S(2)}, u32[]{:S(2)}) collective-permute-start(f32[256,128]{1,0:T(8,128)S(1)} %get-tuple-element.65), channel_id=1, source_target_pairs={{0,1},{2,3},{4,5},{6,7},{1,0},{3,2},{5,4},{7,6},{8,9},{10,11},{12,... | collective-permute-start | bytes 393224 | tf_op jit(solution)/shard_map/ppermute | solution.py:731
  54.6 6.3 %collective-permute-start.13 = (f32[256,128]{1,0:T(8,128)S(1)}, f32[256,128]{1,0:T(8,128)S(1)}, u32[]{:S(2)}, u32[]{:S(2)}) collective-permute-start(f32[256,128]{1,0:T(8,128)S(1)} %get-tuple-element.66), channel_id=1, source_target_pairs={{1,2},{3,4},{5,6},{2,1},{4,3},{6,5},{9,10},{11,12},{13,14},{10,9},... | collective-permute-start | bytes 393224 | tf_op jit(solution)/shard_map/ppermute | solution.py:731

commit v8 on v7

--- a/solution.py
+++ b/solution.py
@@ -124,48 +124,56 @@
 
 
 class Plan:
-    DEEP, SIDE, BESIDE, SECOND, CORNER, ROW, COL, NUMBER = range(8)
-    LEAD, SIDE_STOP, BAND_BEGIN, BAND_END, SECOND_DEEP, BESIDE_END, SECOND_STOP, REST_END, CORNER_END = range(9)
+    DEEP, SIDE, BESIDE, SECOND, CORNER, RIM, RIM_CORNER, ROW, COL, NUMBER = range(10)
+    SIDE_STOP, BAND_BEGIN, BAND_END, SECOND_DEEP, BESIDE_END, SECOND_STOP, REST_END, CORNER_END = range(8)
+    BAND_GROUPS = 3
 
     @staticmethod
     def shape(slot_total):
-        return 8, max(slot_total + 1, 9)
+        return 10, max(slot_total + 1, 8)
 
     @staticmethod
     def fill(plan, positions, live, last):
-        def append(row, kind, begin, skip=0):
-            def visit(slot, carry):
-                found, seen = carry
-                kinds = slot_kinds(positions[0, slot], positions[1, slot], last)
-                of_kind = jnp.where(kind(*kinds), 1, 0)
-                plan[row, found] = slot
-                return found + jnp.where(seen >= skip, of_kind, 0), seen + of_kind
-
-            return lax.fori_loop(0, live, visit, (begin, 0))[0]
-
-        def place(slot, carry):
-            plan[Plan.ROW, slot] = positions[0, slot]
-            plan[Plan.COL, slot] = positions[1, slot]
-            return carry
-
-        lax.fori_loop(0, live, place, 0)
-        deep = append(Plan.DEEP, is_deep, 0)
-        lead = jnp.minimum(deep, MIDDLE)
-        early = append(Plan.SIDE, is_early, 0)
-        side_end = append(Plan.SIDE, is_deep, early, lead)
-        side_stop = jnp.minimum(side_end, round_up(early))
-        done = lead + side_stop - early
-        room = 2 * LARGE - (deep - done + LARGE - 1) // LARGE * LARGE
+        kinds = (
+            (Plan.DEEP, is_deep), (Plan.SIDE, is_early), (Plan.BESIDE, is_beside),
+            (Plan.SECOND, is_reaching), (Plan.RIM, is_rim), (Plan.RIM_CORNER, is_rim_corner),
+            (Plan.CORNER, is_reaching_corner),
+        )
+
+        def visit(slot, found):
+            row, col = positions[0, slot], positions[1, slot]
+            plan[Plan.ROW, slot] = row
+            plan[Plan.COL, slot] = col
+            where = slot_kinds(row, col, last)
+            counted = []
+            for (listed, kind), number in zip(kinds, found):
+                plan[listed, number] = slot
+                counted.append(number + jnp.where(kind(*where), 1, 0))
+            return tuple(counted)
+
+        deep, early, beside, reaching, rim, rim_corner, corner = lax.fori_loop(
+            0, live, visit, (0,) * len(kinds)
+        )
+
+        def extend(listed, begin, source, first, count):
+            def move(index, carry):
+                plan[listed, begin + index - first] = plan[source, index]
+                return carry
+
+            lax.fori_loop(first, count, move, 0)
+            return begin + count - first
+
+        side_stop = jnp.minimum(extend(Plan.SIDE, early, Plan.DEEP, 0, deep), round_up(early))
+        done = side_stop - early
+        room = (Plan.BAND_GROUPS - (deep - done + LARGE - 1) // LARGE) * LARGE
         second_deep = jnp.minimum(deep, jnp.maximum(room, 0))
-        reaching = append(Plan.SECOND, is_reaching, 0)
-        rim = append(Plan.SECOND, is_rim, reaching)
-        rim_corner = append(Plan.SECOND, is_rim_corner, rim)
+        second_end = extend(Plan.SECOND, reaching, Plan.RIM, 0, rim)
+        end = extend(Plan.SECOND, second_end, Plan.RIM_CORNER, 0, rim_corner)
         numbers = (
-            lead, side_stop, done, deep, second_deep,
-            append(Plan.BESIDE, is_beside, 0),
-            jnp.minimum(rim, round_up(reaching)),
-            append(Plan.SECOND, is_deep, rim_corner, second_deep),
-            append(Plan.CORNER, is_reaching_corner, 0),
+            side_stop, done, deep, second_deep, beside,
+            jnp.minimum(second_end, round_up(reaching)),
+            extend(Plan.SECOND, end, Plan.DEEP, second_deep, deep),
+            corner,
         )
         for index, number in enumerate(numbers):
             plan[Plan.NUMBER, index] = number
@@ -175,7 +183,7 @@
     return jnp.maximum((count + LARGE - 1) // LARGE, 1) * LARGE
 
 
-def gradient_slots(cur, acc, doubled, amplitudes, plan, listed, begin, stop, tables, size=LARGE, before_use=None):
+def gradient_slots(cur, acc, doubled, amplitudes, plan, listed, begin, stop, tables, size=LARGE):
     right_f, right_b = tables
     left_f, left_b = right_b, right_f
     probe = doubled.shape[1] // 2
@@ -229,8 +237,6 @@
                 axis=0,
             )
             wave = times_left(left_f[...], stacked)
-            if before_use is not None and pair == 0:
-                before_use()
             for member in range(2):
                 at = places[pair + member][0]
                 real = wave[:probe, member * probe : (member + 1) * probe]
@@ -314,7 +320,7 @@
     ]
 
 
-def inner_start_kernel(
+def start_kernel(
     positions, counts, objects, probe_in, amplitudes, *refs
 ):
     table_count = (len(refs) - 6) // 2
@@ -342,16 +348,8 @@
         load.start()
     acc[...] = jnp.zeros_like(acc)
     Plan.fill(plan, positions, counts[0, 0], tile - probe)
-    lead = plan[Plan.NUMBER, Plan.LEAD]
-    for load in loads[:-1]:
+    for load in loads:
         load.wait()
-    gradient_slots(
-        cur, acc, doubled, held, plan, Plan.DEEP, 0, lead, tables, MIDDLE, loads[-1].wait
-    )
-
-    @pl.when(lead == 0)
-    def unused():
-        loads[-1].wait()
 
 
 def side_kernel(
@@ -622,18 +620,28 @@
     to_left[...], to_right[...] = sides
 
 
-def middle_kernel(probe, acc, held, estimate, correction, estimated, corrected, sems):
+def middle_kernel(
+    probe, up, down, acc, held, estimate, correction, estimated, corrected, sems,
+):
     tile, width = held.shape[1:]
     rate = step_of(probe)
-    rows, lanes = slice(BORDER, tile - BORDER), slice(LANES, width - LANES)
+    lanes = slice(LANES, width - LANES)
+    up, down = by_side("row", up[...], down[...])
     for plane in range(2):
-        corrected[plane] = rate * acc[plane, 2 * BORDER : tile, 2 * LANES : width]
-        estimated[plane] = held[plane, rows, lanes] + corrected[plane]
+        total = acc[plane, BORDER : BORDER + tile, 2 * LANES : width]
+        at = slice(plane * width + LANES, (plane + 1) * width - LANES)
+        corrected[plane] = rate * jnp.concatenate(
+            [
+                total[:BORDER] + up[:, at],
+                total[BORDER : tile - BORDER],
+                total[tile - BORDER :] + down[:, at],
+            ],
+            axis=0,
+        )
+        estimated[plane] = held[plane, :, lanes] + corrected[plane]
     stores = [
         pltpu.make_async_copy(
-            source,
-            target.at[:, pl.ds(BORDER, tile - BAND), pl.ds(LANES, width - 2 * LANES)],
-            sems.at[i],
+            source, target.at[:, :, pl.ds(LANES, width - 2 * LANES)], sems.at[i]
         )
         for i, (source, target) in enumerate(((corrected, correction), (estimated, estimate)))
     ]
@@ -645,7 +653,7 @@
 
 def last_kernel(
     probe, up, down, left, right, acc, held, estimate_in, correction_in,
-    estimate, correction, side_parts, row_parts, sems,
+    estimate, correction, parts, sems,
 ):
     tile, width = held.shape[1:]
     rate = step_of(probe)
@@ -654,12 +662,6 @@
     lefts, rights = map(unfold_side, by_side("col", left[...], right[...]))
     up, down = by_side("row", up[...], down[...])
     stores = []
-
-    def send(index, source, target):
-        store = pltpu.make_async_copy(source, target, sems.at[index])
-        store.start()
-        stores.append(store)
-
     for side, (block, bands) in enumerate(((0, lefts), (width - LANES, rights))):
         keep = (lane < BORDER) if side == 0 else (lane >= LANES - BORDER)
         for plane in range(2):
@@ -674,29 +676,16 @@
                 ],
                 axis=0,
             )
-            side_parts[0, side, plane] = rate * total
-            side_parts[1, side, plane] = (
-                held[plane, :, block : block + LANES] + side_parts[0, side, plane]
-            )
-        for number, target in enumerate((correction, estimate)):
-            send(
-                2 * side + number, side_parts.at[number, side],
-                target.at[:, :, pl.ds(block, LANES)],
-            )
-    lanes = slice(LANES, width - LANES)
-    for end, (row, band) in enumerate(((0, up), (tile - BORDER, down))):
-        for plane in range(2):
-            total = acc[plane, BORDER + row : 2 * BORDER + row, 2 * LANES : width]
-            total += band[:, plane * width + LANES : (plane + 1) * width - LANES]
-            row_parts[0, end, plane] = rate * total
-            row_parts[1, end, plane] = (
-                held[plane, row : row + BORDER, lanes] + row_parts[0, end, plane]
-            )
-        for number, target in enumerate((correction, estimate)):
-            send(
-                4 + 2 * end + number, row_parts.at[number, end],
-                target.at[:, pl.ds(row, BORDER), pl.ds(LANES, width - 2 * LANES)],
-            )
+            parts[0, side, plane] = rate * total
+            parts[1, side, plane] = held[plane, :, block : block + LANES] + parts[0, side, plane]
+            for number, target in enumerate((correction, estimate)):
+                store = pltpu.make_async_copy(
+                    parts.at[number, side, plane],
+                    target.at[plane, :, pl.ds(block, LANES)],
+                    sems.at[side, plane, number],
+                )
+                store.start()
+                stores.append(store)
     for store in stores:
         store.wait()
 
@@ -769,7 +758,7 @@
     table_shapes = tuple(pltpu.VMEM(table.shape, table.dtype) for table in tables)
     up, down = swap_pairs("row", *by_side("row", *strips))
     cur, acc, doubled, held, plan, *tables = pl.pallas_call(
-        inner_start_kernel,
+        start_kernel,
         out_shape=(
             padded, padded, doubled_shape, f32(*amplitudes.shape), plan_shape, *table_shapes,
         ),
@@ -777,7 +766,7 @@
         out_specs=(VMEM,) * 4 + (SMEM,) + (VMEM,) * len(tables),
         scratch_shapes=[pltpu.SemaphoreType.DMA((7 + len(tables),))],
         compiler_params=PARAMS,
-        name="inner_start",
+        name="start",
     )(*slots, *map(in_hbm, (object_field, probe_field, amplitudes, *tables)))
     slots = (in_smem(plan),)
     to_left, to_right = call(
@@ -830,24 +819,23 @@
     )
     left, right = swap_pairs("col", to_left, to_right)
     result = jax.ShapeDtypeStruct((2, tile, width), jnp.float32)
-    middle = f32(2, tile - BAND, width - 2 * LANES)
+    middle = f32(2, tile, width - 2 * LANES)
     estimate, correction = pl.pallas_call(
         middle_kernel,
         out_shape=(result, result),
-        in_specs=[VMEM] * 3,
+        in_specs=[VMEM] * 5,
         out_specs=(HBM, HBM),
         scratch_shapes=[middle, middle, pltpu.SemaphoreType.DMA((2,))],
         compiler_params=PARAMS,
         name="middle",
-    )(probe_field, acc, tile_held)
+    )(probe_field, up, down, acc, tile_held)
     estimate, correction = pl.pallas_call(
         last_kernel,
         out_shape=(result, result),
         in_specs=[VMEM] * 7 + [HBM] * 2,
         out_specs=(HBM, HBM),
         scratch_shapes=[
-            f32(2, 2, 2, tile, LANES), f32(2, 2, 2, BORDER, width - 2 * LANES),
-            pltpu.SemaphoreType.DMA((8,)),
+            f32(2, 2, 2, tile, LANES), pltpu.SemaphoreType.DMA((2, 2, 2)),
         ],
         input_output_aliases={7: 0, 8: 1},
         compiler_params=PARAMS,

time: 63.1 us -> 63.2 us (level)
  waiting for transfers between devices: 9.12 us -> 8.21 us
  starting transfers between devices: 28.1 us -> 28.8 us
    pallas_call x1, Pallas kernels: 2.72 us -> 4.99 us  [on_device(): pl.pallas_call(deep_kernel, out_shape=(padded, padded, f32(2, tile, width...]
    pallas_call x1, Pallas kernels: 5.17 us -> 3.16 us  [on_device(): pl.pallas_call(start_kernel, out_shape=(padded, padded, doubled_shape, f3...]
    ppermute x14, waiting for transfers between devices: 9.12 us -> 8.21 us  [swap(): return in_vmem(lax.ppermute(array, axis, ends + [(j, i) for i, j in ends]))]
    ppermute x14, starting transfers between devices: 28.1 us -> 28.8 us  [swap(): return in_vmem(lax.ppermute(array, axis, ends + [(j, i) for i, j in ends]))]
  transfers between devices with their start and end apart: 14 -> 14, of which waited for: 5 -> 7; matrix products, arithmetic and copies ran while one was open for 0% -> 0% of each run, Pallas kernels for 28% -> 28%
where the time goes in v8:
time: 63.2 us; the launch traced here: 62.8 us
  starting transfers between devices  28.8 us (46%)
  Pallas kernels  23.1 us (37%)
  waiting for transfers between devices  8.21 us (13%)
  between operations  1.69 us (3%)
  local copies, waits for them, and re-layouts  0.96 us (2%)
    ppermute x14, starting transfers between devices, swap(): return in_vmem(lax.ppermute(array, axis, ends + [(j, i) for i, j in ends]))  28.8 us
    pallas_call x8, Pallas kernels, call(): pl.pallas_call(kernel, out_shape=outs, in_specs=[SMEM] * len(scalars) + [...  11.7 us
    ppermute x14, waiting for transfers between devices, swap(): return in_vmem(lax.ppermute(array, axis, ends + [(j, i) for i, j in ends]))  8.21 us
    pallas_call x1, Pallas kernels, on_device(): pl.pallas_call(deep_kernel, out_shape=(padded, padded, f32(2, tile, width...  4.99 us
    pallas_call x1, Pallas kernels, on_device(): pl.pallas_call(start_kernel, out_shape=(padded, padded, doubled_shape, f3...  3.16 us
    pallas_call x1, Pallas kernels, on_device(): pl.pallas_call(middle_kernel, out_shape=(result, result), in_specs=[VMEM]...  1.67 us
    pallas_call x1, Pallas kernels, on_device(): pl.pallas_call(last_kernel, out_shape=(result, result), in_specs=[VMEM] *...  1.63 us
  transfers between devices with their start and end apart: 14, of which 7 were waited for; matrix products, arithmetic and copies ran while one was open for 0% of the time, Pallas kernels for 28%

profile of v8, /device:TPU:11, one launch (start us, length us, event | category | flops | bytes accessed | tf_op | source)
XLA Modules:
  0.0 62.8 jit_solution(13733608952305929502)
XLA Ops:
  0.6 1.0 %slice_bitcast_fusion.3 = (f32[32,512]{1,0:T(8,128)S(1)}, f32[32,512]{1,0:T(8,128)S(1)}, f32[32,512]{1,0:T(8,128)S(1)}, f32[32,512]{1,0:T(8,128)S(1)}) fusion(f32[2,512,512]{2,1,0:T(8,128)} %objects.3), kind=kLoop, calls=%fused_computation.7 | loop fusion | bytes 524288 | tf_op jit(solution)/shard_map/squeeze | solution.py:755
  1.6 3.1 %collective-permute-start.1 = (f32[32,1024]{1,0:T(8,128)S(1)}, f32[32,1024]{1,0:T(8,128)S(1)}, u32[]{:S(2)}, u32[]{:S(2)}) collective-permute-start(f32[32,1024]{1,0:T(8,128)S(1)} %get-tuple-element.74), channel_id=1, source_target_pairs={{8,16},{16,8},{9,17},{17,9},{10,18},{18,10},{11,19},{19,11},{12,20... | collective-permute-start | bytes 393224 | tf_op jit(solution)/shard_map/ppermute | solution.py:720
  5.5 3.2 %start.1 = (f32[2,584,768]{2,1,0:T(8,128)S(1)}, f32[2,584,768]{2,1,0:T(8,128)S(1)}, f32[2,256,128]{2,1,0:T(8,128)S(1)}, f32[24,128,128]{2,1,0:T(8,128)S(1)}, s32...) custom-call(s32[2,24]{1,0:T(2,128)} %bitcast.9, s32[1,1]{1,0:T(1,128)S(6)} %copy.35.counts, ...), custom_call_target="tpu_custom_call" | custom-call | tf_op jit(solution)/shard_map/start/pallas_call | solution.py:760
  8.8 0.9 %collective-permute-done.up = f32[32,1024]{1,0:T(8,128)S(1)} collective-permute-done((f32[32,1024]{1,0:T(8,128)S(1)}, f32[32,1024]{1,0:T(8,128)S(1)}, u32[]{:S(2)}, u32[]{:S(2)}) %collective-permute-start) | collective-permute-done | bytes 131104 | tf_op jit(solution)/shard_map/ppermute | solution.py:720
  10.1 1.8 %collective-permute-start.2 = (f32[288,128]{1,0:T(8,128)S(1)}, f32[288,128]{1,0:T(8,128)S(1)}, u32[]{:S(2)}, u32[]{:S(2)}) collective-permute-start(f32[288,128]{1,0:T(8,128)S(1)} %get-tuple-element.42), channel_id=1, source_target_pairs={{0,1},{2,3},{4,5},{6,7},{1,0},{3,2},{5,4},{7,6},{8,9},{10,11},{12,... | collective-permute-start | bytes 442376 | tf_op jit(solution)/shard_map/ppermute | solution.py:720
  11.9 3.1 %collective-permute-start.3 = (f32[288,128]{1,0:T(8,128)S(1)}, f32[288,128]{1,0:T(8,128)S(1)}, u32[]{:S(2)}, u32[]{:S(2)}) collective-permute-start(f32[288,128]{1,0:T(8,128)S(1)} %get-tuple-element.43), channel_id=1, source_target_pairs={{1,2},{3,4},{5,6},{2,1},{4,3},{6,5},{9,10},{11,12},{13,14},{10,9},... | collective-permute-start | bytes 442376 | tf_op jit(solution)/shard_map/ppermute | solution.py:720
  15.0 2.3 %shard_map.87 = (f32[2,584,768]{2,1,0:T(8,128)S(1)}, f32[2,584,768]{2,1,0:T(8,128)S(1)}) custom-call(s32[10,25]{1,0:T(8,128)S(4)} %get-tuple-element.36.plan, f32[32,1024]{1,0:T(8,128)S(1)} %collective-permute-done.up, f32[32,1024]{1,0:T(8,128)S(1)} %collective-permute-done.1.down, ...), custom_call_target="tpu_custom_call", output_to_operand_aliasing={{0}: (7, {}), {1}: (8, {})} | custom-call | tf_op jit(solution)/shard_map/pallas_call | solution.py:743
  17.3 1.0 %collective-permute-done.3.right = f32[288,128]{1,0:T(8,128)S(1)} collective-permute-done((f32[288,128]{1,0:T(8,128)S(1)}, f32[288,128]{1,0:T(8,128)S(1)}, u32[]{:S(2)}, u32[]{:S(2)}) %collective-permute-start.3) | collective-permute-done | bytes 147488 | tf_op jit(solution)/shard_map/ppermute | solution.py:720
  18.4 2.7 %shard_map.88 = (f32[2,584,768]{2,1,0:T(8,128)S(1)}, f32[2,584,768]{2,1,0:T(8,128)S(1)}, f32[64,1152]{1,0:T(8,128)S(1)}, f32[64,1152]{1,0:T(8,128)S(1)}, f32[576,128]{1,0:T(8,128)S(1)}, /*index=5*/f32[576,128]{1,0:T(8,128)S(1)}) custom-call(s32[10,25]{1,0:T(8,128)S(4)} %get-tuple-element.36.plan, ...), custom_call_target="tpu_custom_call", output_to_operand_aliasing={{0}: (7, {}), {1}: (8, {})} | custom-call | tf_op jit(solution)/shard_map/pallas_call | solution.py:743
  21.1 5.0 %collective-permute-start.5 = (f32[64,1152]{1,0:T(8,128)S(1)}, f32[64,1152]{1,0:T(8,128)S(1)}, u32[]{:S(2)}, u32[]{:S(2)}) collective-permute-start(f32[64,1152]{1,0:T(8,128)S(1)} %get-tuple-element.48), channel_id=1, source_target_pairs={{8,16},{16,8},{9,17},{17,9},{10,18},{18,10},{11,19},{19,11},{12,20... | collective-permute-start | bytes 884744 | tf_op jit(solution)/shard_map/ppermute | solution.py:720
  26.8 3.1 %collective-permute-start.9 = (f32[576,128]{1,0:T(8,128)S(1)}, f32[576,128]{1,0:T(8,128)S(1)}, u32[]{:S(2)}, u32[]{:S(2)}) collective-permute-start(f32[576,128]{1,0:T(8,128)S(1)} %get-tuple-element.55), channel_id=1, source_target_pairs={{1,2},{3,4},{5,6},{2,1},{4,3},{6,5},{9,10},{11,12},{13,14},{10,9},... | collective-permute-start | bytes 884744 | tf_op jit(solution)/shard_map/ppermute | solution.py:720
  29.9 5.0 %deep.1 = (f32[2,584,768]{2,1,0:T(8,128)S(1)}, f32[2,584,768]{2,1,0:T(8,128)S(1)}, f32[2,512,512]{2,1,0:T(8,128)S(1)}) custom-call(s32[10,25]{1,0:T(8,128)S(4)} %get-tuple-element.36.plan, f32[2,512,512]{2,1,0:T(8,128)} %objects.3, f32[2,128,128]{2,1,0:T(8,128)S(1)} %copy-done, ...), custom_call_target="tpu_custom_call", output_to_operand_aliasing={{0}: (7, {}), {1}: (8, {})} | custom-call | tf_op jit(solution)/shard_map/deep/pallas_call | solution.py:787
  34.9 2.8 %collective-permute-done.5.down = f32[64,1152]{1,0:T(8,128)S(1)} collective-permute-done((f32[64,1152]{1,0:T(8,128)S(1)}, f32[64,1152]{1,0:T(8,128)S(1)}, u32[]{:S(2)}, u32[]{:S(2)}) %collective-permute-start.5) | collective-permute-done | bytes 294944 | tf_op jit(solution)/shard_map/ppermute | solution.py:720
  37.9 0.9 %collective-permute-start.6 = (f32[128,128]{1,0:T(8,128)S(1)}, f32[128,128]{1,0:T(8,128)S(1)}, u32[]{:S(2)}, u32[]{:S(2)}) collective-permute-start(f32[128,128]{1,0:T(8,128)S(1)} %get-tuple-element.52), channel_id=1, source_target_pairs={{0,1},{2,3},{4,5},{6,7},{1,0},{3,2},{5,4},{7,6},{8,9},{10,11},{12,... | collective-permute-start | bytes 196616 | tf_op jit(solution)/shard_map/ppermute | solution.py:720
  38.8 1.9 %collective-permute-start.7 = (f32[128,128]{1,0:T(8,128)S(1)}, f32[128,128]{1,0:T(8,128)S(1)}, u32[]{:S(2)}, u32[]{:S(2)}) collective-permute-start(f32[128,128]{1,0:T(8,128)S(1)} %get-tuple-element.53), channel_id=1, source_target_pairs={{1,2},{3,4},{5,6},{2,1},{4,3},{6,5},{9,10},{11,12},{13,14},{10,9},... | collective-permute-start | bytes 196616 | tf_op jit(solution)/shard_map/ppermute | solution.py:720
  40.7 3.0 %shard_map.90 = (f32[2,584,768]{2,1,0:T(8,128)S(1)}, f32[2,584,768]{2,1,0:T(8,128)S(1)}) custom-call(s32[10,25]{1,0:T(8,128)S(4)} %get-tuple-element.36.plan, f32[2,128,128]{2,1,0:T(8,128)S(1)} %copy-done, f32[2,256,128]{2,1,0:T(8,128)S(1)} %get-tuple-element.37.doubled, ...), custom_call_target="tpu_custom_call", output_to_operand_aliasing={{0}: (10, {}), {1}: (11, {})} | custom-call | tf_op jit(solution)/shard_map/pallas_call | solution.py:743
  45.1 3.7 %collective-permute-start.11 = (f32[32,1152]{1,0:T(8,128)S(1)}, f32[32,1152]{1,0:T(8,128)S(1)}, u32[]{:S(2)}, u32[]{:S(2)}) collective-permute-start(f32[32,1152]{1,0:T(8,128)S(1)} %get-tuple-element.60), channel_id=1, source_target_pairs={{8,16},{16,8},{9,17},{17,9},{10,18},{18,10},{11,19},{19,11},{12,20... | collective-permute-start | bytes 442376 | tf_op jit(solution)/shard_map/ppermute | solution.py:720
  48.8 2.3 %shard_map.92.after.acc = f32[2,584,768]{2,1,0:T(8,128)S(1)} custom-call(s32[10,25]{1,0:T(8,128)S(4)} %get-tuple-element.36.plan, f32[2,584,768]{2,1,0:T(8,128)S(1)} %get-tuple-element.63.cur, f32[2,256,128]{2,1,0:T(8,128)S(1)} %get-tuple-element.37.doubled, f32[24,128,128]{2,1,0:T(8,128)S(1)} %get-tuple-element.38.amplitudes, ...), custom_call_target="tpu_custom_call", output_to_operand_aliasing={{}: (6, {})} | custom-call | tf_op jit(solution)/shard_map/pallas_call | solution.py:743
  51.1 1.2 %collective-permute-done.11.down = f32[32,1152]{1,0:T(8,128)S(1)} collective-permute-done((f32[32,1152]{1,0:T(8,128)S(1)}, f32[32,1152]{1,0:T(8,128)S(1)}, u32[]{:S(2)}, u32[]{:S(2)}) %collective-permute-start.11) | collective-permute-done | bytes 147488 | tf_op jit(solution)/shard_map/ppermute | solution.py:720
  52.6 2.2 %collective-permute-start.12 = (f32[256,128]{1,0:T(8,128)S(1)}, f32[256,128]{1,0:T(8,128)S(1)}, u32[]{:S(2)}, u32[]{:S(2)}) collective-permute-start(f32[256,128]{1,0:T(8,128)S(1)} %get-tuple-element.65), channel_id=1, source_target_pairs={{0,1},{2,3},{4,5},{6,7},{1,0},{3,2},{5,4},{7,6},{8,9},{10,11},{12,... | collective-permute-start | bytes 393224 | tf_op jit(solution)/shard_map/ppermute | solution.py:720
  54.8 3.1 %collective-permute-start.13 = (f32[256,128]{1,0:T(8,128)S(1)}, f32[256,128]{1,0:T(8,128)S(1)}, u32[]{:S(2)}, u32[]{:S(2)}) collective-permute-start(f32[256,128]{1,0:T(8,128)S(1)} %get-tuple-element.66), channel_id=1, source_target_pairs={{1,2},{3,4},{5,6},{2,1},{4,3},{6,5},{9,10},{11,12},{13,14},{10,9},... | collective-permute-start | bytes 393224 | tf_op jit(solution)/shard_map/ppermute | solution.py:720
  57.8 1.7 %middle.1 = (f32[2,512,512]{2,1,0:T(8,128)}, f32[2,512,512]{2,1,0:T(8,128)}) custom-call(f32[2,128,128]{2,1,0:T(8,128)S(1)} %copy-done, f32[32,1152]{1,0:T(8,128)S(1)} %collective-permute-done.10.up, f32[32,1152]{1,0:T(8,128)S(1)} %collective-permute-done.11.down, f32[2,584,768]{2,1,0:T(8,128)S(1)} %shard_map.92.after.acc, ...), custom_call_target="tpu_custom_call" | custom-call | tf_op jit(solution)/shard_map/middle/pallas_call | solution.py:823
  59.5 1.5 %collective-permute-done.13.right = f32[256,128]{1,0:T(8,128)S(1)} collective-permute-done((f32[256,128]{1,0:T(8,128)S(1)}, f32[256,128]{1,0:T(8,128)S(1)}, u32[]{:S(2)}, u32[]{:S(2)}) %collective-permute-start.13) | collective-permute-done | bytes 131104 | tf_op jit(solution)/shard_map/ppermute | solution.py:720
  61.0 1.6 %finish.1 = (f32[2,512,512]{2,1,0:T(8,128)}, f32[2,512,512]{2,1,0:T(8,128)}) custom-call(f32[2,128,128]{2,1,0:T(8,128)S(1)} %copy-done, f32[32,1152]{1,0:T(8,128)S(1)} %collective-permute-done.10.up, f32[32,1152]{1,0:T(8,128)S(1)} %collective-permute-done.11.down, ...), custom_call_target="tpu_custom_call", output_to_operand_aliasing={{0}: (7, {}), {1}: (8, {})} | custom-call | tf_op jit(solution)/shard_map/finish/pallas_call | solution.py:832
  (20 shorter events, 3.0 us)
Async XLA Ops:
  1.6 7.2 %collective-permute-start.1 = (f32[32,1024]{1,0:T(8,128)S(1)}, f32[32,1024]{1,0:T(8,128)S(1)}, u32[]{:S(2)}, u32[]{:S(2)}) collective-permute-start(f32[32,1024]{1,0:T(8,128)S(1)} %get-tuple-element.74), channel_id=1, source_target_pairs={{8,16},{16,8},{9,17},{17,9},{10,18},{18,10},{11,19},{19,11},{12,20... | collective-permute-start | bytes 393224 | tf_op jit(solution)/shard_map/ppermute | solution.py:720
  4.8 5.0 %collective-permute-start = (f32[32,1024]{1,0:T(8,128)S(1)}, f32[32,1024]{1,0:T(8,128)S(1)}, u32[]{:S(2)}, u32[]{:S(2)}) collective-permute-start(f32[32,1024]{1,0:T(8,128)S(1)} %get-tuple-element.75), channel_id=1, source_target_pairs={{0,8},{16,24},{8,0},{24,16},{1,9},{17,25},{9,1},{25,17},{2,10},{18... | collective-permute-start | bytes 393224 | tf_op jit(solution)/shard_map/ppermute | solution.py:720
  10.1 7.2 %collective-permute-start.2 = (f32[288,128]{1,0:T(8,128)S(1)}, f32[288,128]{1,0:T(8,128)S(1)}, u32[]{:S(2)}, u32[]{:S(2)}) collective-permute-start(f32[288,128]{1,0:T(8,128)S(1)} %get-tuple-element.42), channel_id=1, source_target_pairs={{0,1},{2,3},{4,5},{6,7},{1,0},{3,2},{5,4},{7,6},{8,9},{10,11},{12,... | collective-permute-start | bytes 442376 | tf_op jit(solution)/shard_map/ppermute | solution.py:720
  11.9 6.5 %collective-permute-start.3 = (f32[288,128]{1,0:T(8,128)S(1)}, f32[288,128]{1,0:T(8,128)S(1)}, u32[]{:S(2)}, u32[]{:S(2)}) collective-permute-start(f32[288,128]{1,0:T(8,128)S(1)} %get-tuple-element.43), channel_id=1, source_target_pairs={{1,2},{3,4},{5,6},{2,1},{4,3},{6,5},{9,10},{11,12},{13,14},{10,9},... | collective-permute-start | bytes 442376 | tf_op jit(solution)/shard_map/ppermute | solution.py:720
  18.4 11.5 %copy-start = (f32[2,128,128]{2,1,0:T(8,128)S(1)}, f32[2,128,128]{2,1,0:T(8,128)}, u32[]{:S(2)}) copy-start(f32[2,128,128]{2,1,0:T(8,128)} %probe.9) | copy-start | bytes 393220
  21.0 13.9 %collective-permute-start.4 = (f32[64,1152]{1,0:T(8,128)S(1)}, f32[64,1152]{1,0:T(8,128)S(1)}, u32[]{:S(2)}, u32[]{:S(2)}) collective-permute-start(f32[64,1152]{1,0:T(8,128)S(1)} %get-tuple-element.47), channel_id=1, source_target_pairs={{0,8},{16,24},{8,0},{24,16},{1,9},{17,25},{9,1},{25,17},{2,10},{18... | collective-permute-start | bytes 884744 | tf_op jit(solution)/shard_map/ppermute | solution.py:720
  21.1 16.6 %collective-permute-start.5 = (f32[64,1152]{1,0:T(8,128)S(1)}, f32[64,1152]{1,0:T(8,128)S(1)}, u32[]{:S(2)}, u32[]{:S(2)}) collective-permute-start(f32[64,1152]{1,0:T(8,128)S(1)} %get-tuple-element.48), channel_id=1, source_target_pairs={{8,16},{16,8},{9,17},{17,9},{10,18},{18,10},{11,19},{19,11},{12,20... | collective-permute-start | bytes 884744 | tf_op jit(solution)/shard_map/ppermute | solution.py:720
  26.2 14.5 %collective-permute-start.8 = (f32[576,128]{1,0:T(8,128)S(1)}, f32[576,128]{1,0:T(8,128)S(1)}, u32[]{:S(2)}, u32[]{:S(2)}) collective-permute-start(f32[576,128]{1,0:T(8,128)S(1)} %get-tuple-element.54), channel_id=1, source_target_pairs={{0,1},{2,3},{4,5},{6,7},{1,0},{3,2},{5,4},{7,6},{8,9},{10,11},{12,... | collective-permute-start | bytes 884744 | tf_op jit(solution)/shard_map/ppermute | solution.py:720
  26.8 13.9 %collective-permute-start.9 = (f32[576,128]{1,0:T(8,128)S(1)}, f32[576,128]{1,0:T(8,128)S(1)}, u32[]{:S(2)}, u32[]{:S(2)}) collective-permute-start(f32[576,128]{1,0:T(8,128)S(1)} %get-tuple-element.55), channel_id=1, source_target_pairs={{1,2},{3,4},{5,6},{2,1},{4,3},{6,5},{9,10},{11,12},{13,14},{10,9},... | collective-permute-start | bytes 884744 | tf_op jit(solution)/shard_map/ppermute | solution.py:720
  37.9 5.9 %collective-permute-start.6 = (f32[128,128]{1,0:T(8,128)S(1)}, f32[128,128]{1,0:T(8,128)S(1)}, u32[]{:S(2)}, u32[]{:S(2)}) collective-permute-start(f32[128,128]{1,0:T(8,128)S(1)} %get-tuple-element.52), channel_id=1, source_target_pairs={{0,1},{2,3},{4,5},{6,7},{1,0},{3,2},{5,4},{7,6},{8,9},{10,11},{12,... | collective-permute-start | bytes 196616 | tf_op jit(solution)/shard_map/ppermute | solution.py:720
  38.8 5.6 %collective-permute-start.7 = (f32[128,128]{1,0:T(8,128)S(1)}, f32[128,128]{1,0:T(8,128)S(1)}, u32[]{:S(2)}, u32[]{:S(2)}) collective-permute-start(f32[128,128]{1,0:T(8,128)S(1)} %get-tuple-element.53), channel_id=1, source_target_pairs={{1,2},{3,4},{5,6},{2,1},{4,3},{6,5},{9,10},{11,12},{13,14},{10,9},... | collective-permute-start | bytes 196616 | tf_op jit(solution)/shard_map/ppermute | solution.py:720
  45.0 6.1 %collective-permute-start.10 = (f32[32,1152]{1,0:T(8,128)S(1)}, f32[32,1152]{1,0:T(8,128)S(1)}, u32[]{:S(2)}, u32[]{:S(2)}) collective-permute-start(f32[32,1152]{1,0:T(8,128)S(1)} %get-tuple-element.59), channel_id=1, source_target_pairs={{0,8},{16,24},{8,0},{24,16},{1,9},{17,25},{9,1},{25,17},{2,10},{18... | collective-permute-start | bytes 442376 | tf_op jit(solution)/shard_map/ppermute | solution.py:720
  45.1 7.3 %collective-permute-start.11 = (f32[32,1152]{1,0:T(8,128)S(1)}, f32[32,1152]{1,0:T(8,128)S(1)}, u32[]{:S(2)}, u32[]{:S(2)}) collective-permute-start(f32[32,1152]{1,0:T(8,128)S(1)} %get-tuple-element.60), channel_id=1, source_target_pairs={{8,16},{16,8},{9,17},{17,9},{10,18},{18,10},{11,19},{19,11},{12,20... | collective-permute-start | bytes 442376 | tf_op jit(solution)/shard_map/ppermute | solution.py:720
  52.6 6.9 %collective-permute-start.12 = (f32[256,128]{1,0:T(8,128)S(1)}, f32[256,128]{1,0:T(8,128)S(1)}, u32[]{:S(2)}, u32[]{:S(2)}) collective-permute-start(f32[256,128]{1,0:T(8,128)S(1)} %get-tuple-element.65), channel_id=1, source_target_pairs={{0,1},{2,3},{4,5},{6,7},{1,0},{3,2},{5,4},{7,6},{8,9},{10,11},{12,... | collective-permute-start | bytes 393224 | tf_op jit(solution)/shard_map/ppermute | solution.py:720
  54.8 6.3 %collective-permute-start.13 = (f32[256,128]{1,0:T(8,128)S(1)}, f32[256,128]{1,0:T(8,128)S(1)}, u32[]{:S(2)}, u32[]{:S(2)}) collective-permute-start(f32[256,128]{1,0:T(8,128)S(1)} %get-tuple-element.66), channel_id=1, source_target_pairs={{1,2},{3,4},{5,6},{2,1},{4,3},{6,5},{9,10},{11,12},{13,14},{10,9},... | collective-permute-start | bytes 393224 | tf_op jit(solution)/shard_map/ppermute | solution.py:720

commit v9 on v8

--- a/solution.py
+++ b/solution.py
@@ -100,7 +100,11 @@
 
 
 def is_beside(row_out, col_out, row_edge, col_edge):
-    return col_out
+    return col_out & jnp.logical_not(row_edge)
+
+
+def is_beside_edge(row_out, col_out, row_edge, col_edge):
+    return col_out & row_edge
 
 
 def is_early(row_out, col_out, row_edge, col_edge):
@@ -124,20 +128,20 @@
 
 
 class Plan:
-    DEEP, SIDE, BESIDE, SECOND, CORNER, RIM, RIM_CORNER, ROW, COL, NUMBER = range(10)
-    SIDE_STOP, BAND_BEGIN, BAND_END, SECOND_DEEP, BESIDE_END, SECOND_STOP, REST_END, CORNER_END = range(8)
-    BAND_GROUPS = 3
+    DEEP, SIDE, BESIDE, SECOND, CORNER, RIM, RIM_CORNER, BESIDE_EDGE, ROW, COL, NUMBER = range(11)
+    SIDE_STOP, BAND_BEGIN, BAND_END, SECOND_DEEP, BESIDE_END, SECOND_STOP, REST_END, CORNER_END, BESIDE_EDGE_END = range(9)
+    BAND_GROUPS = 2
 
     @staticmethod
     def shape(slot_total):
-        return 10, max(slot_total + 1, 8)
+        return 11, max(slot_total + 1, 9)
 
     @staticmethod
     def fill(plan, positions, live, last):
         kinds = (
             (Plan.DEEP, is_deep), (Plan.SIDE, is_early), (Plan.BESIDE, is_beside),
             (Plan.SECOND, is_reaching), (Plan.RIM, is_rim), (Plan.RIM_CORNER, is_rim_corner),
-            (Plan.CORNER, is_reaching_corner),
+            (Plan.CORNER, is_reaching_corner), (Plan.BESIDE_EDGE, is_beside_edge),
         )
 
         def visit(slot, found):
@@ -151,7 +155,7 @@
                 counted.append(number + jnp.where(kind(*where), 1, 0))
             return tuple(counted)
 
-        deep, early, beside, reaching, rim, rim_corner, corner = lax.fori_loop(
+        deep, early, beside, reaching, rim, rim_corner, corner, beside_edge = lax.fori_loop(
             0, live, visit, (0,) * len(kinds)
         )
 
@@ -173,7 +177,7 @@
             side_stop, done, deep, second_deep, beside,
             jnp.minimum(second_end, round_up(reaching)),
             extend(Plan.SECOND, end, Plan.DEEP, second_deep, deep),
-            corner,
+            corner, beside_edge,
         )
         for index, number in enumerate(numbers):
             plan[Plan.NUMBER, index] = number
@@ -286,6 +290,12 @@
     lax.fori_loop(0, (stop - begin + size - 1) // size, group_body, 0)
 
 
+def few_slots(cur, acc, doubled, amplitudes, plan, listed, stop, tables):
+    whole = jnp.minimum((stop + 1) // MIDDLE * MIDDLE, stop)
+    gradient_slots(cur, acc, doubled, amplitudes, plan, listed, 0, whole, tables, MIDDLE)
+    gradient_slots(cur, acc, doubled, amplitudes, plan, listed, whole, stop, tables, SMALL)
+
+
 def step_of(probe):
     return step_gain / (jnp.max(probe[0] * probe[0] + probe[1] * probe[1]) + 1e-06)
 
@@ -411,9 +421,8 @@
 
 
 def outer_kernel(
-    plan, left, right, doubled, amplitudes,
-    forth, back, cur_in, acc_in,
-    cur, acc, to_up, to_down, to_left, to_right,
+    plan, left, right, doubled, amplitudes, forth, back, cur_in, acc_in,
+    cur, acc, to_up, to_down,
 ):
     extent = 2 * left.shape[0]
     tile, width = extent - BAND, cur.shape[2] - 2 * LANES
@@ -422,11 +431,23 @@
     for plane in range(2):
         cur[plane, :extent, :LANES] = jnp.where(lane >= LANES - BORDER, lefts[plane], 0.0)
         cur[plane, :extent, LANES + width :] = jnp.where(lane < BORDER, rights[plane], 0.0)
-    gradient_slots(
-        cur, acc, doubled, amplitudes, plan, Plan.BESIDE, 0, plan[Plan.NUMBER, Plan.BESIDE_END],
-        (forth, back), MIDDLE,
-    )
-    store_bands(acc, 0, tile, BAND, to_up, to_down, to_left, to_right)
+    few_slots(
+        cur, acc, doubled, amplitudes, plan, Plan.BESIDE_EDGE,
+        plan[Plan.NUMBER, Plan.BESIDE_EDGE_END], (forth, back),
+    )
+    store_rows(acc, 0, tile, BAND, to_up, to_down)
+
+
+def outer_rest_kernel(
+    plan, cur, doubled, amplitudes, forth, back, acc_in,
+    acc, to_left, to_right,
+):
+    few_slots(
+        cur, acc, doubled, amplitudes, plan, Plan.BESIDE,
+        plan[Plan.NUMBER, Plan.BESIDE_END], (forth, back),
+    )
+    sides = pack_side_bands(acc, to_left.shape[0])
+    to_left[...], to_right[...] = by_side("col", *sides)
 
 
 def corner_parts(band, width):
@@ -593,11 +614,12 @@
                 acc[plane, row + own_at : row + own_at + BORDER, own] += own_part[
                     own_at : own_at + BORDER
                 ]
-    gradient_slots(
-        cur, acc, doubled, amplitudes, plan, Plan.CORNER, 0, plan[Plan.NUMBER, Plan.CORNER_END],
-        (forth, back), SMALL,
-    )
-    store_bands(acc, 0, BORDER + tile, BORDER, to_up, to_down, to_left, to_right)
+    few_slots(
+        cur, acc, doubled, amplitudes, plan, Plan.CORNER,
+        plan[Plan.NUMBER, Plan.CORNER_END], (forth, back),
+    )
+    store_rows(acc, 0, BORDER + tile, BORDER, to_up, to_down)
+    to_left[...], to_right[...] = pack_side_bands(acc, to_left.shape[0])
 
 
 def second_rest_kernel(
@@ -611,13 +633,9 @@
     )
 
 
-def store_bands(acc, top, bottom, count, to_up, to_down, to_left, to_right):
+def store_rows(acc, top, bottom, count, to_up, to_down):
     ups = pack_row_band(acc, top, count), pack_row_band(acc, bottom, count)
     to_up[...], to_down[...] = by_side("row", *ups)
-    sides = pack_side_bands(acc, to_left.shape[0])
-    if count == BAND:
-        sides = by_side("col", *sides)
-    to_left[...], to_right[...] = sides
 
 
 def middle_kernel(
@@ -778,11 +796,15 @@
         side_kernel, slots, (up, down, doubled, held, *tables, cur, acc),
         (padded, padded), (), {7: 0, 8: 1},
     )
-    cur, acc, to_up, to_down, to_left, to_right = call(
+    cur, acc, to_up, to_down = call(
         outer_kernel, slots, (left, right, doubled, held, *tables, cur, acc),
-        (padded, padded, *row_bands(BAND), *sides), (), {7: 0, 8: 1},
+        (padded, padded, *row_bands(BAND)), (), {7: 0, 8: 1},
     )
     up, down = swap_pairs("row", to_up, to_down)
+    acc, to_left, to_right = call(
+        outer_rest_kernel, slots, (cur, doubled, held, *tables, acc),
+        (padded, *sides), (), {6: 0},
+    )
     left, right = swap_pairs("col", to_left, to_right)
     cur, acc, tile_held = pl.pallas_call(
         deep_kernel,

time: 63.2 us -> 61.7 us (0.976)
  the two profiles are of different devices: /device:TPU:11 before, /device:TPU:21 now
where the time goes in v9:
time: 61.7 us; the launch traced here: 61.4 us
  starting transfers between devices  24.4 us (40%)
  Pallas kernels  24.1 us (39%)
  waiting for transfers between devices  10.2 us (17%)
  between operations  1.69 us (3%)
  local copies, waits for them, and re-layouts  0.96 us (2%)
    ppermute x14, starting transfers between devices, swap(): return in_vmem(lax.ppermute(array, axis, ends + [(j, i) for i, j in ends]))  24.4 us
    pallas_call x9, Pallas kernels, call(): pl.pallas_call(kernel, out_shape=outs, in_specs=[SMEM] * len(scalars) + [...  12.6 us
    ppermute x14, waiting for transfers between devices, swap(): return in_vmem(lax.ppermute(array, axis, ends + [(j, i) for i, j in ends]))  10.2 us
    pallas_call x1, Pallas kernels, on_device(): pl.pallas_call(deep_kernel, out_shape=(padded, padded, f32(2, tile, width...  5 us
    pallas_call x1, Pallas kernels, on_device(): pl.pallas_call(start_kernel, out_shape=(padded, padded, doubled_shape, f3...  3.16 us
    pallas_call x1, Pallas kernels, on_device(): pl.pallas_call(middle_kernel, out_shape=(result, result), in_specs=[VMEM]...  1.67 us
    pallas_call x1, Pallas kernels, on_device(): pl.pallas_call(last_kernel, out_shape=(result, result), in_specs=[VMEM] *...  1.63 us
  transfers between devices with their start and end apart: 14, of which 8 were waited for; matrix products, arithmetic and copies ran while one was open for 0% of the time, Pallas kernels for 29%

profile of v9, /device:TPU:21, one launch (start us, length us, event | category | flops | bytes accessed | tf_op | source)
XLA Modules:
  0.0 61.4 jit_solution(15532104119172903767)
XLA Ops:
  0.6 1.0 %slice_bitcast_fusion.3 = (f32[32,512]{1,0:T(8,128)S(1)}, f32[32,512]{1,0:T(8,128)S(1)}, f32[32,512]{1,0:T(8,128)S(1)}, f32[32,512]{1,0:T(8,128)S(1)}) fusion(f32[2,512,512]{2,1,0:T(8,128)} %objects.3), kind=kLoop, calls=%fused_computation.7 | loop fusion | bytes 524288 | tf_op jit(solution)/shard_map/squeeze | solution.py:773
  1.6 3.1 %collective-permute-start.1 = (f32[32,1024]{1,0:T(8,128)S(1)}, f32[32,1024]{1,0:T(8,128)S(1)}, u32[]{:S(2)}, u32[]{:S(2)}) collective-permute-start(f32[32,1024]{1,0:T(8,128)S(1)} %get-tuple-element.76), channel_id=1, source_target_pairs={{8,16},{16,8},{9,17},{17,9},{10,18},{18,10},{11,19},{19,11},{12,20... | collective-permute-start | bytes 393224 | tf_op jit(solution)/shard_map/ppermute | solution.py:738
  5.4 3.2 %start.1 = (f32[2,584,768]{2,1,0:T(8,128)S(1)}, f32[2,584,768]{2,1,0:T(8,128)S(1)}, f32[2,256,128]{2,1,0:T(8,128)S(1)}, f32[24,128,128]{2,1,0:T(8,128)S(1)}, s32...) custom-call(s32[2,24]{1,0:T(2,128)} %bitcast.9, s32[1,1]{1,0:T(1,128)S(6)} %copy.37.counts, ...), custom_call_target="tpu_custom_call" | custom-call | tf_op jit(solution)/shard_map/start/pallas_call | solution.py:778
  10.0 1.9 %collective-permute-start.2 = (f32[288,128]{1,0:T(8,128)S(1)}, f32[288,128]{1,0:T(8,128)S(1)}, u32[]{:S(2)}, u32[]{:S(2)}) collective-permute-start(f32[288,128]{1,0:T(8,128)S(1)} %get-tuple-element.43), channel_id=1, source_target_pairs={{0,1},{2,3},{4,5},{6,7},{1,0},{3,2},{5,4},{7,6},{8,9},{10,11},{12,... | collective-permute-start | bytes 442376 | tf_op jit(solution)/shard_map/ppermute | solution.py:738
  11.9 3.1 %collective-permute-start.3 = (f32[288,128]{1,0:T(8,128)S(1)}, f32[288,128]{1,0:T(8,128)S(1)}, u32[]{:S(2)}, u32[]{:S(2)}) collective-permute-start(f32[288,128]{1,0:T(8,128)S(1)} %get-tuple-element.44), channel_id=1, source_target_pairs={{1,2},{3,4},{5,6},{2,1},{4,3},{6,5},{9,10},{11,12},{13,14},{10,9},... | collective-permute-start | bytes 442376 | tf_op jit(solution)/shard_map/ppermute | solution.py:738
  15.0 2.3 %shard_map.87 = (f32[2,584,768]{2,1,0:T(8,128)S(1)}, f32[2,584,768]{2,1,0:T(8,128)S(1)}) custom-call(s32[11,25]{1,0:T(8,128)S(4)} %get-tuple-element.37.plan, f32[32,1024]{1,0:T(8,128)S(1)} %collective-permute-done.up, f32[32,1024]{1,0:T(8,128)S(1)} %collective-permute-done.1.down, ...), custom_call_target="tpu_custom_call", output_to_operand_aliasing={{0}: (7, {}), {1}: (8, {})} | custom-call | tf_op jit(solution)/shard_map/pallas_call | solution.py:761
  17.3 1.0 %collective-permute-done.3.right = f32[288,128]{1,0:T(8,128)S(1)} collective-permute-done((f32[288,128]{1,0:T(8,128)S(1)}, f32[288,128]{1,0:T(8,128)S(1)}, u32[]{:S(2)}, u32[]{:S(2)}) %collective-permute-start.3) | collective-permute-done | bytes 147488 | tf_op jit(solution)/shard_map/ppermute | solution.py:738
  18.4 1.9 %shard_map.88 = (f32[2,584,768]{2,1,0:T(8,128)S(1)}, f32[2,584,768]{2,1,0:T(8,128)S(1)}, f32[64,1152]{1,0:T(8,128)S(1)}, f32[64,1152]{1,0:T(8,128)S(1)}) custom-call(s32[11,25]{1,0:T(8,128)S(4)} %get-tuple-element.37.plan, f32[288,128]{1,0:T(8,128)S(1)} %collective-permute-done.2.left, ...), custom_call_target="tpu_custom_call", output_to_operand_aliasing={{0}: (7, {}), {1}: (8, {})} | custom-call | tf_op jit(solution)/shard_map/pallas_call | solution.py:761
  20.8 4.6 %collective-permute-start.5 = (f32[64,1152]{1,0:T(8,128)S(1)}, f32[64,1152]{1,0:T(8,128)S(1)}, u32[]{:S(2)}, u32[]{:S(2)}) collective-permute-start(f32[64,1152]{1,0:T(8,128)S(1)} %get-tuple-element.49), channel_id=1, source_target_pairs={{8,16},{16,8},{9,17},{17,9},{10,18},{18,10},{11,19},{19,11},{12,20... | collective-permute-start | bytes 884744 | tf_op jit(solution)/shard_map/ppermute | solution.py:738
  25.6 2.1 %collective-permute-start.8 = (f32[576,128]{1,0:T(8,128)S(1)}, f32[576,128]{1,0:T(8,128)S(1)}, u32[]{:S(2)}, u32[]{:S(2)}) collective-permute-start(f32[576,128]{1,0:T(8,128)S(1)} %get-tuple-element.56), channel_id=1, source_target_pairs={{0,1},{2,3},{4,5},{6,7},{1,0},{3,2},{5,4},{7,6},{8,9},{10,11},{12,... | collective-permute-start | bytes 884744 | tf_op jit(solution)/shard_map/ppermute | solution.py:738
  27.7 1.9 %collective-permute-start.9 = (f32[576,128]{1,0:T(8,128)S(1)}, f32[576,128]{1,0:T(8,128)S(1)}, u32[]{:S(2)}, u32[]{:S(2)}) collective-permute-start(f32[576,128]{1,0:T(8,128)S(1)} %get-tuple-element.57), channel_id=1, source_target_pairs={{1,2},{3,4},{5,6},{2,1},{4,3},{6,5},{9,10},{11,12},{13,14},{10,9},... | collective-permute-start | bytes 884744 | tf_op jit(solution)/shard_map/ppermute | solution.py:738
  29.7 5.0 %deep.1 = (f32[2,584,768]{2,1,0:T(8,128)S(1)}, f32[2,584,768]{2,1,0:T(8,128)S(1)}, f32[2,512,512]{2,1,0:T(8,128)S(1)}) custom-call(s32[11,25]{1,0:T(8,128)S(4)} %get-tuple-element.37.plan, f32[2,512,512]{2,1,0:T(8,128)} %objects.3, f32[2,128,128]{2,1,0:T(8,128)S(1)} %copy-done, ...), custom_call_target="tpu_custom_call", output_to_operand_aliasing={{0}: (7, {}), {1}: (8, {})} | custom-call | tf_op jit(solution)/shard_map/deep/pallas_call | solution.py:809
  34.7 2.1 %collective-permute-done.5.down = f32[64,1152]{1,0:T(8,128)S(1)} collective-permute-done((f32[64,1152]{1,0:T(8,128)S(1)}, f32[64,1152]{1,0:T(8,128)S(1)}, u32[]{:S(2)}, u32[]{:S(2)}) %collective-permute-start.5) | collective-permute-done | bytes 294944 | tf_op jit(solution)/shard_map/ppermute | solution.py:738
  37.0 0.9 %collective-permute-start.6 = (f32[128,128]{1,0:T(8,128)S(1)}, f32[128,128]{1,0:T(8,128)S(1)}, u32[]{:S(2)}, u32[]{:S(2)}) collective-permute-start(f32[128,128]{1,0:T(8,128)S(1)} %get-tuple-element.54), channel_id=1, source_target_pairs={{0,1},{2,3},{4,5},{6,7},{1,0},{3,2},{5,4},{7,6},{8,9},{10,11},{12,... | collective-permute-start | bytes 196616 | tf_op jit(solution)/shard_map/ppermute | solution.py:738
  38.0 1.9 %collective-permute-start.7 = (f32[128,128]{1,0:T(8,128)S(1)}, f32[128,128]{1,0:T(8,128)S(1)}, u32[]{:S(2)}, u32[]{:S(2)}) collective-permute-start(f32[128,128]{1,0:T(8,128)S(1)} %get-tuple-element.55), channel_id=1, source_target_pairs={{1,2},{3,4},{5,6},{2,1},{4,3},{6,5},{9,10},{11,12},{13,14},{10,9},... | collective-permute-start | bytes 196616 | tf_op jit(solution)/shard_map/ppermute | solution.py:738
  39.9 3.2 %shard_map.91 = (f32[2,584,768]{2,1,0:T(8,128)S(1)}, f32[2,584,768]{2,1,0:T(8,128)S(1)}) custom-call(s32[11,25]{1,0:T(8,128)S(4)} %get-tuple-element.37.plan, f32[2,128,128]{2,1,0:T(8,128)S(1)} %copy-done, f32[2,256,128]{2,1,0:T(8,128)S(1)} %get-tuple-element.38.doubled, ...), custom_call_target="tpu_custom_call", output_to_operand_aliasing={{0}: (10, {}), {1}: (11, {})} | custom-call | tf_op jit(solution)/shard_map/pallas_call | solution.py:761
  43.5 1.9 %shard_map.92 = (f32[2,584,768]{2,1,0:T(8,128)S(1)}, f32[2,584,768]{2,1,0:T(8,128)S(1)}, f32[32,1152]{1,0:T(8,128)S(1)}, f32[32,1152]{1,0:T(8,128)S(1)}, f32[576,128]{1,0:T(8,128)S(1)}, /*index=5*/f32[576,128]{1,0:T(8,128)S(1)}) custom-call(s32[11,25]{1,0:T(8,128)S(4)} %get-tuple-element.37.plan, ...), custom_call_target="tpu_custom_call", output_to_operand_aliasing={{0}: (8, {}), {1}: (9, {})} | custom-call | tf_op jit(solution)/shard_map/pallas_call | solution.py:761
  45.5 1.9 %collective-permute-start.11 = (f32[32,1152]{1,0:T(8,128)S(1)}, f32[32,1152]{1,0:T(8,128)S(1)}, u32[]{:S(2)}, u32[]{:S(2)}) collective-permute-start(f32[32,1152]{1,0:T(8,128)S(1)} %get-tuple-element.62), channel_id=1, source_target_pairs={{8,16},{16,8},{9,17},{17,9},{10,18},{18,10},{11,19},{19,11},{12,20... | collective-permute-start | bytes 442376 | tf_op jit(solution)/shard_map/ppermute | solution.py:738
  47.5 2.3 %shard_map.93.after.acc = f32[2,584,768]{2,1,0:T(8,128)S(1)} custom-call(s32[11,25]{1,0:T(8,128)S(4)} %get-tuple-element.37.plan, f32[2,584,768]{2,1,0:T(8,128)S(1)} %get-tuple-element.65.cur, f32[2,256,128]{2,1,0:T(8,128)S(1)} %get-tuple-element.38.doubled, f32[24,128,128]{2,1,0:T(8,128)S(1)} %get-tuple-element.39.amplitudes, ...), custom_call_target="tpu_custom_call", output_to_operand_aliasing={{}: (6, {})} | custom-call | tf_op jit(solution)/shard_map/pallas_call | solution.py:761
  50.4 2.5 %collective-permute-done.11.down = f32[32,1152]{1,0:T(8,128)S(1)} collective-permute-done((f32[32,1152]{1,0:T(8,128)S(1)}, f32[32,1152]{1,0:T(8,128)S(1)}, u32[]{:S(2)}, u32[]{:S(2)}) %collective-permute-start.11) | collective-permute-done | bytes 147488 | tf_op jit(solution)/shard_map/ppermute | solution.py:738
  53.2 2.3 %collective-permute-start.13 = (f32[256,128]{1,0:T(8,128)S(1)}, f32[256,128]{1,0:T(8,128)S(1)}, u32[]{:S(2)}, u32[]{:S(2)}) collective-permute-start(f32[256,128]{1,0:T(8,128)S(1)} %get-tuple-element.68), channel_id=1, source_target_pairs={{1,2},{3,4},{5,6},{2,1},{4,3},{6,5},{9,10},{11,12},{13,14},{10,9},... | collective-permute-start | bytes 393224 | tf_op jit(solution)/shard_map/ppermute | solution.py:738
  55.5 1.7 %middle.1 = (f32[2,512,512]{2,1,0:T(8,128)}, f32[2,512,512]{2,1,0:T(8,128)}) custom-call(f32[2,128,128]{2,1,0:T(8,128)S(1)} %copy-done, f32[32,1152]{1,0:T(8,128)S(1)} %collective-permute-done.10.up, f32[32,1152]{1,0:T(8,128)S(1)} %collective-permute-done.11.down, f32[2,584,768]{2,1,0:T(8,128)S(1)} %shard_map.93.after.acc, ...), custom_call_target="tpu_custom_call" | custom-call | tf_op jit(solution)/shard_map/middle/pallas_call | solution.py:845
  57.2 2.4 %collective-permute-done.13.right = f32[256,128]{1,0:T(8,128)S(1)} collective-permute-done((f32[256,128]{1,0:T(8,128)S(1)}, f32[256,128]{1,0:T(8,128)S(1)}, u32[]{:S(2)}, u32[]{:S(2)}) %collective-permute-start.13) | collective-permute-done | bytes 131104 | tf_op jit(solution)/shard_map/ppermute | solution.py:738
  59.6 1.6 %finish.1 = (f32[2,512,512]{2,1,0:T(8,128)}, f32[2,512,512]{2,1,0:T(8,128)}) custom-call(f32[2,128,128]{2,1,0:T(8,128)S(1)} %copy-done, f32[32,1152]{1,0:T(8,128)S(1)} %collective-permute-done.10.up, f32[32,1152]{1,0:T(8,128)S(1)} %collective-permute-done.11.down, ...), custom_call_target="tpu_custom_call", output_to_operand_aliasing={{0}: (7, {}), {1}: (8, {})} | custom-call | tf_op jit(solution)/shard_map/finish/pallas_call | solution.py:854
  (21 shorter events, 4.0 us)
Async XLA Ops:
  1.6 7.2 %collective-permute-start.1 = (f32[32,1024]{1,0:T(8,128)S(1)}, f32[32,1024]{1,0:T(8,128)S(1)}, u32[]{:S(2)}, u32[]{:S(2)}) collective-permute-start(f32[32,1024]{1,0:T(8,128)S(1)} %get-tuple-element.76), channel_id=1, source_target_pairs={{8,16},{16,8},{9,17},{17,9},{10,18},{18,10},{11,19},{19,11},{12,20... | collective-permute-start | bytes 393224 | tf_op jit(solution)/shard_map/ppermute | solution.py:738
  4.7 5.0 %collective-permute-start = (f32[32,1024]{1,0:T(8,128)S(1)}, f32[32,1024]{1,0:T(8,128)S(1)}, u32[]{:S(2)}, u32[]{:S(2)}) collective-permute-start(f32[32,1024]{1,0:T(8,128)S(1)} %get-tuple-element.77), channel_id=1, source_target_pairs={{0,8},{16,24},{8,0},{24,16},{1,9},{17,25},{9,1},{25,17},{2,10},{18... | collective-permute-start | bytes 393224 | tf_op jit(solution)/shard_map/ppermute | solution.py:738
  10.0 7.3 %collective-permute-start.2 = (f32[288,128]{1,0:T(8,128)S(1)}, f32[288,128]{1,0:T(8,128)S(1)}, u32[]{:S(2)}, u32[]{:S(2)}) collective-permute-start(f32[288,128]{1,0:T(8,128)S(1)} %get-tuple-element.43), channel_id=1, source_target_pairs={{0,1},{2,3},{4,5},{6,7},{1,0},{3,2},{5,4},{7,6},{8,9},{10,11},{12,... | collective-permute-start | bytes 442376 | tf_op jit(solution)/shard_map/ppermute | solution.py:738
  11.9 6.5 %collective-permute-start.3 = (f32[288,128]{1,0:T(8,128)S(1)}, f32[288,128]{1,0:T(8,128)S(1)}, u32[]{:S(2)}, u32[]{:S(2)}) collective-permute-start(f32[288,128]{1,0:T(8,128)S(1)} %get-tuple-element.44), channel_id=1, source_target_pairs={{1,2},{3,4},{5,6},{2,1},{4,3},{6,5},{9,10},{11,12},{13,14},{10,9},... | collective-permute-start | bytes 442376 | tf_op jit(solution)/shard_map/ppermute | solution.py:738
  20.2 14.4 %collective-permute-start.4 = (f32[64,1152]{1,0:T(8,128)S(1)}, f32[64,1152]{1,0:T(8,128)S(1)}, u32[]{:S(2)}, u32[]{:S(2)}) collective-permute-start(f32[64,1152]{1,0:T(8,128)S(1)} %get-tuple-element.48), channel_id=1, source_target_pairs={{0,8},{16,24},{8,0},{24,16},{1,9},{17,25},{9,1},{25,17},{2,10},{18... | collective-permute-start | bytes 884744 | tf_op jit(solution)/shard_map/ppermute | solution.py:738
  20.8 16.1 %collective-permute-start.5 = (f32[64,1152]{1,0:T(8,128)S(1)}, f32[64,1152]{1,0:T(8,128)S(1)}, u32[]{:S(2)}, u32[]{:S(2)}) collective-permute-start(f32[64,1152]{1,0:T(8,128)S(1)} %get-tuple-element.49), channel_id=1, source_target_pairs={{8,16},{16,8},{9,17},{17,9},{10,18},{18,10},{11,19},{19,11},{12,20... | collective-permute-start | bytes 884744 | tf_op jit(solution)/shard_map/ppermute | solution.py:738
  25.3 4.3 %copy-start = (f32[2,128,128]{2,1,0:T(8,128)S(1)}, f32[2,128,128]{2,1,0:T(8,128)}, u32[]{:S(2)}) copy-start(f32[2,128,128]{2,1,0:T(8,128)} %probe.9) | copy-start | bytes 393220
  25.6 14.3 %collective-permute-start.8 = (f32[576,128]{1,0:T(8,128)S(1)}, f32[576,128]{1,0:T(8,128)S(1)}, u32[]{:S(2)}, u32[]{:S(2)}) collective-permute-start(f32[576,128]{1,0:T(8,128)S(1)} %get-tuple-element.56), channel_id=1, source_target_pairs={{0,1},{2,3},{4,5},{6,7},{1,0},{3,2},{5,4},{7,6},{8,9},{10,11},{12,... | collective-permute-start | bytes 884744 | tf_op jit(solution)/shard_map/ppermute | solution.py:738
  27.7 12.2 %collective-permute-start.9 = (f32[576,128]{1,0:T(8,128)S(1)}, f32[576,128]{1,0:T(8,128)S(1)}, u32[]{:S(2)}, u32[]{:S(2)}) collective-permute-start(f32[576,128]{1,0:T(8,128)S(1)} %get-tuple-element.57), channel_id=1, source_target_pairs={{1,2},{3,4},{5,6},{2,1},{4,3},{6,5},{9,10},{11,12},{13,14},{10,9},... | collective-permute-start | bytes 884744 | tf_op jit(solution)/shard_map/ppermute | solution.py:738
  37.0 6.1 %collective-permute-start.6 = (f32[128,128]{1,0:T(8,128)S(1)}, f32[128,128]{1,0:T(8,128)S(1)}, u32[]{:S(2)}, u32[]{:S(2)}) collective-permute-start(f32[128,128]{1,0:T(8,128)S(1)} %get-tuple-element.54), channel_id=1, source_target_pairs={{0,1},{2,3},{4,5},{6,7},{1,0},{3,2},{5,4},{7,6},{8,9},{10,11},{12,... | collective-permute-start | bytes 196616 | tf_op jit(solution)/shard_map/ppermute | solution.py:738
  38.0 5.6 %collective-permute-start.7 = (f32[128,128]{1,0:T(8,128)S(1)}, f32[128,128]{1,0:T(8,128)S(1)}, u32[]{:S(2)}, u32[]{:S(2)}) collective-permute-start(f32[128,128]{1,0:T(8,128)S(1)} %get-tuple-element.55), channel_id=1, source_target_pairs={{1,2},{3,4},{5,6},{2,1},{4,3},{6,5},{9,10},{11,12},{13,14},{10,9},... | collective-permute-start | bytes 196616 | tf_op jit(solution)/shard_map/ppermute | solution.py:738
  45.5 5.0 %collective-permute-start.10 = (f32[32,1152]{1,0:T(8,128)S(1)}, f32[32,1152]{1,0:T(8,128)S(1)}, u32[]{:S(2)}, u32[]{:S(2)}) collective-permute-start(f32[32,1152]{1,0:T(8,128)S(1)} %get-tuple-element.61), channel_id=1, source_target_pairs={{0,8},{16,24},{8,0},{24,16},{1,9},{17,25},{9,1},{25,17},{2,10},{18... | collective-permute-start | bytes 442376 | tf_op jit(solution)/shard_map/ppermute | solution.py:738
  45.5 7.4 %collective-permute-start.11 = (f32[32,1152]{1,0:T(8,128)S(1)}, f32[32,1152]{1,0:T(8,128)S(1)}, u32[]{:S(2)}, u32[]{:S(2)}) collective-permute-start(f32[32,1152]{1,0:T(8,128)S(1)} %get-tuple-element.62), channel_id=1, source_target_pairs={{8,16},{16,8},{9,17},{17,9},{10,18},{18,10},{11,19},{19,11},{12,20... | collective-permute-start | bytes 442376 | tf_op jit(solution)/shard_map/ppermute | solution.py:738
  53.2 4.0 %collective-permute-start.12 = (f32[256,128]{1,0:T(8,128)S(1)}, f32[256,128]{1,0:T(8,128)S(1)}, u32[]{:S(2)}, u32[]{:S(2)}) collective-permute-start(f32[256,128]{1,0:T(8,128)S(1)} %get-tuple-element.67), channel_id=1, source_target_pairs={{0,1},{2,3},{4,5},{6,7},{1,0},{3,2},{5,4},{7,6},{8,9},{10,11},{12,... | collective-permute-start | bytes 393224 | tf_op jit(solution)/shard_map/ppermute | solution.py:738
  53.2 6.4 %collective-permute-start.13 = (f32[256,128]{1,0:T(8,128)S(1)}, f32[256,128]{1,0:T(8,128)S(1)}, u32[]{:S(2)}, u32[]{:S(2)}) collective-permute-start(f32[256,128]{1,0:T(8,128)S(1)} %get-tuple-element.68), channel_id=1, source_target_pairs={{1,2},{3,4},{5,6},{2,1},{4,3},{6,5},{9,10},{11,12},{13,14},{10,9},... | collective-permute-start | bytes 393224 | tf_op jit(solution)/shard_map/ppermute | solution.py:738

commit v10 on v9

--- a/solution.py
+++ b/solution.py
@@ -57,7 +57,7 @@
 def right_groups(members, block):
     rows = members[0].shape[0]
     results = []
-    count = min(RIGHT, len(members))
+    count = min(RIGHT, len(members) // 2)
     for start in range(0, len(members), count):
         product = times_right(jnp.concatenate(members[start : start + count], axis=0), block[...])
         results += [product[i * rows : (i + 1) * rows] for i in range(count)]
@@ -130,7 +130,7 @@
 class Plan:
     DEEP, SIDE, BESIDE, SECOND, CORNER, RIM, RIM_CORNER, BESIDE_EDGE, ROW, COL, NUMBER = range(11)
     SIDE_STOP, BAND_BEGIN, BAND_END, SECOND_DEEP, BESIDE_END, SECOND_STOP, REST_END, CORNER_END, BESIDE_EDGE_END = range(9)
-    BAND_GROUPS = 2
+    BAND_GROUPS, REST_GROUPS = 2, 2
 
     @staticmethod
     def shape(slot_total):
@@ -169,13 +169,20 @@
 
         side_stop = jnp.minimum(extend(Plan.SIDE, early, Plan.DEEP, 0, deep), round_up(early))
         done = side_stop - early
-        room = (Plan.BAND_GROUPS - (deep - done + LARGE - 1) // LARGE) * LARGE
-        second_deep = jnp.minimum(deep, jnp.maximum(room, 0))
         second_end = extend(Plan.SECOND, reaching, Plan.RIM, 0, rim)
+        second_stop = jnp.minimum(second_end, round_up(reaching))
+
+        def deep_taken(groups):
+            room = (groups - (deep - done + LARGE - 1) // LARGE) * LARGE
+            return jnp.minimum(deep, jnp.maximum(room, 0))
+
+        left = second_end - second_stop + rim_corner + deep - deep_taken(Plan.BAND_GROUPS)
+        crowded = left > Plan.REST_GROUPS * LARGE
+        second_deep = deep_taken(Plan.BAND_GROUPS + jnp.where(crowded, 1, 0))
         end = extend(Plan.SECOND, second_end, Plan.RIM_CORNER, 0, rim_corner)
         numbers = (
             side_stop, done, deep, second_deep, beside,
-            jnp.minimum(second_end, round_up(reaching)),
+            second_stop,
             extend(Plan.SECOND, end, Plan.DEEP, second_deep, deep),
             corner, beside_edge,
         )

time: 61.7 us -> 61.6 us (level)
  transfers between devices with their start and end apart: 14 -> 14, of which waited for: 8 -> 8; matrix products, arithmetic and copies ran while one was open for 0% -> 0% of each run, Pallas kernels for 29% -> 30%
where the time goes in v10:
time: 61.6 us; the launch traced here: 61.2 us
  starting transfers between devices  24.3 us (39%)
  Pallas kernels  23.8 us (39%)
  waiting for transfers between devices  10.5 us (17%)
  between operations  1.69 us (3%)
  local copies, waits for them, and re-layouts  0.96 us (2%)
    ppermute x14, starting transfers between devices, swap(): return in_vmem(lax.ppermute(array, axis, ends + [(j, i) for i, j in ends]))  24.3 us
    pallas_call x9, Pallas kernels, call(): pl.pallas_call(kernel, out_shape=outs, in_specs=[SMEM] * len(scalars) + [...  12.3 us
    ppermute x14, waiting for transfers between devices, swap(): return in_vmem(lax.ppermute(array, axis, ends + [(j, i) for i, j in ends]))  10.5 us
    pallas_call x1, Pallas kernels, on_device(): pl.pallas_call(deep_kernel, out_shape=(padded, padded, f32(2, tile, width...  5 us
    pallas_call x1, Pallas kernels, on_device(): pl.pallas_call(start_kernel, out_shape=(padded, padded, doubled_shape, f3...  3.16 us
    pallas_call x1, Pallas kernels, on_device(): pl.pallas_call(middle_kernel, out_shape=(result, result), in_specs=[VMEM]...  1.67 us
    pallas_call x1, Pallas kernels, on_device(): pl.pallas_call(last_kernel, out_shape=(result, result), in_specs=[VMEM] *...  1.63 us
  transfers between devices with their start and end apart: 14, of which 8 were waited for; matrix products, arithmetic and copies ran while one was open for 0% of the time, Pallas kernels for 30%

profile of v10, /device:TPU:21, one launch (start us, length us, event | category | flops | bytes accessed | tf_op | source)
XLA Modules:
  0.0 61.2 jit_solution(16523499526784882492)
XLA Ops:
  0.6 1.0 %slice_bitcast_fusion.3 = (f32[32,512]{1,0:T(8,128)S(1)}, f32[32,512]{1,0:T(8,128)S(1)}, f32[32,512]{1,0:T(8,128)S(1)}, f32[32,512]{1,0:T(8,128)S(1)}) fusion(f32[2,512,512]{2,1,0:T(8,128)} %objects.3), kind=kLoop, calls=%fused_computation.7 | loop fusion | bytes 524288 | tf_op jit(solution)/shard_map/squeeze | solution.py:780
  1.6 3.1 %collective-permute-start.1 = (f32[32,1024]{1,0:T(8,128)S(1)}, f32[32,1024]{1,0:T(8,128)S(1)}, u32[]{:S(2)}, u32[]{:S(2)}) collective-permute-start(f32[32,1024]{1,0:T(8,128)S(1)} %get-tuple-element.76), channel_id=1, source_target_pairs={{8,16},{16,8},{9,17},{17,9},{10,18},{18,10},{11,19},{19,11},{12,20... | collective-permute-start | bytes 393224 | tf_op jit(solution)/shard_map/ppermute | solution.py:745
  5.4 3.2 %start.1 = (f32[2,584,768]{2,1,0:T(8,128)S(1)}, f32[2,584,768]{2,1,0:T(8,128)S(1)}, f32[2,256,128]{2,1,0:T(8,128)S(1)}, f32[24,128,128]{2,1,0:T(8,128)S(1)}, s32...) custom-call(s32[2,24]{1,0:T(2,128)} %bitcast.9, s32[1,1]{1,0:T(1,128)S(6)} %copy.37.counts, ...), custom_call_target="tpu_custom_call" | custom-call | tf_op jit(solution)/shard_map/start/pallas_call | solution.py:785
  10.0 1.9 %collective-permute-start.2 = (f32[288,128]{1,0:T(8,128)S(1)}, f32[288,128]{1,0:T(8,128)S(1)}, u32[]{:S(2)}, u32[]{:S(2)}) collective-permute-start(f32[288,128]{1,0:T(8,128)S(1)} %get-tuple-element.43), channel_id=1, source_target_pairs={{0,1},{2,3},{4,5},{6,7},{1,0},{3,2},{5,4},{7,6},{8,9},{10,11},{12,... | collective-permute-start | bytes 442376 | tf_op jit(solution)/shard_map/ppermute | solution.py:745
  11.9 3.1 %collective-permute-start.3 = (f32[288,128]{1,0:T(8,128)S(1)}, f32[288,128]{1,0:T(8,128)S(1)}, u32[]{:S(2)}, u32[]{:S(2)}) collective-permute-start(f32[288,128]{1,0:T(8,128)S(1)} %get-tuple-element.44), channel_id=1, source_target_pairs={{1,2},{3,4},{5,6},{2,1},{4,3},{6,5},{9,10},{11,12},{13,14},{10,9},... | collective-permute-start | bytes 442376 | tf_op jit(solution)/shard_map/ppermute | solution.py:745
  15.0 2.3 %shard_map.87 = (f32[2,584,768]{2,1,0:T(8,128)S(1)}, f32[2,584,768]{2,1,0:T(8,128)S(1)}) custom-call(s32[11,25]{1,0:T(8,128)S(4)} %get-tuple-element.37.plan, f32[32,1024]{1,0:T(8,128)S(1)} %collective-permute-done.up, f32[32,1024]{1,0:T(8,128)S(1)} %collective-permute-done.1.down, ...), custom_call_target="tpu_custom_call", output_to_operand_aliasing={{0}: (7, {}), {1}: (8, {})} | custom-call | tf_op jit(solution)/shard_map/pallas_call | solution.py:768
  17.3 1.0 %collective-permute-done.3.right = f32[288,128]{1,0:T(8,128)S(1)} collective-permute-done((f32[288,128]{1,0:T(8,128)S(1)}, f32[288,128]{1,0:T(8,128)S(1)}, u32[]{:S(2)}, u32[]{:S(2)}) %collective-permute-start.3) | collective-permute-done | bytes 147488 | tf_op jit(solution)/shard_map/ppermute | solution.py:745
  18.4 1.7 %shard_map.88 = (f32[2,584,768]{2,1,0:T(8,128)S(1)}, f32[2,584,768]{2,1,0:T(8,128)S(1)}, f32[64,1152]{1,0:T(8,128)S(1)}, f32[64,1152]{1,0:T(8,128)S(1)}) custom-call(s32[11,25]{1,0:T(8,128)S(4)} %get-tuple-element.37.plan, f32[288,128]{1,0:T(8,128)S(1)} %collective-permute-done.2.left, ...), custom_call_target="tpu_custom_call", output_to_operand_aliasing={{0}: (7, {}), {1}: (8, {})} | custom-call | tf_op jit(solution)/shard_map/pallas_call | solution.py:768
  20.8 4.4 %collective-permute-start.5 = (f32[64,1152]{1,0:T(8,128)S(1)}, f32[64,1152]{1,0:T(8,128)S(1)}, u32[]{:S(2)}, u32[]{:S(2)}) collective-permute-start(f32[64,1152]{1,0:T(8,128)S(1)} %get-tuple-element.49), channel_id=1, source_target_pairs={{8,16},{16,8},{9,17},{17,9},{10,18},{18,10},{11,19},{19,11},{12,20... | collective-permute-start | bytes 884744 | tf_op jit(solution)/shard_map/ppermute | solution.py:745
  25.5 2.0 %collective-permute-start.8 = (f32[576,128]{1,0:T(8,128)S(1)}, f32[576,128]{1,0:T(8,128)S(1)}, u32[]{:S(2)}, u32[]{:S(2)}) collective-permute-start(f32[576,128]{1,0:T(8,128)S(1)} %get-tuple-element.56), channel_id=1, source_target_pairs={{0,1},{2,3},{4,5},{6,7},{1,0},{3,2},{5,4},{7,6},{8,9},{10,11},{12,... | collective-permute-start | bytes 884744 | tf_op jit(solution)/shard_map/ppermute | solution.py:745
  27.5 1.9 %collective-permute-start.9 = (f32[576,128]{1,0:T(8,128)S(1)}, f32[576,128]{1,0:T(8,128)S(1)}, u32[]{:S(2)}, u32[]{:S(2)}) collective-permute-start(f32[576,128]{1,0:T(8,128)S(1)} %get-tuple-element.57), channel_id=1, source_target_pairs={{1,2},{3,4},{5,6},{2,1},{4,3},{6,5},{9,10},{11,12},{13,14},{10,9},... | collective-permute-start | bytes 884744 | tf_op jit(solution)/shard_map/ppermute | solution.py:745
  29.4 5.0 %deep.1 = (f32[2,584,768]{2,1,0:T(8,128)S(1)}, f32[2,584,768]{2,1,0:T(8,128)S(1)}, f32[2,512,512]{2,1,0:T(8,128)S(1)}) custom-call(s32[11,25]{1,0:T(8,128)S(4)} %get-tuple-element.37.plan, f32[2,512,512]{2,1,0:T(8,128)} %objects.3, f32[2,128,128]{2,1,0:T(8,128)S(1)} %copy-done, ...), custom_call_target="tpu_custom_call", output_to_operand_aliasing={{0}: (7, {}), {1}: (8, {})} | custom-call | tf_op jit(solution)/shard_map/deep/pallas_call | solution.py:816
  34.4 2.3 %collective-permute-done.5.down = f32[64,1152]{1,0:T(8,128)S(1)} collective-permute-done((f32[64,1152]{1,0:T(8,128)S(1)}, f32[64,1152]{1,0:T(8,128)S(1)}, u32[]{:S(2)}, u32[]{:S(2)}) %collective-permute-start.5) | collective-permute-done | bytes 294944 | tf_op jit(solution)/shard_map/ppermute | solution.py:745
  36.9 0.9 %collective-permute-start.6 = (f32[128,128]{1,0:T(8,128)S(1)}, f32[128,128]{1,0:T(8,128)S(1)}, u32[]{:S(2)}, u32[]{:S(2)}) collective-permute-start(f32[128,128]{1,0:T(8,128)S(1)} %get-tuple-element.54), channel_id=1, source_target_pairs={{0,1},{2,3},{4,5},{6,7},{1,0},{3,2},{5,4},{7,6},{8,9},{10,11},{12,... | collective-permute-start | bytes 196616 | tf_op jit(solution)/shard_map/ppermute | solution.py:745
  37.8 1.9 %collective-permute-start.7 = (f32[128,128]{1,0:T(8,128)S(1)}, f32[128,128]{1,0:T(8,128)S(1)}, u32[]{:S(2)}, u32[]{:S(2)}) collective-permute-start(f32[128,128]{1,0:T(8,128)S(1)} %get-tuple-element.55), channel_id=1, source_target_pairs={{1,2},{3,4},{5,6},{2,1},{4,3},{6,5},{9,10},{11,12},{13,14},{10,9},... | collective-permute-start | bytes 196616 | tf_op jit(solution)/shard_map/ppermute | solution.py:745
  39.8 3.2 %shard_map.91 = (f32[2,584,768]{2,1,0:T(8,128)S(1)}, f32[2,584,768]{2,1,0:T(8,128)S(1)}) custom-call(s32[11,25]{1,0:T(8,128)S(4)} %get-tuple-element.37.plan, f32[2,128,128]{2,1,0:T(8,128)S(1)} %copy-done, f32[2,256,128]{2,1,0:T(8,128)S(1)} %get-tuple-element.38.doubled, ...), custom_call_target="tpu_custom_call", output_to_operand_aliasing={{0}: (10, {}), {1}: (11, {})} | custom-call | tf_op jit(solution)/shard_map/pallas_call | solution.py:768
  43.4 1.8 %shard_map.92 = (f32[2,584,768]{2,1,0:T(8,128)S(1)}, f32[2,584,768]{2,1,0:T(8,128)S(1)}, f32[32,1152]{1,0:T(8,128)S(1)}, f32[32,1152]{1,0:T(8,128)S(1)}, f32[576,128]{1,0:T(8,128)S(1)}, /*index=5*/f32[576,128]{1,0:T(8,128)S(1)}) custom-call(s32[11,25]{1,0:T(8,128)S(4)} %get-tuple-element.37.plan, ...), custom_call_target="tpu_custom_call", output_to_operand_aliasing={{0}: (8, {}), {1}: (9, {})} | custom-call | tf_op jit(solution)/shard_map/pallas_call | solution.py:768
  45.2 1.9 %collective-permute-start.11 = (f32[32,1152]{1,0:T(8,128)S(1)}, f32[32,1152]{1,0:T(8,128)S(1)}, u32[]{:S(2)}, u32[]{:S(2)}) collective-permute-start(f32[32,1152]{1,0:T(8,128)S(1)} %get-tuple-element.62), channel_id=1, source_target_pairs={{8,16},{16,8},{9,17},{17,9},{10,18},{18,10},{11,19},{19,11},{12,20... | collective-permute-start | bytes 442376 | tf_op jit(solution)/shard_map/ppermute | solution.py:745
  47.2 2.3 %shard_map.93.after.acc = f32[2,584,768]{2,1,0:T(8,128)S(1)} custom-call(s32[11,25]{1,0:T(8,128)S(4)} %get-tuple-element.37.plan, f32[2,584,768]{2,1,0:T(8,128)S(1)} %get-tuple-element.65.cur, f32[2,256,128]{2,1,0:T(8,128)S(1)} %get-tuple-element.38.doubled, f32[24,128,128]{2,1,0:T(8,128)S(1)} %get-tuple-element.39.amplitudes, ...), custom_call_target="tpu_custom_call", output_to_operand_aliasing={{}: (6, {})} | custom-call | tf_op jit(solution)/shard_map/pallas_call | solution.py:768
  50.3 2.5 %collective-permute-done.11.down = f32[32,1152]{1,0:T(8,128)S(1)} collective-permute-done((f32[32,1152]{1,0:T(8,128)S(1)}, f32[32,1152]{1,0:T(8,128)S(1)}, u32[]{:S(2)}, u32[]{:S(2)}) %collective-permute-start.11) | collective-permute-done | bytes 147488 | tf_op jit(solution)/shard_map/ppermute | solution.py:745
  53.1 2.3 %collective-permute-start.13 = (f32[256,128]{1,0:T(8,128)S(1)}, f32[256,128]{1,0:T(8,128)S(1)}, u32[]{:S(2)}, u32[]{:S(2)}) collective-permute-start(f32[256,128]{1,0:T(8,128)S(1)} %get-tuple-element.68), channel_id=1, source_target_pairs={{1,2},{3,4},{5,6},{2,1},{4,3},{6,5},{9,10},{11,12},{13,14},{10,9},... | collective-permute-start | bytes 393224 | tf_op jit(solution)/shard_map/ppermute | solution.py:745
  55.4 1.7 %middle.1 = (f32[2,512,512]{2,1,0:T(8,128)}, f32[2,512,512]{2,1,0:T(8,128)}) custom-call(f32[2,128,128]{2,1,0:T(8,128)S(1)} %copy-done, f32[32,1152]{1,0:T(8,128)S(1)} %collective-permute-done.10.up, f32[32,1152]{1,0:T(8,128)S(1)} %collective-permute-done.11.down, f32[2,584,768]{2,1,0:T(8,128)S(1)} %shard_map.93.after.acc, ...), custom_call_target="tpu_custom_call" | custom-call | tf_op jit(solution)/shard_map/middle/pallas_call | solution.py:852
  57.1 2.4 %collective-permute-done.13.right = f32[256,128]{1,0:T(8,128)S(1)} collective-permute-done((f32[256,128]{1,0:T(8,128)S(1)}, f32[256,128]{1,0:T(8,128)S(1)}, u32[]{:S(2)}, u32[]{:S(2)}) %collective-permute-start.13) | collective-permute-done | bytes 131104 | tf_op jit(solution)/shard_map/ppermute | solution.py:745
  59.5 1.6 %finish.1 = (f32[2,512,512]{2,1,0:T(8,128)}, f32[2,512,512]{2,1,0:T(8,128)}) custom-call(f32[2,128,128]{2,1,0:T(8,128)S(1)} %copy-done, f32[32,1152]{1,0:T(8,128)S(1)} %collective-permute-done.10.up, f32[32,1152]{1,0:T(8,128)S(1)} %collective-permute-done.11.down, ...), custom_call_target="tpu_custom_call", output_to_operand_aliasing={{0}: (7, {}), {1}: (8, {})} | custom-call | tf_op jit(solution)/shard_map/finish/pallas_call | solution.py:861
  (21 shorter events, 4.3 us)
Async XLA Ops:
  1.6 7.2 %collective-permute-start.1 = (f32[32,1024]{1,0:T(8,128)S(1)}, f32[32,1024]{1,0:T(8,128)S(1)}, u32[]{:S(2)}, u32[]{:S(2)}) collective-permute-start(f32[32,1024]{1,0:T(8,128)S(1)} %get-tuple-element.76), channel_id=1, source_target_pairs={{8,16},{16,8},{9,17},{17,9},{10,18},{18,10},{11,19},{19,11},{12,20... | collective-permute-start | bytes 393224 | tf_op jit(solution)/shard_map/ppermute | solution.py:745
  4.7 5.0 %collective-permute-start = (f32[32,1024]{1,0:T(8,128)S(1)}, f32[32,1024]{1,0:T(8,128)S(1)}, u32[]{:S(2)}, u32[]{:S(2)}) collective-permute-start(f32[32,1024]{1,0:T(8,128)S(1)} %get-tuple-element.77), channel_id=1, source_target_pairs={{0,8},{16,24},{8,0},{24,16},{1,9},{17,25},{9,1},{25,17},{2,10},{18... | collective-permute-start | bytes 393224 | tf_op jit(solution)/shard_map/ppermute | solution.py:745
  10.0 7.3 %collective-permute-start.2 = (f32[288,128]{1,0:T(8,128)S(1)}, f32[288,128]{1,0:T(8,128)S(1)}, u32[]{:S(2)}, u32[]{:S(2)}) collective-permute-start(f32[288,128]{1,0:T(8,128)S(1)} %get-tuple-element.43), channel_id=1, source_target_pairs={{0,1},{2,3},{4,5},{6,7},{1,0},{3,2},{5,4},{7,6},{8,9},{10,11},{12,... | collective-permute-start | bytes 442376 | tf_op jit(solution)/shard_map/ppermute | solution.py:745
  11.9 6.5 %collective-permute-start.3 = (f32[288,128]{1,0:T(8,128)S(1)}, f32[288,128]{1,0:T(8,128)S(1)}, u32[]{:S(2)}, u32[]{:S(2)}) collective-permute-start(f32[288,128]{1,0:T(8,128)S(1)} %get-tuple-element.44), channel_id=1, source_target_pairs={{1,2},{3,4},{5,6},{2,1},{4,3},{6,5},{9,10},{11,12},{13,14},{10,9},... | collective-permute-start | bytes 442376 | tf_op jit(solution)/shard_map/ppermute | solution.py:745
  20.1 14.3 %collective-permute-start.4 = (f32[64,1152]{1,0:T(8,128)S(1)}, f32[64,1152]{1,0:T(8,128)S(1)}, u32[]{:S(2)}, u32[]{:S(2)}) collective-permute-start(f32[64,1152]{1,0:T(8,128)S(1)} %get-tuple-element.48), channel_id=1, source_target_pairs={{0,8},{16,24},{8,0},{24,16},{1,9},{17,25},{9,1},{25,17},{2,10},{18... | collective-permute-start | bytes 884744 | tf_op jit(solution)/shard_map/ppermute | solution.py:745
  20.8 15.9 %collective-permute-start.5 = (f32[64,1152]{1,0:T(8,128)S(1)}, f32[64,1152]{1,0:T(8,128)S(1)}, u32[]{:S(2)}, u32[]{:S(2)}) collective-permute-start(f32[64,1152]{1,0:T(8,128)S(1)} %get-tuple-element.49), channel_id=1, source_target_pairs={{8,16},{16,8},{9,17},{17,9},{10,18},{18,10},{11,19},{19,11},{12,20... | collective-permute-start | bytes 884744 | tf_op jit(solution)/shard_map/ppermute | solution.py:745
  25.2 4.2 %copy-start = (f32[2,128,128]{2,1,0:T(8,128)S(1)}, f32[2,128,128]{2,1,0:T(8,128)}, u32[]{:S(2)}) copy-start(f32[2,128,128]{2,1,0:T(8,128)} %probe.9) | copy-start | bytes 393220
  25.5 14.3 %collective-permute-start.8 = (f32[576,128]{1,0:T(8,128)S(1)}, f32[576,128]{1,0:T(8,128)S(1)}, u32[]{:S(2)}, u32[]{:S(2)}) collective-permute-start(f32[576,128]{1,0:T(8,128)S(1)} %get-tuple-element.56), channel_id=1, source_target_pairs={{0,1},{2,3},{4,5},{6,7},{1,0},{3,2},{5,4},{7,6},{8,9},{10,11},{12,... | collective-permute-start | bytes 884744 | tf_op jit(solution)/shard_map/ppermute | solution.py:745
  27.5 12.3 %collective-permute-start.9 = (f32[576,128]{1,0:T(8,128)S(1)}, f32[576,128]{1,0:T(8,128)S(1)}, u32[]{:S(2)}, u32[]{:S(2)}) collective-permute-start(f32[576,128]{1,0:T(8,128)S(1)} %get-tuple-element.57), channel_id=1, source_target_pairs={{1,2},{3,4},{5,6},{2,1},{4,3},{6,5},{9,10},{11,12},{13,14},{10,9},... | collective-permute-start | bytes 884744 | tf_op jit(solution)/shard_map/ppermute | solution.py:745
  36.9 6.1 %collective-permute-start.6 = (f32[128,128]{1,0:T(8,128)S(1)}, f32[128,128]{1,0:T(8,128)S(1)}, u32[]{:S(2)}, u32[]{:S(2)}) collective-permute-start(f32[128,128]{1,0:T(8,128)S(1)} %get-tuple-element.54), channel_id=1, source_target_pairs={{0,1},{2,3},{4,5},{6,7},{1,0},{3,2},{5,4},{7,6},{8,9},{10,11},{12,... | collective-permute-start | bytes 196616 | tf_op jit(solution)/shard_map/ppermute | solution.py:745
  37.8 5.6 %collective-permute-start.7 = (f32[128,128]{1,0:T(8,128)S(1)}, f32[128,128]{1,0:T(8,128)S(1)}, u32[]{:S(2)}, u32[]{:S(2)}) collective-permute-start(f32[128,128]{1,0:T(8,128)S(1)} %get-tuple-element.55), channel_id=1, source_target_pairs={{1,2},{3,4},{5,6},{2,1},{4,3},{6,5},{9,10},{11,12},{13,14},{10,9},... | collective-permute-start | bytes 196616 | tf_op jit(solution)/shard_map/ppermute | solution.py:745
  45.2 5.1 %collective-permute-start.10 = (f32[32,1152]{1,0:T(8,128)S(1)}, f32[32,1152]{1,0:T(8,128)S(1)}, u32[]{:S(2)}, u32[]{:S(2)}) collective-permute-start(f32[32,1152]{1,0:T(8,128)S(1)} %get-tuple-element.61), channel_id=1, source_target_pairs={{0,8},{16,24},{8,0},{24,16},{1,9},{17,25},{9,1},{25,17},{2,10},{18... | collective-permute-start | bytes 442376 | tf_op jit(solution)/shard_map/ppermute | solution.py:745
  45.2 7.5 %collective-permute-start.11 = (f32[32,1152]{1,0:T(8,128)S(1)}, f32[32,1152]{1,0:T(8,128)S(1)}, u32[]{:S(2)}, u32[]{:S(2)}) collective-permute-start(f32[32,1152]{1,0:T(8,128)S(1)} %get-tuple-element.62), channel_id=1, source_target_pairs={{8,16},{16,8},{9,17},{17,9},{10,18},{18,10},{11,19},{19,11},{12,20... | collective-permute-start | bytes 442376 | tf_op jit(solution)/shard_map/ppermute | solution.py:745
  53.0 4.0 %collective-permute-start.12 = (f32[256,128]{1,0:T(8,128)S(1)}, f32[256,128]{1,0:T(8,128)S(1)}, u32[]{:S(2)}, u32[]{:S(2)}) collective-permute-start(f32[256,128]{1,0:T(8,128)S(1)} %get-tuple-element.67), channel_id=1, source_target_pairs={{0,1},{2,3},{4,5},{6,7},{1,0},{3,2},{5,4},{7,6},{8,9},{10,11},{12,... | collective-permute-start | bytes 393224 | tf_op jit(solution)/shard_map/ppermute | solution.py:745
  53.1 6.4 %collective-permute-start.13 = (f32[256,128]{1,0:T(8,128)S(1)}, f32[256,128]{1,0:T(8,128)S(1)}, u32[]{:S(2)}, u32[]{:S(2)}) collective-permute-start(f32[256,128]{1,0:T(8,128)S(1)} %get-tuple-element.68), channel_id=1, source_target_pairs={{1,2},{3,4},{5,6},{2,1},{4,3},{6,5},{9,10},{11,12},{13,14},{10,9},... | collective-permute-start | bytes 393224 | tf_op jit(solution)/shard_map/ppermute | solution.py:745

commit v11 on v10

--- a/solution.py
+++ b/solution.py
@@ -170,7 +170,9 @@
         side_stop = jnp.minimum(extend(Plan.SIDE, early, Plan.DEEP, 0, deep), round_up(early))
         done = side_stop - early
         second_end = extend(Plan.SECOND, reaching, Plan.RIM, 0, rim)
-        second_stop = jnp.minimum(second_end, round_up(reaching))
+        second_stop = jnp.where(
+            reaching <= MIDDLE, reaching, jnp.minimum(second_end, round_up(reaching))
+        )
 
         def deep_taken(groups):
             room = (groups - (deep - done + LARGE - 1) // LARGE) * LARGE
@@ -585,9 +587,11 @@
                 acc[plane, :extent, out] + jnp.where(keep_out, band, 0.0)
             )
             acc[plane, :extent, out] = jnp.zeros_like(acc[plane, :extent, out])
+    stop = plan[Plan.NUMBER, Plan.SECOND_STOP]
+    few = jnp.where(stop <= MIDDLE, stop, 0)
+    few_slots(cur, acc, doubled, amplitudes, plan, Plan.SECOND, few, (forth, back))
     gradient_slots(
-        cur, acc, doubled, amplitudes, plan, Plan.SECOND, 0, plan[Plan.NUMBER, Plan.SECOND_STOP],
-        (forth, back),
+        cur, acc, doubled, amplitudes, plan, Plan.SECOND, few, stop, (forth, back)
     )
 
 

time: 61.6 us -> 61.9 us (level)
  the two profiles are of different devices: /device:TPU:21 before, /device:TPU:5 now
where the time goes in v11:
time: 61.9 us; the launch traced here: 61.5 us
  Pallas kernels  28.7 us (46%)
  starting transfers between devices  25 us (40%)
  waiting for transfers between devices  5.11 us (8%)
  between operations  1.73 us (3%)
  local copies, waits for them, and re-layouts  0.96 us (2%)
    ppermute x14, starting transfers between devices, swap(): return in_vmem(lax.ppermute(array, axis, ends + [(j, i) for i, j in ends]))  25 us
    pallas_call x9, Pallas kernels, call(): pl.pallas_call(kernel, out_shape=outs, in_specs=[SMEM] * len(scalars) + [...  15 us
    pallas_call x1, Pallas kernels, on_device(): pl.pallas_call(deep_kernel, out_shape=(padded, padded, f32(2, tile, width...  7.28 us
    ppermute x14, waiting for transfers between devices, swap(): return in_vmem(lax.ppermute(array, axis, ends + [(j, i) for i, j in ends]))  5.11 us
    pallas_call x1, Pallas kernels, on_device(): pl.pallas_call(start_kernel, out_shape=(padded, padded, doubled_shape, f3...  3.16 us
    pallas_call x1, Pallas kernels, on_device(): pl.pallas_call(middle_kernel, out_shape=(result, result), in_specs=[VMEM]...  1.67 us
    pallas_call x1, Pallas kernels, on_device(): pl.pallas_call(last_kernel, out_shape=(result, result), in_specs=[VMEM] *...  1.63 us
  transfers between devices with their start and end apart: 14, of which 5 were waited for; matrix products, arithmetic and copies ran while one was open for 0% of the time, Pallas kernels for 37%

profile of v11, /device:TPU:5, one launch (start us, length us, event | category | flops | bytes accessed | tf_op | source)
XLA Modules:
  0.0 61.5 jit_solution(9934567765337025244)
XLA Ops:
  0.6 1.0 %slice_bitcast_fusion.3 = (f32[32,512]{1,0:T(8,128)S(1)}, f32[32,512]{1,0:T(8,128)S(1)}, f32[32,512]{1,0:T(8,128)S(1)}, f32[32,512]{1,0:T(8,128)S(1)}) fusion(f32[2,512,512]{2,1,0:T(8,128)} %objects.3), kind=kLoop, calls=%fused_computation.7 | loop fusion | bytes 524288 | tf_op jit(solution)/shard_map/squeeze | solution.py:784
  1.6 3.1 %collective-permute-start.1 = (f32[32,1024]{1,0:T(8,128)S(1)}, f32[32,1024]{1,0:T(8,128)S(1)}, u32[]{:S(2)}, u32[]{:S(2)}) collective-permute-start(f32[32,1024]{1,0:T(8,128)S(1)} %get-tuple-element.76), channel_id=1, source_target_pairs={{8,16},{16,8},{9,17},{17,9},{10,18},{18,10},{11,19},{19,11},{12,20... | collective-permute-start | bytes 393224 | tf_op jit(solution)/shard_map/ppermute | solution.py:749
  5.4 3.2 %start.1 = (f32[2,584,768]{2,1,0:T(8,128)S(1)}, f32[2,584,768]{2,1,0:T(8,128)S(1)}, f32[2,256,128]{2,1,0:T(8,128)S(1)}, f32[24,128,128]{2,1,0:T(8,128)S(1)}, s32...) custom-call(s32[2,24]{1,0:T(2,128)} %bitcast.9, s32[1,1]{1,0:T(1,128)S(6)} %copy.37.counts, ...), custom_call_target="tpu_custom_call" | custom-call | tf_op jit(solution)/shard_map/start/pallas_call | solution.py:789
  8.8 0.9 %collective-permute-done.up = f32[32,1024]{1,0:T(8,128)S(1)} collective-permute-done((f32[32,1024]{1,0:T(8,128)S(1)}, f32[32,1024]{1,0:T(8,128)S(1)}, u32[]{:S(2)}, u32[]{:S(2)}) %collective-permute-start) | collective-permute-done | bytes 131104 | tf_op jit(solution)/shard_map/ppermute | solution.py:749
  10.0 1.9 %collective-permute-start.2 = (f32[288,128]{1,0:T(8,128)S(1)}, f32[288,128]{1,0:T(8,128)S(1)}, u32[]{:S(2)}, u32[]{:S(2)}) collective-permute-start(f32[288,128]{1,0:T(8,128)S(1)} %get-tuple-element.43), channel_id=1, source_target_pairs={{0,1},{2,3},{4,5},{6,7},{1,0},{3,2},{5,4},{7,6},{8,9},{10,11},{12,... | collective-permute-start | bytes 442376 | tf_op jit(solution)/shard_map/ppermute | solution.py:749
  11.9 3.1 %collective-permute-start.3 = (f32[288,128]{1,0:T(8,128)S(1)}, f32[288,128]{1,0:T(8,128)S(1)}, u32[]{:S(2)}, u32[]{:S(2)}) collective-permute-start(f32[288,128]{1,0:T(8,128)S(1)} %get-tuple-element.44), channel_id=1, source_target_pairs={{1,2},{3,4},{5,6},{2,1},{4,3},{6,5},{9,10},{11,12},{13,14},{10,9},... | collective-permute-start | bytes 442376 | tf_op jit(solution)/shard_map/ppermute | solution.py:749
  15.0 2.3 %shard_map.87 = (f32[2,584,768]{2,1,0:T(8,128)S(1)}, f32[2,584,768]{2,1,0:T(8,128)S(1)}) custom-call(s32[11,25]{1,0:T(8,128)S(4)} %get-tuple-element.37.plan, f32[32,1024]{1,0:T(8,128)S(1)} %collective-permute-done.up, f32[32,1024]{1,0:T(8,128)S(1)} %collective-permute-done.1.down, ...), custom_call_target="tpu_custom_call", output_to_operand_aliasing={{0}: (7, {}), {1}: (8, {})} | custom-call | tf_op jit(solution)/shard_map/pallas_call | solution.py:772
  17.3 1.0 %collective-permute-done.3.right = f32[288,128]{1,0:T(8,128)S(1)} collective-permute-done((f32[288,128]{1,0:T(8,128)S(1)}, f32[288,128]{1,0:T(8,128)S(1)}, u32[]{:S(2)}, u32[]{:S(2)}) %collective-permute-start.3) | collective-permute-done | bytes 147488 | tf_op jit(solution)/shard_map/ppermute | solution.py:749
  18.4 1.7 %shard_map.88 = (f32[2,584,768]{2,1,0:T(8,128)S(1)}, f32[2,584,768]{2,1,0:T(8,128)S(1)}, f32[64,1152]{1,0:T(8,128)S(1)}, f32[64,1152]{1,0:T(8,128)S(1)}) custom-call(s32[11,25]{1,0:T(8,128)S(4)} %get-tuple-element.37.plan, f32[288,128]{1,0:T(8,128)S(1)} %collective-permute-done.2.left, ...), custom_call_target="tpu_custom_call", output_to_operand_aliasing={{0}: (7, {}), {1}: (8, {})} | custom-call | tf_op jit(solution)/shard_map/pallas_call | solution.py:772
  20.1 1.0 %collective-permute-start.4 = (f32[64,1152]{1,0:T(8,128)S(1)}, f32[64,1152]{1,0:T(8,128)S(1)}, u32[]{:S(2)}, u32[]{:S(2)}) collective-permute-start(f32[64,1152]{1,0:T(8,128)S(1)} %get-tuple-element.48), channel_id=1, source_target_pairs={{0,8},{16,24},{8,0},{24,16},{1,9},{17,25},{9,1},{25,17},{2,10},{18... | collective-permute-start | bytes 884744 | tf_op jit(solution)/shard_map/ppermute | solution.py:749
  21.1 3.1 %collective-permute-start.5 = (f32[64,1152]{1,0:T(8,128)S(1)}, f32[64,1152]{1,0:T(8,128)S(1)}, u32[]{:S(2)}, u32[]{:S(2)}) collective-permute-start(f32[64,1152]{1,0:T(8,128)S(1)} %get-tuple-element.49), channel_id=1, source_target_pairs={{8,16},{16,8},{9,17},{17,9},{10,18},{18,10},{11,19},{19,11},{12,20... | collective-permute-start | bytes 884744 | tf_op jit(solution)/shard_map/ppermute | solution.py:749
  24.2 1.6 %shard_map.89 = (f32[2,584,768]{2,1,0:T(8,128)S(1)}, f32[576,128]{1,0:T(8,128)S(1)}, f32[576,128]{1,0:T(8,128)S(1)}) custom-call(s32[11,25]{1,0:T(8,128)S(4)} %get-tuple-element.37.plan, f32[2,584,768]{2,1,0:T(8,128)S(1)} %get-tuple-element.50.cur.cur_in, f32[2,256,128]{2,1,0:T(8,128)S(1)} %get-tuple-element.38.doubled, ...), custom_call_target="tpu_custom_call", output_to_operand_aliasing={{0}: (6, {})} | custom-call | tf_op jit(solution)/shard_map/pallas_call | solution.py:772
  25.9 3.4 %collective-permute-start.9 = (f32[576,128]{1,0:T(8,128)S(1)}, f32[576,128]{1,0:T(8,128)S(1)}, u32[]{:S(2)}, u32[]{:S(2)}) collective-permute-start(f32[576,128]{1,0:T(8,128)S(1)} %get-tuple-element.57), channel_id=1, source_target_pairs={{1,2},{3,4},{5,6},{2,1},{4,3},{6,5},{9,10},{11,12},{13,14},{10,9},... | collective-permute-start | bytes 884744 | tf_op jit(solution)/shard_map/ppermute | solution.py:749
  29.3 7.3 %deep.1 = (f32[2,584,768]{2,1,0:T(8,128)S(1)}, f32[2,584,768]{2,1,0:T(8,128)S(1)}, f32[2,512,512]{2,1,0:T(8,128)S(1)}) custom-call(s32[11,25]{1,0:T(8,128)S(4)} %get-tuple-element.37.plan, f32[2,512,512]{2,1,0:T(8,128)} %objects.3, f32[2,128,128]{2,1,0:T(8,128)S(1)} %copy-done, ...), custom_call_target="tpu_custom_call", output_to_operand_aliasing={{0}: (7, {}), {1}: (8, {})} | custom-call | tf_op jit(solution)/shard_map/deep/pallas_call | solution.py:820
  36.9 2.8 %collective-permute-start.7 = (f32[128,128]{1,0:T(8,128)S(1)}, f32[128,128]{1,0:T(8,128)S(1)}, u32[]{:S(2)}, u32[]{:S(2)}) collective-permute-start(f32[128,128]{1,0:T(8,128)S(1)} %get-tuple-element.55), channel_id=1, source_target_pairs={{1,2},{3,4},{5,6},{2,1},{4,3},{6,5},{9,10},{11,12},{13,14},{10,9},... | collective-permute-start | bytes 196616 | tf_op jit(solution)/shard_map/ppermute | solution.py:749
  39.6 2.3 %shard_map.91 = (f32[2,584,768]{2,1,0:T(8,128)S(1)}, f32[2,584,768]{2,1,0:T(8,128)S(1)}) custom-call(s32[11,25]{1,0:T(8,128)S(4)} %get-tuple-element.37.plan, f32[2,128,128]{2,1,0:T(8,128)S(1)} %copy-done, f32[2,256,128]{2,1,0:T(8,128)S(1)} %get-tuple-element.38.doubled, ...), custom_call_target="tpu_custom_call", output_to_operand_aliasing={{0}: (10, {}), {1}: (11, {})} | custom-call | tf_op jit(solution)/shard_map/pallas_call | solution.py:772
  41.9 0.5 collective-permute-done.7.right
  42.4 1.8 %shard_map.92 = (f32[2,584,768]{2,1,0:T(8,128)S(1)}, f32[2,584,768]{2,1,0:T(8,128)S(1)}, f32[32,1152]{1,0:T(8,128)S(1)}, f32[32,1152]{1,0:T(8,128)S(1)}, f32[576,128]{1,0:T(8,128)S(1)}, /*index=5*/f32[576,128]{1,0:T(8,128)S(1)}) custom-call(s32[11,25]{1,0:T(8,128)S(4)} %get-tuple-element.37.plan, ...), custom_call_target="tpu_custom_call", output_to_operand_aliasing={{0}: (8, {}), {1}: (9, {})} | custom-call | tf_op jit(solution)/shard_map/pallas_call | solution.py:772
  44.3 4.3 %collective-permute-start.11 = (f32[32,1152]{1,0:T(8,128)S(1)}, f32[32,1152]{1,0:T(8,128)S(1)}, u32[]{:S(2)}, u32[]{:S(2)}) collective-permute-start(f32[32,1152]{1,0:T(8,128)S(1)} %get-tuple-element.62), channel_id=1, source_target_pairs={{8,16},{16,8},{9,17},{17,9},{10,18},{18,10},{11,19},{19,11},{12,20... | collective-permute-start | bytes 442376 | tf_op jit(solution)/shard_map/ppermute | solution.py:749
  48.6 4.5 %shard_map.93.after.acc = f32[2,584,768]{2,1,0:T(8,128)S(1)} custom-call(s32[11,25]{1,0:T(8,128)S(4)} %get-tuple-element.37.plan, f32[2,584,768]{2,1,0:T(8,128)S(1)} %get-tuple-element.65.cur, f32[2,256,128]{2,1,0:T(8,128)S(1)} %get-tuple-element.38.doubled, f32[24,128,128]{2,1,0:T(8,128)S(1)} %get-tuple-element.39.amplitudes, ...), custom_call_target="tpu_custom_call", output_to_operand_aliasing={{}: (6, {})} | custom-call | tf_op jit(solution)/shard_map/pallas_call | solution.py:772
  53.5 2.1 %collective-permute-start.13 = (f32[256,128]{1,0:T(8,128)S(1)}, f32[256,128]{1,0:T(8,128)S(1)}, u32[]{:S(2)}, u32[]{:S(2)}) collective-permute-start(f32[256,128]{1,0:T(8,128)S(1)} %get-tuple-element.68), channel_id=1, source_target_pairs={{1,2},{3,4},{5,6},{2,1},{4,3},{6,5},{9,10},{11,12},{13,14},{10,9},... | collective-permute-start | bytes 393224 | tf_op jit(solution)/shard_map/ppermute | solution.py:749
  55.6 1.7 %middle.1 = (f32[2,512,512]{2,1,0:T(8,128)}, f32[2,512,512]{2,1,0:T(8,128)}) custom-call(f32[2,128,128]{2,1,0:T(8,128)S(1)} %copy-done, f32[32,1152]{1,0:T(8,128)S(1)} %collective-permute-done.10.up, f32[32,1152]{1,0:T(8,128)S(1)} %collective-permute-done.11.down, f32[2,584,768]{2,1,0:T(8,128)S(1)} %shard_map.93.after.acc, ...), custom_call_target="tpu_custom_call" | custom-call | tf_op jit(solution)/shard_map/middle/pallas_call | solution.py:856
  57.3 2.5 %collective-permute-done.13.right = f32[256,128]{1,0:T(8,128)S(1)} collective-permute-done((f32[256,128]{1,0:T(8,128)S(1)}, f32[256,128]{1,0:T(8,128)S(1)}, u32[]{:S(2)}, u32[]{:S(2)}) %collective-permute-start.13) | collective-permute-done | bytes 131104 | tf_op jit(solution)/shard_map/ppermute | solution.py:749
  59.7 1.6 %finish.1 = (f32[2,512,512]{2,1,0:T(8,128)}, f32[2,512,512]{2,1,0:T(8,128)}) custom-call(f32[2,128,128]{2,1,0:T(8,128)S(1)} %copy-done, f32[32,1152]{1,0:T(8,128)S(1)} %collective-permute-done.10.up, f32[32,1152]{1,0:T(8,128)S(1)} %collective-permute-done.11.down, ...), custom_call_target="tpu_custom_call", output_to_operand_aliasing={{0}: (7, {}), {1}: (8, {})} | custom-call | tf_op jit(solution)/shard_map/finish/pallas_call | solution.py:865
  (21 shorter events, 1.4 us)
Async XLA Ops:
  1.6 7.2 %collective-permute-start.1 = (f32[32,1024]{1,0:T(8,128)S(1)}, f32[32,1024]{1,0:T(8,128)S(1)}, u32[]{:S(2)}, u32[]{:S(2)}) collective-permute-start(f32[32,1024]{1,0:T(8,128)S(1)} %get-tuple-element.76), channel_id=1, source_target_pairs={{8,16},{16,8},{9,17},{17,9},{10,18},{18,10},{11,19},{19,11},{12,20... | collective-permute-start | bytes 393224 | tf_op jit(solution)/shard_map/ppermute | solution.py:749
  4.7 5.0 %collective-permute-start = (f32[32,1024]{1,0:T(8,128)S(1)}, f32[32,1024]{1,0:T(8,128)S(1)}, u32[]{:S(2)}, u32[]{:S(2)}) collective-permute-start(f32[32,1024]{1,0:T(8,128)S(1)} %get-tuple-element.77), channel_id=1, source_target_pairs={{0,8},{16,24},{8,0},{24,16},{1,9},{17,25},{9,1},{25,17},{2,10},{18... | collective-permute-start | bytes 393224 | tf_op jit(solution)/shard_map/ppermute | solution.py:749
  10.0 7.3 %collective-permute-start.2 = (f32[288,128]{1,0:T(8,128)S(1)}, f32[288,128]{1,0:T(8,128)S(1)}, u32[]{:S(2)}, u32[]{:S(2)}) collective-permute-start(f32[288,128]{1,0:T(8,128)S(1)} %get-tuple-element.43), channel_id=1, source_target_pairs={{0,1},{2,3},{4,5},{6,7},{1,0},{3,2},{5,4},{7,6},{8,9},{10,11},{12,... | collective-permute-start | bytes 442376 | tf_op jit(solution)/shard_map/ppermute | solution.py:749
  11.9 6.5 %collective-permute-start.3 = (f32[288,128]{1,0:T(8,128)S(1)}, f32[288,128]{1,0:T(8,128)S(1)}, u32[]{:S(2)}, u32[]{:S(2)}) collective-permute-start(f32[288,128]{1,0:T(8,128)S(1)} %get-tuple-element.44), channel_id=1, source_target_pairs={{1,2},{3,4},{5,6},{2,1},{4,3},{6,5},{9,10},{11,12},{13,14},{10,9},... | collective-permute-start | bytes 442376 | tf_op jit(solution)/shard_map/ppermute | solution.py:749
  20.1 16.5 %collective-permute-start.4 = (f32[64,1152]{1,0:T(8,128)S(1)}, f32[64,1152]{1,0:T(8,128)S(1)}, u32[]{:S(2)}, u32[]{:S(2)}) collective-permute-start(f32[64,1152]{1,0:T(8,128)S(1)} %get-tuple-element.48), channel_id=1, source_target_pairs={{0,8},{16,24},{8,0},{24,16},{1,9},{17,25},{9,1},{25,17},{2,10},{18... | collective-permute-start | bytes 884744 | tf_op jit(solution)/shard_map/ppermute | solution.py:749
  21.1 15.5 %collective-permute-start.5 = (f32[64,1152]{1,0:T(8,128)S(1)}, f32[64,1152]{1,0:T(8,128)S(1)}, u32[]{:S(2)}, u32[]{:S(2)}) collective-permute-start(f32[64,1152]{1,0:T(8,128)S(1)} %get-tuple-element.49), channel_id=1, source_target_pairs={{8,16},{16,8},{9,17},{17,9},{10,18},{18,10},{11,19},{19,11},{12,20... | collective-permute-start | bytes 884744 | tf_op jit(solution)/shard_map/ppermute | solution.py:749
  24.2 5.1 %copy-start = (f32[2,128,128]{2,1,0:T(8,128)S(1)}, f32[2,128,128]{2,1,0:T(8,128)}, u32[]{:S(2)}) copy-start(f32[2,128,128]{2,1,0:T(8,128)} %probe.9) | copy-start | bytes 393220
  25.8 13.8 %collective-permute-start.8 = (f32[576,128]{1,0:T(8,128)S(1)}, f32[576,128]{1,0:T(8,128)S(1)}, u32[]{:S(2)}, u32[]{:S(2)}) collective-permute-start(f32[576,128]{1,0:T(8,128)S(1)} %get-tuple-element.56), channel_id=1, source_target_pairs={{0,1},{2,3},{4,5},{6,7},{1,0},{3,2},{5,4},{7,6},{8,9},{10,11},{12,... | collective-permute-start | bytes 884744 | tf_op jit(solution)/shard_map/ppermute | solution.py:749
  25.9 13.8 %collective-permute-start.9 = (f32[576,128]{1,0:T(8,128)S(1)}, f32[576,128]{1,0:T(8,128)S(1)}, u32[]{:S(2)}, u32[]{:S(2)}) collective-permute-start(f32[576,128]{1,0:T(8,128)S(1)} %get-tuple-element.57), channel_id=1, source_target_pairs={{1,2},{3,4},{5,6},{2,1},{4,3},{6,5},{9,10},{11,12},{13,14},{10,9},... | collective-permute-start | bytes 884744 | tf_op jit(solution)/shard_map/ppermute | solution.py:749
  36.8 5.1 %collective-permute-start.6 = (f32[128,128]{1,0:T(8,128)S(1)}, f32[128,128]{1,0:T(8,128)S(1)}, u32[]{:S(2)}, u32[]{:S(2)}) collective-permute-start(f32[128,128]{1,0:T(8,128)S(1)} %get-tuple-element.54), channel_id=1, source_target_pairs={{0,1},{2,3},{4,5},{6,7},{1,0},{3,2},{5,4},{7,6},{8,9},{10,11},{12,... | collective-permute-start | bytes 196616 | tf_op jit(solution)/shard_map/ppermute | solution.py:749
  36.9 5.6 %collective-permute-start.7 = (f32[128,128]{1,0:T(8,128)S(1)}, f32[128,128]{1,0:T(8,128)S(1)}, u32[]{:S(2)}, u32[]{:S(2)}) collective-permute-start(f32[128,128]{1,0:T(8,128)S(1)} %get-tuple-element.55), channel_id=1, source_target_pairs={{1,2},{3,4},{5,6},{2,1},{4,3},{6,5},{9,10},{11,12},{13,14},{10,9},... | collective-permute-start | bytes 196616 | tf_op jit(solution)/shard_map/ppermute | solution.py:749
  44.2 8.9 %collective-permute-start.10 = (f32[32,1152]{1,0:T(8,128)S(1)}, f32[32,1152]{1,0:T(8,128)S(1)}, u32[]{:S(2)}, u32[]{:S(2)}) collective-permute-start(f32[32,1152]{1,0:T(8,128)S(1)} %get-tuple-element.61), channel_id=1, source_target_pairs={{0,8},{16,24},{8,0},{24,16},{1,9},{17,25},{9,1},{25,17},{2,10},{18... | collective-permute-start | bytes 442376 | tf_op jit(solution)/shard_map/ppermute | solution.py:749
  44.3 8.9 %collective-permute-start.11 = (f32[32,1152]{1,0:T(8,128)S(1)}, f32[32,1152]{1,0:T(8,128)S(1)}, u32[]{:S(2)}, u32[]{:S(2)}) collective-permute-start(f32[32,1152]{1,0:T(8,128)S(1)} %get-tuple-element.62), channel_id=1, source_target_pairs={{8,16},{16,8},{9,17},{17,9},{10,18},{18,10},{11,19},{19,11},{12,20... | collective-permute-start | bytes 442376 | tf_op jit(solution)/shard_map/ppermute | solution.py:749
  53.4 3.8 %collective-permute-start.12 = (f32[256,128]{1,0:T(8,128)S(1)}, f32[256,128]{1,0:T(8,128)S(1)}, u32[]{:S(2)}, u32[]{:S(2)}) collective-permute-start(f32[256,128]{1,0:T(8,128)S(1)} %get-tuple-element.67), channel_id=1, source_target_pairs={{0,1},{2,3},{4,5},{6,7},{1,0},{3,2},{5,4},{7,6},{8,9},{10,11},{12,... | collective-permute-start | bytes 393224 | tf_op jit(solution)/shard_map/ppermute | solution.py:749
  53.5 6.3 %collective-permute-start.13 = (f32[256,128]{1,0:T(8,128)S(1)}, f32[256,128]{1,0:T(8,128)S(1)}, u32[]{:S(2)}, u32[]{:S(2)}) collective-permute-start(f32[256,128]{1,0:T(8,128)S(1)} %get-tuple-element.68), channel_id=1, source_target_pairs={{1,2},{3,4},{5,6},{2,1},{4,3},{6,5},{9,10},{11,12},{13,14},{10,9},... | collective-permute-start | bytes 393224 | tf_op jit(solution)/shard_map/ppermute | solution.py:749
